TPU v7x, 32 devices: a whole 2x2x4 slice. The times are simulated.
32 devices in a mesh: batch: 8 (over z, y), seq: 4 (over x, core).
Axes of the slice: x: 2, y: 2, z: 4, core: 2. Of those that a mesh axis runs over, the one named last changes fastest.
Arguments:
- encoder_layer_input: bfloat16 [8, 1024, 768], P('batch', 'seq'), may hold values from -6 to 6
- decoder_layer_input: bfloat16 [8, 512, 768], P('batch', 'seq'), may hold values from -6 to 6
- cotangent: bfloat16 [8, 512, 768], P('batch', 'seq'), may hold values from -6 to 6
- encoder_used_lengths: int32 [8], P('batch'), may hold values from 512 to 1024, as said below
- decoder_used_lengths: int32 [8], P('batch'), may hold values from 128 to 512, as said below
- attn_master: float32 [9216, 768], P(('batch', 'seq'))
- inner_master: float32 [3072, 2048], P(('batch', 'seq')), may hold values from -0.21875 to 0.21875
- outer_master: float32 [4096, 768], P(('batch', 'seq')), may hold values from -0.125 to 0.125
- gain_master: float32 [4608], P(('batch', 'seq')), may hold values from 0.5 to 1.5
- attn_first: float32 [9216, 768], P(('batch', 'seq')), may hold values from -512 to 512
- inner_first: float32 [3072, 2048], P(('batch', 'seq')), may hold values from -512 to 512
- outer_first: float32 [4096, 768], P(('batch', 'seq')), may hold values from -512 to 512
- gain_first: float32 [4608], P(('batch', 'seq')), may hold values from -512 to 512
- attn_second: float32 [9216, 768], P(('batch', 'seq')), may hold values from 8192 to 32768
- inner_second: float32 [3072, 2048], P(('batch', 'seq')), may hold values from 8192 to 32768
- outer_second: float32 [4096, 768], P(('batch', 'seq')), may hold values from 8192 to 32768
- gain_second: float32 [4608], P(('batch', 'seq')), may hold values from 8192 to 32768
Outputs:
- decoder_layer_output: bfloat16 [8, 512, 768], P('batch', 'seq')
- encoder_input_gradient: float32 [8, 1024, 768], P('batch', 'seq')
- decoder_input_gradient: float32 [8, 512, 768], P('batch', 'seq')
- attn_grad: float32 [9216, 768], P(('batch', 'seq'))
- inner_grad: float32 [3072, 2048], P(('batch', 'seq'))
- outer_grad: float32 [4096, 768], P(('batch', 'seq'))
- gain_grad: float32 [4608], P(('batch', 'seq'))
- attn_first_new: float32 [9216, 768], P(('batch', 'seq'))
- inner_first_new: float32 [3072, 2048], P(('batch', 'seq'))
- outer_first_new: float32 [4096, 768], P(('batch', 'seq'))
- gain_first_new: float32 [4608], P(('batch', 'seq'))
- attn_second_new: float32 [9216, 768], P(('batch', 'seq'))
- inner_second_new: float32 [3072, 2048], P(('batch', 'seq'))
- outer_second_new: float32 [4096, 768], P(('batch', 'seq'))
- gain_second_new: float32 [4608], P(('batch', 'seq'))
- attn_new: float32 [9216, 768], P(('batch', 'seq'))
- inner_new: float32 [3072, 2048], P(('batch', 'seq'))
- outer_new: float32 [4096, 768], P(('batch', 'seq'))
- gain_new: float32 [4608], P(('batch', 'seq'))
- attn_copy: bfloat16 [9216, 768], P(('batch', 'seq'))
- inner_copy: bfloat16 [3072, 2048], P(('batch', 'seq'))
- outer_copy: bfloat16 [4096, 768], P(('batch', 'seq'))
- gain_copy: bfloat16 [4608], P(('batch', 'seq'))
- weight_norms: float32 [24], replicated
- update_norms: float32 [24], replicated
Inputs may be any that keep to these rules, and one draw needn't show every extreme that they name: `encoder_used_lengths`: some sequence uses all 1024 encoder positions. `decoder_used_lengths`: some sequence uses all 512 decoder positions.
All inputs are finite; a program needn't handle non-finite values.
Results may differ from a plain program's by a relative error of at most 0.019.
Values may be sent and summed in bfloat16 or wider, within the bound.
No kernel may reach another device: no remote copies, remote signals or barrier semaphores. Data moves between devices by JAX's collectives and lax.ppermute only.
A program may use at most 384 MiB of HBM per device.

v0:
```python
import functools
import math

import jax
import jax.numpy as jnp
from jax import lax
from jax.experimental import pallas as pl
from jax.experimental.pallas import tpu as pltpu
from jax.sharding import PartitionSpec as P

D = 768
HEADS = 12
HEAD = 64
FF = 2048
STEP = 5

eps_norm = 1e-06
adam_eps = 1e-06
lamb_rate = 0.5
decay_weight = 0.01
masked_score = -1000000000.0

F32 = jnp.float32
BF16 = jnp.bfloat16


def seq_swap(x, k):
    n = lax.axis_size("seq")
    return lax.ppermute(x, "seq", [(i, i ^ k) for i in range(n)])


def batch_swap(x, k):
    n = lax.axis_size("batch")
    return lax.ppermute(x, "batch", [(i, i ^ k) for i in range(n)])


def gather_blocks(x):
    other = seq_swap(x, 2)
    return [x, seq_swap(x, 1), other, seq_swap(other, 1)]


def far_payload(keep_far, send_far):
    return (keep_far + seq_swap(send_far, 1).astype(F32)).astype(BF16)


def xor_blocks(x, s):
    n = x.shape[0]
    for k in (1, 2):
        swapped = jnp.stack([x[j ^ k] for j in range(n)])
        x = jnp.where((s & k) != 0, swapped, x)
    return x


def seq_exchange(blocks, s):
    n = blocks.shape[0]
    mine = xor_blocks(blocks, s)
    got = jnp.stack([mine[0]] + [seq_swap(mine[j], j) for j in range(1, n)])
    return xor_blocks(got, s)


def tie(x, *others):
    return lax.optimization_barrier((x, others))[0]


def ring_gathers(blocks):
    nb = lax.axis_size("batch")
    rounds = nb // 2
    shift = [(i, (i + 2) % nb) for i in range(nb)]
    results, before = [], None
    for group in blocks:
        current = list(group)
        if before is not None:
            current = [tie(x, *before) for x in current]
        got = [[] for _ in group]
        for k in range(rounds):
            if k:
                current = [lax.ppermute(x, "batch", shift) for x in current]
            if k == max(rounds - 2, 0):
                before = current
            for g, x in zip(got, current):
                g += [x, batch_swap(x, 1)]
        results += got
    return results


def assemble_body(by_lanes, moves, count, groups, *refs):
    ins, outs, sem = refs[: count * groups], refs[count * groups : -1], refs[-1]
    b = lax.axis_index("batch")
    z, y = b // 2, b % 2
    ring, copies = count // 2, []
    for n in range(count):
        k, e = n // 2, n % 2
        at = lax.rem(z + ring - k, ring) * 2 + (y + e - 2 * y * e)
        for group, which, (r0, r1), (c0, c1), (to_row, to_lane) in moves:
            ref, out = ins[group * count + n], outs[which]
            rows = pl.ds(to_row, r1 - r0)
            if by_lanes:
                width = out.shape[1] // count
                start = pl.multiple_of(at * width + to_lane, 128)
                target = out.at[rows, pl.ds(start, c1 - c0)]
            else:
                target = out.at[at, rows, pl.ds(to_lane, c1 - c0)]
            copies.append(pltpu.make_async_copy(ref.at[r0:r1, c0:c1], target, sem.at[len(copies)]))
    for copy in copies:
        copy.start()
    for copy in copies:
        copy.wait()


def assemble(groups, moves, shapes, by_lanes, name):
    count = len(groups[0])
    blocks = [x for g in groups for x in g]
    outs = [
        jax.ShapeDtypeStruct((h, count * w) if by_lanes else (count, h, w), BF16) for h, w in shapes
    ]
    return pl.pallas_call(
        functools.partial(assemble_body, by_lanes, moves, count, len(groups)),
        in_specs=[pl.BlockSpec(memory_space=pltpu.VMEM)] * len(blocks),
        out_specs=[pl.BlockSpec(memory_space=pl.ANY)] * len(outs),
        out_shape=outs,
        scratch_shapes=[pltpu.SemaphoreType.DMA((count * len(moves),))],
        cost_estimate=pl.CostEstimate(flops=10**13, bytes_accessed=10**10, transcendentals=0),
        name=name,
    )(*blocks)


def gathered_rows(got, name):
    h, w = got[0].shape
    return assemble([got], [(0, 0, (0, h), (0, w), (0, 0))], [(h, w)], False, name)[0]


def gathered_lanes(got, name):
    h, w = got[0].shape
    if w % 128 == 0:
        return assemble([got], [(0, 0, (0, h), (0, w), (0, 0))], [(h, w)], True, name)[0]
    return gathered_rows(got, name).swapaxes(0, 1).reshape(h, -1)


def gathered_feeds(got, rows, name):
    h, w = got[0].shape
    fc = w - 256
    moves = [(0, 0, (0, h), (0, fc), (0, 0))]
    for g in range(D // 128):
        r, c = g % 3 * rows, fc + g // 3 * 128
        moves.append((0, 1, (r, r + rows), (c, c + 128), (0, 128 * g)))
    return assemble([got], moves, [(h, fc), (rows, D)], False, name)


def pair_blocks(blocks):
    y = lax.axis_index("batch") % 2
    pairs = blocks.reshape((blocks.shape[0] // 2, 2) + blocks.shape[1:])
    return [lax.dynamic_index_in_dim(pairs, i, 1, keepdims=False) for i in (y, 1 - y)]


def own_block(parts, dest):
    per = parts[0][0].shape[0]
    total = None
    for n, (kept, got) in enumerate(parts):
        at = jnp.clip(dest - n * per, 0, per - 1)
        x = lax.dynamic_index_in_dim(kept, at, 0, keepdims=False).astype(F32)
        x = x + lax.dynamic_index_in_dim(got, at, 0, keepdims=False).astype(F32)
        total = x if n == 0 else jnp.where(dest >= n * per, x, total)
    return total


def ring_reduce(parts, first):
    nb = lax.axis_size("batch")
    ring, z = nb // 2, lax.axis_index("batch") // 2
    last = first + len(parts) * parts[0][0].shape[0]
    after = yield None
    moved = None
    for k in range(1, ring + 1):
        dest = (z + 2 * ring - k) % ring
        held = [(tie(kept, after), got) for kept, got in parts]
        total = own_block(held, dest - first)
        if moved is not None:
            total = total + moved.astype(F32)
        if k == ring:
            yield [total]
            return
        active = [i for i in range(nb) if first <= (i // 2 - k) % ring < last]
        sent = total.astype(BF16)
        moved = lax.ppermute(sent, "batch", [(i, (i + 2) % nb) for i in active])
        after = yield sent


def tree_reduce(parts, first):
    nb = lax.axis_size("batch")
    if nb != 8 or first or len(parts) > 1:
        yield from ring_reduce(parts, first)
        return

    def places(pairs_of):
        return [(2 * i + e, 2 * j + e) for i, j in pairs_of for e in range(2)]

    after = yield None
    kept, got = parts[0]
    total = tie(kept, after)[0].astype(F32) + got[0].astype(F32)
    for hop in (((3, 2), (1, 0)), ((2, 0),)):
        sent = total.astype(BF16)
        moved = lax.ppermute(sent, "batch", places(hop))
        after = yield sent
        total = total + tie(moved, after).astype(F32)
    yield [total]


def sum_steps(x):
    nb = lax.axis_size("batch")
    hops = [(seq_swap, 1), (seq_swap, 2)]
    k = 1
    while k < nb:
        hops.append((batch_swap, k))
        k *= 2
    after = None
    for swap, k in hops:
        got = swap(x if after is None else tie(x, after), k)
        after = yield x
        x = x + (got if after is None else tie(got, after))
    yield [x]


def sum_all(x):
    for x in sum_steps(x):
        pass
    return x[0]


class Clock:
    def __init__(self):
        self.last = None

    def now(self, x):
        return x if self.last is None else tie(x, self.last)

    def mark(self, x):
        self.last = x
        return x

    def step(self, work):
        got = work.send(self.last)
        return got if isinstance(got, list) else self.mark(got)

    def finish(self, work):
        got = None
        while not isinstance(got, list):
            got = self.step(work)
        return got


def nt(a, b):
    return lax.dot_general(a, b, (((1,), (1,)), ((), ())), preferred_element_type=F32)


def nn(a, b):
    return lax.dot_general(a, b, (((1,), (0,)), ((), ())), preferred_element_type=F32)


def tn(a, b):
    return lax.dot_general(a, b, (((0,), (0,)), ((), ())), preferred_element_type=F32)


def whole(x):
    shape = x.shape
    return pl.BlockSpec(shape, lambda i: (0,) * len(shape))


def part(shape, *index):
    return pl.BlockSpec(shape, lambda i: index)


def plain(arrays):
    return [(x, whole(x)) for x in arrays]


SCALARS = pl.BlockSpec(memory_space=pltpu.SMEM)


def call(body, ins, outs, flops, scratch=(), name=None):
    arrays = [a for a, _ in ins]
    specs = [whole(a) if s is None else s for a, s in ins]
    shapes = [jax.ShapeDtypeStruct(s, d) for s, d in outs]
    moved = sum(2 * math.prod(s) for s, _ in outs) + sum(2 * min(a.size, 2**20) for a in arrays)
    return pl.pallas_call(
        body,
        grid=(1,),
        in_specs=specs,
        out_specs=[whole(o) for o in shapes],
        out_shape=shapes,
        scratch_shapes=list(scratch),
        cost_estimate=pl.CostEstimate(flops=10**13, bytes_accessed=10**10, transcendentals=0),
        name=name,
    )(*arrays)


def positions(shape, axis, owner, rows):
    at = lax.broadcasted_iota(jnp.int32, shape, axis)
    shift = rows.bit_length() - 1
    return ((owner ^ (at >> shift)) << shift) + (at & (rows - 1))


def score_bias(meta, first_row, tile, q_rows, k_rows, causal):
    keys = positions((1, 4 * k_rows), 1, meta[0], k_rows)
    if not causal:
        return jnp.where(keys < meta[1], 0.0, masked_score)
    at = first_row + lax.broadcasted_iota(jnp.int32, (tile, 1), 0)
    shift = q_rows.bit_length() - 1
    queries = ((meta[0] ^ (at >> shift)) << shift) + (at & (q_rows - 1))
    return jnp.where((keys <= queries) & (keys < meta[1]), 0.0, masked_score)


def head_mask(shape, h):
    lane = lax.broadcasted_iota(jnp.int32, shape, 1)
    return (lane >= h * HEAD) & (lane < (h + 1) * HEAD)


def attend_tile(q, k, v, bias, heads):
    mixed = jnp.zeros(q.shape, F32)
    logs = jnp.zeros((q.shape[0], 128), F32)
    q = (q.astype(F32) * 0.125).astype(BF16)
    lane = lax.broadcasted_iota(jnp.int32, logs.shape, 1)
    for h in range(heads):
        mask = head_mask(q.shape, h)
        scores = nt(jnp.where(mask, q, jnp.zeros_like(q)), k) + bias
        peak = jnp.max(scores, axis=-1, keepdims=True)
        expo = jnp.exp(scores - peak)
        total = jnp.sum(expo, axis=-1, keepdims=True)
        probs = (expo * (1.0 / total)).astype(BF16)
        mixed = jnp.where(mask, nn(probs, v), mixed)
        logs = jnp.where(lane == h, peak + jnp.log(total), logs)
    return mixed, logs


def attend_rows(meta, q_ref, k_ref, v_ref, wo_ref, first, q_rows, k_rows, causal, outs, total_ref):
    logs_ref, mixed_ref = outs[:2]
    heads = q_ref.shape[1] // HEAD

    def step(t, carry):
        at = pl.multiple_of(t * q_rows, q_rows)
        q = q_ref[pl.ds(first + at, q_rows), :]
        bias = score_bias(meta, first + at, q_rows, q_rows, k_rows, causal)
        mixed, logs = attend_tile(q, k_ref[...], v_ref[...], bias, heads)
        low = mixed.astype(BF16)
        logs_ref[pl.ds(at, q_rows), :] = logs
        mixed_ref[pl.ds(at, q_rows), :] = low
        if wo_ref is not None:
            total_ref[pl.ds(at, q_rows), :] = nn(low, wo_ref[...])
        return carry

    lax.fori_loop(0, 2, step, 0)
    if wo_ref is not None:
        outs[2][...] = total_ref[:q_rows, :]
        outs[3][...] = total_ref[q_rows:, :].astype(BF16)


def project_body(rows, mixed_ref, wo_ref, keep_ref, send_ref):
    keep_ref[...] = nn(mixed_ref[:rows, :], wo_ref[...])
    send_ref[...] = nn(mixed_ref[rows:, :], wo_ref[...]).astype(BF16)


def project(mixed, out_w, group, name):
    rows, dc = mixed.shape[0] // 2, mixed.shape[1]
    return call(
        functools.partial(project_body, rows),
        [(mixed, None), out_weights(out_w, group)],
        [((rows, D), F32), ((rows, D), BF16)],
        4 * rows * dc * D,
        name=name,
    )


def attend_far_body(cross, raw, fused, causal, q_rows, k_rows, *refs):
    refs = list(refs)
    meta = refs.pop(0)
    queries, refs = refs[:4], refs[4:]
    sources = queries
    if cross:
        sources, refs = refs[:4], refs[4:]
    if raw:
        gain = refs.pop(0)
    wq, wk, wv = refs[:3]
    refs = refs[3:]
    wo = refs.pop(0) if fused else None
    if raw:
        rows_ref = refs.pop(0)
        for j in range(4):
            h = queries[j][...].astype(F32)
            inverse = lax.rsqrt(jnp.mean(h * h, axis=-1, keepdims=True) + eps_norm)
            rows_ref[j * q_rows : (j + 1) * q_rows, :] = (h * inverse * gain[...]).astype(BF16)
        queries = sources = [rows_ref.at[j * q_rows : (j + 1) * q_rows, :] for j in range(4)]
    q_ref, k_ref, v_ref = refs[:3]
    outs, total_ref = refs[3 : 7 if fused else 5], (refs[7] if fused else None)
    for j in range(4):
        q_ref[j * q_rows : (j + 1) * q_rows, :] = nt(queries[j][...], wq[...]).astype(BF16)
        rows = sources[j][...]
        k_ref[j * k_rows : (j + 1) * k_rows, :] = nt(rows, wk[...]).astype(BF16)
        v_ref[j * k_rows : (j + 1) * k_rows, :] = nt(rows, wv[...]).astype(BF16)
    attend_rows(meta, q_ref, k_ref, v_ref, wo, 2 * q_rows, q_rows, k_rows, causal, outs, total_ref)


def attend_near_body(causal, q_rows, k_rows, meta, q_ref, k_ref, v_ref, wo, *rest):
    attend_rows(meta, q_ref, k_ref, v_ref, wo, 0, q_rows, k_rows, causal, rest[:4], rest[4])


def attn_weights(attn_t, group):
    return [(attn_t, part((D // 4, D), 0, 4 * group + i)) for i in range(3)]


def out_weights(out_w, group):
    dc = out_w.shape[1]
    return (out_w, pl.BlockSpec((None, dc, D), lambda i: (group, 0, 0)))


def half_outs(q_rows, dc):
    return [((2 * q_rows, 128), F32), ((2 * q_rows, dc), BF16), ((q_rows, D), F32), ((q_rows, D), BF16)]


def attend_far(meta, queries, sources, attn_t, out_w, group, causal, gain=None):
    cross, raw, fused = sources is not None, gain is not None, out_w is not None
    q_rows, dc = queries[0][1].block_shape[0], D // 4
    k_rows = sources[0][1].block_shape[0] if cross else q_rows
    flops = 2 * D * dc * (4 * q_rows + 8 * k_rows) + 16 * q_rows * k_rows * D
    return call(
        functools.partial(attend_far_body, cross, raw, fused, causal, q_rows, k_rows),
        [(meta, SCALARS)]
        + list(queries)
        + (list(sources) if cross else [])
        + ([(gain, None)] if raw else [])
        + attn_weights(attn_t, group)
        + ([out_weights(out_w, group)] if fused else []),
        ([((4 * q_rows, D), BF16)] if raw else [])
        + [((4 * q_rows, dc), BF16), ((4 * k_rows, dc), BF16), ((4 * k_rows, dc), BF16)]
        + half_outs(q_rows, dc)[: 4 if fused else 2],
        flops,
        [pltpu.VMEM((2 * q_rows, D), F32)] if fused else [],
        f"attend_far_{group}",
    )


def attend_near(meta, q, k, v, out_w, group, causal):
    q_rows, k_rows, dc = q.shape[0] // 4, k.shape[0] // 4, q.shape[1]
    return call(
        functools.partial(attend_near_body, causal, q_rows, k_rows),
        [(meta, SCALARS), (q, part((2 * q_rows, dc), 0, 0)), (k, None), (v, None), out_weights(out_w, group)],
        half_outs(q_rows, dc),
        16 * q_rows * k_rows * D,
        [pltpu.VMEM((2 * q_rows, D), F32)],
        f"attend_near_{group}",
    )


def close_body(near_ref, core_ref, far_ref, residual_ref, gain_ref, out_ref, normed_ref):
    h = residual_ref[...].astype(F32) + near_ref[...] + core_ref[...].astype(F32) + far_ref[...].astype(F32)
    inverse = lax.rsqrt(jnp.mean(h * h, axis=-1, keepdims=True) + eps_norm)
    out_ref[...] = h
    normed_ref[...] = (h * inverse * gain_ref[...]).astype(BF16)


def close(near, core, far, residual, gain, name):
    shape = near.shape
    return call(
        close_body,
        [(x, None) for x in (near, core, far, residual, gain)],
        [(shape, F32), (shape, BF16)],
        10 * near.size,
        name=name,
    )


def close_back_body(near_ref, core_ref, far_ref, stream_ref, gain_ref, *rest):
    if len(rest) == 4:
        upstream_ref, rest = rest[0], rest[1:]
    else:
        upstream_ref = None
    out_ref, low_ref, dgain_ref = rest
    h = stream_ref[...].astype(F32)
    up = near_ref[...] + core_ref[...].astype(F32) + far_ref[...].astype(F32)
    inverse = lax.rsqrt(jnp.mean(h * h, axis=-1, keepdims=True) + eps_norm)
    unit = h * inverse
    scaled = up * gain_ref[...]
    grad = inverse * (scaled - unit * jnp.mean(scaled * unit, axis=-1, keepdims=True))
    if upstream_ref is not None:
        grad = upstream_ref[...].astype(F32) + grad
    out_ref[...] = grad
    low_ref[...] = grad.astype(BF16)
    dgain_ref[...] = jnp.sum(up * unit, axis=0, keepdims=True)


def close_back(near, core, far, stream, gain, upstream, name):
    shape = near.shape
    ins = [near, core, far, stream, gain] + ([] if upstream is None else [upstream])
    return call(
        close_back_body,
        [(x, None) for x in ins],
        [(shape, F32), (shape, BF16), ((1, shape[1]), F32)],
        20 * near.size,
        name=name,
    )


def attend_back_body(cross, causal, q_rows, k_rows, tile, *refs):
    meta = refs[0]
    dz = refs[1:5]
    q_ref, qt_ref, k_ref, v_ref, logs_near, logs_far, wq, wk, wv, wo = refs[5:15]
    dq_ref, dkt_ref, dvt_ref = refs[15:18]
    outs = refs[18 : 18 + (8 if cross else 4)]
    do_ref, dot_ref, dkt_sum, dvt_sum, logs_ref = refs[18 + len(outs) :]
    heads = q_ref.shape[1] // HEAD
    for j in range(4):
        at = slice(j * q_rows, (j + 1) * q_rows)
        rows = dz[j][...]
        do_ref[at, :] = nt(rows, wo[...]).astype(BF16)
        dot_ref[:, at] = nt(wo[...], rows).astype(BF16)
    logs_ref[: 2 * q_rows, :] = logs_near[...]
    logs_ref[2 * q_rows :, :] = logs_far[...]
    dkt_sum[...] = jnp.zeros_like(dkt_sum)
    dvt_sum[...] = jnp.zeros_like(dvt_sum)

    def step(t, carry):
        at = pl.ds(pl.multiple_of(t * tile, tile), tile)
        q, do = q_ref[at, :], do_ref[at, :]
        q = (q.astype(F32) * 0.125).astype(BF16)
        qt, dot = qt_ref[:, at], dot_ref[:, at]
        logs = logs_ref[at, :]
        bias = score_bias(meta, t * tile, tile, q_rows, k_rows, causal)
        dq = jnp.zeros(q.shape, F32)
        for h in range(heads):
            mask = head_mask(q.shape, h)
            zero = jnp.zeros_like(q)
            probs = jnp.exp(nt(jnp.where(mask, q, zero), k_ref[...]) + bias - logs[:, h : h + 1])
            grad_probs = nt(jnp.where(mask, do, zero), v_ref[...])
            weighted = probs * grad_probs
            center = jnp.sum(weighted, axis=-1, keepdims=True)
            grad_scores = (weighted - probs * center).astype(BF16)
            feats = slice(h * HEAD, (h + 1) * HEAD)
            dvt_sum[feats, :] += nn(dot[feats, :], probs.astype(BF16))
            dkt_sum[feats, :] += nn(qt[feats, :], grad_scores)
            dq = jnp.where(mask, nn(grad_scores, k_ref[...]), dq)
        dq_ref[at, :] = (dq * 0.125).astype(BF16)
        return carry

    lax.fori_loop(0, 4 * q_rows // tile, step, 0)
    dkt_ref[...] = (dkt_sum[...] * 0.125).astype(BF16)
    dvt_ref[...] = dvt_sum[...].astype(BF16)

    def query_part(j):
        return nn(dq_ref[j * q_rows : (j + 1) * q_rows, :], wq[...])

    def source_part(j):
        at = slice(j * k_rows, (j + 1) * k_rows)
        return tn(dkt_ref[:, at], wk[...]) + tn(dvt_ref[:, at], wv[...])

    parts = (query_part, source_part) if cross else ((lambda j: query_part(j) + source_part(j)),)
    for n, make in enumerate(parts):
        for j in range(4):
            outs[4 * n + j][...] = make(j).astype(outs[4 * n + j].dtype)


def attend_back(meta, dz, qt, attn_t, out_w, group, saved, q_rows, k_rows, causal, cross):
    q, k, v, logs_near, logs_far = saved
    dc = q.shape[1]
    tile = min(256, 4 * q_rows)

    def four(rows):
        return [((rows, D), F32), ((rows, D), BF16)] * 2

    outs = call(
        functools.partial(attend_back_body, cross, causal, q_rows, k_rows, tile),
        [(meta, SCALARS)]
        + list(dz)
        + [(q, None), (qt, None), (k, None), (v, None), (logs_near, None), (logs_far, None)]
        + attn_weights(attn_t, group)
        + [out_weights(out_w, group)],
        [((4 * q_rows, dc), BF16), ((dc, 4 * k_rows), BF16), ((dc, 4 * k_rows), BF16)]
        + (four(q_rows) + four(k_rows) if cross else four(q_rows)),
        80 * q_rows * k_rows * D + 4 * D * dc * (4 * q_rows + 4 * k_rows),
        [
            pltpu.VMEM((4 * q_rows, dc), BF16),
            pltpu.VMEM((dc, 4 * q_rows), BF16),
            pltpu.VMEM((dc, 4 * k_rows), F32),
            pltpu.VMEM((dc, 4 * k_rows), F32),
            pltpu.VMEM((4 * q_rows, 128), F32),
        ],
        f"attend_back_{group}",
    )
    return outs[:3], outs[3:]


def attend_weights_body(cross, q_rows, k_rows, *refs):
    queries = refs[0:4]
    sources = refs[4:8] if cross else queries
    rest = refs[8:] if cross else refs[4:]
    dq, dkt, dvt, dwq, dwk, dwv = rest
    gq = gk = gv = None
    for j in range(4):
        at, ak = slice(j * q_rows, (j + 1) * q_rows), slice(j * k_rows, (j + 1) * k_rows)
        x, y = queries[j][...], sources[j][...]
        a, b, c = tn(dq[at, :], x), nn(dkt[:, ak], y), nn(dvt[:, ak], y)
        gq, gk, gv = (a, b, c) if j == 0 else (gq + a, gk + b, gv + c)
    for ref, g in ((dwq, gq), (dwk, gk), (dwv, gv)):
        ref[...] = g.astype(BF16)


def attend_weights(queries, sources, grads, name):
    cross = sources is not None
    dq, dkt, dvt = grads
    q_rows, k_rows, dc = dq.shape[0] // 4, dkt.shape[1] // 4, dq.shape[1]
    return call(
        functools.partial(attend_weights_body, cross, q_rows, k_rows),
        list(queries)
        + (list(sources) if cross else [])
        + [(dq, None), (dkt, None), (dvt, None)],
        [((dc, D), BF16)] * 3,
        2 * D * dc * (4 * q_rows + 8 * k_rows),
        name=name,
    )


def out_weight_body(q_rows, d0, d1, d2, d3, near, far, out):
    total = None
    for j, ref in enumerate((d0, d1, d2, d3)):
        mixed = (near, far)[j // 2][(j % 2) * q_rows : (j % 2 + 1) * q_rows, :]
        x = tn(ref[...], mixed)
        total = x if j == 0 else total + x
    out[...] = total.astype(BF16)


def out_weight(dz, near, far, name):
    q_rows, dc = near.shape[0] // 2, near.shape[1]
    return call(
        functools.partial(out_weight_body, q_rows),
        list(dz) + [(near, None), (far, None)],
        [((D, dc), BF16)],
        8 * D * dc * q_rows,
        name=name,
    )[0]


GELU_A, GELU_B = math.sqrt(2.0 / math.pi), 0.044715


def feed_forward_body(rows, x0, x1, wg, wu, wd, gate_ref, up_ref, hidden_ref, keep_ref, send_ref):
    for j, x_ref in enumerate((x0, x1)):
        at = slice(j * rows, (j + 1) * rows)
        x = x_ref[...]
        gate, up = nn(x, wg[...]), nn(x, wu[...])
        gate_ref[at, :] = gate
        up_ref[at, :] = up
        inner = jnp.tanh(GELU_A * (gate + GELU_B * (gate * gate * gate)))
        hidden_ref[at, :] = (0.5 * gate * (1.0 + inner) * up).astype(BF16)
        out = (keep_ref, send_ref)[j]
        out[...] = nn(hidden_ref[at, :], wd[...]).astype(out.dtype)


def feed_weights(inner_cols, outer_rows, which):
    fc = inner_cols.shape[1]
    return [
        (inner_cols, part((D, fc), 2 * which, 0)),
        (inner_cols, part((D, fc), 2 * which + 1, 0)),
        (outer_rows, part((fc, D), which, 0)),
    ]


def feed_forward(half, inner_cols, outer_rows, which, name):
    rows, fc = half[0].shape[0], inner_cols.shape[1]
    return call(
        functools.partial(feed_forward_body, rows),
        plain(half) + feed_weights(inner_cols, outer_rows, which),
        [((2 * rows, fc), F32), ((2 * rows, fc), F32), ((2 * rows, fc), BF16), ((rows, D), F32), ((rows, D), BF16)],
        12 * rows * fc * D,
        name=name,
    )


def feed_back_body(rows, d0, d1, gate_ref, up_ref, wg, wu, wd, dgate_ref, dup_ref, keep_ref, send_ref):
    for j, d_ref in enumerate((d0, d1)):
        at = slice(j * rows, (j + 1) * rows)
        dh = nt(d_ref[...], wd[...])
        t, up = gate_ref[at, :], up_ref[at, :]
        square = t * t
        inner = jnp.tanh(GELU_A * t * (1.0 + GELU_B * square))
        slope = 0.5 * (1.0 + inner) + 0.5 * t * (1.0 - inner * inner) * (
            GELU_A * (1.0 + 3.0 * GELU_B * square)
        )
        dgate_ref[at, :] = (dh * up * slope).astype(BF16)
        dup_ref[at, :] = (dh * (0.5 * t * (1.0 + inner))).astype(BF16)
        out = (keep_ref, send_ref)[j]
        out[...] = (nt(dgate_ref[at, :], wg[...]) + nt(dup_ref[at, :], wu[...])).astype(out.dtype)


def feed_back(dz_half, gate, up, inner_cols, outer_rows, which, name):
    rows, fc = gate.shape[0] // 2, inner_cols.shape[1]
    return call(
        functools.partial(feed_back_body, rows),
        list(dz_half) + [(gate, None), (up, None)] + feed_weights(inner_cols, outer_rows, which),
        [((2 * rows, fc), BF16), ((2 * rows, fc), BF16), ((rows, D), F32), ((rows, D), BF16)],
        12 * rows * fc * D,
        name=name,
    )


def feed_weight_body(rows, packed, *refs):
    xs, dzs = refs[0:4], refs[4:8]
    dg, du, hid = refs[8:10], refs[10:12], refs[12:14]
    outs = refs[14:]
    gate = up = down = None
    for j in range(4):
        at = slice((j % 2) * rows, (j % 2 + 1) * rows)
        x = xs[j][...]
        a, b = tn(x, dg[j // 2][at, :]), tn(x, du[j // 2][at, :])
        c = tn(hid[j // 2][at, :], dzs[j][...])
        gate, up, down = (a, b, c) if j == 0 else (gate + a, up + b, down + c)
    fc = gate.shape[1]
    if not packed:
        outs[0][:D, :] = gate.astype(BF16)
        outs[0][D:, :] = up.astype(BF16)
        outs[1][...] = down.astype(BF16)
        return
    out = outs[0]
    height = out.shape[1]
    for n, grad in enumerate((gate, up)):
        for k in range(2):
            out[2 * n + k, :, :fc] = grad[k * height : (k + 1) * height, :].astype(BF16)
    short = fc // 4
    for q in range(4):
        for g in range(D // 128):
            piece = down[q * short : (q + 1) * short, g * 128 : (g + 1) * 128].astype(BF16)
            r, c = g % 3 * short, fc + g // 3 * 128
            out[q, r : r + short, c : c + 128] = piece


def feed_weight(xs, dzs, dgate, dup, hidden, packed, name):
    rows, fc = xs[0].shape[0], dgate[0].shape[1]
    return call(
        functools.partial(feed_weight_body, rows, packed),
        plain(xs) + list(dzs) + plain((*dgate, *dup, *hidden)),
        [((4, D // 2, fc + 256), BF16)] if packed else [((2 * D, fc), BF16), ((fc, D), BF16)],
        24 * rows * fc * D,
        name=name,
    )


def send_blocks(mine):
    return [mine[0]] + [seq_swap(mine[j], j) for j in range(1, 4)]


def place(scratch, refs, s):
    for j, ref in enumerate(refs):
        scratch[s ^ j] = ref[...]


def head_pack_body(ar, gr, lines, attn_ref, gain_ref, inner_ref, *refs):
    outs, scratch = refs[0:4], refs[4]
    s = lax.axis_index("seq")
    ir, width = inner_ref.shape[0], scratch.shape[2]
    dc, room, short = D // 4, width - ar, ir // 3
    turned = attn_ref[...].T
    gains = jnp.concatenate([gain_ref[...], jnp.zeros((1, lines * room - gr), F32)], axis=1)
    for t in range(4):
        at = s ^ t
        scratch[at, :dc, ar:] = jnp.zeros((dc, room), BF16)
        scratch[at, :dc, :ar] = turned[t * dc : (t + 1) * dc, :].astype(BF16)
        for n in range(lines):
            scratch[at, n : n + 1, ar:] = gains[:, n * room : (n + 1) * room].astype(BF16)
        for q in range(4):
            low = (4 * q + t) * 128
            piece = inner_ref[:, low : low + 128].astype(BF16)
            if q < 3:
                scratch[at, dc : dc + ir, q * 128 : (q + 1) * 128] = piece
            else:
                for n in range(3):
                    scratch[at, dc + ir :, n * 128 : (n + 1) * 128] = piece[n * short : (n + 1) * short, :]
    for j in range(4):
        outs[j][...] = scratch[j]


def head_unpack_body(ar, gr, lines, ir, *refs):
    ins, outer_ref = refs[0:4], refs[4]
    attn_ref, feed_ref, scratch = refs[5:8]
    place(scratch, ins, lax.axis_index("seq"))
    dc, room, short, orow = D // 4, scratch.shape[2] - ar, ir // 3, outer_ref.shape[0]
    pieces = []
    for k in range(4):
        attn_ref[:dc, k * ar : (k + 1) * ar] = scratch[k, :dc, :ar]
        rows = slice(k * ir, (k + 1) * ir)
        feed_ref[rows, :384] = scratch[k, dc : dc + ir, :]
        for n in range(3):
            feed_ref[k * ir + n * short : k * ir + (n + 1) * short, 384:512] = scratch[
                k, dc + ir :, n * 128 : (n + 1) * 128
            ]
        pieces += [scratch[k, n : n + 1, ar : ar + min(room, gr - n * room)].astype(F32) for n in range(lines)]
    for g in range(D // 128):
        r, c = g % 3 * orow, 512 + g // 3 * 128
        feed_ref[r : r + orow, c : c + 128] = outer_ref[:, g * 128 : (g + 1) * 128].astype(BF16)
    pieces.append(jnp.zeros((1, attn_ref.shape[1] - 4 * gr), F32))
    line = jnp.concatenate(pieces, axis=1)
    fill = jnp.zeros((attn_ref.shape[0] - dc - 1, line.shape[1]), F32)
    attn_ref[dc:, :] = jnp.concatenate([line, fill], axis=0).astype(BF16)


def head_exchange(attn_master, inner_master, outer_master, gain_master):
    ar, dc, gr = attn_master.shape[0], D // 4, gain_master.shape[0]
    ir = inner_master.shape[0]
    width = (ar // 128 + 1) * 128
    lines = -(-gr // (width - ar))
    tall = dc + ir + ir // 3
    scratch = [pltpu.VMEM((4, tall, width), BF16)]
    outs = call(
        functools.partial(head_pack_body, ar, gr, lines),
        plain([attn_master, gain_master[None], inner_master]),
        [((tall, width), BF16)] * 4,
        0,
        scratch,
        "head_pack",
    )
    return call(
        functools.partial(head_unpack_body, ar, gr, lines, ir),
        plain(send_blocks(outs) + [outer_master]),
        [((dc + 16, 4 * ar), BF16), ((4 * ir, D), BF16)],
        0,
        scratch,
        "head_unpack",
    )


def turn_pack_body(count, *refs):
    ins, outs, scratch = refs[:count], refs[count : count + 4], refs[count + 4]
    s = lax.axis_index("seq")
    dc = scratch.shape[2]
    for t in range(4):
        for g in range(count):
            scratch[s ^ t, g] = ins[g][:, t * dc : (t + 1) * dc].T
    for j in range(4):
        outs[j][...] = scratch[j]


def lanes_unpack_body(*refs):
    ins, out, scratch = refs[:4], refs[4], refs[5]
    place(scratch, ins, lax.axis_index("seq"))
    width = scratch.shape[3]
    for k in range(4):
        for g in range(scratch.shape[1]):
            out[g, :, k * width : (k + 1) * width] = scratch[k, g]


def rows_pack_body(count, *refs):
    ins, outs, scratch = refs[:count], refs[count : count + 4], refs[count + 4]
    s = lax.axis_index("seq")
    dc = scratch.shape[2]
    for t in range(4):
        for g in range(count):
            scratch[s ^ t, g] = ins[g][t * dc : (t + 1) * dc, :]
    for j in range(4):
        outs[j][...] = scratch[j]


def square_pack(body, ins, name):
    count, dc = len(ins), D // 4
    return call(
        functools.partial(body, count),
        ins,
        [((count, dc, dc), BF16)] * 4,
        0,
        [pltpu.VMEM((4, count, dc, dc), BF16)],
        name,
    )


def lanes_unpack(got, name):
    shape = got[0].shape
    return call(
        lanes_unpack_body,
        plain(got),
        [(shape[:2] + (4 * shape[2],), BF16)],
        0,
        [pltpu.VMEM((4,) + shape, BF16)],
        name,
    )[0]


def tail_pack_body(first_ref, rest_ref, *refs):
    outs, scratch = refs[:4], refs[4]
    s, z = lax.axis_index("seq"), lax.axis_index("batch") // (lax.axis_size("batch") // 4)
    total = jnp.where(z == 0, first_ref[...], rest_ref[...])
    width = scratch.shape[2]
    for t in range(4):
        scratch[s ^ t] = total[:, t * width : (t + 1) * width].astype(BF16)
    for j in range(4):
        outs[j][...] = scratch[j]


def tail_unpack_body(*refs):
    ins, out, scratch = refs[:4], refs[4], refs[5]
    place(scratch, ins, lax.axis_index("seq"))
    dc = scratch.shape[1]
    for k in range(4):
        out[:, k * dc : (k + 1) * dc] = scratch[k].astype(F32).T


def tail_exchange(first, rest, s, ar):
    dc = first.shape[0]
    if ar % 16:
        total = jnp.where(lax.axis_index("batch") < lax.axis_size("batch") // 4, first, rest)
        got = seq_exchange(total.astype(BF16).reshape(dc, 4, ar).swapaxes(0, 1), s)
        return got.reshape(4 * dc, ar).T.astype(F32)
    mine = call(
        tail_pack_body, plain([first, rest]), [((dc, ar), BF16)] * 4, 0, [pltpu.VMEM((4, dc, ar), BF16)], "tail_pack"
    )
    return call(
        tail_unpack_body,
        plain(send_blocks(mine)),
        [((ar, 4 * dc), F32)],
        0,
        [pltpu.VMEM((4, dc, ar), BF16)],
        "tail_unpack",
    )[0]


def split_lanes(scratch, pieces):
    width = scratch.shape[2]
    for n, piece in enumerate(pieces):
        for low in range(n * D, (n + 1) * D, D // 2):
            to = low % width
            scratch[low // width, :, to : to + D // 2] = piece[:, low - n * D : low - n * D + D // 2]


def part_pack_body(position, *refs):
    got, others = refs[0:4], refs[4:6]
    kept_ref, sent_ref, squares, scratch = refs[6:10]
    place(squares, got, lax.axis_index("seq"))
    pieces = [x[...] for x in others]
    pieces.insert(position, jnp.concatenate([squares[k, 0] for k in range(4)], axis=1))
    split_lanes(scratch, pieces)
    y = lax.axis_index("batch") % 2
    kept_ref[0] = scratch[y]
    sent_ref[0] = scratch[1 - y]


def attn_part(got, others, position, width, name):
    dc = D // 4
    if width % 128 or lax.axis_size("batch") != 8:
        pieces = list(others)
        if got is not None:
            pieces.insert(position, lanes_unpack(got, name)[0])
        joined = jnp.concatenate(pieces, axis=1)
        return pair_blocks(joined.reshape(dc, 3 * D // width, width).swapaxes(0, 1))
    return call(
        functools.partial(part_pack_body, position),
        plain(list(got) + list(others)),
        [((1, dc, width), BF16)] * 2,
        0,
        [pltpu.VMEM((4, 1, dc, dc), BF16), pltpu.VMEM((2, dc, width), BF16)],
        name,
    )


def self_part_body(rows, *refs):
    x = refs[0:4]
    dq, dkt, dvt, kept_ref, sent_ref, scratch = refs[4:10]
    gq = gk = gv = None
    for j in range(4):
        at = slice(j * rows, (j + 1) * rows)
        y = x[j][...]
        a, b, c = tn(dq[at, :], y), nn(dkt[:, at], y), nn(dvt[:, at], y)
        gq, gk, gv = (a, b, c) if j == 0 else (gq + a, gk + b, gv + c)
    split_lanes(scratch, [g.astype(BF16) for g in (gq, gk, gv)])
    y = lax.axis_index("batch") % 2
    kept_ref[0] = scratch[y]
    sent_ref[0] = scratch[1 - y]


def self_part(rows, grads, width, name):
    dq, dkt, dvt = grads
    per, dc = dq.shape[0] // 4, dq.shape[1]
    if width % 128 or lax.axis_size("batch") != 8:
        return attn_part(None, attend_weights(rows, None, grads, name), 0, width, name)
    return call(
        functools.partial(self_part_body, per),
        list(rows) + plain([dq, dkt, dvt]),
        [((1, dc, width), BF16)] * 2,
        0,
        [pltpu.VMEM((2, dc, width), BF16)],
        name,
    )


def group_ids(rows, per_group, offset):
    start = lax.axis_index(("batch", "seq")) * rows
    return offset + (start + jnp.arange(rows, dtype=jnp.int32)) // per_group


def one_hot(row_ids):
    labels = jnp.arange(24, dtype=jnp.int32)
    return (row_ids[:, None] == labels[None, :]).astype(F32)


def group_sums(arrays, id_list):
    running = jnp.zeros((24,), F32)
    for group_member, row_ids in zip(arrays, id_list):
        squares = group_member * group_member
        if group_member.ndim == 2:
            squares = jnp.sum(squares, axis=1)
        running = running + jnp.sum(one_hot(row_ids) * squares[:, None], axis=0)
    return running


def per_device(
    encoder_layer_input,
    decoder_layer_input,
    cotangent,
    encoder_used_lengths,
    decoder_used_lengths,
    attn_master,
    inner_master,
    outer_master,
    gain_master,
    attn_first,
    inner_first,
    outer_first,
    gain_first,
    attn_second,
    inner_second,
    outer_second,
    gain_second,
):
    ns, nb = lax.axis_size("seq"), lax.axis_size("batch")
    s, b = lax.axis_index("seq"), lax.axis_index("batch")
    masters = (attn_master, inner_master, outer_master, gain_master)
    id_list = (
        group_ids(attn_master.shape[0], D, 0),
        group_ids(inner_master.shape[0], D, 12),
        group_ids(outer_master.shape[0], FF, 16),
        group_ids(gain_master.shape[0], D, 18),
    )
    ar, ir, orow = attn_master.shape[0], inner_master.shape[0], outer_master.shape[0]
    dc, fc = D // ns, FF // ns
    cuts = FF // (ns * orow)

    gr = gain_master.shape[0]
    packed = nb == 8 and ar % 16 == 0 and 3 * orow == ns * ir and cuts == 4
    if packed:
        attn_mine, feed_mine = head_exchange(attn_master, inner_master, outer_master, gain_master)
        attn_got, feed_got = ring_gathers([(attn_mine,), (feed_mine,)])
        inner_cols, outer_rows = gathered_feeds(feed_got, orow, "gather_feeds")
    else:
        width = (ar // 128 + 1) * 128
        lines = -(-gr // (width - ar))
        corner = jnp.pad(gain_master.astype(BF16), (0, lines * (width - ar) - gr)).reshape(lines, width - ar)
        corner = jnp.broadcast_to(jnp.pad(corner, ((0, dc - lines), (0, 0))), (ns, dc, width - ar))
        attn_low = attn_master.astype(BF16).T.reshape(ns, dc, ar)
        got = seq_exchange(jnp.concatenate([attn_low, corner], axis=2), s)
        attn_mine = got[:, :, :ar].swapaxes(0, 1).reshape(dc, ns * ar)
        gains_mine = got[:, :lines, ar:].reshape(ns, -1)[:, :gr].reshape(1, ns * gr)
        attn_mine = jnp.concatenate([attn_mine, jnp.pad(gains_mine, ((0, 15), (0, ns * (ar - gr))))])
        inner_low = inner_master.astype(BF16).reshape(ir, cuts, ns, orow).transpose(2, 0, 1, 3)
        inner_mine = seq_exchange(inner_low.reshape(ns, ir, fc), s).reshape(ns * ir, fc)
        attn_got, inner_got, outer_got = ring_gathers(
            [(attn_mine,), (inner_mine,), (outer_master.astype(BF16),)]
        )
        inner_cols = gathered_rows(inner_got, "gather_inner")
        outer_rows = gathered_rows(outer_got, "gather_outer")
    inner_cols, outer_rows = inner_cols.reshape(4 * D, fc), outer_rows.reshape(2 * fc, D)
    attn_t = gathered_lanes(attn_got, "gather_attn")
    gains = attn_t[dc].reshape(nb, ns * ar)[:, : ns * gr].reshape(6, D).astype(F32)
    gain = [gains[i : i + 1] for i in range(6)]
    out_mine = square_pack(
        turn_pack_body, [(attn_t, part((dc, D), 0, 4 * g + 3)) for g in range(3)], "out_pack"
    )
    out_got = send_blocks(out_mine)

    enc_in, dec_in = encoder_layer_input[0], decoder_layer_input[0]
    er, dr = enc_in.shape[0], dec_in.shape[0]
    enc_meta = jnp.stack([s, encoder_used_lengths[0]]).astype(jnp.int32)
    dec_meta = jnp.stack([s, decoder_used_lengths[0]]).astype(jnp.int32)
    alive = (s * dr + jnp.arange(dr, dtype=jnp.int32)) < decoder_used_lengths[0]
    seed = jnp.where(alive[:, None], cotangent[0], jnp.zeros_like(cotangent[0]))
    blocks = gather_blocks(jnp.concatenate([enc_in, dec_in, seed]))
    enc_blocks = [(x, part((er, D), 0, 0)) for x in blocks]
    dec_blocks = [(x, part((dr, D), er // dr, 0)) for x in blocks]
    seed_blocks = [(x, part((dr, D), er // dr + 1, 0)) for x in blocks]

    def quarters(rows):
        return [(rows, part((rows.shape[0] // 4, D), j, 0)) for j in range(4)]

    clock = Clock()
    now, mark = clock.now, clock.mark

    rows_a, q0, k0, v0, logs_far0, mixed_far0 = attend_far(
        tie(enc_meta, out_mine[1]), enc_blocks, None, attn_t, None, 0, False, gain[0]
    )
    out_w = lanes_unpack([out_got[0]] + [tie(x, mixed_far0) for x in out_got[1:]], "out_unpack")
    far = mark(far_payload(*project(mixed_far0, out_w, 0, "project_far_0")))
    x_enc = seq_swap(far, 2)
    logs_near0, mixed_near0, kn_enc, sn = attend_near(enc_meta, now(q0), k0, v0, out_w, 0, False)
    mark(sn)
    c_enc = seq_swap(sn, 1)
    rows_c, q1, k1, v1, logs_far1, mixed_far1, kf, sf = attend_far(
        now(dec_meta), dec_blocks, None, attn_t, out_w, 1, True, gain[3]
    )
    mark(sf)
    enc_mid, norm_b = close(now(kn_enc), c_enc, x_enc, enc_in, gain[1], "close_enc_attn")
    mark(norm_b)
    rows_b = gather_blocks(norm_b)
    x_self = seq_swap(mark(far_payload(kf, now(sf))), 2)
    logs_near1, mixed_near1, kn, sn = attend_near(dec_meta, now(q1), k1, v1, out_w, 1, True)
    mark(sn)
    c_self = seq_swap(sn, 1)
    eg1, eu1, eh1, kf, sf = feed_forward((now(rows_b[2]), rows_b[3]), inner_cols, outer_rows, 0, "enc_feed_far")
    far = mark(far_payload(kf, sf))
    x_enc = seq_swap(far, 2)
    eg0, eu0, eh0, kn_enc, sn = feed_forward((now(rows_b[0]), rows_b[1]), inner_cols, outer_rows, 0, "enc_feed_near")
    mark(sn)
    c_enc = seq_swap(sn, 1)
    dec_mid, norm_d = close(now(kn), c_self, x_self, dec_in, gain[4], "close_self")
    mark(norm_d)
    enc_out, norm_e = close(now(kn_enc), c_enc, x_enc, enc_mid, gain[2], "close_enc_feed")
    mark(norm_e)
    rows_e = gather_blocks(norm_e)
    rows_d = gather_blocks(now(norm_d))
    q2, k2, v2, logs_far2, mixed_far2, kf, sf = attend_far(
        now(enc_meta), plain(rows_d), plain(rows_e), attn_t, out_w, 2, False
    )
    far = mark(far_payload(kf, sf))
    x_dec = seq_swap(far, 2)
    logs_near2, mixed_near2, kn, sn = attend_near(enc_meta, now(q2), k2, v2, out_w, 2, False)
    mark(sn)
    dec_late, norm_f = close(now(kn), seq_swap(sn, 1), x_dec, dec_mid, gain[5], "close_cross")
    mark(norm_f)
    rows_f = gather_blocks(norm_f)
    dg0, du0, dh0, kn_out, sn_out = feed_forward(
        (now(rows_f[0]), rows_f[1]), inner_cols, outer_rows, 1, "dec_feed_near"
    )
    mark(dh0)
    a0, b0, kn_dec, sn_dec = feed_back(
        seed_blocks[:2], now(dg0), du0, inner_cols, outer_rows, 1, "dec_feed_back_near"
    )
    mark(sn_dec)
    c_dec = seq_swap(sn_dec, 1)
    dg1, du1, dh1, kf_out, sf_out = feed_forward(
        (now(rows_f[2]), rows_f[3]), inner_cols, outer_rows, 1, "dec_feed_far"
    )
    mark(dh1)
    a1, b1, kf, sf = feed_back(seed_blocks[2:], now(dg1), du1, inner_cols, outer_rows, 1, "dec_feed_back_far")

    far = mark(far_payload(kf, sf))
    x_dec = seq_swap(far, 2)
    dec_feed = feed_weight(
        rows_f, seed_blocks, (now(a0), a1), (b0, b1), (dh0, dh1), packed, "dec_feed_weight"
    )
    mark(dec_feed[-1])
    up_five, low, gain_five = close_back(now(kn_dec), c_dec, x_dec, dec_late, gain[5], seed, "back_dec_feed")
    mark(low)
    dz_cross = plain(gather_blocks(low))
    half = nb // 2
    feed_shapes = [(D // 2, fc + 256)] if packed else [(ns * ir, fc), (orow, D)]

    def pair_send(kept, sent):
        return kept, batch_swap(mark(sent), 1)

    def feed_parts(grads):
        blocks = [now(x).reshape((half,) + shape) for x, shape in zip(grads, feed_shapes)]
        return [pair_send(*pair_blocks(x)) for x in blocks]

    dec_parts = feed_parts(dec_feed)

    c_out, x_out = seq_swap(now(sn_out), 1), seq_swap(mark(far_payload(kf_out, now(sf_out))), 2)
    decoder_layer_output = (dec_late + kn_out + c_out.astype(F32) + x_out.astype(F32)).astype(BF16)

    cross_d, outs = attend_back(
        enc_meta, dz_cross, now(q2).T, attn_t, out_w, 2, (q2, k2, v2, logs_near2, logs_far2), dr, er, False, True
    )
    far = mark(far_payload(outs[6], outs[7]))
    x_enc, c_enc = seq_swap(far, 2), seq_swap(now(outs[5]), 1)
    cross_w = attend_weights(plain(rows_d), plain(rows_e), (now(cross_d[0]), *cross_d[1:]), "cross_weights")
    mark(cross_w[0])
    far_dec = mark(far_payload(outs[2], now(outs[3])))
    cross_out = out_weight(dz_cross, now(mixed_near2), mixed_far2, "cross_out_weight")
    mark(cross_out)
    out_sent = square_pack(rows_pack_body, plain([now(cross_out)]), "cross_out_pack")
    mark(out_sent[1])
    up_two, low, gain_two = close_back(now(outs[4]), c_enc, x_enc, enc_out, gain[2], None, "back_encoded")
    mark(low)
    dz = plain(gather_blocks(low))
    out_got = send_blocks([out_sent[0]] + [now(x) for x in out_sent[1:]])
    x_dec, c_dec = seq_swap(now(far_dec), 2), seq_swap(now(outs[1]), 1)
    kn_dec = outs[0]
    a0, b0, kn_enc, sn = feed_back(dz[:2], now(eg0), eu0, inner_cols, outer_rows, 0, "enc_feed_back_near")
    mark(sn)
    c_enc = seq_swap(sn, 1)
    out_got = [out_got[0]] + [now(x) for x in out_got[1:]]
    part_three = pair_send(*attn_part(out_got, cross_w[1:], 2, ns * ar, "part_three"))
    a1, b1, kf, sf = feed_back(dz[2:], now(eg1), eu1, inner_cols, outer_rows, 0, "enc_feed_back_far")
    far = mark(far_payload(kf, sf))
    x_enc = seq_swap(far, 2)
    up_four, low_self, gain_four = close_back(now(kn_dec), c_dec, x_dec, dec_mid, gain[4], up_five, "back_cross")
    mark(low_self)
    dz_self = plain(gather_blocks(low_self))
    enc_feed = feed_weight(
        rows_b, dz, (now(a0), a1), (b0, b1), (eh0, eh1), packed, "enc_feed_weight"
    )
    mark(enc_feed[-1])
    enc_parts = feed_parts(enc_feed)
    up_one, low, gain_one = close_back(now(kn_enc), c_enc, x_enc, enc_mid, gain[1], up_two, "back_enc_feed")
    mark(low)
    dz_enc = plain(gather_blocks(low))
    self_d, outs = attend_back(
        dec_meta, dz_self, now(q1).T, attn_t, out_w, 1, (q1, k1, v1, logs_near1, logs_far1), dr, dr, True, False
    )
    mark(outs[3])
    self_out = out_weight(dz_self, now(mixed_near1), mixed_far1, "self_out_weight")
    mark(self_out)
    out_sent = square_pack(rows_pack_body, plain([now(self_out)]), "self_out_pack")
    mark(out_sent[1])
    out_got = send_blocks(out_sent)
    self_w = attend_weights(quarters(rows_c), None, (now(self_d[0]), *self_d[1:]), "self_weights")
    mark(self_w[0])
    kn_self, c_self = outs[0], seq_swap(now(outs[1]), 1)
    x_self = seq_swap(mark(far_payload(outs[2], now(outs[3]))), 2)
    feeds = [ring_reduce([e, d], 0) for e, d in zip(enc_parts, dec_parts)]
    for x in feeds:
        next(x)
        clock.step(x)
    out_got = [out_got[0]] + [now(x) for x in out_got[1:]]
    part_two = pair_send(*attn_part(out_got, (self_w[2], cross_w[0]), 1, ns * ar, "part_two"))
    enc_out_w = out_weight(dz_enc, now(mixed_near0), mixed_far0, "enc_out_weight")
    mark(enc_out_w)
    out_sent = square_pack(rows_pack_body, plain([now(enc_out_w)]), "enc_out_pack")
    mark(out_sent[1])
    out_got = send_blocks(out_sent)
    for x in feeds:
        clock.step(x)
    enc_d, outs = attend_back(
        enc_meta, dz_enc, now(q0).T, attn_t, out_w, 0, (q0, k0, v0, logs_near0, logs_far0), er, er, False, False
    )
    far = mark(far_payload(outs[2], outs[3]))
    x_enc, c_enc = seq_swap(far, 2), seq_swap(now(outs[1]), 1)
    part_zero = pair_send(
        *self_part(quarters(rows_a), (now(enc_d[0]), *enc_d[1:]), ns * ar, "part_zero")
    )
    for x in feeds:
        clock.step(x)
    out_got = [out_got[0]] + [now(x) for x in out_got[1:]]
    part_one = pair_send(*attn_part(out_got, self_w[:2], 0, ns * ar, "part_one"))
    decoder_input_gradient, _, gain_three = close_back(
        now(kn_self), c_self, x_self, dec_in, gain[3], up_four, "back_self"
    )
    mark(gain_three)
    encoder_input_gradient, _, gain_zero = close_back(
        now(outs[0]), c_enc, x_enc, enc_in, gain[0], up_one, "back_enc_attn"
    )
    mark(gain_zero)

    gain_parts = [x[0] for x in (now(gain_zero), gain_one, gain_two, gain_three, gain_four, gain_five)]
    totals = sum_steps(jnp.concatenate(gain_parts + [group_sums(masters, id_list)]))
    mark(next(totals))
    place_zero = tree_reduce([part_zero], 0)
    next(place_zero)
    clock.step(place_zero)
    clock.step(totals)
    rest = ring_reduce([part_one, part_two, part_three], nb // 8)
    next(rest)
    clock.step(rest)
    clock.step(totals)
    clock.step(totals)
    clock.step(place_zero)
    clock.step(rest)
    clock.step(totals)
    feed_sums = [mark(clock.finish(x)[0]) for x in feeds]
    if packed:
        inner_part = feed_sums[0][:, :fc]
        outer_grad = jnp.concatenate(
            [feed_sums[0][g % 3 * orow :, fc + g // 3 * 128 :][:orow, :128] for g in range(D // 128)], axis=1
        )
    else:
        inner_part, outer_grad = feed_sums
    inner_part = seq_exchange(inner_part.astype(BF16).reshape(ns, ir, fc), s)
    inner_grad = inner_part.reshape(ns, ir, cuts, orow).transpose(1, 2, 0, 3).reshape(ir, FF).astype(F32)
    clock.step(rest)
    (all_sums,) = clock.finish(totals)
    (sum_rest,), (sum_zero,) = clock.finish(rest), clock.finish(place_zero)
    attn_grad = tail_exchange(sum_zero, sum_rest, s, ar)
    gain_sum, weight_squares = all_sums[: 6 * D], all_sums[6 * D :]
    gain_grad = lax.dynamic_slice_in_dim(gain_sum, lax.axis_index(("batch", "seq")) * gr, gr)

    grads = (attn_grad, inner_grad, outer_grad, gain_grad)
    firsts = (attn_first, inner_first, outer_first, gain_first)
    seconds = (attn_second, inner_second, outer_second, gain_second)
    decays = (decay_weight, decay_weight, decay_weight, 0.0)
    correction = 1.0 - 0.5**STEP
    first_list, second_list, update_list = ([], [], [])
    for master, first_old, second_old, gradient, decay_rate in zip(
        masters, firsts, seconds, grads, decays
    ):
        first_new = 0.5 * first_old + 0.5 * gradient
        second_new = 0.5 * second_old + 0.5 * gradient * gradient
        update = (
            first_new / correction / (jnp.sqrt(second_new / correction) + adam_eps)
            + decay_rate * master
        )
        first_list.append(first_new)
        second_list.append(second_new)
        update_list.append(update)
    update_squares = sum_all(group_sums(update_list, id_list))
    weight_norms = jnp.sqrt(weight_squares)
    update_norms = jnp.sqrt(update_squares)
    trust_ratio = weight_norms / (update_norms + 1e-06)
    master_list, copy_list = ([], [])
    for master, update, row_ids in zip(masters, update_list, id_list):
        row_scale = jnp.sum(one_hot(row_ids) * trust_ratio[None, :], axis=1)
        if master.ndim == 2:
            row_scale = row_scale[:, None]
        master_new = master - lamb_rate * row_scale * update
        master_list.append(master_new)
        copy_list.append(master_new.astype(BF16))
    return (
        decoder_layer_output[None],
        encoder_input_gradient[None],
        decoder_input_gradient[None],
        *grads,
        *first_list,
        *second_list,
        *master_list,
        *copy_list,
        weight_norms,
        update_norms,
    )


def solution(mesh):
    rows = P("batch", "seq", None)
    matrix = P(("batch", "seq"), None)
    vector = P(("batch", "seq"))
    kinds = (matrix, matrix, matrix, vector)
    return jax.shard_map(
        per_device,
        mesh=mesh,
        in_specs=(rows, rows, rows, P("batch"), P("batch")) + kinds * 3,
        out_specs=(rows, rows, rows) + kinds * 5 + (P(), P()),
        check_vma=False,
    )
```

profile of v0, /device:TPU:0, one launch (start us, length us, event | category | flops | bytes accessed | tf_op | source)
XLA Modules:
  0.0 645.1 jit_solution(1675130591947746896)
XLA Ops:
  6.5 6.9 %collective-permute-done.1.refs_2_ = bf16[320,384]{1,0:T(8,128)(2,1)S(1)} collective-permute-done((bf16[320,384]{1,0:T(8,128)(2,1)}, bf16[320,384]{1,0:T(8,128)(2,1)S(1)}, u32[]{:S(2)}, u32[]{:S(2)}) %collective-permute-start.1) | collective-permute-done | bytes 245792 | tf_op jit(solution)/shard_map/ppermute | solution.py:29
  13.4 4.9 collective-permute-done.2.refs_3_
  19.0 2.8 head_unpack.1
  23.4 13.6 %collective-permute-done.4.refs_2_ = bf16[208,1152]{1,0:T(8,128)(2,1)S(1)} collective-permute-done((bf16[208,1152]{1,0:T(8,128)(2,1)}, bf16[208,1152]{1,0:T(8,128)(2,1)S(1)}, u32[]{:S(2)}, u32[]{:S(2)}) %collective-permute-start.4) | collective-permute-done | bytes 479264 | tf_op jit(solution)/shard_map/ppermute | solution.py:77
  39.2 11.9 %collective-permute-done.6.refs_4_ = bf16[208,1152]{1,0:T(8,128)(2,1)S(1)} collective-permute-done((bf16[208,1152]{1,0:T(8,128)(2,1)S(1)}, bf16[208,1152]{1,0:T(8,128)(2,1)S(1)}, u32[]{:S(2)}, u32[]{:S(2)}) %collective-permute-start.6) | collective-permute-done | bytes 479264 | tf_op jit(solution)/shard_map/ppermute | solution.py:77
  56.4 10.4 %collective-permute-done.8.refs_6_ = bf16[208,1152]{1,0:T(8,128)(2,1)S(1)} collective-permute-done((bf16[208,1152]{1,0:T(8,128)(2,1)S(1)}, bf16[208,1152]{1,0:T(8,128)(2,1)S(1)}, u32[]{:S(2)}, u32[]{:S(2)}) %collective-permute-start.8) | collective-permute-done | bytes 479264 | tf_op jit(solution)/shard_map/ppermute | solution.py:77
  71.8 5.3 collective-permute-done.23.refs_2_
  78.5 7.6 %collective-permute-done.9.refs_7_ = bf16[208,1152]{1,0:T(8,128)(2,1)} collective-permute-done((bf16[208,1152]{1,0:T(8,128)(2,1)S(1)}, bf16[208,1152]{1,0:T(8,128)(2,1)}, u32[]{:S(2)}, u32[]{:S(2)}) %collective-permute-start.9) | collective-permute-done | bytes 479264 | tf_op jit(solution)/shard_map/ppermute | solution.py:34
  86.1 4.0 gather_attn.1.refs_0_.refs_1_.refs_2_.refs_6_.refs_7_.refs_8_.refs_9_.refs_10_.refs_11_.refs_12_.refs_13_
  90.2 3.0 out_pack.1
  96.9 7.3 %attend_far_0.1 = (bf16[1024,768]{1,0:T(8,128)(2,1)}, bf16[1024,192]{1,0:T(8,128)(2,1)}, bf16[1024,192]{1,0:T(8,128)(2,1)}, bf16[1024,192]{1,0:T(8,128)(2,1)}, f...) custom-call(s32[2]{0:T(128)} %get-tuple-element.331.refs_0_.meta, bf16[512,768]{1,0:T(8,128)(2,1)} %pad_maximum_fusion.refs_1_.d0.refs_4_, ...), custom_call_target="tpu_custom_call" | custom-call | flops 9999999827968 | bytes 10000000000 | tf_op jit(solution)/shard_map/attend_far_0/pallas_call | solution.py:283
  104.4 5.5 collective-permute-done.15.refs_3_
  119.3 6.1 attend_near_0.1
  125.4 6.9 %attend_far_1.1 = (bf16[512,768]{1,0:T(8,128)(2,1)}, bf16[512,192]{1,0:T(8,128)(2,1)}, bf16[512,192]{1,0:T(8,128)(2,1)}, bf16[512,192]{1,0:T(8,128)(2,1)}, f32[2...) custom-call(s32[2]{0:T(128)} %get-tuple-element.304.refs_0_.meta, ...), custom_call_target="tpu_custom_call" | custom-call | flops 9999999827968 | bytes 10000000000 | tf_op jit(solution)/shard_map/attend_far_1/pallas_call | solution.py:283
  132.4 2.7 close_enc_attn.1
  141.8 5.1 attend_near_1.1
  146.9 3.1 collective-permute-done.19.x0.refs_2_
  152.1 12.6 %collective-permute-done.24.refs_3_ = bf16[384,768]{1,0:T(8,128)(2,1)} collective-permute-done((bf16[384,768]{1,0:T(8,128)(2,1)}, bf16[384,768]{1,0:T(8,128)(2,1)}, u32[]{:S(2)}, u32[]{:S(2)}) %collective-permute-start.24) | collective-permute-done | bytes 589856 | tf_op jit(solution)/shard_map/ppermute | solution.py:34
  164.8 12.6 %collective-permute-done.26.refs_5_ = bf16[384,768]{1,0:T(8,128)(2,1)} collective-permute-done((bf16[384,768]{1,0:T(8,128)(2,1)}, bf16[384,768]{1,0:T(8,128)(2,1)}, u32[]{:S(2)}, u32[]{:S(2)}) %collective-permute-start.26) | collective-permute-done | bytes 589856 | tf_op jit(solution)/shard_map/ppermute | solution.py:34
  177.4 11.8 %collective-permute-done.28.refs_7_ = bf16[384,768]{1,0:T(8,128)(2,1)} collective-permute-done((bf16[384,768]{1,0:T(8,128)(2,1)}, bf16[384,768]{1,0:T(8,128)(2,1)}, u32[]{:S(2)}, u32[]{:S(2)}) %collective-permute-start.28) | collective-permute-done | bytes 589856 | tf_op jit(solution)/shard_map/ppermute | solution.py:34
  189.2 4.9 gather_feeds.1
  194.1 4.7 enc_feed_far.1
  204.8 4.7 enc_feed_near.1
  211.7 3.7 collective-permute-done.34.far_ref
  215.4 2.8 close_enc_feed.1
  220.2 10.2 %collective-permute-done.39.refs_7_.refs_6_ = bf16[256,768]{1,0:T(8,128)(2,1)S(1)} collective-permute-done((bf16[256,768]{1,0:T(8,128)(2,1)}, bf16[256,768]{1,0:T(8,128)(2,1)S(1)}, u32[]{:S(2)}, u32[]{:S(2)}) %collective-permute-start.39) | collective-permute-done | bytes 393248 | tf_op jit(solution)/shard_map/ppermute | solution.py:29
  236.3 8.4 %attend_far_2.1 = (bf16[512,192]{1,0:T(8,128)(2,1)}, bf16[1024,192]{1,0:T(8,128)(2,1)}, bf16[1024,192]{1,0:T(8,128)(2,1)}, f32[256,128]{1,0:T(8,128)}, bf16[256,...) custom-call(s32[2]{0:T(128)} %get-tuple-element.331.refs_0_.meta, ...), custom_call_target="tpu_custom_call" | custom-call | flops 9999999827968 | bytes 10000000000 | tf_op jit(solution)/shard_map/attend_far_2/pallas_call | solution.py:283
  248.1 6.1 attend_near_2.1
  255.8 5.7 collective-permute-done.43.far_ref
  266.7 3.7 dec_feed_near.1
  272.0 4.5 dec_feed_back_near.1
  276.5 3.7 dec_feed_far.1
  280.2 4.5 dec_feed_back_far.1
  289.8 6.0 dec_feed_weight.1
  299.8 3.2 dynamic-slice_bitcast_fusion.1
  307.8 11.3 %attend_back_2.1 = (bf16[512,192]{1,0:T(8,128)(2,1)}, bf16[192,1024]{1,0:T(8,128)(2,1)}, bf16[192,1024]{1,0:T(8,128)(2,1)}, f32[128,768]{1,0:T(8,128)}, bf16[128...) custom-call(s32[2]{0:T(128)} %get-tuple-element.331.refs_0_.meta, ...), custom_call_target="tpu_custom_call" | custom-call | flops 9999999827968 | bytes 10000000000 | tf_op jit(solution)/shard_map/attend_back_2/pallas_call | solution.py:283
  323.1 3.9 cross_weights.1
  333.6 5.3 collective-permute-done.59.far_ref
  338.9 3.0 back_encoded.1
  346.1 5.2 enc_feed_back_near.1
  351.3 5.6 collective-permute-done.64.refs_2_
  360.9 5.3 enc_feed_back_far.1
  372.6 4.7 collective-permute-done.68.far_ref
  381.4 6.8 %enc_feed_weight.1 = bf16[4,384,768]{2,1,0:T(8,128)(2,1)} custom-call(bf16[256,768]{1,0:T(8,128)(2,1)} %get-tuple-element.322.x0.refs_0_, bf16[256,768]{1,0:T(8,128)(2,1)} %copy-done.88, bf16[256,768]{1,0:T(8,128)(2,1)} %collective-permute-done.19.x0.refs_2_, bf16[256,768]{1,0:T(8,128)(2,1)} %collective-permute-done.21.x1.refs_3_, ...), custom_call_target="tpu_custom_call" | custom-call | flops 9999999827968 | bytes 10000000000 | tf_op jit(solution)/shard_map/enc_feed_weight/pallas_call | solution.py:283
  388.2 3.2 dynamic-slice_bitcast_fusion
  392.4 3.6 back_enc_feed.1
  397.8 7.9 %attend_back_1.1 = (bf16[512,192]{1,0:T(8,128)(2,1)}, bf16[192,512]{1,0:T(8,128)(2,1)}, bf16[192,512]{1,0:T(8,128)(2,1)}, f32[128,768]{1,0:T(8,128)}, bf16[128,7...) custom-call(s32[2]{0:T(128)} %get-tuple-element.304.refs_0_.meta, ...), custom_call_target="tpu_custom_call" | custom-call | flops 9999999827968 | bytes 10000000000 | tf_op jit(solution)/shard_map/attend_back_1/pallas_call | solution.py:283
  410.2 3.4 self_weights.1
  417.7 4.0 collective-permute-done.80
  424.0 2.8 collective-permute-start.83
  430.0 2.9 enc_out_weight.1.refs_0_
  434.8 7.1 %collective-permute-done.83 = bf16[384,768]{1,0:T(8,128)(2,1)} collective-permute-done((bf16[384,768]{1,0:T(8,128)(2,1)}, bf16[384,768]{1,0:T(8,128)(2,1)}, u32[]{:S(2)}, u32[]{:S(2)}) %collective-permute-start.83) | collective-permute-done | bytes 589856 | tf_op jit(solution)/shard_map/ppermute | solution.py:183
  445.6 17.7 %attend_back_0.1 = (bf16[1024,192]{1,0:T(8,128)(2,1)}, bf16[192,1024]{1,0:T(8,128)(2,1)}, bf16[192,1024]{1,0:T(8,128)(2,1)}, f32[256,768]{1,0:T(8,128)}, bf16[25...) custom-call(s32[2]{0:T(128)} %get-tuple-element.331.refs_0_.meta, ...), custom_call_target="tpu_custom_call" | custom-call | flops 9999999827968 | bytes 10000000000 | tf_op jit(solution)/shard_map/attend_back_0/pallas_call | solution.py:283
  472.1 4.0 part_zero.1
  476.1 11.4 %collective-permute-done.86 = bf16[384,768]{1,0:T(8,128)(2,1)} collective-permute-done((bf16[384,768]{1,0:T(8,128)(2,1)}, bf16[384,768]{1,0:T(8,128)(2,1)}, u32[]{:S(2)}, u32[]{:S(2)}) %collective-permute-start.86) | collective-permute-done | bytes 589856 | tf_op jit(solution)/shard_map/ppermute | solution.py:183
  502.9 3.7 collective-permute-done.92.far_ref
  506.6 3.3 back_enc_attn.1
  511.3 2.8 collective-permute-done.93
  517.6 5.8 collective-permute-done.99
  533.7 20.8 %collective-permute-done.103 = bf16[192,1152]{1,0:T(8,128)(2,1)S(1)} collective-permute-done((bf16[192,1152]{1,0:T(8,128)(2,1)}, bf16[192,1152]{1,0:T(8,128)(2,1)S(1)}, u32[]{:S(2)}, u32[]{:S(2)}) %collective-permute-start.103) | collective-permute-done | bytes 442400 | tf_op jit(solution)/shard_map/ppermute | solution.py:183
  573.2 3.7 collective-permute-start.113
  583.5 3.4 multiply_reduce_fusion.2
  589.5 3.4 collective-permute-start.106
  609.4 4.4 collective-permute-done.108.refs_2_
  (602 shorter events, 250.1 us)
Async XLA Ops:
  6.3 11.9 %collective-permute-start.2 = (bf16[320,384]{1,0:T(8,128)(2,1)}, bf16[320,384]{1,0:T(8,128)(2,1)S(1)}, u32[]{:S(2)}, u32[]{:S(2)}) collective-permute-start(bf16[320,384]{1,0:T(8,128)(2,1)} %get-tuple-element.285), channel_id=1, source_target_pairs={{0,3},{1,2},{2,1},{3,0},{4,7},{5,6},{6,5},{7,4},{8,11},{9,10},{10,... | collective-permute-start | bytes 737288 | tf_op jit(solution)/shard_map/ppermute | solution.py:29
  21.7 15.2 %collective-permute-start.4 = (bf16[208,1152]{1,0:T(8,128)(2,1)}, bf16[208,1152]{1,0:T(8,128)(2,1)S(1)}, u32[]{:S(2)}, u32[]{:S(2)}) collective-permute-start(bf16[208,1152]{1,0:T(8,128)(2,1)} %get-tuple-element.286.refs_0_), channel_id=1, source_target_pairs={{0,8},{4,12},{8,16},{12,20},{16,24},{20,28},{24,0},{28,4},{1,9},{5... | collective-permute-start | bytes 1437704 | tf_op jit(solution)/shard_map/ppermute | solution.py:77
  36.9 14.2 %collective-permute-start.6 = (bf16[208,1152]{1,0:T(8,128)(2,1)S(1)}, bf16[208,1152]{1,0:T(8,128)(2,1)S(1)}, u32[]{:S(2)}, u32[]{:S(2)}) collective-permute-start(bf16[208,1152]{1,0:T(8,128)(2,1)S(1)} %collective-permute-done.4.refs_2_), channel_id=1, source_target_pairs={{0,8},{4,12},{8,16},{12,20},{16,24},{20,28},{24,0},{28,4},{1,9},{5... | collective-permute-start | bytes 1437704 | tf_op jit(solution)/shard_map/ppermute | solution.py:77
  37.6 18.3 %collective-permute-start.3 = (bf16[208,1152]{1,0:T(8,128)(2,1)}, bf16[208,1152]{1,0:T(8,128)(2,1)S(1)}, u32[]{:S(2)}, u32[]{:S(2)}) collective-permute-start(bf16[208,1152]{1,0:T(8,128)(2,1)} %get-tuple-element.286.refs_0_), channel_id=1, source_target_pairs={{0,4},{4,0},{8,12},{12,8},{16,20},{20,16},{24,28},{28,24},{1,5},{5... | collective-permute-start | bytes 1437704 | tf_op jit(solution)/shard_map/ppermute | solution.py:34
  51.1 15.7 %collective-permute-start.8 = (bf16[208,1152]{1,0:T(8,128)(2,1)S(1)}, bf16[208,1152]{1,0:T(8,128)(2,1)S(1)}, u32[]{:S(2)}, u32[]{:S(2)}) collective-permute-start(bf16[208,1152]{1,0:T(8,128)(2,1)S(1)} %collective-permute-done.6.refs_4_), channel_id=1, source_target_pairs={{0,8},{4,12},{8,16},{12,20},{16,24},{20,28},{24,0},{28,4},{1,9},{5... | collective-permute-start | bytes 1437704 | tf_op jit(solution)/shard_map/ppermute | solution.py:77
  52.9 18.4 %collective-permute-start.11 = (bf16[512,768]{1,0:T(8,128)(2,1)}, bf16[512,768]{1,0:T(8,128)(2,1)}, u32[]{:S(2)}, u32[]{:S(2)}) collective-permute-start(bf16[512,768]{1,0:T(8,128)(2,1)} %pad_maximum_fusion.refs_1_.d0.refs_4_), channel_id=1, source_target_pairs={{0,2},{1,3},{2,0},{3,1},{4,6},{5,7},{6,4},{7,5},{8,10},{9,11},{10,... | collective-permute-start | bytes 2359304 | tf_op jit(solution)/shard_map/ppermute | solution.py:29
  54.3 22.8 %collective-permute-start.23 = (bf16[384,768]{1,0:T(8,128)(2,1)}, bf16[384,768]{1,0:T(8,128)(2,1)}, u32[]{:S(2)}, u32[]{:S(2)}) collective-permute-start(bf16[384,768]{1,0:T(8,128)(2,1)} %get-tuple-element.317.refs_0_), channel_id=1, source_target_pairs={{0,8},{4,12},{8,16},{12,20},{16,24},{20,28},{24,0},{28,4},{1,9},{5... | collective-permute-start | bytes 1769480 | tf_op jit(solution)/shard_map/ppermute | solution.py:77
  54.3 16.9 %collective-permute-start.5 = (bf16[208,1152]{1,0:T(8,128)(2,1)S(1)}, bf16[208,1152]{1,0:T(8,128)(2,1)S(1)}, u32[]{:S(2)}, u32[]{:S(2)}) collective-permute-start(bf16[208,1152]{1,0:T(8,128)(2,1)S(1)} %collective-permute-done.4.refs_2_), channel_id=1, source_target_pairs={{0,4},{4,0},{8,12},{12,8},{16,20},{20,16},{24,28},{28,24},{1,5},{5... | collective-permute-start | bytes 1437704 | tf_op jit(solution)/shard_map/ppermute | solution.py:34
  55.9 22.6 %collective-permute-start.7 = (bf16[208,1152]{1,0:T(8,128)(2,1)S(1)}, bf16[208,1152]{1,0:T(8,128)(2,1)S(1)}, u32[]{:S(2)}, u32[]{:S(2)}) collective-permute-start(bf16[208,1152]{1,0:T(8,128)(2,1)S(1)} %collective-permute-done.6.refs_4_), channel_id=1, source_target_pairs={{0,4},{4,0},{8,12},{12,8},{16,20},{20,16},{24,28},{28,24},{1,5},{5... | collective-permute-start | bytes 1437704 | tf_op jit(solution)/shard_map/ppermute | solution.py:34
  66.8 19.3 %collective-permute-start.9 = (bf16[208,1152]{1,0:T(8,128)(2,1)S(1)}, bf16[208,1152]{1,0:T(8,128)(2,1)}, u32[]{:S(2)}, u32[]{:S(2)}) collective-permute-start(bf16[208,1152]{1,0:T(8,128)(2,1)S(1)} %collective-permute-done.8.refs_6_), channel_id=1, source_target_pairs={{0,4},{4,0},{8,12},{12,8},{16,20},{20,16},{24,28},{28,24},{1,5},{5... | collective-permute-start | bytes 1437704 | tf_op jit(solution)/shard_map/ppermute | solution.py:34
  71.3 24.3 %collective-permute-start.10 = (bf16[512,768]{1,0:T(8,128)(2,1)}, bf16[512,768]{1,0:T(8,128)(2,1)}, u32[]{:S(2)}, u32[]{:S(2)}) collective-permute-start(bf16[512,768]{1,0:T(8,128)(2,1)} %pad_maximum_fusion.refs_1_.d0.refs_4_), channel_id=1, source_target_pairs={{0,1},{1,0},{2,3},{3,2},{4,5},{5,4},{6,7},{7,6},{8,9},{9,8},{10,11... | collective-permute-start | bytes 2359304 | tf_op jit(solution)/shard_map/ppermute | solution.py:29
  71.3 25.6 %collective-permute-start.12 = (bf16[512,768]{1,0:T(8,128)(2,1)}, bf16[512,768]{1,0:T(8,128)(2,1)}, u32[]{:S(2)}, u32[]{:S(2)}) collective-permute-start(bf16[512,768]{1,0:T(8,128)(2,1)} %collective-permute-done.11.refs_3_.d0.refs_6_), channel_id=1, source_target_pairs={{0,1},{1,0},{2,3},{3,2},{4,5},{5,4},{6,7},{7,6},{8,9},{9,8},{10,11... | collective-permute-start | bytes 2359304 | tf_op jit(solution)/shard_map/ppermute | solution.py:29
  77.1 37.9 %collective-permute-start.25 = (bf16[384,768]{1,0:T(8,128)(2,1)}, bf16[384,768]{1,0:T(8,128)(2,1)}, u32[]{:S(2)}, u32[]{:S(2)}) collective-permute-start(bf16[384,768]{1,0:T(8,128)(2,1)} %collective-permute-done.23.refs_2_), channel_id=1, source_target_pairs={{0,8},{4,12},{8,16},{12,20},{16,24},{20,28},{24,0},{28,4},{1,9},{5... | collective-permute-start | bytes 1769480 | tf_op jit(solution)/shard_map/ppermute | solution.py:77
  93.2 11.0 %collective-permute-start.13 = (bf16[3,192,192]{2,1,0:T(8,128)(2,1)}, bf16[3,192,192]{2,1,0:T(8,128)(2,1)}, u32[]{:S(2)}, u32[]{:S(2)}) collective-permute-start(bf16[3,192,192]{2,1,0:T(8,128)(2,1)} %get-tuple-element.287), channel_id=1, source_target_pairs={{0,1},{1,0},{2,3},{3,2},{4,5},{5,4},{6,7},{7,6},{8,9},{9,8},{10,11... | collective-permute-start | bytes 663560 | tf_op jit(solution)/shard_map/ppermute | solution.py:29
  94.3 10.1 %collective-permute-start.14 = (bf16[3,192,192]{2,1,0:T(8,128)(2,1)}, bf16[3,192,192]{2,1,0:T(8,128)(2,1)}, u32[]{:S(2)}, u32[]{:S(2)}) collective-permute-start(bf16[3,192,192]{2,1,0:T(8,128)(2,1)} %get-tuple-element.293), channel_id=1, source_target_pairs={{0,2},{1,3},{2,0},{3,1},{4,6},{5,7},{6,4},{7,5},{8,10},{9,11},{10,... | collective-permute-start | bytes 663560 | tf_op jit(solution)/shard_map/ppermute | solution.py:29
  95.6 14.4 %collective-permute-start.15 = (bf16[3,192,192]{2,1,0:T(8,128)(2,1)}, bf16[3,192,192]{2,1,0:T(8,128)(2,1)}, u32[]{:S(2)}, u32[]{:S(2)}) collective-permute-start(bf16[3,192,192]{2,1,0:T(8,128)(2,1)} %get-tuple-element.295), channel_id=1, source_target_pairs={{0,3},{1,2},{2,1},{3,0},{4,7},{5,6},{6,5},{7,4},{8,11},{9,10},{10,... | collective-permute-start | bytes 663560 | tf_op jit(solution)/shard_map/ppermute | solution.py:29
  115.0 24.1 %collective-permute-start.27 = (bf16[384,768]{1,0:T(8,128)(2,1)}, bf16[384,768]{1,0:T(8,128)(2,1)}, u32[]{:S(2)}, u32[]{:S(2)}) collective-permute-start(bf16[384,768]{1,0:T(8,128)(2,1)} %collective-permute-done.25.refs_4_), channel_id=1, source_target_pairs={{0,8},{4,12},{8,16},{12,20},{16,24},{20,28},{24,0},{28,4},{1,9},{5... | collective-permute-start | bytes 1769480 | tf_op jit(solution)/shard_map/ppermute | solution.py:77
  118.7 13.7 %collective-permute-start.18 = (bf16[256,768]{1,0:T(8,128)(2,1)}, bf16[256,768]{1,0:T(8,128)(2,1)}, u32[]{:S(2)}, u32[]{:S(2)}) collective-permute-start(bf16[256,768]{1,0:T(8,128)(2,1)} %add_convert_fusion.4), channel_id=1, source_target_pairs={{0,2},{1,3},{2,0},{3,1},{4,6},{5,7},{6,4},{7,5},{8,10},{9,11},{10,... | collective-permute-start | bytes 1179656 | tf_op jit(solution)/shard_map/ppermute | solution.py:29
  135.6 16.5 %collective-permute-start.22 = (bf16[384,768]{1,0:T(8,128)(2,1)}, bf16[384,768]{1,0:T(8,128)(2,1)}, u32[]{:S(2)}, u32[]{:S(2)}) collective-permute-start(bf16[384,768]{1,0:T(8,128)(2,1)} %get-tuple-element.317.refs_0_), channel_id=1, source_target_pairs={{0,4},{4,0},{8,12},{12,8},{16,20},{20,16},{24,28},{28,24},{1,5},{5... | collective-permute-start | bytes 1769480 | tf_op jit(solution)/shard_map/ppermute | solution.py:34
  137.1 27.7 %collective-permute-start.24 = (bf16[384,768]{1,0:T(8,128)(2,1)}, bf16[384,768]{1,0:T(8,128)(2,1)}, u32[]{:S(2)}, u32[]{:S(2)}) collective-permute-start(bf16[384,768]{1,0:T(8,128)(2,1)} %collective-permute-done.23.refs_2_), channel_id=1, source_target_pairs={{0,4},{4,0},{8,12},{12,8},{16,20},{20,16},{24,28},{28,24},{1,5},{5... | collective-permute-start | bytes 1769480 | tf_op jit(solution)/shard_map/ppermute | solution.py:34
  137.7 39.8 %collective-permute-start.26 = (bf16[384,768]{1,0:T(8,128)(2,1)}, bf16[384,768]{1,0:T(8,128)(2,1)}, u32[]{:S(2)}, u32[]{:S(2)}) collective-permute-start(bf16[384,768]{1,0:T(8,128)(2,1)} %collective-permute-done.25.refs_4_), channel_id=1, source_target_pairs={{0,4},{4,0},{8,12},{12,8},{16,20},{20,16},{24,28},{28,24},{1,5},{5... | collective-permute-start | bytes 1769480 | tf_op jit(solution)/shard_map/ppermute | solution.py:34
  139.1 50.1 %collective-permute-start.28 = (bf16[384,768]{1,0:T(8,128)(2,1)}, bf16[384,768]{1,0:T(8,128)(2,1)}, u32[]{:S(2)}, u32[]{:S(2)}) collective-permute-start(bf16[384,768]{1,0:T(8,128)(2,1)} %collective-permute-done.27.refs_6_), channel_id=1, source_target_pairs={{0,4},{4,0},{8,12},{12,8},{16,20},{20,16},{24,28},{28,24},{1,5},{5... | collective-permute-start | bytes 1769480 | tf_op jit(solution)/shard_map/ppermute | solution.py:34
  139.7 10.3 %collective-permute-start.19 = (bf16[256,768]{1,0:T(8,128)(2,1)}, bf16[256,768]{1,0:T(8,128)(2,1)}, u32[]{:S(2)}, u32[]{:S(2)}) collective-permute-start(bf16[256,768]{1,0:T(8,128)(2,1)} %get-tuple-element.322.x0.refs_0_), channel_id=1, source_target_pairs={{0,2},{1,3},{2,0},{3,1},{4,6},{5,7},{6,4},{7,5},{8,10},{9,11},{10,... | collective-permute-start | bytes 1179656 | tf_op jit(solution)/shard_map/ppermute | solution.py:29
  150.0 44.1 %collective-permute-start.21 = (bf16[256,768]{1,0:T(8,128)(2,1)}, bf16[256,768]{1,0:T(8,128)(2,1)}, u32[]{:S(2)}, u32[]{:S(2)}) collective-permute-start(bf16[256,768]{1,0:T(8,128)(2,1)} %collective-permute-done.19.x0.refs_2_), channel_id=1, source_target_pairs={{0,1},{1,0},{2,3},{3,2},{4,5},{5,4},{6,7},{7,6},{8,9},{9,8},{10,11... | collective-permute-start | bytes 1179656 | tf_op jit(solution)/shard_map/ppermute | solution.py:29
  199.3 10.2 %collective-permute-start.31 = (bf16[128,768]{1,0:T(8,128)(2,1)}, bf16[128,768]{1,0:T(8,128)(2,1)}, u32[]{:S(2)}, u32[]{:S(2)}) collective-permute-start(bf16[128,768]{1,0:T(8,128)(2,1)} %get-tuple-element.314), channel_id=1, source_target_pairs={{0,1},{1,0},{2,3},{3,2},{4,5},{5,4},{6,7},{7,6},{8,9},{9,8},{10,11... | collective-permute-start | bytes 589832 | tf_op jit(solution)/shard_map/ppermute | solution.py:29
  199.4 10.1 %collective-permute-start.32 = (bf16[128,768]{1,0:T(8,128)(2,1)}, bf16[128,768]{1,0:T(8,128)(2,1)}, u32[]{:S(2)}, u32[]{:S(2)}) collective-permute-start(bf16[128,768]{1,0:T(8,128)(2,1)} %add_convert_fusion.11), channel_id=1, source_target_pairs={{0,2},{1,3},{2,0},{3,1},{4,6},{5,7},{6,4},{7,5},{8,10},{9,11},{10,... | collective-permute-start | bytes 589832 | tf_op jit(solution)/shard_map/ppermute | solution.py:29
  202.7 12.7 %collective-permute-start.34 = (bf16[256,768]{1,0:T(8,128)(2,1)}, bf16[256,768]{1,0:T(8,128)(2,1)}, u32[]{:S(2)}, u32[]{:S(2)}) collective-permute-start(bf16[256,768]{1,0:T(8,128)(2,1)} %add_convert_fusion.3), channel_id=1, source_target_pairs={{0,2},{1,3},{2,0},{3,1},{4,6},{5,7},{6,4},{7,5},{8,10},{9,11},{10,... | collective-permute-start | bytes 1179656 | tf_op jit(solution)/shard_map/ppermute | solution.py:29
  218.2 12.2 %collective-permute-start.39 = (bf16[256,768]{1,0:T(8,128)(2,1)}, bf16[256,768]{1,0:T(8,128)(2,1)S(1)}, u32[]{:S(2)}, u32[]{:S(2)}) collective-permute-start(bf16[256,768]{1,0:T(8,128)(2,1)} %get-tuple-element.330.refs_5_.refs_4_), channel_id=1, source_target_pairs={{0,2},{1,3},{2,0},{3,1},{4,6},{5,7},{6,4},{7,5},{8,10},{9,11},{10,... | collective-permute-start | bytes 1179656 | tf_op jit(solution)/shard_map/ppermute | solution.py:29
  219.6 13.7 %collective-permute-start.36 = (bf16[128,768]{1,0:T(8,128)(2,1)S(1)}, bf16[128,768]{1,0:T(8,128)(2,1)S(1)}, u32[]{:S(2)}, u32[]{:S(2)}) collective-permute-start(bf16[128,768]{1,0:T(8,128)(2,1)S(1)} %copy-done.96), channel_id=1, source_target_pairs={{0,2},{1,3},{2,0},{3,1},{4,6},{5,7},{6,4},{7,5},{8,10},{9,11},{10,... | collective-permute-start | bytes 589832 | tf_op jit(solution)/shard_map/ppermute | solution.py:29
  220.2 14.5 %collective-permute-start.38 = (bf16[256,768]{1,0:T(8,128)(2,1)}, bf16[256,768]{1,0:T(8,128)(2,1)S(1)}, u32[]{:S(2)}, u32[]{:S(2)}) collective-permute-start(bf16[256,768]{1,0:T(8,128)(2,1)} %get-tuple-element.330.refs_5_.refs_4_), channel_id=1, source_target_pairs={{0,1},{1,0},{2,3},{3,2},{4,5},{5,4},{6,7},{7,6},{8,9},{9,8},{10,11... | collective-permute-start | bytes 1179656 | tf_op jit(solution)/shard_map/ppermute | solution.py:29
  285.2 10.6 %collective-permute-start.48 = (bf16[128,768]{1,0:T(8,128)(2,1)}, bf16[128,768]{1,0:T(8,128)(2,1)}, u32[]{:S(2)}, u32[]{:S(2)}) collective-permute-start(bf16[128,768]{1,0:T(8,128)(2,1)} %get-tuple-element.353), channel_id=1, source_target_pairs={{0,1},{1,0},{2,3},{3,2},{4,5},{5,4},{6,7},{7,6},{8,9},{9,8},{10,11... | collective-permute-start | bytes 589832 | tf_op jit(solution)/shard_map/ppermute | solution.py:29
  327.4 11.5 %collective-permute-start.59 = (bf16[256,768]{1,0:T(8,128)(2,1)}, bf16[256,768]{1,0:T(8,128)(2,1)}, u32[]{:S(2)}, u32[]{:S(2)}) collective-permute-start(bf16[256,768]{1,0:T(8,128)(2,1)} %add_convert_fusion.2), channel_id=1, source_target_pairs={{0,2},{1,3},{2,0},{3,1},{4,6},{5,7},{6,4},{7,5},{8,10},{9,11},{10,... | collective-permute-start | bytes 1179656 | tf_op jit(solution)/shard_map/ppermute | solution.py:29
  342.5 15.7 %collective-permute-start.61 = (bf16[256,768]{1,0:T(8,128)(2,1)}, bf16[256,768]{1,0:T(8,128)(2,1)}, u32[]{:S(2)}, u32[]{:S(2)}) collective-permute-start(bf16[256,768]{1,0:T(8,128)(2,1)} %get-tuple-element.395.d0.refs_4_), channel_id=1, source_target_pairs={{0,2},{1,3},{2,0},{3,1},{4,6},{5,7},{6,4},{7,5},{8,10},{9,11},{10,... | collective-permute-start | bytes 1179656 | tf_op jit(solution)/shard_map/ppermute | solution.py:29
  343.7 13.1 %collective-permute-start.64 = (bf16[1,192,192]{2,1,0:T(8,128)(2,1)}, bf16[1,192,192]{2,1,0:T(8,128)(2,1)}, u32[]{:S(2)}, u32[]{:S(2)}) collective-permute-start(bf16[1,192,192]{2,1,0:T(8,128)(2,1)} %get-tuple-element.408), channel_id=1, source_target_pairs={{0,2},{1,3},{2,0},{3,1},{4,6},{5,7},{6,4},{7,5},{8,10},{9,11},{10,... | collective-permute-start | bytes 221192 | tf_op jit(solution)/shard_map/ppermute | solution.py:29
  344.8 13.4 %collective-permute-start.65 = (bf16[1,192,192]{2,1,0:T(8,128)(2,1)}, bf16[1,192,192]{2,1,0:T(8,128)(2,1)}, u32[]{:S(2)}, u32[]{:S(2)}) collective-permute-start(bf16[1,192,192]{2,1,0:T(8,128)(2,1)} %get-tuple-element.411), channel_id=1, source_target_pairs={{0,3},{1,2},{2,1},{3,0},{4,7},{5,6},{6,5},{7,4},{8,11},{9,10},{10,... | collective-permute-start | bytes 221192 | tf_op jit(solution)/shard_map/ppermute | solution.py:29
  368.0 48.0 %collective-permute-start.79 = (bf16[2,384,768]{2,1,0:T(8,128)(2,1)}, bf16[2,384,768]{2,1,0:T(8,128)(2,1)}, u32[]{:S(2)}, u32[]{:S(2)}) collective-permute-start(bf16[2,384,768]{2,1,0:T(8,128)(2,1)} %get-tuple-element.567), channel_id=1, source_target_pairs={{0,4},{4,0},{8,12},{12,8},{16,20},{20,16},{24,28},{28,24},{1,5},{5... | collective-permute-start | bytes 3538952 | tf_op jit(solution)/shard_map/ppermute | solution.py:34
  370.5 21.3 %collective-permute-start.69 = (bf16[256,768]{1,0:T(8,128)(2,1)}, bf16[256,768]{1,0:T(8,128)(2,1)}, u32[]{:S(2)}, u32[]{:S(2)}) collective-permute-start(bf16[256,768]{1,0:T(8,128)(2,1)} %get-tuple-element.405), channel_id=1, source_target_pairs={{0,1},{1,0},{2,3},{3,2},{4,5},{5,4},{6,7},{7,6},{8,9},{9,8},{10,11... | collective-permute-start | bytes 1179656 | tf_op jit(solution)/shard_map/ppermute | solution.py:29
  371.5 20.8 %collective-permute-start.70 = (bf16[256,768]{1,0:T(8,128)(2,1)}, bf16[256,768]{1,0:T(8,128)(2,1)}, u32[]{:S(2)}, u32[]{:S(2)}) collective-permute-start(bf16[256,768]{1,0:T(8,128)(2,1)} %add_convert_fusion.1), channel_id=1, source_target_pairs={{0,2},{1,3},{2,0},{3,1},{4,6},{5,7},{6,4},{7,5},{8,10},{9,11},{10,... | collective-permute-start | bytes 1179656 | tf_op jit(solution)/shard_map/ppermute | solution.py:29
  380.4 11.4 %collective-permute-start.75 = (bf16[128,768]{1,0:T(8,128)(2,1)}, bf16[128,768]{1,0:T(8,128)(2,1)}, u32[]{:S(2)}, u32[]{:S(2)}) collective-permute-start(bf16[128,768]{1,0:T(8,128)(2,1)} %get-tuple-element.425.refs_1_.d0), channel_id=1, source_target_pairs={{0,2},{1,3},{2,0},{3,1},{4,6},{5,7},{6,4},{7,5},{8,10},{9,11},{10,... | collective-permute-start | bytes 589832 | tf_op jit(solution)/shard_map/ppermute | solution.py:29
  391.3 30.3 %collective-permute-start.80 = (bf16[2,384,768]{2,1,0:T(8,128)(2,1)}, bf16[2,384,768]{2,1,0:T(8,128)(2,1)}, u32[]{:S(2)}, u32[]{:S(2)}) collective-permute-start(bf16[2,384,768]{2,1,0:T(8,128)(2,1)} %get-tuple-element.569), channel_id=1, source_target_pairs={{0,4},{4,0},{8,12},{12,8},{16,20},{20,16},{24,28},{28,24},{1,5},{5... | collective-permute-start | bytes 3538952 | tf_op jit(solution)/shard_map/ppermute | solution.py:34
  395.9 21.0 %collective-permute-start.72 = (bf16[256,768]{1,0:T(8,128)(2,1)}, bf16[256,768]{1,0:T(8,128)(2,1)}, u32[]{:S(2)}, u32[]{:S(2)}) collective-permute-start(bf16[256,768]{1,0:T(8,128)(2,1)} %get-tuple-element.434.d0.refs_1_), channel_id=1, source_target_pairs={{0,2},{1,3},{2,0},{3,1},{4,6},{5,7},{6,4},{7,5},{8,10},{9,11},{10,... | collective-permute-start | bytes 1179656 | tf_op jit(solution)/shard_map/ppermute | solution.py:29
  414.4 15.7 %collective-permute-start.71 = (bf16[256,768]{1,0:T(8,128)(2,1)}, bf16[256,768]{1,0:T(8,128)(2,1)}, u32[]{:S(2)}, u32[]{:S(2)}) collective-permute-start(bf16[256,768]{1,0:T(8,128)(2,1)} %get-tuple-element.434.d0.refs_1_), channel_id=1, source_target_pairs={{0,1},{1,0},{2,3},{3,2},{4,5},{5,4},{6,7},{7,6},{8,9},{9,8},{10,11... | collective-permute-start | bytes 1179656 | tf_op jit(solution)/shard_map/ppermute | solution.py:29
  415.9 10.9 %collective-permute-start.81 = (bf16[1,192,192]{2,1,0:T(8,128)(2,1)S(1)}, bf16[1,192,192]{2,1,0:T(8,128)(2,1)S(1)}, u32[]{:S(2)}, u32[]{:S(2)}) collective-permute-start(bf16[1,192,192]{2,1,0:T(8,128)(2,1)S(1)} %copy-done.118), channel_id=1, source_target_pairs={{0,2},{1,3},{2,0},{3,1},{4,6},{5,7},{6,4},{7,5},{8,10},{9,11},{10,... | collective-permute-start | bytes 221192 | tf_op jit(solution)/shard_map/ppermute | solution.py:29
  424.0 17.9 %collective-permute-start.83 = (bf16[384,768]{1,0:T(8,128)(2,1)}, bf16[384,768]{1,0:T(8,128)(2,1)}, u32[]{:S(2)}, u32[]{:S(2)}) collective-permute-start(bf16[384,768]{1,0:T(8,128)(2,1)} %fusion.21), channel_id=1, source_target_pairs={{0,8},{4,12},{8,16},{12,20},{16,24},{20,28},{24,0},{28,4},{1,9},{5... | collective-permute-start | bytes 1769480 | tf_op jit(solution)/shard_map/ppermute | solution.py:183
  466.1 51.5 %collective-permute-start.97 = (bf16[1,192,1152]{2,1,0:T(8,128)(2,1)}, bf16[1,192,1152]{2,1,0:T(8,128)(2,1)}, u32[]{:S(2)}, u32[]{:S(2)}) collective-permute-start(bf16[1,192,1152]{2,1,0:T(8,128)(2,1)} %get-tuple-element.415), channel_id=1, source_target_pairs={{0,4},{4,0},{8,12},{12,8},{16,20},{20,16},{24,28},{28,24},{1,5},{5... | collective-permute-start | bytes 1327112 | tf_op jit(solution)/shard_map/ppermute | solution.py:34
  468.2 27.5 %collective-permute-start.89 = (bf16[128,768]{1,0:T(8,128)(2,1)}, bf16[128,768]{1,0:T(8,128)(2,1)}, u32[]{:S(2)}, u32[]{:S(2)}) collective-permute-start(bf16[128,768]{1,0:T(8,128)(2,1)} %get-tuple-element.491), channel_id=1, source_target_pairs={{0,1},{1,0},{2,3},{3,2},{4,5},{5,4},{6,7},{7,6},{8,9},{9,8},{10,11... | collective-permute-start | bytes 589832 | tf_op jit(solution)/shard_map/ppermute | solution.py:29
  469.0 21.2 %collective-permute-start.84 = (bf16[1,192,192]{2,1,0:T(8,128)(2,1)}, bf16[1,192,192]{2,1,0:T(8,128)(2,1)}, u32[]{:S(2)}, u32[]{:S(2)}) collective-permute-start(bf16[1,192,192]{2,1,0:T(8,128)(2,1)} %get-tuple-element.463), channel_id=1, source_target_pairs={{0,1},{1,0},{2,3},{3,2},{4,5},{5,4},{6,7},{7,6},{8,9},{9,8},{10,11... | collective-permute-start | bytes 221192 | tf_op jit(solution)/shard_map/ppermute | solution.py:29
  469.3 21.9 %collective-permute-start.87 = (bf16[1,192,192]{2,1,0:T(8,128)(2,1)}, bf16[1,192,192]{2,1,0:T(8,128)(2,1)}, u32[]{:S(2)}, u32[]{:S(2)}) collective-permute-start(bf16[1,192,192]{2,1,0:T(8,128)(2,1)} %get-tuple-element.483), channel_id=1, source_target_pairs={{0,2},{1,3},{2,0},{3,1},{4,6},{5,7},{6,4},{7,5},{8,10},{9,11},{10,... | collective-permute-start | bytes 221192 | tf_op jit(solution)/shard_map/ppermute | solution.py:29
  470.3 17.3 %collective-permute-start.86 = (bf16[384,768]{1,0:T(8,128)(2,1)}, bf16[384,768]{1,0:T(8,128)(2,1)}, u32[]{:S(2)}, u32[]{:S(2)}) collective-permute-start(bf16[384,768]{1,0:T(8,128)(2,1)} %fusion.1), channel_id=1, source_target_pairs={{0,8},{4,12},{8,16},{12,20},{16,24},{20,28},{24,0},{28,4},{1,9},{5... | collective-permute-start | bytes 1769480 | tf_op jit(solution)/shard_map/ppermute | solution.py:183
  491.3 26.3 %collective-permute-start.98 = (bf16[1,192,1152]{2,1,0:T(8,128)(2,1)}, bf16[1,192,1152]{2,1,0:T(8,128)(2,1)}, u32[]{:S(2)}, u32[]{:S(2)}) collective-permute-start(bf16[1,192,1152]{2,1,0:T(8,128)(2,1)} %get-tuple-element.461), channel_id=1, source_target_pairs={{0,4},{4,0},{8,12},{12,8},{16,20},{20,16},{24,28},{28,24},{1,5},{5... | collective-permute-start | bytes 1327112 | tf_op jit(solution)/shard_map/ppermute | solution.py:34
  492.3 14.2 %collective-permute-start.92 = (bf16[256,768]{1,0:T(8,128)(2,1)}, bf16[256,768]{1,0:T(8,128)(2,1)}, u32[]{:S(2)}, u32[]{:S(2)}) collective-permute-start(bf16[256,768]{1,0:T(8,128)(2,1)} %add_convert_fusion), channel_id=1, source_target_pairs={{0,2},{1,3},{2,0},{3,1},{4,6},{5,7},{6,4},{7,5},{8,10},{9,11},{10,... | collective-permute-start | bytes 1179656 | tf_op jit(solution)/shard_map/ppermute | solution.py:29
  495.7 18.4 %collective-permute-start.93 = (bf16[1,192,1152]{2,1,0:T(8,128)(2,1)}, bf16[1,192,1152]{2,1,0:T(8,128)(2,1)}, u32[]{:S(2)}, u32[]{:S(2)}) collective-permute-start(bf16[1,192,1152]{2,1,0:T(8,128)(2,1)} %get-tuple-element.479), channel_id=1, source_target_pairs={{0,4},{4,0},{8,12},{12,8},{16,20},{20,16},{24,28},{28,24},{1,5},{5... | collective-permute-start | bytes 1327112 | tf_op jit(solution)/shard_map/ppermute | solution.py:34
  502.3 21.1 %collective-permute-start.99 = (bf16[1,192,1152]{2,1,0:T(8,128)(2,1)}, bf16[1,192,1152]{2,1,0:T(8,128)(2,1)}, u32[]{:S(2)}, u32[]{:S(2)}) collective-permute-start(bf16[1,192,1152]{2,1,0:T(8,128)(2,1)} %get-tuple-element.488), channel_id=1, source_target_pairs={{0,4},{4,0},{8,12},{12,8},{16,20},{20,16},{24,28},{28,24},{1,5},{5... | collective-permute-start | bytes 1327112 | tf_op jit(solution)/shard_map/ppermute | solution.py:34
  515.2 16.3 %collective-permute-start.94 = (bf16[192,1152]{1,0:T(8,128)(2,1)S(1)}, bf16[192,1152]{1,0:T(8,128)(2,1)S(1)}, u32[]{:S(2)}, u32[]{:S(2)}) collective-permute-start(bf16[192,1152]{1,0:T(8,128)(2,1)S(1)} %bitcast_convert_fusion), channel_id=1, source_target_pairs={{24,16},{28,20},{8,0},{12,4},{25,17},{29,21},{9,1},{13,5},{26,18},... | collective-permute-start | bytes 1327112 | tf_op jit(solution)/shard_map/ppermute | solution.py:201
  526.4 110.0 %collective-permute-start.50 = (bf16[128,768]{1,0:T(8,128)(2,1)}, bf16[128,768]{1,0:T(8,128)(2,1)}, u32[]{:S(2)}, u32[]{:S(2)}) collective-permute-start(bf16[128,768]{1,0:T(8,128)(2,1)} %get-tuple-element.369), channel_id=1, source_target_pairs={{0,1},{1,0},{2,3},{3,2},{4,5},{5,4},{6,7},{7,6},{8,9},{9,8},{10,11... | collective-permute-start | bytes 589832 | tf_op jit(solution)/shard_map/ppermute | solution.py:29
  526.4 110.0 %collective-permute-start.52 = (bf16[128,768]{1,0:T(8,128)(2,1)}, bf16[128,768]{1,0:T(8,128)(2,1)}, u32[]{:S(2)}, u32[]{:S(2)}) collective-permute-start(bf16[128,768]{1,0:T(8,128)(2,1)} %add_convert_fusion.8), channel_id=1, source_target_pairs={{0,2},{1,3},{2,0},{3,1},{4,6},{5,7},{6,4},{7,5},{8,10},{9,11},{10,... | collective-permute-start | bytes 589832 | tf_op jit(solution)/shard_map/ppermute | solution.py:29
  527.5 30.1 %collective-permute-start.104 = (bf16[384,768]{1,0:T(8,128)(2,1)S(1)}, bf16[384,768]{1,0:T(8,128)(2,1)S(1)}, u32[]{:S(2)}, u32[]{:S(2)}) collective-permute-start(bf16[384,768]{1,0:T(8,128)(2,1)S(1)} %copy-done.34), channel_id=1, source_target_pairs={{0,8},{4,12},{8,16},{12,20},{16,24},{20,28},{24,0},{28,4},{1,9},{5... | collective-permute-start | bytes 1769480 | tf_op jit(solution)/shard_map/ppermute | solution.py:183
  529.6 24.8 %collective-permute-start.103 = (bf16[192,1152]{1,0:T(8,128)(2,1)}, bf16[192,1152]{1,0:T(8,128)(2,1)S(1)}, u32[]{:S(2)}, u32[]{:S(2)}) collective-permute-start(bf16[192,1152]{1,0:T(8,128)(2,1)} %fusion.23), channel_id=1, source_target_pairs={{0,8},{4,12},{16,24},{20,28},{24,0},{28,4},{1,9},{5,13},{17,25},{2... | collective-permute-start | bytes 1327112 | tf_op jit(solution)/shard_map/ppermute | solution.py:183
  531.6 25.3 %collective-permute-start.102 = (f32[4632]{0:T(1024)S(1)}, f32[4632]{0:T(1024)S(1)}, u32[]{:S(2)}, u32[]{:S(2)}) collective-permute-start(f32[4632]{0:T(1024)S(1)} %add.538), channel_id=1, source_target_pairs={{0,8},{4,12},{8,0},{12,4},{16,24},{20,28},{24,16},{28,20},{1,9},{5... | collective-permute-start | bytes 55592 | tf_op jit(solution)/shard_map/ppermute | solution.py:34
  561.8 11.4 %collective-permute-start.110 = (bf16[96,512]{1,0:T(8,128)(2,1)}, bf16[96,512]{1,0:T(8,128)(2,1)}, u32[]{:S(2)}, u32[]{:S(2)}) collective-permute-start(bf16[96,512]{1,0:T(8,128)(2,1)} %get-tuple-element.576), channel_id=1, source_target_pairs={{0,1},{1,0},{2,3},{3,2},{4,5},{5,4},{6,7},{7,6},{8,9},{9,8},{10,11... | collective-permute-start | bytes 294920 | tf_op jit(solution)/shard_map/ppermute | solution.py:29
  569.8 25.3 %collective-permute-start.101 = (bf16[192,1152]{1,0:T(8,128)(2,1)}, bf16[192,1152]{1,0:T(8,128)(2,1)}, u32[]{:S(2)}, u32[]{:S(2)}) collective-permute-start(bf16[192,1152]{1,0:T(8,128)(2,1)} %fusion.22), channel_id=1, source_target_pairs={{16,0},{20,4},{17,1},{21,5},{18,2},{22,6},{19,3},{23,7}} | collective-permute-start | bytes 1327112 | tf_op jit(solution)/shard_map/ppermute | solution.py:201
  571.1 16.6 %collective-permute-start.105 = (bf16[192,1152]{1,0:T(8,128)(2,1)}, bf16[192,1152]{1,0:T(8,128)(2,1)}, u32[]{:S(2)}, u32[]{:S(2)}) collective-permute-start(bf16[192,1152]{1,0:T(8,128)(2,1)} %fusion.8), channel_id=1, source_target_pairs={{0,8},{4,12},{8,16},{12,20},{24,0},{28,4},{1,9},{5,13},{9,17},{13,... | collective-permute-start | bytes 1327112 | tf_op jit(solution)/shard_map/ppermute | solution.py:183
  573.2 22.0 %collective-permute-start.113 = (f32[4632]{0:T(1024)}, f32[4632]{0:T(1024)S(1)}, u32[]{:S(2)}, u32[]{:S(2)}) collective-permute-start(f32[4632]{0:T(1024)} %add.545), channel_id=1, source_target_pairs={{0,16},{4,20},{8,24},{12,28},{16,0},{20,4},{24,8},{28,12},{1,17},{... | collective-permute-start | bytes 55592 | tf_op jit(solution)/shard_map/ppermute | solution.py:34
  589.5 12.4 %collective-permute-start.106 = (bf16[192,1152]{1,0:T(8,128)(2,1)S(1)}, bf16[192,1152]{1,0:T(8,128)(2,1)S(1)}, u32[]{:S(2)}, u32[]{:S(2)}) collective-permute-start(bf16[192,1152]{1,0:T(8,128)(2,1)S(1)} %fusion.12), channel_id=1, source_target_pairs={{0,8},{4,12},{8,16},{12,20},{16,24},{20,28},{1,9},{5,13},{9,17},{1... | collective-permute-start | bytes 1327112 | tf_op jit(solution)/shard_map/ppermute | solution.py:183
  (186 other events, 1413.1 us)
where the time goes:
time: 653 us; the launch traced here: 645 us
  waiting for transfers between devices  241 us (37%)
  Pallas kernels  213 us (33%)
  starting transfers between devices  88 us (13%)
  other arithmetic  69.6 us (11%)
  local copies, waits for them, and re-layouts  30.5 us (5%)
    pallas_call x48, Pallas kernels, call(): pl.pallas_call(body, grid=(1,), in_specs=specs, out_specs=[whole(o) for o...  204 us
    ppermute x85, waiting for transfers between devices, seq_swap(): return lax.ppermute(x, 'seq', [(i, i ^ k) for i in range(n)])  88.7 us
    ppermute x20, waiting for transfers between devices, batch_swap(): return lax.ppermute(x, 'batch', [(i, i ^ k) for i in range(n)])  66.9 us
    ppermute x85, starting transfers between devices, seq_swap(): return lax.ppermute(x, 'seq', [(i, i ^ k) for i in range(n)])  46.6 us
    ppermute x6, waiting for transfers between devices, ring_reduce(): moved = lax.ppermute(sent, 'batch', [(i, (i + 2) % nb) for i in active])  41.7 us
    ppermute x6, waiting for transfers between devices, ring_gathers(): current = [lax.ppermute(x, 'batch', shift) for x in current]  41.3 us
    ppermute x20, starting transfers between devices, batch_swap(): return lax.ppermute(x, 'batch', [(i, i ^ k) for i in range(n)])  25.4 us
    convert_element_type x11, other arithmetic, far_payload(): return (keep_far + seq_swap(send_far, 1).astype(F32)).astype(BF16)  13.8 us
  transfers between devices with their start and end apart: 119, of which 56 were waited for; matrix products, arithmetic and copies ran while one was open for 12% of the time, Pallas kernels for 20%

commit v1 on v0

v1 whole, which is shorter than its diff:
```python
import functools
import math

import jax
import jax.numpy as jnp
from jax import lax
from jax.experimental import pallas as pl
from jax.experimental.pallas import tpu as pltpu
from jax.sharding import PartitionSpec as P

D = 768
HEADS = 12
HEAD = 64
FF = 2048
STEP = 5

eps_norm = 1e-06
adam_eps = 1e-06
lamb_rate = 0.5
decay_weight = 0.01
masked_score = -1000000000.0

F32 = jnp.float32
BF16 = jnp.bfloat16

FLOPS, BYTES = 10**13, 10**10


def seq_swap(x, k):
    n = lax.axis_size("seq")
    return lax.ppermute(x, "seq", [(i, i ^ k) for i in range(n)])


def batch_swap(x, k):
    n = lax.axis_size("batch")
    return lax.ppermute(x, "batch", [(i, i ^ k) for i in range(n)])


def gather_blocks(x):
    other, near = seq_swap(x, 2), seq_swap(x, 1)
    return [x, near, other, seq_swap(tie(other, near), 1)]


def xor_blocks(x, s):
    n = x.shape[0]
    for k in (1, 2):
        swapped = jnp.stack([x[j ^ k] for j in range(n)])
        x = jnp.where((s & k) != 0, swapped, x)
    return x


def seq_exchange(blocks, s):
    n = blocks.shape[0]
    mine = xor_blocks(blocks, s)
    got = jnp.stack([mine[0]] + [seq_swap(mine[j], j) for j in range(1, n)])
    return xor_blocks(got, s)


def tie(x, *others):
    return lax.optimization_barrier((x, others))[0]


def ring_shift(x, active=None):
    nb = lax.axis_size("batch")
    return lax.ppermute(x, "batch", [(i, (i + 2) % nb) for i in (range(nb) if active is None else active)])


def ring_gather(block):
    rounds = lax.axis_size("batch") // 2
    after = yield None
    moving, got, paired = block if after is None else tie(block, after), [], None
    for k in range(rounds):
        following = None
        if k + 1 < rounds:
            payload = moving if paired is None else tie(moving, paired)
            following = ring_shift(payload)
        got.append(moving)
        paired = batch_swap(moving if following is not None or paired is None else tie(moving, paired), 1)
        got.append(paired)
        after = yield moving if following is None else payload
        if following is not None:
            moving = following if after is None else tie(following, after)
            paired = got[-1]
    yield got


def assemble_body(by_lanes, moves, count, low, *refs):
    here = len(refs) - 1 - low[1]
    ins, outs, sem = refs[:here], refs[here:-1], refs[-1]
    b = lax.axis_index("batch")
    z, y = b // 2, b % 2
    ring, copies = count // 2, []
    for i, ref in enumerate(ins):
        k, e = (low[0] + i) // 2, (low[0] + i) % 2
        at = lax.rem(z + ring - k, ring) * 2 + (y + e - 2 * y * e)
        for which, (r0, r1), (c0, c1), (to_row, to_lane) in moves:
            out = outs[which]
            rows = pl.ds(to_row, r1 - r0)
            if by_lanes:
                start = pl.multiple_of(at * (out.shape[1] // count) + to_lane, 128)
                target = out.at[rows, pl.ds(start, c1 - c0)]
            else:
                target = out.at[at, rows, pl.ds(to_lane, c1 - c0)]
            copies.append(pltpu.make_async_copy(ref.at[r0:r1, c0:c1], target, sem.at[len(copies)]))
    for copy in copies:
        copy.start()
    for copy in copies:
        copy.wait()


def assemble(blocks, moves, shapes, by_lanes, name, last=0):
    count = len(blocks)
    outs = [jax.ShapeDtypeStruct((h, count * w) if by_lanes else (count, h, w), BF16) for h, w in shapes]
    any_space = pl.BlockSpec(memory_space=pl.ANY)
    made = []
    for low, high in ((0, count - last), (count - last, count)):
        if low == high:
            continue
        part_of = blocks[low:high]

        def body(*refs, low=low, made=tuple(made), part_of=part_of):
            given = refs[: len(part_of)]
            assemble_body(by_lanes, moves, count, (low, len(outs)), *given, *refs[len(part_of) + len(made) :])

        made = pl.pallas_call(
            body,
            in_specs=[pl.BlockSpec(memory_space=pltpu.VMEM)] * len(part_of) + [any_space] * len(made),
            out_specs=[any_space] * len(outs),
            out_shape=outs,
            input_output_aliases={len(part_of) + i: i for i in range(len(made))},
            scratch_shapes=[pltpu.SemaphoreType.DMA((len(part_of) * len(moves),))],
            cost_estimate=pl.CostEstimate(flops=FLOPS, bytes_accessed=BYTES, transcendentals=0),
            name=f"{name}_{low}",
        )(*part_of, *made)
    return made


def gathered_rows(got, name):
    h, w = got[0].shape
    return assemble(got, [(0, (0, h), (0, w), (0, 0))], [(h, w)], False, name)[0]


def gathered_lanes(got, name):
    h, w = got[0].shape
    if w % 128 == 0:
        return assemble(got, [(0, (0, h), (0, w), (0, 0))], [(h, w)], True, name)[0]
    return gathered_rows(got, name).swapaxes(0, 1).reshape(h, -1)


def gathered_feeds(got, rows, name):
    h, w = got[0].shape
    fc = w - 256
    moves = [(0, (0, h), (0, fc), (0, 0))]
    for g in range(D // 128):
        r, c = g % 3 * rows, fc + g // 3 * 128
        moves.append((1, (r, r + rows), (c, c + 128), (0, 128 * g)))
    return assemble(got, moves, [(h, fc), (rows, D)], False, name, 2)


def pair_blocks(blocks):
    y = lax.axis_index("batch") % 2
    pairs = blocks.reshape((blocks.shape[0] // 2, 2) + blocks.shape[1:])
    return [lax.dynamic_index_in_dim(pairs, i, 1, keepdims=False) for i in (y, 1 - y)]


def hop_body(step, counts, moving, riding, *refs):
    count = len(counts)
    kept, got = refs[:count], refs[count : 2 * count]
    refs = list(refs[2 * count :])
    moved = refs.pop(0) if moving else None
    extra = refs.pop(0) if riding else None
    out, one, two, sem = refs
    ring = lax.axis_size("batch") // 2
    dest = lax.rem(lax.axis_index("batch") // 2 + 2 * ring - step, ring)
    for n in range(count):
        low = sum(counts[:n])

        @pl.when((dest >= low) & (dest < low + counts[n]))
        def _(n=n, low=low):
            mine = pltpu.make_async_copy(kept[n].at[dest - low], one, sem.at[0])
            other = pltpu.make_async_copy(got[n].at[dest - low], two, sem.at[1])
            mine.start()
            other.start()
            mine.wait()
            other.wait()

    total = one[...].astype(F32) + two[...].astype(F32)
    rows = one.shape[0]
    if moving:
        total = total + moved[:rows, :].astype(F32)
    out[:rows, :] = total.astype(out.dtype)
    if riding:
        lines = jnp.concatenate([extra[dest * 2], extra[dest * 2 + 1]], axis=0)
        if moving:
            lines = lines + moved[rows : rows + 2, :].astype(F32)
        out[rows:, :] = jnp.concatenate([lines, jnp.zeros((14, lines.shape[1]), F32)], axis=0).astype(out.dtype)


def hop(parts, step, moved, extra, dtype, name):
    shape = parts[0][0].shape[1:]
    arrays = [k for k, _ in parts] + [g for _, g in parts]
    specs = [pl.BlockSpec(memory_space=pl.ANY)] * len(arrays)
    for x in (moved, extra):
        if x is not None:
            arrays.append(x)
            specs.append(pl.BlockSpec(memory_space=pltpu.VMEM))
    out = shape if extra is None else (shape[0] + 16, shape[1])
    return pl.pallas_call(
        functools.partial(hop_body, step, [k.shape[0] for k, _ in parts], moved is not None, extra is not None),
        in_specs=specs,
        out_specs=pl.BlockSpec(memory_space=pltpu.VMEM),
        out_shape=jax.ShapeDtypeStruct(out, dtype),
        scratch_shapes=[pltpu.VMEM(shape, BF16), pltpu.VMEM(shape, BF16), pltpu.SemaphoreType.DMA((2,))],
        cost_estimate=pl.CostEstimate(flops=FLOPS, bytes_accessed=BYTES, transcendentals=0),
        name=f"{name}_{step}",
    )(*arrays)


def ring_reduce(parts, name, extra=None, flight=None):
    ring = lax.axis_size("batch") // 2
    after = yield None
    moved = None
    for k in range(1, ring + 1):
        if moved is None:
            held = [(kept if after is None else tie(kept, after), got) for kept, got in parts]
        else:
            held, moved = parts, tie(moved, after)
        if k == ring:
            yield [hop(held, k, moved, extra, F32, name)]
            return
        sent = hop(held, k, moved, extra, BF16, name)
        moved = ring_shift(sent)
        if flight is not None:
            flight.append(moved)
        after = yield sent


def sum_seq(x):
    for k in (1, 2):
        x = x + seq_swap(x, k)
    return x


def sum_all(x):
    x = sum_seq(x)
    k = 1
    while k < lax.axis_size("batch"):
        x = x + batch_swap(x, k)
        k *= 2
    return x


class Clock:
    def __init__(self):
        self.last = None

    def now(self, x):
        return x if self.last is None else tie(x, self.last)

    def mark(self, x):
        self.last = x
        return x

    def step(self, work):
        got = work.send(self.last)
        return got if isinstance(got, list) else self.mark(got)

    def finish(self, work):
        got = None
        while not isinstance(got, list):
            got = self.step(work)
        return got


def nt(a, b):
    return lax.dot_general(a, b, (((1,), (1,)), ((), ())), preferred_element_type=F32)


def nn(a, b):
    return lax.dot_general(a, b, (((1,), (0,)), ((), ())), preferred_element_type=F32)


def tn(a, b):
    return lax.dot_general(a, b, (((0,), (0,)), ((), ())), preferred_element_type=F32)


def whole(x):
    shape = x.shape
    return pl.BlockSpec(shape, lambda i: (0,) * len(shape))


def part(shape, *index):
    return pl.BlockSpec(shape, lambda i: index)


def plain(arrays):
    return [(x, whole(x)) for x in arrays]


SCALARS = pl.BlockSpec(memory_space=pltpu.SMEM)


def call(body, ins, outs, flops, scratch=(), name=None):
    arrays = [a for a, _ in ins]
    specs = [whole(a) if s is None else s for a, s in ins]
    shapes = [jax.ShapeDtypeStruct(s, d) for s, d in outs]
    return pl.pallas_call(
        body,
        grid=(1,),
        in_specs=specs,
        out_specs=[whole(o) for o in shapes],
        out_shape=shapes,
        scratch_shapes=list(scratch),
        cost_estimate=pl.CostEstimate(flops=FLOPS, bytes_accessed=BYTES, transcendentals=0),
        name=name,
    )(*arrays)


def positions(shape, axis, owner, rows):
    at = lax.broadcasted_iota(jnp.int32, shape, axis)
    shift = rows.bit_length() - 1
    return ((owner ^ (at >> shift)) << shift) + (at & (rows - 1))


def score_bias(meta, first_row, tile, q_rows, k_rows, causal):
    keys = positions((1, 4 * k_rows), 1, meta[0], k_rows)
    if not causal:
        return jnp.where(keys < meta[1], 0.0, masked_score)
    at = first_row + lax.broadcasted_iota(jnp.int32, (tile, 1), 0)
    shift = q_rows.bit_length() - 1
    queries = ((meta[0] ^ (at >> shift)) << shift) + (at & (q_rows - 1))
    return jnp.where((keys <= queries) & (keys < meta[1]), 0.0, masked_score)


def head_mask(shape, h):
    lane = lax.broadcasted_iota(jnp.int32, shape, 1)
    return (lane >= h * HEAD) & (lane < (h + 1) * HEAD)


def attend_tile(q, k, v, bias, heads):
    mixed = jnp.zeros(q.shape, F32)
    logs = jnp.zeros((q.shape[0], 128), F32)
    q = (q.astype(F32) * 0.125).astype(BF16)
    lane = lax.broadcasted_iota(jnp.int32, logs.shape, 1)
    for h in range(heads):
        mask = head_mask(q.shape, h)
        scores = nt(jnp.where(mask, q, jnp.zeros_like(q)), k) + bias
        peak = jnp.max(scores, axis=-1, keepdims=True)
        expo = jnp.exp(scores - peak)
        total = jnp.sum(expo, axis=-1, keepdims=True)
        probs = (expo * (1.0 / total)).astype(BF16)
        mixed = jnp.where(mask, nn(probs, v), mixed)
        logs = jnp.where(lane == h, peak + jnp.log(total), logs)
    return mixed, logs


def attend_rows(meta, q_ref, k_ref, v_ref, wo_ref, first, q_rows, k_rows, causal, outs, total_ref):
    logs_ref, mixed_ref = outs[:2]
    heads = q_ref.shape[1] // HEAD

    def step(t, carry):
        at = pl.multiple_of(t * q_rows, q_rows)
        q = q_ref[pl.ds(first + at, q_rows), :]
        bias = score_bias(meta, first + at, q_rows, q_rows, k_rows, causal)
        mixed, logs = attend_tile(q, k_ref[...], v_ref[...], bias, heads)
        low = mixed.astype(BF16)
        logs_ref[pl.ds(at, q_rows), :] = logs
        mixed_ref[pl.ds(at, q_rows), :] = low
        if wo_ref is not None:
            total_ref[pl.ds(at, q_rows), :] = nn(low, wo_ref[...])
        return carry

    lax.fori_loop(0, 2, step, 0)
    if wo_ref is not None:
        outs[2][...] = total_ref[:q_rows, :].astype(outs[2].dtype)
        outs[3][...] = total_ref[q_rows:, :].astype(BF16)


def project_body(rows, mixed_ref, wo_ref, keep_ref, send_ref):
    keep_ref[...] = nn(mixed_ref[:rows, :], wo_ref[...]).astype(BF16)
    send_ref[...] = nn(mixed_ref[rows:, :], wo_ref[...]).astype(BF16)


def project(mixed, out_w, name):
    rows, dc = mixed.shape[0] // 2, mixed.shape[1]
    return call(
        functools.partial(project_body, rows),
        [(mixed, None), out_weights(out_w)],
        [((rows, D), BF16), ((rows, D), BF16)],
        4 * rows * dc * D,
        name=name,
    )


def attend_far_body(cross, raw, fused, causal, q_rows, k_rows, *refs):
    refs = list(refs)
    meta = refs.pop(0)
    queries, refs = refs[:4], refs[4:]
    sources = queries
    if cross:
        sources, refs = refs[:4], refs[4:]
    if raw:
        gain = refs.pop(0)
    wq, wk, wv = refs[:3]
    refs = refs[3:]
    wo = refs.pop(0) if fused else None
    if raw:
        rows_ref = refs.pop(0)
        for j in range(4):
            h = queries[j][...].astype(F32)
            inverse = lax.rsqrt(jnp.mean(h * h, axis=-1, keepdims=True) + eps_norm)
            rows_ref[j * q_rows : (j + 1) * q_rows, :] = (h * inverse * gain[...]).astype(BF16)
        queries = sources = [rows_ref.at[j * q_rows : (j + 1) * q_rows, :] for j in range(4)]
    q_ref, k_ref, v_ref = refs[:3]
    outs, total_ref = refs[3 : 7 if fused else 5], (refs[7] if fused else None)
    for j in range(4):
        q_ref[j * q_rows : (j + 1) * q_rows, :] = nt(queries[j][...], wq[...]).astype(BF16)
        rows = sources[j][...]
        k_ref[j * k_rows : (j + 1) * k_rows, :] = nt(rows, wk[...]).astype(BF16)
        v_ref[j * k_rows : (j + 1) * k_rows, :] = nt(rows, wv[...]).astype(BF16)
    attend_rows(meta, q_ref, k_ref, v_ref, wo, 2 * q_rows, q_rows, k_rows, causal, outs, total_ref)


def attend_near_body(causal, q_rows, k_rows, meta, q_ref, k_ref, v_ref, wo, *rest):
    attend_rows(meta, q_ref, k_ref, v_ref, wo, 0, q_rows, k_rows, causal, rest[:4], rest[4])


def attn_weights(attn_t, group):
    return [(attn_t, part((D // 4, D), 0, 4 * group + i)) for i in range(3)]


def out_weights(out_w):
    stack, place = out_w
    return (stack, pl.BlockSpec((None, stack.shape[1], D), lambda i: (place, 0, 0)))


def half_outs(q_rows, dc, keep):
    return [((2 * q_rows, 128), F32), ((2 * q_rows, dc), BF16), ((q_rows, D), keep), ((q_rows, D), BF16)]


def attend_far(meta, queries, sources, attn_t, out_w, group, causal, gain=None):
    cross, raw, fused = sources is not None, gain is not None, out_w is not None
    q_rows, dc = queries[0][1].block_shape[0], D // 4
    k_rows = sources[0][1].block_shape[0] if cross else q_rows
    flops = 2 * D * dc * (4 * q_rows + 8 * k_rows) + 16 * q_rows * k_rows * D
    return call(
        functools.partial(attend_far_body, cross, raw, fused, causal, q_rows, k_rows),
        [(meta, SCALARS)]
        + list(queries)
        + (list(sources) if cross else [])
        + ([(gain, None)] if raw else [])
        + attn_weights(attn_t, group)
        + ([out_weights(out_w)] if fused else []),
        ([((4 * q_rows, D), BF16)] if raw else [])
        + [((4 * q_rows, dc), BF16), ((4 * k_rows, dc), BF16), ((4 * k_rows, dc), BF16)]
        + half_outs(q_rows, dc, BF16)[: 4 if fused else 2],
        flops,
        [pltpu.VMEM((2 * q_rows, D), F32)] if fused else [],
        f"attend_far_{group}",
    )


def attend_near(meta, q, k, v, out_w, group, causal):
    q_rows, k_rows, dc = q.shape[0] // 4, k.shape[0] // 4, q.shape[1]
    return call(
        functools.partial(attend_near_body, causal, q_rows, k_rows),
        [(meta, SCALARS), (q, part((2 * q_rows, dc), 0, 0)), (k, None), (v, None), out_weights(out_w)],
        half_outs(q_rows, dc, F32),
        16 * q_rows * k_rows * D,
        [pltpu.VMEM((2 * q_rows, D), F32)],
        f"attend_near_{group}",
    )


STEPS = 1


def row_call(body, ins, outs, name):
    rows = ins[0].shape[0]

    def spec(shape):
        if shape[0] == 1:
            return pl.BlockSpec(shape, lambda i: (0, 0))
        return pl.BlockSpec((rows // STEPS,) + tuple(shape[1:]), lambda i: (i, 0))

    return pl.pallas_call(
        body,
        grid=(STEPS,),
        in_specs=[spec(x.shape) for x in ins],
        out_specs=[spec(s) for s, _ in outs],
        out_shape=[jax.ShapeDtypeStruct(s, d) for s, d in outs],
        cost_estimate=pl.CostEstimate(flops=FLOPS, bytes_accessed=BYTES, transcendentals=0),
        name=name,
    )(*ins)


def add_low(a, b):
    return (a.astype(F32) + b.astype(F32)).astype(BF16)


def far_payload(keep_far, send_far):
    return add_low(keep_far, seq_swap(send_far, 1))


def close_body(near_ref, core_ref, far_ref, residual_ref, gain_ref, out_ref, normed_ref):
    h = residual_ref[...].astype(F32) + near_ref[...] + core_ref[...].astype(F32) + far_ref[...].astype(F32)
    inverse = lax.rsqrt(jnp.mean(h * h, axis=-1, keepdims=True) + eps_norm)
    out_ref[...] = h
    normed_ref[...] = (h * inverse * gain_ref[...]).astype(BF16)


def close(near, core, far, residual, gain, name):
    return row_call(
        close_body, [near, core, far, residual, gain], [(near.shape, F32), (near.shape, BF16)], name
    )


def close_back_body(near_ref, core_ref, far_ref, stream_ref, gain_ref, *rest):
    if len(rest) == 4:
        upstream_ref, rest = rest[0], rest[1:]
    else:
        upstream_ref = None
    out_ref, low_ref, dgain_ref = rest
    h = stream_ref[...].astype(F32)
    up = near_ref[...] + core_ref[...].astype(F32) + far_ref[...].astype(F32)
    inverse = lax.rsqrt(jnp.mean(h * h, axis=-1, keepdims=True) + eps_norm)
    unit = h * inverse
    scaled = up * gain_ref[...]
    grad = inverse * (scaled - unit * jnp.mean(scaled * unit, axis=-1, keepdims=True))
    if upstream_ref is not None:
        grad = upstream_ref[...].astype(F32) + grad
    out_ref[...] = grad
    low_ref[...] = grad.astype(BF16)

    @pl.when(pl.program_id(0) == 0)
    def _():
        dgain_ref[...] = jnp.zeros_like(dgain_ref)

    dgain_ref[...] += jnp.sum(up * unit, axis=0, keepdims=True)


def close_back(near, core, far, stream, gain, upstream, name):
    shape = near.shape
    ins = [near, core, far, stream, gain] + ([] if upstream is None else [upstream])
    return row_call(close_back_body, ins, [(shape, F32), (shape, BF16), ((1, shape[1]), F32)], name)


def attend_back_body(cross, causal, q_rows, k_rows, tile, *refs):
    meta = refs[0]
    dz = refs[1:5]
    q_ref, qt_ref, k_ref, v_ref, logs_near, logs_far, wq, wk, wv, wo = refs[5:15]
    dq_ref, dkt_ref, dvt_ref = refs[15:18]
    outs = refs[18 : 18 + (8 if cross else 4)]
    do_ref, dot_ref, dkt_sum, dvt_sum, logs_ref = refs[18 + len(outs) :]
    heads = q_ref.shape[1] // HEAD
    for j in range(4):
        at = slice(j * q_rows, (j + 1) * q_rows)
        rows = dz[j][...]
        do_ref[at, :] = nt(rows, wo[...]).astype(BF16)
        dot_ref[:, at] = nt(wo[...], rows).astype(BF16)
    logs_ref[: 2 * q_rows, :] = logs_near[...]
    logs_ref[2 * q_rows :, :] = logs_far[...]
    dkt_sum[...] = jnp.zeros_like(dkt_sum)
    dvt_sum[...] = jnp.zeros_like(dvt_sum)

    def step(t, carry):
        at = pl.ds(pl.multiple_of(t * tile, tile), tile)
        q, do = q_ref[at, :], do_ref[at, :]
        q = (q.astype(F32) * 0.125).astype(BF16)
        qt, dot = qt_ref[:, at], dot_ref[:, at]
        logs = logs_ref[at, :]
        bias = score_bias(meta, t * tile, tile, q_rows, k_rows, causal)
        dq = jnp.zeros(q.shape, F32)
        for h in range(heads):
            mask = head_mask(q.shape, h)
            zero = jnp.zeros_like(q)
            probs = jnp.exp(nt(jnp.where(mask, q, zero), k_ref[...]) + bias - logs[:, h : h + 1])
            grad_probs = nt(jnp.where(mask, do, zero), v_ref[...])
            weighted = probs * grad_probs
            center = jnp.sum(weighted, axis=-1, keepdims=True)
            grad_scores = (weighted - probs * center).astype(BF16)
            feats = slice(h * HEAD, (h + 1) * HEAD)
            dvt_sum[feats, :] += nn(dot[feats, :], probs.astype(BF16))
            dkt_sum[feats, :] += nn(qt[feats, :], grad_scores)
            dq = jnp.where(mask, nn(grad_scores, k_ref[...]), dq)
        dq_ref[at, :] = (dq * 0.125).astype(BF16)
        return carry

    lax.fori_loop(0, 4 * q_rows // tile, step, 0)
    dkt_ref[...] = (dkt_sum[...] * 0.125).astype(BF16)
    dvt_ref[...] = dvt_sum[...].astype(BF16)

    def query_part(j):
        return nn(dq_ref[j * q_rows : (j + 1) * q_rows, :], wq[...])

    def source_part(j):
        at = slice(j * k_rows, (j + 1) * k_rows)
        return tn(dkt_ref[:, at], wk[...]) + tn(dvt_ref[:, at], wv[...])

    parts = (query_part, source_part) if cross else ((lambda j: query_part(j) + source_part(j)),)
    for n, make in enumerate(parts):
        for j in range(4):
            outs[4 * n + j][...] = make(j).astype(outs[4 * n + j].dtype)


def attend_back(meta, dz, qt, attn_t, out_w, group, saved, q_rows, k_rows, causal, cross):
    q, k, v, logs_near, logs_far = saved
    dc = q.shape[1]
    tile = min(256, 4 * q_rows)

    def four(rows):
        return [((rows, D), F32), ((rows, D), BF16), ((rows, D), BF16), ((rows, D), BF16)]

    outs = call(
        functools.partial(attend_back_body, cross, causal, q_rows, k_rows, tile),
        [(meta, SCALARS)]
        + list(dz)
        + [(q, None), (qt, None), (k, None), (v, None), (logs_near, None), (logs_far, None)]
        + attn_weights(attn_t, group)
        + [out_weights(out_w)],
        [((4 * q_rows, dc), BF16), ((dc, 4 * k_rows), BF16), ((dc, 4 * k_rows), BF16)]
        + (four(q_rows) + four(k_rows) if cross else four(q_rows)),
        80 * q_rows * k_rows * D + 4 * D * dc * (4 * q_rows + 4 * k_rows),
        [
            pltpu.VMEM((4 * q_rows, dc), BF16),
            pltpu.VMEM((dc, 4 * q_rows), BF16),
            pltpu.VMEM((dc, 4 * k_rows), F32),
            pltpu.VMEM((dc, 4 * k_rows), F32),
            pltpu.VMEM((4 * q_rows, 128), F32),
        ],
        f"attend_back_{group}",
    )
    return outs[:3], outs[3:]


def attend_weights_body(cross, q_rows, k_rows, *refs):
    queries = refs[0:4]
    sources = refs[4:8] if cross else queries
    dq, dkt, dvt, *outs = refs[8:] if cross else refs[4:]
    gq = gk = gv = None
    for j in range(4):
        at, ak = slice(j * q_rows, (j + 1) * q_rows), slice(j * k_rows, (j + 1) * k_rows)
        x, y = queries[j][...], sources[j][...]
        a, b, c = tn(dq[at, :], x), nn(dkt[:, ak], y), nn(dvt[:, ak], y)
        gq, gk, gv = (a, b, c) if j == 0 else (gq + a, gk + b, gv + c)
    for ref, g in zip(outs, (gq, gk, gv)):
        ref[...] = g.astype(BF16)


def attend_weights(queries, sources, grads, name):
    cross = sources is not None
    dq, dkt, dvt = grads
    q_rows, k_rows, dc = dq.shape[0] // 4, dkt.shape[1] // 4, dq.shape[1]
    return call(
        functools.partial(attend_weights_body, cross, q_rows, k_rows),
        list(queries) + (list(sources) if cross else []) + [(dq, None), (dkt, None), (dvt, None)],
        [((dc, D), BF16)] * 3,
        0,
        name=name,
    )


def out_total(dz, near, far, q_rows):
    total = None
    for j, ref in enumerate(dz):
        mixed = (near, far)[j // 2][(j % 2) * q_rows : (j % 2 + 1) * q_rows, :]
        x = tn(ref[...], mixed)
        total = x if j == 0 else total + x
    return total


def out_weight_body(sizes, *refs):
    outs, scratch = refs[6 * len(sizes) : -1], refs[-1]
    s, rows = lax.axis_index("seq"), scratch.shape[2]
    for n, q_rows in enumerate(sizes):
        total = out_total(refs[6 * n : 6 * n + 4], refs[6 * n + 4], refs[6 * n + 5], q_rows)
        for t in range(4):
            scratch[s ^ t, n] = total[t * rows : (t + 1) * rows, :].astype(BF16)
    hand_out(scratch, outs)


def out_weight(groups, name):
    dc = D // 4
    ins, sizes = [], []
    for dz, near, far in groups:
        ins += list(dz) + [(near, None), (far, None)]
        sizes.append(near.shape[0] // 2)
    return call(
        functools.partial(out_weight_body, sizes),
        ins,
        sent_shapes((len(groups), dc, dc), BF16),
        0,
        [pltpu.VMEM((4, len(groups), dc, dc), BF16)],
        name,
    )


GELU_A, GELU_B = math.sqrt(2.0 / math.pi), 0.044715


def feed_forward_body(rows, x0, x1, wg, wu, wd, gate_ref, up_ref, hidden_ref, keep_ref, send_ref):
    for j, x_ref in enumerate((x0, x1)):
        at = slice(j * rows, (j + 1) * rows)
        x = x_ref[...]
        gate, up = nn(x, wg[...]), nn(x, wu[...])
        gate_ref[at, :] = gate
        up_ref[at, :] = up
        inner = jnp.tanh(GELU_A * (gate + GELU_B * (gate * gate * gate)))
        hidden_ref[at, :] = (0.5 * gate * (1.0 + inner) * up).astype(BF16)
        out = (keep_ref, send_ref)[j]
        out[...] = nn(hidden_ref[at, :], wd[...]).astype(out.dtype)


def feed_weights(inner_cols, outer_rows, which):
    fc = inner_cols.shape[1]
    return [
        (inner_cols, part((D, fc), 2 * which, 0)),
        (inner_cols, part((D, fc), 2 * which + 1, 0)),
        (outer_rows, part((fc, D), which, 0)),
    ]


def feed_forward(half, inner_cols, outer_rows, which, keep, name):
    rows, fc = half[0].shape[0], inner_cols.shape[1]
    return call(
        functools.partial(feed_forward_body, rows),
        plain(half) + feed_weights(inner_cols, outer_rows, which),
        [((2 * rows, fc), F32), ((2 * rows, fc), F32), ((2 * rows, fc), BF16), ((rows, D), keep), ((rows, D), BF16)],
        12 * rows * fc * D,
        name=name,
    )


def feed_back_body(rows, d0, d1, gate_ref, up_ref, wg, wu, wd, dgate_ref, dup_ref, keep_ref, send_ref):
    for j, d_ref in enumerate((d0, d1)):
        at = slice(j * rows, (j + 1) * rows)
        dh = nt(d_ref[...], wd[...])
        t, up = gate_ref[at, :], up_ref[at, :]
        square = t * t
        inner = jnp.tanh(GELU_A * t * (1.0 + GELU_B * square))
        slope = 0.5 * (1.0 + inner) + 0.5 * t * (1.0 - inner * inner) * (
            GELU_A * (1.0 + 3.0 * GELU_B * square)
        )
        dgate_ref[at, :] = (dh * up * slope).astype(BF16)
        dup_ref[at, :] = (dh * (0.5 * t * (1.0 + inner))).astype(BF16)
        out = (keep_ref, send_ref)[j]
        out[...] = (nt(dgate_ref[at, :], wg[...]) + nt(dup_ref[at, :], wu[...])).astype(out.dtype)


def feed_back(dz_half, gate, up, inner_cols, outer_rows, which, keep, name):
    rows, fc = gate.shape[0] // 2, inner_cols.shape[1]
    return call(
        functools.partial(feed_back_body, rows),
        list(dz_half) + [(gate, None), (up, None)] + feed_weights(inner_cols, outer_rows, which),
        [((2 * rows, fc), BF16), ((2 * rows, fc), BF16), ((rows, D), keep), ((rows, D), BF16)],
        12 * rows * fc * D,
        name=name,
    )


def feed_weight_body(rows, packed, *refs):
    xs, dzs = refs[0:4], refs[4:8]
    dg, du, hid = refs[8:10], refs[10:12], refs[12:14]
    outs = refs[14:]
    gate = up = down = None
    for j in range(4):
        at = slice((j % 2) * rows, (j % 2 + 1) * rows)
        x = xs[j][...]
        a, b = tn(x, dg[j // 2][at, :]), tn(x, du[j // 2][at, :])
        c = tn(hid[j // 2][at, :], dzs[j][...])
        gate, up, down = (a, b, c) if j == 0 else (gate + a, up + b, down + c)
    fc = gate.shape[1]
    if not packed:
        outs[0][:D, :] = gate.astype(BF16)
        outs[0][D:, :] = up.astype(BF16)
        outs[1][...] = down.astype(BF16)
        return
    out = refs[-1]
    height = out.shape[1]
    for n, grad in enumerate((gate, up)):
        for k in range(2):
            out[2 * n + k, :, :fc] = grad[k * height : (k + 1) * height, :].astype(BF16)
    short = fc // 4
    for q in range(4):
        for g in range(D // 128):
            piece = down[q * short : (q + 1) * short, g * 128 : (g + 1) * 128].astype(BF16)
            r, c = g % 3 * short, fc + g // 3 * 128
            out[q, r : r + short, c : c + 128] = piece
    y = lax.axis_index("batch") % 2
    for i in range(2):
        outs[0][i] = out[2 * i + y]
        outs[1][i] = out[2 * i + 1 - y]


def feed_weight(xs, dzs, dgate, dup, hidden, packed, name):
    rows, fc = xs[0].shape[0], dgate[0].shape[1]
    return call(
        functools.partial(feed_weight_body, rows, packed),
        plain(xs) + list(dzs) + plain((*dgate, *dup, *hidden)),
        [((2, D // 2, fc + 256), BF16)] * 2 if packed else [((2 * D, fc), BF16), ((fc, D), BF16)],
        24 * rows * fc * D,
        [pltpu.VMEM((4, D // 2, fc + 256), BF16)] if packed else [],
        name,
    )


def send_some(mine):
    return [mine[0], seq_swap(mine[1], 1), seq_swap(mine[2], 2)]


def send_rest(got, *after):
    return [*got, seq_swap(tie(got[2], got[1], *after), 1)]


def send_blocks(mine):
    return send_rest(send_some(mine))


def place(scratch, refs, s):
    for j, ref in enumerate(refs):
        scratch[s ^ j] = ref[...] if j < 2 else ref[j - 2]


def hand_out(scratch, outs):
    outs[0][...] = scratch[0]
    outs[1][...] = scratch[1]
    outs[2][0] = scratch[2]
    outs[2][1] = scratch[3]


def sent_shapes(shape, dtype):
    return [(shape, dtype), (shape, dtype), ((2,) + shape, dtype)]


def head_pack_body(ar, gr, lines, attn_ref, gain_ref, inner_ref, *refs):
    outs, scratch = refs[0:3], refs[3]
    s = lax.axis_index("seq")
    ir, width = inner_ref.shape[0], scratch.shape[2]
    dc, room, short = D // 4, width - ar, ir // 3
    turned = attn_ref[...].T
    gains = jnp.concatenate([gain_ref[...], jnp.zeros((1, lines * room - gr), F32)], axis=1)
    for t in range(4):
        at = s ^ t
        scratch[at, :dc, ar:] = jnp.zeros((dc, room), BF16)
        scratch[at, :dc, :ar] = turned[t * dc : (t + 1) * dc, :].astype(BF16)
        for n in range(lines):
            scratch[at, n : n + 1, ar:] = gains[:, n * room : (n + 1) * room].astype(BF16)
        for q in range(4):
            low = (4 * q + t) * 128
            piece = inner_ref[:, low : low + 128].astype(BF16)
            if q < 3:
                scratch[at, dc : dc + ir, q * 128 : (q + 1) * 128] = piece
            else:
                for n in range(3):
                    scratch[at, dc + ir :, n * 128 : (n + 1) * 128] = piece[n * short : (n + 1) * short, :]
    hand_out(scratch, outs)


def head_unpack_body(ar, gr, lines, ir, *refs):
    ins, outer_ref = refs[0:4], refs[4]
    attn_ref, feed_ref, scratch = refs[5:8]
    place(scratch, ins, lax.axis_index("seq"))
    dc, room, short, orow = D // 4, scratch.shape[2] - ar, ir // 3, outer_ref.shape[0]
    pieces = []
    for k in range(4):
        attn_ref[:dc, k * ar : (k + 1) * ar] = scratch[k, :dc, :ar]
        rows = slice(k * ir, (k + 1) * ir)
        feed_ref[rows, :384] = scratch[k, dc : dc + ir, :]
        for n in range(3):
            feed_ref[k * ir + n * short : k * ir + (n + 1) * short, 384:512] = scratch[
                k, dc + ir :, n * 128 : (n + 1) * 128
            ]
        pieces += [scratch[k, n : n + 1, ar : ar + min(room, gr - n * room)].astype(F32) for n in range(lines)]
    for g in range(D // 128):
        r, c = g % 3 * orow, 512 + g // 3 * 128
        feed_ref[r : r + orow, c : c + 128] = outer_ref[:, g * 128 : (g + 1) * 128].astype(BF16)
    pieces.append(jnp.zeros((1, attn_ref.shape[1] - 4 * gr), F32))
    line = jnp.concatenate(pieces, axis=1)
    fill = jnp.zeros((attn_ref.shape[0] - dc - 1, line.shape[1]), F32)
    attn_ref[dc:, :] = jnp.concatenate([line, fill], axis=0).astype(BF16)


def head_exchange(attn_master, inner_master, outer_master, gain_master):
    ar, dc, gr = attn_master.shape[0], D // 4, gain_master.shape[0]
    ir = inner_master.shape[0]
    width = (ar // 128 + 1) * 128
    lines = -(-gr // (width - ar))
    tall = dc + ir + ir // 3
    scratch = [pltpu.VMEM((4, tall, width), BF16)]
    outs = call(
        functools.partial(head_pack_body, ar, gr, lines),
        plain([attn_master, gain_master[None], inner_master]),
        sent_shapes((tall, width), BF16),
        0,
        scratch,
        "head_pack",
    )
    return call(
        functools.partial(head_unpack_body, ar, gr, lines, ir),
        plain(send_blocks(outs) + [outer_master]),
        [((dc + 16, 4 * ar), BF16), ((4 * ir, D), BF16)],
        0,
        scratch,
        "head_unpack",
    )


def turn_pack_body(count, *refs):
    ins, outs, scratch = refs[:count], refs[count : count + 3], refs[count + 3]
    s = lax.axis_index("seq")
    dc = scratch.shape[2]
    for t in range(4):
        for g in range(count):
            scratch[s ^ t, g] = ins[g][:, t * dc : (t + 1) * dc].T
    hand_out(scratch, outs)


def turn_pack(ins, name):
    count, dc = len(ins), D // 4
    return call(
        functools.partial(turn_pack_body, count),
        ins,
        sent_shapes((count, dc, dc), BF16),
        0,
        [pltpu.VMEM((4, count, dc, dc), BF16)],
        name,
    )


def lanes_unpack_body(*refs):
    ins, out, scratch = refs[:4], refs[4], refs[5]
    place(scratch, ins, lax.axis_index("seq"))
    width = scratch.shape[3]
    for k in range(4):
        for g in range(scratch.shape[1]):
            out[g, :, k * width : (k + 1) * width] = scratch[k, g]


def lanes_unpack(got, name):
    shape = got[0].shape
    return call(
        lanes_unpack_body,
        plain(got),
        [(shape[:2] + (4 * shape[2],), BF16)],
        0,
        [pltpu.VMEM((4,) + shape, BF16)],
        name,
    )[0]


def tail_pack_body(gr, total_ref, *refs):
    outs, scratch = refs[:3], refs[3]
    s, width = lax.axis_index("seq"), scratch.shape[2]
    dc = D // 4
    for t in range(4):
        scratch[s ^ t, :dc] = total_ref[:dc, t * width : (t + 1) * width].astype(BF16)
        lines = [total_ref[dc + e : dc + e + 1, t * gr : (t + 1) * gr] for e in range(2)]
        lines = jnp.concatenate(lines + [jnp.zeros((1, width - 2 * gr), F32)] * (width > 2 * gr), axis=1)
        scratch[s ^ t, dc:] = jnp.concatenate([lines, jnp.zeros((15, width), F32)], axis=0).astype(BF16)
    hand_out(scratch, outs)


def tail_unpack_body(gr, *refs):
    ins, (out, kept_ref, sent_ref, scratch) = refs[:4], refs[4:]
    place(scratch, ins, lax.axis_index("seq"))
    dc = D // 4
    lines = None
    for k in range(4):
        out[:, k * dc : (k + 1) * dc] = scratch[k, :dc].astype(F32).T
        line = scratch[k, dc:].astype(F32)[:1]
        lines = line if k == 0 else lines + line
    halves = lines[:, :gr], lines[:, gr : 2 * gr]
    first = lax.axis_index("batch") % 2 == 0
    kept_ref[...] = jnp.where(first, halves[0], halves[1])
    sent_ref[...] = jnp.where(first, halves[1], halves[0])


def feed_pack_body(total_ref, *refs):
    outs, outer_ref, scratch = refs[:3], refs[3], refs[4]
    s, (rows, fc), orow = lax.axis_index("seq"), scratch.shape[1:], outer_ref.shape[0]
    for t in range(4):
        scratch[s ^ t] = total_ref[t * rows : (t + 1) * rows, :fc].astype(BF16)
    hand_out(scratch, outs)
    for g in range(D // 128):
        r, c = g % 3 * orow, fc + g // 3 * 128
        outer_ref[:, g * 128 : (g + 1) * 128] = total_ref[r : r + orow, c : c + 128]


def feed_pack(total, ir, fc, orow):
    outs = call(
        feed_pack_body,
        plain([total]),
        sent_shapes((ir, fc), BF16) + [((orow, D), F32)],
        0,
        [pltpu.VMEM((4, ir, fc), BF16)],
        "feed_pack",
    )
    return outs[:3], outs[3]


def feed_unpack_body(*refs):
    ins, out, scratch = refs[:4], refs[4], refs[5]
    place(scratch, ins, lax.axis_index("seq"))
    for k in range(4):
        for q in range(4):
            low = (4 * q + k) * 128
            out[:, low : low + 128] = scratch[k, :, q * 128 : (q + 1) * 128].astype(F32)


def feed_unpack(got):
    ir, fc = got[0].shape
    return call(
        feed_unpack_body, plain(got), [((ir, 4 * fc), F32)], 0, [pltpu.VMEM((4, ir, fc), BF16)], "feed_unpack"
    )[0]


def spread_body(*refs):
    out_ref = refs[6]
    count, width = out_ref.shape[0], out_ref.shape[2]
    per = 6 * D // count
    line = jnp.concatenate([x[...] for x in refs[:6]], axis=1)
    for n in range(count):
        piece = line[:, n * per : (n + 1) * per]
        out_ref[n] = jnp.concatenate([piece, jnp.zeros((1, width - per), F32)], axis=1)


def spread(rows, count, width):
    return call(spread_body, plain(rows), [((count, 1, width), F32)], 0, name="spread")[0]


def tail_pack(total, ar, gr):
    if ar % 16:
        return [total, total]
    shape = (D // 4 + 16, ar)
    mine = call(
        functools.partial(tail_pack_body, gr),
        plain([total]),
        sent_shapes(shape, BF16),
        0,
        [pltpu.VMEM((4,) + shape, BF16)],
        "tail_pack",
    )
    return send_some(mine) + [mine[1]]


def tail_unpack(mine, s, ar, gr, now, *after):
    dc = D // 4
    if ar % 16:
        got = seq_exchange(mine[0][:dc].astype(BF16).reshape(dc, 4, ar).swapaxes(0, 1), s)
        lines = lax.dynamic_slice_in_dim(sum_seq(mine[0][dc : dc + 2]), s * gr, gr, axis=1)
        y = lax.axis_index("batch") % 2
        pair = [lax.dynamic_slice_in_dim(lines, i, 1, axis=0) for i in (y, 1 - y)]
        return (got.reshape(4 * dc, ar).T.astype(F32), *pair)
    got = send_rest(mine[:3], *after)
    return call(
        functools.partial(tail_unpack_body, gr),
        plain([now(got[0]), *got[1:]]),
        [((ar, 4 * dc), F32), ((1, gr), F32), ((1, gr), F32)],
        0,
        [pltpu.VMEM((4, dc + 16, ar), BF16)],
        "tail_unpack",
    )


def split_lanes(scratch, pieces):
    width = scratch.shape[2]
    for n, piece in enumerate(pieces):
        for low in range(n * D, (n + 1) * D, D // 2):
            to = low % width
            scratch[low // width, :, to : to + D // 2] = piece[:, low - n * D : low - n * D + D // 2]


def part_pack_body(positions, *refs):
    count = len(positions)
    ins = refs[4 : 4 + 2 * count]
    kept_ref, sent_ref, squares, scratch = refs[4 + 2 * count :]
    y = lax.axis_index("batch") % 2
    place(squares, refs[:4], lax.axis_index("seq"))
    for n, position in enumerate(positions):
        pieces = [x[...] for x in ins[2 * n : 2 * n + 2]]
        pieces.insert(position, jnp.concatenate([squares[k, n] for k in range(4)], axis=1))
        split_lanes(scratch, pieces)
        kept_ref[n] = scratch[y]
        sent_ref[n] = scratch[1 - y]


def attn_parts(got, parts, width, name):
    dc = D // 4
    if width % 128 or lax.axis_size("batch") != 8:
        joined = []
        matrices = None if got is None else lanes_unpack(got, name)
        for n, (others, position) in enumerate(parts):
            pieces = list(others)
            if got is not None:
                pieces.insert(position, matrices[n])
            joined.append(jnp.concatenate(pieces, axis=1))
        joined = jnp.concatenate(joined, axis=1)
        return pair_blocks(joined.reshape(dc, -1, width).swapaxes(0, 1))
    return call(
        functools.partial(part_pack_body, [position for _, position in parts]),
        plain([*got, *(x for others, _ in parts for x in others)]),
        [((len(parts), dc, width), BF16)] * 2,
        0,
        [pltpu.VMEM((4, len(parts), dc, dc), BF16), pltpu.VMEM((2, dc, width), BF16)],
        name,
    )


def self_part_body(rows, *refs):
    x = refs[0:4]
    dq, dkt, dvt, kept_ref, sent_ref, scratch = refs[4:10]
    gq = gk = gv = None
    for j in range(4):
        at = slice(j * rows, (j + 1) * rows)
        y = x[j][...]
        a, b, c = tn(dq[at, :], y), nn(dkt[:, at], y), nn(dvt[:, at], y)
        gq, gk, gv = (a, b, c) if j == 0 else (gq + a, gk + b, gv + c)
    split_lanes(scratch, [g.astype(BF16) for g in (gq, gk, gv)])
    y = lax.axis_index("batch") % 2
    kept_ref[0] = scratch[y]
    sent_ref[0] = scratch[1 - y]


def self_part(rows, grads, width, name):
    dq, dkt, dvt = grads
    per, dc = dq.shape[0] // 4, dq.shape[1]
    if width % 128 or lax.axis_size("batch") != 8:
        gq, gk, gv = (g.reshape(4, per, dc) for g in (dq, dkt.T, dvt.T))
        made = [
            sum(tn(g[j], x.reshape(4, per, D)[j]) for j, (x, _) in enumerate(rows)).astype(BF16)
            for g in (gq, gk, gv)
        ]
        return attn_parts(None, [(made, 0)], width, name)
    return call(
        functools.partial(self_part_body, per),
        list(rows) + plain([dq, dkt, dvt]),
        [((1, dc, width), BF16)] * 2,
        0,
        [pltpu.VMEM((2, dc, width), BF16)],
        name,
    )


KINDS = ((D, 0), (D, 12), (FF, 16), (D, 18))


def group_mask(count, kind):
    per_group, offset = KINDS[kind]
    axis = 1 if kind < 3 else 0
    shape = (count, 128) if kind < 3 else (128, count)
    at = lax.axis_index(("batch", "seq")) * count + lax.broadcasted_iota(jnp.int32, shape, 1 - axis)
    low = (lax.broadcasted_iota(jnp.int32, shape, axis) - offset) * per_group
    return (at >= low) & (at < low + per_group) & (low >= 0)


def diagonal():
    return lax.broadcasted_iota(jnp.int32, (128, 128), 0) == lax.broadcasted_iota(jnp.int32, (128, 128), 1)


def by_group(values, kind):
    if kind == 3:
        mask = group_mask(values.shape[1], kind)
        column = jnp.sum(jnp.where(mask, values * values, 0.0), axis=1, keepdims=True)
        return jnp.sum(jnp.where(diagonal(), column, 0.0), axis=0, keepdims=True)
    squares = jnp.sum(values * values, axis=1, keepdims=True)
    return jnp.sum(jnp.where(group_mask(values.shape[0], kind), squares, 0.0), axis=0, keepdims=True)


def of_group(row, count, kind):
    if kind == 3:
        column = jnp.sum(jnp.where(diagonal(), row, 0.0), axis=1, keepdims=True)
        return jnp.sum(jnp.where(group_mask(count, kind), column, 0.0), axis=0, keepdims=True)
    return jnp.sum(jnp.where(group_mask(count, kind), row, 0.0), axis=1, keepdims=True)


def square_sums_body(*refs):
    total = by_group(refs[0][...], 0)
    for kind in range(1, 4):
        total = total + by_group(refs[kind][...], kind)
    refs[4][...] = total


def square_sums(masters):
    return call(square_sums_body, plain(masters), [((1, 128), F32)], 0, name="square_sums")[0]


def adam_body(kind, w_ref, m_ref, v_ref, g_ref, first_ref, second_ref, update_ref, sums_ref):
    gradient = g_ref[...]
    correction = 1.0 - 0.5**STEP
    first = 0.5 * m_ref[...] + 0.5 * gradient
    second = 0.5 * v_ref[...] + 0.5 * gradient * gradient
    update = first / correction / (jnp.sqrt(second / correction) + adam_eps)
    update = update + (decay_weight if kind < 3 else 0.0) * w_ref[...]
    first_ref[...] = first
    second_ref[...] = second
    update_ref[...] = update
    sums_ref[...] = by_group(update, kind)


def adam(kind, w, m, v, g):
    return call(
        functools.partial(adam_body, kind),
        plain([w, m, v, g]),
        [(w.shape, F32)] * 3 + [((1, 128), F32)],
        0,
        name=f"adam_{kind}",
    )


def lamb_body(*refs):
    weight_norms, update_norms = jnp.sqrt(refs[0][:, :128]), jnp.sqrt(refs[0][:, 128:])
    ratio = weight_norms / (update_norms + 1e-06)
    masters, updates, news, copies = (refs[1 + 4 * n : 5 + 4 * n] for n in range(4))
    for kind in range(4):
        w = masters[kind]
        scale = of_group(ratio, w.shape[1] if kind == 3 else w.shape[0], kind)
        new = w[...] - lamb_rate * scale * updates[kind][...]
        if kind == 3:
            new = new[0]
        news[kind][...] = new
        copies[kind][...] = new.astype(BF16)
    refs[17][...] = weight_norms[0, :24]
    refs[18][...] = update_norms[0, :24]


def lamb(squares, masters, updates):
    shapes = [w.shape for w in masters[:3]] + [masters[3].shape[1:]]
    return call(
        lamb_body,
        plain([squares, *masters, *updates]),
        [(s, F32) for s in shapes] + [(s, BF16) for s in shapes] + [((24,), F32)] * 2,
        0,
        name="lamb",
    )


def per_device(
    encoder_layer_input,
    decoder_layer_input,
    cotangent,
    encoder_used_lengths,
    decoder_used_lengths,
    attn_master,
    inner_master,
    outer_master,
    gain_master,
    attn_first,
    inner_first,
    outer_first,
    gain_first,
    attn_second,
    inner_second,
    outer_second,
    gain_second,
):
    ns, nb = lax.axis_size("seq"), lax.axis_size("batch")
    s, b = lax.axis_index("seq"), lax.axis_index("batch")
    ar, ir, orow = attn_master.shape[0], inner_master.shape[0], outer_master.shape[0]
    dc, fc = D // ns, FF // ns
    cuts = FF // (ns * orow)

    gr = gain_master.shape[0]
    packed = nb == 8 and ar % 16 == 0 and 3 * orow == ns * ir and cuts == 4
    clock = Clock()
    now, mark = clock.now, clock.mark
    masters = [attn_master, inner_master, outer_master, gain_master[None]]
    if packed:
        attn_mine, feed_mine = head_exchange(attn_master, inner_master, outer_master, gain_master)
        feeds_mine = [feed_mine]
    else:
        width = (ar // 128 + 1) * 128
        lines = -(-gr // (width - ar))
        corner = jnp.pad(gain_master.astype(BF16), (0, lines * (width - ar) - gr)).reshape(lines, width - ar)
        corner = jnp.broadcast_to(jnp.pad(corner, ((0, dc - lines), (0, 0))), (ns, dc, width - ar))
        attn_low = attn_master.astype(BF16).T.reshape(ns, dc, ar)
        got = seq_exchange(jnp.concatenate([attn_low, corner], axis=2), s)
        attn_mine = got[:, :, :ar].swapaxes(0, 1).reshape(dc, ns * ar)
        gains_mine = got[:, :lines, ar:].reshape(ns, -1)[:, :gr].reshape(1, ns * gr)
        attn_mine = jnp.concatenate([attn_mine, jnp.pad(gains_mine, ((0, 15), (0, ns * (ar - gr))))])
        inner_low = inner_master.astype(BF16).reshape(ir, cuts, ns, orow).transpose(2, 0, 1, 3)
        inner_mine = seq_exchange(inner_low.reshape(ns, ir, fc), s).reshape(ns * ir, fc)
        feeds_mine = [inner_mine, outer_master.astype(BF16)]
    attn_got = None
    attn_ring = ring_gather(attn_mine)
    next(attn_ring)
    while not isinstance(attn_got, list):
        attn_last, attn_got = attn_got, attn_ring.send(None)
    squares = square_sums(masters)
    attn_t = gathered_lanes([attn_got[0], *(tie(x, squares) for x in attn_got[1:])], "gather_attn")
    feed_rings = [ring_gather(x) for x in feeds_mine]
    for x in feed_rings:
        next(x)
        x.send(attn_last)

    def feed_step():
        for x in feed_rings:
            clock.step(x)

    gains = attn_t[dc].reshape(nb, ns * ar)[:, : ns * gr].reshape(6, D).astype(F32)
    gain = [gains[i : i + 1] for i in range(6)]
    out_mine = turn_pack([(attn_t, part((dc, D), 0, 3))], "out_pack_0")
    out_got = send_blocks(out_mine)
    out_mine = turn_pack(
        [(tie(attn_t, out_mine[1]), part((dc, D), 0, 7)), (attn_t, part((dc, D), 0, 11))], "out_pack_1"
    )
    rest_got = send_some(out_mine)

    enc_in, dec_in = encoder_layer_input[0], decoder_layer_input[0]
    er, dr = enc_in.shape[0], dec_in.shape[0]
    enc_meta = jnp.stack([s, encoder_used_lengths[0]]).astype(jnp.int32)
    dec_meta = jnp.stack([s, decoder_used_lengths[0]]).astype(jnp.int32)
    alive = (s * dr + jnp.arange(dr, dtype=jnp.int32)) < decoder_used_lengths[0]
    seed = jnp.where(alive[:, None], cotangent[0], jnp.zeros_like(cotangent[0]))
    blocks = gather_blocks(jnp.concatenate([enc_in, dec_in, seed]))
    enc_blocks = [(x, part((er, D), 0, 0)) for x in blocks]
    dec_blocks = [(x, part((dr, D), er // dr, 0)) for x in blocks]
    seed_blocks = [(x, part((dr, D), er // dr + 1, 0)) for x in blocks]

    def quarters(rows):
        return [(rows, part((rows.shape[0] // 4, D), j, 0)) for j in range(4)]

    mark(out_mine[1])
    feed_step()
    rows_a, q0, k0, v0, logs_far0, mixed_far0 = attend_far(
        tie(now(enc_meta), *out_got[1:]), enc_blocks, None, attn_t, None, 0, False, gain[0]
    )
    mark([mixed_far0, rest_got[2]])
    rest_got = send_rest(rest_got, mixed_far0)
    out_w = lanes_unpack([now(out_got[0]), *out_got[1:]], "out_unpack_0")
    kf, sf = project(mixed_far0, (out_w, 0), "project_far_0")
    mark(sf)
    feed_step()
    far = mark(far_payload(kf, now(sf)))
    x_enc = seq_swap(far, 2)
    logs_near0, mixed_near0, kn_enc, sn = attend_near(enc_meta, now(q0), k0, v0, (out_w, 0), 0, False)
    mark(sn)
    c_enc = seq_swap(sn, 1)
    out_rest = lanes_unpack([now(rest_got[0]), *rest_got[1:]], "out_unpack_1")
    mark(out_rest)
    rows_c, q1, k1, v1, logs_far1, mixed_far1, kf, sf = attend_far(
        now(dec_meta), dec_blocks, None, attn_t, (out_rest, 0), 1, True, gain[3]
    )
    mark(sf)
    feed_step()
    enc_mid, norm_b = close(now(kn_enc), c_enc, x_enc, enc_in, gain[1], "close_enc_attn")
    mark(norm_b)
    rows_b = gather_blocks(norm_b)
    x_self = seq_swap(mark(far_payload(kf, now(sf))), 2)
    logs_near1, mixed_near1, kn, sn = attend_near(dec_meta, now(q1), k1, v1, (out_rest, 0), 1, True)
    mark(sn)
    c_self = seq_swap(sn, 1)
    feed_got = [clock.finish(x) for x in feed_rings]
    if packed:
        inner_cols, outer_rows = gathered_feeds(feed_got[0], orow, "gather_feeds")
    else:
        inner_cols = gathered_rows(feed_got[0], "gather_inner")
        outer_rows = gathered_rows(feed_got[1], "gather_outer")
    inner_cols, outer_rows = inner_cols.reshape(4 * D, fc), outer_rows.reshape(2 * fc, D)
    eg1, eu1, eh1, kf, sf = feed_forward((now(rows_b[2]), rows_b[3]), inner_cols, outer_rows, 0, BF16, "enc_feed_far")
    far = mark(far_payload(kf, sf))
    x_enc = seq_swap(far, 2)
    eg0, eu0, eh0, kn_enc, sn = feed_forward((now(rows_b[0]), rows_b[1]), inner_cols, outer_rows, 0, F32, "enc_feed_near")
    mark(sn)
    c_enc = seq_swap(sn, 1)
    dec_mid, norm_d = close(now(kn), c_self, x_self, dec_in, gain[4], "close_self")
    mark(norm_d)
    enc_out, norm_e = close(now(kn_enc), c_enc, x_enc, enc_mid, gain[2], "close_enc_feed")
    mark(norm_e)
    rows_e = gather_blocks(norm_e)
    q0t, q1t = now(q0).T, now(q1).T
    mark(q1t)
    rows_d = gather_blocks(now(norm_d))
    q2, k2, v2, logs_far2, mixed_far2, kf, sf = attend_far(
        now(enc_meta), plain(rows_d), plain(rows_e), attn_t, (out_rest, 1), 2, False
    )
    far = mark(far_payload(kf, sf))
    x_dec = seq_swap(far, 2)
    logs_near2, mixed_near2, kn, sn = attend_near(enc_meta, now(q2), k2, v2, (out_rest, 1), 2, False)
    mark(sn)
    dec_late, norm_f = close(now(kn), seq_swap(tie(sn, x_dec), 1), x_dec, dec_mid, gain[5], "close_cross")
    mark(norm_f)
    rows_f = gather_blocks(norm_f)
    dg0, du0, dh0, kn_out, sn_out = feed_forward(
        (now(rows_f[0]), rows_f[1]), inner_cols, outer_rows, 1, F32, "dec_feed_near"
    )
    mark(dh0)
    a0, b0, kn_dec, sn_dec = feed_back(
        seed_blocks[:2], now(dg0), du0, inner_cols, outer_rows, 1, F32, "dec_feed_back_near"
    )
    mark(sn_dec)
    c_dec = seq_swap(sn_dec, 1)
    dg1, du1, dh1, kf_out, sf_out = feed_forward(
        (now(rows_f[2]), rows_f[3]), inner_cols, outer_rows, 1, BF16, "dec_feed_far"
    )
    mark(dh1)
    a1, b1, kf, sf = feed_back(seed_blocks[2:], now(dg1), du1, inner_cols, outer_rows, 1, BF16, "dec_feed_back_far")

    far = mark(far_payload(kf, sf))
    x_dec = seq_swap(far, 2)
    dec_feed = feed_weight(
        rows_f, seed_blocks, (now(a0), a1), (b0, b1), (dh0, dh1), packed, "dec_feed_weight"
    )
    mark(dec_feed[-1])
    up_five, low, gain_five = close_back(now(kn_dec), c_dec, x_dec, dec_late, gain[5], seed, "back_dec_feed")
    mark(low)
    dz_cross = plain(gather_blocks(low))
    half = nb // 2
    feed_shapes = [(ns * ir, fc), (orow, D)]

    def pair_send(kept, sent):
        return kept, batch_swap(mark(sent), 1)

    def feed_parts(grads):
        if packed:
            return [pair_send(*grads)]
        blocks = [now(x).reshape((half,) + shape) for x, shape in zip(grads, feed_shapes)]
        return [pair_send(*pair_blocks(x)) for x in blocks]

    dec_parts = feed_parts(dec_feed)
    far_out = mark(far_payload(kf_out, sf_out))

    q2t = mark(now(q2).T)
    out_sent = out_weight([(dz_cross, now(mixed_near2), mixed_far2)], "cross_out_weight")
    mark(out_sent[1])
    out_got = send_blocks(out_sent)
    x_out = seq_swap(tie(far_out, out_sent[1]), 2)
    c_out = seq_swap(tie(sn_out, out_sent[1]), 1)
    decoder_layer_output = (dec_late + kn_out + c_out.astype(F32) + x_out.astype(F32)).astype(BF16)
    cross_d, outs = attend_back(
        now(enc_meta), dz_cross, q2t, attn_t, (out_rest, 1), 2, (q2, k2, v2, logs_near2, logs_far2), dr, er, False, True
    )
    far = mark(far_payload(outs[6], tie(outs[7], x_out, c_out, out_got[2])))
    x_enc, c_enc = seq_swap(far, 2), seq_swap(now(outs[5]), 1)
    c_far, c_dec = seq_swap(now(outs[3]), 1), seq_swap(now(outs[1]), 1)
    kf_dec, kn_dec = outs[2], outs[0]
    cross_w = attend_weights(plain(rows_d), plain(rows_e), (now(cross_d[0]), *cross_d[1:]), "cross_weights")
    mark(cross_w[0])
    three = attn_parts([now(out_got[0]), *out_got[1:]], [(cross_w[1:], 2)], ns * ar, "part_three")
    mark(three[1])
    up_two, low, gain_two = close_back(now(outs[4]), c_enc, x_enc, enc_out, gain[2], None, "back_encoded")
    mark(low)
    dz = gather_blocks(low)
    far_dec = mark(add_low(kf_dec, now(c_far)))
    part_three = (three[0], batch_swap(three[1], 1))
    mark([far_dec] + [got for _, got in dec_parts])
    a0, b0, kn_enc, sn = feed_back(plain(dz[:2]), now(eg0), eu0, inner_cols, outer_rows, 0, F32, "enc_feed_back_near")
    mark(sn)
    c_enc = seq_swap(sn, 1)
    x_dec = seq_swap(tie(far_dec, dz[2], sn), 2)
    mark([sn, part_three[1]])
    dz = plain(dz)
    a1, b1, kf, sf = feed_back(dz[2:], now(eg1), eu1, inner_cols, outer_rows, 0, BF16, "enc_feed_back_far")
    far = mark(far_payload(kf, tie(sf, x_dec)))
    x_enc = seq_swap(far, 2)
    enc_feed = feed_weight(
        rows_b, dz, (now(a0), a1), (b0, b1), (eh0, eh1), packed, "enc_feed_weight"
    )
    mark(enc_feed[-1])
    enc_parts = feed_parts(enc_feed)
    up_four, low_self, gain_four = close_back(now(kn_dec), c_dec, x_dec, dec_mid, gain[4], up_five, "back_cross")
    mark(low_self)
    dz_self = plain(gather_blocks(low_self))
    up_one, low, gain_one = close_back(now(kn_enc), c_enc, x_enc, enc_mid, gain[1], up_two, "back_enc_feed")
    mark(low)
    dz_enc = gather_blocks(low)
    self_d, outs = attend_back(
        now(dec_meta), dz_self, q1t, attn_t, (out_rest, 0), 1, (q1, k1, v1, logs_near1, logs_far1), dr, dr, True, False
    )
    mark(outs[3])
    self_w = attend_weights(quarters(rows_c), None, (now(self_d[0]), *self_d[1:]), "self_weights")
    mark(self_w[0])
    flight = []
    feeds = [ring_reduce([e, d], "feed_hop", None, flight) for e, d in zip(enc_parts, dec_parts)]
    for x in feeds:
        next(x)
    kn_self, c_self = outs[0], seq_swap(tie(outs[1], dz_enc[2]), 1)
    sf_self = seq_swap(tie(outs[3], dz_enc[2]), 1)
    dz_enc = plain(dz_enc)
    out_late = out_weight(
        [(dz_enc, now(mixed_near0), mixed_far0), (dz_self, mixed_near1, mixed_far1)], "late_out_weight"
    )
    mark(out_late[1])
    got_late = send_blocks(out_late)
    x_self = seq_swap(mark(add_low(outs[2], now(sf_self))), 2)
    for x in feeds:
        clock.step(x)
    enc_d, outs = attend_back(
        now(enc_meta), dz_enc, q0t, attn_t, (out_w, 0), 0, (q0, k0, v0, logs_near0, logs_far0), er, er, False, False
    )
    far = mark(far_payload(outs[2], tie(outs[3], x_self, got_late[2], *flight)))
    x_enc, c_enc = seq_swap(far, 2), seq_swap(now(outs[1]), 1)
    part_zero = pair_send(
        *self_part(quarters(rows_a), (now(enc_d[0]), *enc_d[1:]), ns * ar, "part_zero")
    )
    part_middle = pair_send(
        *attn_parts(
            [now(got_late[0]), *got_late[1:]],
            [(self_w[:2], 0), ((self_w[2], cross_w[0]), 1)],
            ns * ar,
            "part_middle",
        )
    )
    for x in feeds:
        clock.step(x)
    decoder_input_gradient, _, gain_three = close_back(
        now(kn_self), c_self, x_self, dec_in, gain[3], up_four, "back_self"
    )
    mark(gain_three)
    encoder_input_gradient, _, gain_zero = close_back(
        now(outs[0]), c_enc, x_enc, enc_in, gain[0], up_one, "back_enc_attn"
    )
    mark(gain_zero)

    gain_lines = spread(
        [now(gain_zero), gain_one, gain_two, gain_three, gain_four, gain_five], nb, ns * ar
    )
    mark(gain_lines)
    last_ring = ring_reduce([part_zero, part_middle, part_three], "attn_hop", gain_lines)
    next(last_ring)
    clock.step(last_ring)
    for x in feeds:
        clock.step(x)
    clock.step(last_ring)
    feeds_done = [clock.finish(x)[0] for x in feeds]
    clock.step(last_ring)
    if packed:
        feed_sent, outer_grad = feed_pack(mark(feeds_done[0]), ir, fc, orow)
        mark(feed_sent[1])
        feed_got = send_blocks(feed_sent)
    else:
        inner_part, outer_grad = feeds_done
        inner_part = mark(now(inner_part).astype(BF16).reshape(ns, ir, fc))
        inner_part = seq_exchange(inner_part, s)
    outer_new = adam(2, outer_master, outer_first, outer_second, now(outer_grad))
    mark(outer_new[3])
    (attn_sum,) = clock.finish(last_ring)
    mine = tail_pack(mark(attn_sum), ar, gr)
    if packed:
        mark(mine[1])
        inner_grad = feed_unpack([now(feed_got[0]), *feed_got[1:]])
    else:
        inner_grad = inner_part.reshape(ns, ir, cuts, orow).transpose(1, 2, 0, 3).reshape(ir, FF).astype(F32)
    inner_new = adam(1, inner_master, inner_first, inner_second, mark(inner_grad))
    mark(inner_new[3])
    attn_grad, gain_kept, gain_sent = tail_unpack(mine, s, ar, gr, now, clock.last)
    gain_grad = gain_kept + batch_swap(gain_sent, 1)
    attn_new = adam(0, attn_master, attn_first, attn_second, attn_grad)
    gain_new = adam(3, masters[3], gain_first[None], gain_second[None], tie(gain_grad, attn_new[3]))
    results = (attn_new, inner_new, outer_new, gain_new)
    all_squares = sum_all(jnp.concatenate([squares, sum(x[3] for x in results)], axis=1))
    last = lamb(all_squares, masters, [x[2] for x in results])
    grads = (attn_grad, inner_grad, outer_grad, gain_grad)

    def flat(four):
        return (*four[:3], four[3][0])

    return (
        decoder_layer_output[None],
        encoder_input_gradient[None],
        decoder_input_gradient[None],
        *flat(grads),
        *flat([x[0] for x in results]),
        *flat([x[1] for x in results]),
        *last,
    )


def solution(mesh):
    rows = P("batch", "seq", None)
    matrix = P(("batch", "seq"), None)
    vector = P(("batch", "seq"))
    kinds = (matrix, matrix, matrix, vector)
    return jax.shard_map(
        per_device,
        mesh=mesh,
        in_specs=(rows, rows, rows, P("batch"), P("batch")) + kinds * 3,
        out_specs=(rows, rows, rows) + kinds * 5 + (P(), P()),
        check_vma=False,
    )
```

time: 653 us -> 558 us (0.85)
  waiting for transfers between devices: 241 us -> 191 us
  other arithmetic: 69.6 us -> 24.5 us
  Pallas kernels: 213 us -> 257 us
  starting transfers between devices: 88 us -> 61.7 us
  local copies, waits for them, and re-layouts: 30.5 us -> 12.1 us
    pallas_call x2 -> x21, Pallas kernels: 8.94 us -> 62.4 us  [the longest x10 26.9 us: row_call(): pl.pallas_call(body, grid=(STEPS,), in_specs=[spec(x.shape) for x in ins]...]
    ppermute x14 -> x12, waiting for transfers between devices: 85.2 us -> 45.3 us  [ring_shift(): lax.ppermute(x, 'batch', [(i, (i + 2) % nb) for i in (range(nb) if active...]
    convert_element_type x23 -> x11, other arithmetic: 33.9 us -> 18.2 us  [add_low(): return (a.astype(F32) + b.astype(F32)).astype(BF16)]
    reduce_sum x18 -> x0, other arithmetic: 13.6 us -> none  [the longest x6 8.7 us: group_sums(): squares = jnp.sum(squares, axis=1)]
    ppermute x20 -> x17, starting transfers between devices: 25.4 us -> 15.9 us  [batch_swap(): return lax.ppermute(x, 'batch', [(i, i ^ k) for i in range(n)])]
    ppermute x85 -> x83, starting transfers between devices: 46.6 us -> 37.7 us  [seq_swap(): return lax.ppermute(x, 'seq', [(i, i ^ k) for i in range(n)])]
    pallas_call x48 -> x44, Pallas kernels: 204 us -> 195 us  [call(): pl.pallas_call(body, grid=(1,), in_specs=specs, out_specs=[whole(o) for o...]
    ppermute x14 -> x12, starting transfers between devices: 15.9 us -> 8.1 us  [ring_shift(): lax.ppermute(x, 'batch', [(i, (i + 2) % nb) for i in (range(nb) if active...]
  transfers between devices with their start and end apart: 119 -> 112, of which waited for: 56 -> 49; matrix products, arithmetic and copies ran while one was open for 12% -> 5% of each run, Pallas kernels for 20% -> 38%
where the time goes in v1:
time: 558 us; the launch traced here: 550 us
  Pallas kernels  257 us (46%)
  waiting for transfers between devices  191 us (34%)
  starting transfers between devices  61.7 us (11%)
  other arithmetic  24.5 us (4%)
  local copies, waits for them, and re-layouts  12.1 us (2%)
    pallas_call x44, Pallas kernels, call(): pl.pallas_call(body, grid=(1,), in_specs=specs, out_specs=[whole(o) for o...  195 us
    ppermute x83, waiting for transfers between devices, seq_swap(): return lax.ppermute(x, 'seq', [(i, i ^ k) for i in range(n)])  84.8 us
    ppermute x17, waiting for transfers between devices, batch_swap(): return lax.ppermute(x, 'batch', [(i, i ^ k) for i in range(n)])  60.9 us
    ppermute x12, waiting for transfers between devices, ring_shift(): lax.ppermute(x, 'batch', [(i, (i + 2) % nb) for i in (range(nb) if active...  45.3 us
    ppermute x83, starting transfers between devices, seq_swap(): return lax.ppermute(x, 'seq', [(i, i ^ k) for i in range(n)])  37.7 us
    pallas_call x10, Pallas kernels, row_call(): pl.pallas_call(body, grid=(STEPS,), in_specs=[spec(x.shape) for x in ins]...  26.9 us
    pallas_call x8, Pallas kernels, hop(): pl.pallas_call(functools.partial(hop_body, step, [k.shape[0] for k, _ in...  24.8 us
    convert_element_type x11, other arithmetic, add_low(): return (a.astype(F32) + b.astype(F32)).astype(BF16)  18.2 us
  transfers between devices with their start and end apart: 112, of which 49 were waited for; matrix products, arithmetic and copies ran while one was open for 5% of the time, Pallas kernels for 38%

profile of v1, /device:TPU:0, one launch (start us, length us, event | category | flops | bytes accessed | tf_op | source)
XLA Modules:
  0.0 549.6 jit_solution(9281976631543496522)
XLA Ops:
  0.7 2.7 head_pack.1
  3.4 2.9 collective-permute-start.1
  8.1 9.7 %collective-permute-done.1.refs_2_ = bf16[2,320,384]{2,1,0:T(8,128)(2,1)S(1)} collective-permute-done((bf16[2,320,384]{2,1,0:T(8,128)(2,1)}, bf16[2,320,384]{2,1,0:T(8,128)(2,1)S(1)}, u32[]{:S(2)}, u32[]{:S(2)}) %collective-permute-start.1) | collective-permute-done | bytes 491552 | tf_op jit(solution)/shard_map/ppermute | solution.py:31
  20.4 2.8 head_unpack.1
  26.6 10.0 %collective-permute-done.3.refs_1_ = bf16[208,1152]{1,0:T(8,128)(2,1)} collective-permute-done((bf16[208,1152]{1,0:T(8,128)(2,1)}, bf16[208,1152]{1,0:T(8,128)(2,1)}, u32[]{:S(2)}, u32[]{:S(2)}) %collective-permute-start.3) | collective-permute-done | bytes 479264 | tf_op jit(solution)/shard_map/ppermute | solution.py:36
  36.6 3.2 collective-permute-done.4.refs_2_
  40.6 11.2 %collective-permute-done.5.refs_3_ = bf16[208,1152]{1,0:T(8,128)(2,1)S(1)} collective-permute-done((bf16[208,1152]{1,0:T(8,128)(2,1)S(1)}, bf16[208,1152]{1,0:T(8,128)(2,1)S(1)}, u32[]{:S(2)}, u32[]{:S(2)}) %collective-permute-start.5) | collective-permute-done | bytes 479264 | tf_op jit(solution)/shard_map/ppermute | solution.py:36
  59.3 6.2 %collective-permute-done.7.refs_5_ = bf16[208,1152]{1,0:T(8,128)(2,1)S(1)} collective-permute-done((bf16[208,1152]{1,0:T(8,128)(2,1)S(1)}, bf16[208,1152]{1,0:T(8,128)(2,1)S(1)}, u32[]{:S(2)}, u32[]{:S(2)}) %collective-permute-start.7) | collective-permute-done | bytes 479264 | tf_op jit(solution)/shard_map/ppermute | solution.py:36
  72.6 5.4 collective-permute-done.16.refs_3_.d0.refs_6_
  79.1 4.1 gather_attn_0.1.refs_0_.refs_1_.refs_6_.refs_7_.refs_8_.refs_9_.refs_10_.refs_11_.refs_12_.refs_13_
  91.2 4.5 collective-permute-done.13.refs_2_
  98.7 7.3 %attend_far_0.1 = (bf16[1024,768]{1,0:T(8,128)(2,1)}, bf16[1024,192]{1,0:T(8,128)(2,1)}, bf16[1024,192]{1,0:T(8,128)(2,1)}, bf16[1024,192]{1,0:T(8,128)(2,1)}, f...) custom-call(s32[2]{0:T(128)} %pad_add_fusion.refs_0_.meta, bf16[512,768]{1,0:T(8,128)(2,1)} %pad_maximum_fusion.refs_1_.d0.refs_4_, ...), custom_call_target="tpu_custom_call" | custom-call | flops 9999999827968 | bytes 10000000000 | tf_op jit(solution)/shard_map/attend_far_0/pallas_call | solution.py:307
  110.3 5.0 collective-permute-done.19.refs_4_
  122.1 6.1 %attend_near_0.1 = (f32[512,128]{1,0:T(8,128)}, bf16[512,192]{1,0:T(8,128)(2,1)}, f32[256,768]{1,0:T(8,128)}, bf16[256,768]{1,0:T(8,128)(2,1)}) custom-call(s32[2]{0:T(128)} %pad_add_fusion.refs_0_.meta, bf16[1024,192]{1,0:T(8,128)(2,1)} %get-tuple-element.538.q_ref.refs_5_, bf16[1024,192]{1,0:T(8,128)(2,1)} %get-tuple-element.366.k_ref.refs_7_, ...), custom_call_target="tpu_custom_call" | custom-call | flops 9999999827968 | bytes 10000000000 | tf_op jit(solution)/shard_map/attend_near_0/pallas_call | solution.py:307
  130.6 6.8 %attend_far_1.1 = (bf16[512,768]{1,0:T(8,128)(2,1)}, bf16[512,192]{1,0:T(8,128)(2,1)}, bf16[512,192]{1,0:T(8,128)(2,1)}, bf16[512,192]{1,0:T(8,128)(2,1)}, f32[2...) custom-call(s32[2]{0:T(128)} %pad_add_fusion.1.refs_0_.meta, ...), custom_call_target="tpu_custom_call" | custom-call | flops 9999999827968 | bytes 10000000000 | tf_op jit(solution)/shard_map/attend_far_1/pallas_call | solution.py:307
  141.4 4.1 gather_feeds_0.1
  147.8 5.1 attend_near_1.1
  152.9 4.3 collective-permute-done.27.x0.refs_2_
  159.7 4.6 enc_feed_far.1
  169.0 4.7 enc_feed_near.1
  175.9 4.9 collective-permute-done.37.far_ref
  180.8 2.8 close_enc_feed.1
  186.7 9.1 %collective-permute-done.42.refs_7_.refs_6_ = bf16[256,768]{1,0:T(8,128)(2,1)S(1)} collective-permute-done((bf16[256,768]{1,0:T(8,128)(2,1)}, bf16[256,768]{1,0:T(8,128)(2,1)S(1)}, u32[]{:S(2)}, u32[]{:S(2)}) %collective-permute-start.42) | collective-permute-done | bytes 393248 | tf_op jit(solution)/shard_map/ppermute | solution.py:31
  195.8 3.8 collective-permute-done.39.refs_3_.refs_2_
  202.5 8.0 %attend_far_2.1 = (bf16[512,192]{1,0:T(8,128)(2,1)}, bf16[1024,192]{1,0:T(8,128)(2,1)}, bf16[1024,192]{1,0:T(8,128)(2,1)}, f32[256,128]{1,0:T(8,128)}, bf16[256,...) custom-call(s32[2]{0:T(128)} %pad_add_fusion.refs_0_.meta, ...), custom_call_target="tpu_custom_call" | custom-call | flops 9999999827968 | bytes 10000000000 | tf_op jit(solution)/shard_map/attend_far_2/pallas_call | solution.py:307
  214.3 6.5 %attend_near_2.1 = (f32[256,128]{1,0:T(8,128)}, bf16[256,192]{1,0:T(8,128)(2,1)}, f32[128,768]{1,0:T(8,128)}, bf16[128,768]{1,0:T(8,128)(2,1)}) custom-call(s32[2]{0:T(128)} %pad_add_fusion.refs_0_.meta, bf16[512,192]{1,0:T(8,128)(2,1)} %get-tuple-element.449.q_ref.refs_5_, bf16[1024,192]{1,0:T(8,128)(2,1)} %get-tuple-element.411.k_ref.refs_7_, ...), custom_call_target="tpu_custom_call" | custom-call | flops 9999999827968 | bytes 10000000000 | tf_op jit(solution)/shard_map/attend_near_2/pallas_call | solution.py:307
  227.9 3.8 dec_feed_near.1
  233.2 4.5 dec_feed_back_near.1
  237.7 3.6 dec_feed_far.1
  241.3 4.5 dec_feed_back_far.1
  250.8 6.7 %dec_feed_weight.1 = (bf16[2,384,768]{2,1,0:T(8,128)(2,1)}, bf16[2,384,768]{2,1,0:T(8,128)(2,1)}) custom-call(bf16[128,768]{1,0:T(8,128)(2,1)} %get-tuple-element.420.x0.refs_0_, bf16[128,768]{1,0:T(8,128)(2,1)} %copy-done.38, bf16[128,768]{1,0:T(8,128)(2,1)} %collective-permute-done.48.x0.refs_2_, bf16[128,768]{1,0:T(8,128)(2,1)} %collective-permute-done.49.x1.refs_3_, ...), custom_call_target="tpu_custom_call" | custom-call | flops 9999999827968 | bytes 10000000000 | tf_op jit(solution)/shard_map/dec_feed_weight/pallas_call | solution.py:307
  261.6 5.9 %collective-permute-done.54.refs_2_.refs_3_ = bf16[128,768]{1,0:T(8,128)(2,1)S(1)} collective-permute-done((bf16[128,768]{1,0:T(8,128)(2,1)}, bf16[128,768]{1,0:T(8,128)(2,1)S(1)}, u32[]{:S(2)}, u32[]{:S(2)}) %collective-permute-start.54) | collective-permute-done | bytes 196640 | tf_op jit(solution)/shard_map/ppermute | solution.py:31
  274.6 11.1 %attend_back_2.1 = (bf16[512,192]{1,0:T(8,128)(2,1)}, bf16[192,1024]{1,0:T(8,128)(2,1)}, bf16[192,1024]{1,0:T(8,128)(2,1)}, f32[128,768]{1,0:T(8,128)}, bf16[128...) custom-call(s32[2]{0:T(128)} %pad_add_fusion.refs_0_.meta, ...), custom_call_target="tpu_custom_call" | custom-call | flops 9999999827968 | bytes 10000000000 | tf_op jit(solution)/shard_map/attend_back_2/pallas_call | solution.py:307
  291.0 3.9 cross_weights.1
  297.9 3.8 collective-permute-done.64.far_ref
  301.6 3.1 back_encoded.1
  308.2 7.3 %collective-permute-done.69.refs_3_ = bf16[2,384,768]{2,1,0:T(8,128)(2,1)} collective-permute-done((bf16[2,384,768]{2,1,0:T(8,128)(2,1)}, bf16[2,384,768]{2,1,0:T(8,128)(2,1)}, u32[]{:S(2)}, u32[]{:S(2)}) %collective-permute-start.69) | collective-permute-done | bytes 1179680 | tf_op jit(solution)/shard_map/ppermute | solution.py:36
  316.6 5.2 enc_feed_back_near.1
  324.9 5.1 enc_feed_back_far.1
  335.0 7.3 %enc_feed_weight.1 = (bf16[2,384,768]{2,1,0:T(8,128)(2,1)}, bf16[2,384,768]{2,1,0:T(8,128)(2,1)}) custom-call(bf16[256,768]{1,0:T(8,128)(2,1)} %get-tuple-element.393.x0.refs_0_, bf16[256,768]{1,0:T(8,128)(2,1)} %collective-permute-done.29.x1.refs_1_, bf16[256,768]{1,0:T(8,128)(2,1)} %collective-permute-done.27.x0.refs_2_, ...), custom_call_target="tpu_custom_call" | custom-call | flops 9999999827968 | bytes 10000000000 | tf_op jit(solution)/shard_map/enc_feed_weight/pallas_call | solution.py:307
  348.6 3.9 collective-permute-done.77.refs_3_.refs_8_
  352.5 3.3 back_enc_feed.1
  357.8 8.0 %attend_back_1.1 = (bf16[512,192]{1,0:T(8,128)(2,1)}, bf16[192,512]{1,0:T(8,128)(2,1)}, bf16[192,512]{1,0:T(8,128)(2,1)}, f32[128,768]{1,0:T(8,128)}, bf16[128,7...) custom-call(s32[2]{0:T(128)} %pad_add_fusion.1.refs_0_.meta, ...), custom_call_target="tpu_custom_call" | custom-call | flops 9999999827968 | bytes 10000000000 | tf_op jit(solution)/shard_map/attend_back_1/pallas_call | solution.py:307
  367.7 3.3 self_weights.1
  371.5 3.8 late_out_weight.1
  383.7 17.0 %attend_back_0.1 = (bf16[1024,192]{1,0:T(8,128)(2,1)}, bf16[192,1024]{1,0:T(8,128)(2,1)}, bf16[192,1024]{1,0:T(8,128)(2,1)}, f32[256,768]{1,0:T(8,128)}, bf16[25...) custom-call(s32[2]{0:T(128)} %pad_add_fusion.refs_0_.meta, ...), custom_call_target="tpu_custom_call" | custom-call | flops 9999999827968 | bytes 10000000000 | tf_op jit(solution)/shard_map/attend_back_0/pallas_call | solution.py:307
  407.2 3.9 part_zero.1
  412.2 3.4 part_middle.1
  416.5 3.3 feed_hop_2.1
  422.6 3.2 back_enc_attn.1
  427.3 15.0 %collective-permute-done.94.refs_4_ = bf16[2,192,1152]{2,1,0:T(8,128)(2,1)} collective-permute-done((bf16[2,192,1152]{2,1,0:T(8,128)(2,1)}, bf16[2,192,1152]{2,1,0:T(8,128)(2,1)}, u32[]{:S(2)}, u32[]{:S(2)}) %collective-permute-start.94) | collective-permute-done | bytes 884768 | tf_op jit(solution)/shard_map/ppermute | solution.py:36
  442.3 2.8 attn_hop_1.1
  445.4 3.3 feed_hop_3.1
  451.0 10.2 %collective-permute-done.95.refs_6_ = bf16[208,1152]{1,0:T(8,128)(2,1)} collective-permute-done((bf16[208,1152]{1,0:T(8,128)(2,1)}, bf16[208,1152]{1,0:T(8,128)(2,1)}, u32[]{:S(2)}, u32[]{:S(2)}) %collective-permute-start.95) | collective-permute-done | bytes 479264 | tf_op jit(solution)/shard_map/ppermute | solution.py:65
  461.2 3.1 attn_hop_2.1
  464.4 9.4 %collective-permute-done.99.refs_4_ = bf16[384,768]{1,0:T(8,128)(2,1)} collective-permute-done((bf16[384,768]{1,0:T(8,128)(2,1)}, bf16[384,768]{1,0:T(8,128)(2,1)}, u32[]{:S(2)}, u32[]{:S(2)}) %collective-permute-start.99) | collective-permute-done | bytes 589856 | tf_op jit(solution)/shard_map/ppermute | solution.py:65
  473.8 3.5 feed_hop_4.1.total_ref
  482.1 3.1 attn_hop_3.1
  488.3 10.3 %collective-permute-done.98.refs_6_ = bf16[208,1152]{1,0:T(8,128)(2,1)} collective-permute-done((bf16[208,1152]{1,0:T(8,128)(2,1)}, bf16[208,1152]{1,0:T(8,128)(2,1)}, u32[]{:S(2)}, u32[]{:S(2)}) %collective-permute-start.98) | collective-permute-done | bytes 479264 | tf_op jit(solution)/shard_map/ppermute | solution.py:65
  498.5 3.4 attn_hop_4.1.total_ref
  508.0 3.9 adam_1.1
  520.7 4.1 adam_0.1
  536.5 3.6 collective-permute-done.110
  545.1 4.1 lamb.1
  (358 shorter events, 192.0 us)
Async XLA Ops:
  3.4 14.4 %collective-permute-start.1 = (bf16[2,320,384]{2,1,0:T(8,128)(2,1)}, bf16[2,320,384]{2,1,0:T(8,128)(2,1)S(1)}, u32[]{:S(2)}, u32[]{:S(2)}) collective-permute-start(bf16[2,320,384]{2,1,0:T(8,128)(2,1)} %get-tuple-element.329), channel_id=1, source_target_pairs={{0,2},{1,3},{2,0},{3,1},{4,6},{5,7},{6,4},{7,5},{8,10},{9,11},{10,... | collective-permute-start | bytes 1474568 | tf_op jit(solution)/shard_map/ppermute | solution.py:31
  23.3 13.3 %collective-permute-start.3 = (bf16[208,1152]{1,0:T(8,128)(2,1)}, bf16[208,1152]{1,0:T(8,128)(2,1)}, u32[]{:S(2)}, u32[]{:S(2)}) collective-permute-start(bf16[208,1152]{1,0:T(8,128)(2,1)} %get-tuple-element.331.refs_0_), channel_id=1, source_target_pairs={{0,4},{4,0},{8,12},{12,8},{16,20},{20,16},{24,28},{28,24},{1,5},{5... | collective-permute-start | bytes 1437704 | tf_op jit(solution)/shard_map/ppermute | solution.py:36
  25.0 14.8 %collective-permute-start.4 = (bf16[208,1152]{1,0:T(8,128)(2,1)}, bf16[208,1152]{1,0:T(8,128)(2,1)S(1)}, u32[]{:S(2)}, u32[]{:S(2)}) collective-permute-start(bf16[208,1152]{1,0:T(8,128)(2,1)} %get-tuple-element.331.refs_0_), channel_id=1, source_target_pairs={{0,8},{4,12},{8,16},{12,20},{16,24},{20,28},{24,0},{28,4},{1,9},{5... | collective-permute-start | bytes 1437704 | tf_op jit(solution)/shard_map/ppermute | solution.py:65
  39.9 12.0 %collective-permute-start.5 = (bf16[208,1152]{1,0:T(8,128)(2,1)S(1)}, bf16[208,1152]{1,0:T(8,128)(2,1)S(1)}, u32[]{:S(2)}, u32[]{:S(2)}) collective-permute-start(bf16[208,1152]{1,0:T(8,128)(2,1)S(1)} %collective-permute-done.4.refs_2_), channel_id=1, source_target_pairs={{0,4},{4,0},{8,12},{12,8},{16,20},{20,16},{24,28},{28,24},{1,5},{5... | collective-permute-start | bytes 1437704 | tf_op jit(solution)/shard_map/ppermute | solution.py:36
  40.6 13.8 %collective-permute-start.6 = (bf16[208,1152]{1,0:T(8,128)(2,1)S(1)}, bf16[208,1152]{1,0:T(8,128)(2,1)S(1)}, u32[]{:S(2)}, u32[]{:S(2)}) collective-permute-start(bf16[208,1152]{1,0:T(8,128)(2,1)S(1)} %collective-permute-done.4.refs_2_), channel_id=1, source_target_pairs={{0,8},{4,12},{8,16},{12,20},{16,24},{20,28},{24,0},{28,4},{1,9},{5... | collective-permute-start | bytes 1437704 | tf_op jit(solution)/shard_map/ppermute | solution.py:65
  54.4 11.0 %collective-permute-start.7 = (bf16[208,1152]{1,0:T(8,128)(2,1)S(1)}, bf16[208,1152]{1,0:T(8,128)(2,1)S(1)}, u32[]{:S(2)}, u32[]{:S(2)}) collective-permute-start(bf16[208,1152]{1,0:T(8,128)(2,1)S(1)} %collective-permute-done.6.refs_4_), channel_id=1, source_target_pairs={{0,4},{4,0},{8,12},{12,8},{16,20},{20,16},{24,28},{28,24},{1,5},{5... | collective-permute-start | bytes 1437704 | tf_op jit(solution)/shard_map/ppermute | solution.py:36
  55.4 12.4 %collective-permute-start.8 = (bf16[208,1152]{1,0:T(8,128)(2,1)S(1)}, bf16[208,1152]{1,0:T(8,128)(2,1)}, u32[]{:S(2)}, u32[]{:S(2)}) collective-permute-start(bf16[208,1152]{1,0:T(8,128)(2,1)S(1)} %collective-permute-done.6.refs_4_), channel_id=1, source_target_pairs={{0,8},{4,12},{8,16},{12,20},{16,24},{20,28},{24,0},{28,4},{1,9},{5... | collective-permute-start | bytes 1437704 | tf_op jit(solution)/shard_map/ppermute | solution.py:65
  57.8 14.8 %collective-permute-start.15 = (bf16[512,768]{1,0:T(8,128)(2,1)}, bf16[512,768]{1,0:T(8,128)(2,1)}, u32[]{:S(2)}, u32[]{:S(2)}) collective-permute-start(bf16[512,768]{1,0:T(8,128)(2,1)} %pad_maximum_fusion.refs_1_.d0.refs_4_), channel_id=1, source_target_pairs={{0,1},{1,0},{2,3},{3,2},{4,5},{5,4},{6,7},{7,6},{8,9},{9,8},{10,11... | collective-permute-start | bytes 2359304 | tf_op jit(solution)/shard_map/ppermute | solution.py:31
  57.8 20.3 %collective-permute-start.16 = (bf16[512,768]{1,0:T(8,128)(2,1)}, bf16[512,768]{1,0:T(8,128)(2,1)}, u32[]{:S(2)}, u32[]{:S(2)}) collective-permute-start(bf16[512,768]{1,0:T(8,128)(2,1)} %pad_maximum_fusion.refs_1_.d0.refs_4_), channel_id=1, source_target_pairs={{0,2},{1,3},{2,0},{3,1},{4,6},{5,7},{6,4},{7,5},{8,10},{9,11},{10,... | collective-permute-start | bytes 2359304 | tf_op jit(solution)/shard_map/ppermute | solution.py:31
  67.7 11.4 %collective-permute-start.9 = (bf16[208,1152]{1,0:T(8,128)(2,1)}, bf16[208,1152]{1,0:T(8,128)(2,1)}, u32[]{:S(2)}, u32[]{:S(2)}) collective-permute-start(bf16[208,1152]{1,0:T(8,128)(2,1)} %collective-permute-done.8.refs_6_), channel_id=1, source_target_pairs={{0,4},{4,0},{8,12},{12,8},{16,20},{20,16},{24,28},{28,24},{1,5},{5... | collective-permute-start | bytes 1437704 | tf_op jit(solution)/shard_map/ppermute | solution.py:36
  78.0 20.7 %collective-permute-start.17 = (bf16[512,768]{1,0:T(8,128)(2,1)}, bf16[512,768]{1,0:T(8,128)(2,1)}, u32[]{:S(2)}, u32[]{:S(2)}) collective-permute-start(bf16[512,768]{1,0:T(8,128)(2,1)} %collective-permute-done.16.refs_3_.d0.refs_6_), channel_id=1, source_target_pairs={{0,1},{1,0},{2,3},{3,2},{4,5},{5,4},{6,7},{7,6},{8,9},{9,8},{10,11... | collective-permute-start | bytes 2359304 | tf_op jit(solution)/shard_map/ppermute | solution.py:31
  78.0 18.3 %collective-permute-start.10 = (bf16[384,768]{1,0:T(8,128)(2,1)}, bf16[384,768]{1,0:T(8,128)(2,1)}, u32[]{:S(2)}, u32[]{:S(2)}) collective-permute-start(bf16[384,768]{1,0:T(8,128)(2,1)} %get-tuple-element.346.refs_0_), channel_id=1, source_target_pairs={{0,8},{4,12},{8,16},{12,20},{16,24},{20,28},{24,0},{28,4},{1,9},{5... | collective-permute-start | bytes 1769480 | tf_op jit(solution)/shard_map/ppermute | solution.py:65
  78.0 19.4 %collective-permute-start.11 = (bf16[384,768]{1,0:T(8,128)(2,1)}, bf16[384,768]{1,0:T(8,128)(2,1)}, u32[]{:S(2)}, u32[]{:S(2)}) collective-permute-start(bf16[384,768]{1,0:T(8,128)(2,1)} %get-tuple-element.346.refs_0_), channel_id=1, source_target_pairs={{0,4},{4,0},{8,12},{12,8},{16,20},{20,16},{24,28},{28,24},{1,5},{5... | collective-permute-start | bytes 1769480 | tf_op jit(solution)/shard_map/ppermute | solution.py:36
  90.6 15.4 %collective-permute-start.18 = (bf16[2,2,192,192]{3,2,1,0:T(8,128)(2,1)}, bf16[2,2,192,192]{3,2,1,0:T(8,128)(2,1)}, u32[]{:S(2)}, u32[]{:S(2)}) collective-permute-start(bf16[2,2,192,192]{3,2,1,0:T(8,128)(2,1)} %get-tuple-element.358), channel_id=1, source_target_pairs={{0,2},{1,3},{2,0},{3,1},{4,6},{5,7},{6,4},{7,5},{8,10},{9,11},{10,... | collective-permute-start | bytes 884744 | tf_op jit(solution)/shard_map/ppermute | solution.py:31
  96.4 18.9 %collective-permute-start.20 = (bf16[384,768]{1,0:T(8,128)(2,1)}, bf16[384,768]{1,0:T(8,128)(2,1)}, u32[]{:S(2)}, u32[]{:S(2)}) collective-permute-start(bf16[384,768]{1,0:T(8,128)(2,1)} %collective-permute-done.10.refs_2_), channel_id=1, source_target_pairs={{0,4},{4,0},{8,12},{12,8},{16,20},{20,16},{24,28},{28,24},{1,5},{5... | collective-permute-start | bytes 1769480 | tf_op jit(solution)/shard_map/ppermute | solution.py:36
  97.4 17.8 %collective-permute-start.19 = (bf16[384,768]{1,0:T(8,128)(2,1)}, bf16[384,768]{1,0:T(8,128)(2,1)}, u32[]{:S(2)}, u32[]{:S(2)}) collective-permute-start(bf16[384,768]{1,0:T(8,128)(2,1)} %collective-permute-done.10.refs_2_), channel_id=1, source_target_pairs={{0,8},{4,12},{8,16},{12,20},{16,24},{20,28},{24,0},{28,4},{1,9},{5... | collective-permute-start | bytes 1769480 | tf_op jit(solution)/shard_map/ppermute | solution.py:65
  117.3 10.9 %collective-permute-start.23 = (bf16[2,2,192,192]{3,2,1,0:T(8,128)(2,1)}, bf16[2,2,192,192]{3,2,1,0:T(8,128)(2,1)}, u32[]{:S(2)}, u32[]{:S(2)}) collective-permute-start(bf16[2,2,192,192]{3,2,1,0:T(8,128)(2,1)} %collective-permute-done.18.refs_2_), channel_id=1, source_target_pairs={{0,1},{1,0},{2,3},{3,2},{4,5},{5,4},{6,7},{7,6},{8,9},{9,8},{10,11... | collective-permute-start | bytes 884744 | tf_op jit(solution)/shard_map/ppermute | solution.py:31
  117.4 20.0 %collective-permute-start.24 = (bf16[384,768]{1,0:T(8,128)(2,1)}, bf16[384,768]{1,0:T(8,128)(2,1)}, u32[]{:S(2)}, u32[]{:S(2)}) collective-permute-start(bf16[384,768]{1,0:T(8,128)(2,1)} %collective-permute-done.19.refs_4_), channel_id=1, source_target_pairs={{0,8},{4,12},{8,16},{12,20},{16,24},{20,28},{24,0},{28,4},{1,9},{5... | collective-permute-start | bytes 1769480 | tf_op jit(solution)/shard_map/ppermute | solution.py:65
  117.7 19.7 %collective-permute-start.31 = (bf16[384,768]{1,0:T(8,128)(2,1)}, bf16[384,768]{1,0:T(8,128)(2,1)}, u32[]{:S(2)}, u32[]{:S(2)}) collective-permute-start(bf16[384,768]{1,0:T(8,128)(2,1)} %collective-permute-done.19.refs_4_), channel_id=1, source_target_pairs={{0,4},{4,0},{8,12},{12,8},{16,20},{20,16},{24,28},{28,24},{1,5},{5... | collective-permute-start | bytes 1769480 | tf_op jit(solution)/shard_map/ppermute | solution.py:36
  120.6 17.9 %collective-permute-start.26 = (bf16[256,768]{1,0:T(8,128)(2,1)}, bf16[256,768]{1,0:T(8,128)(2,1)}, u32[]{:S(2)}, u32[]{:S(2)}) collective-permute-start(bf16[256,768]{1,0:T(8,128)(2,1)} %add_convert_fusion.4), channel_id=1, source_target_pairs={{0,2},{1,3},{2,0},{3,1},{4,6},{5,7},{6,4},{7,5},{8,10},{9,11},{10,... | collective-permute-start | bytes 1179656 | tf_op jit(solution)/shard_map/ppermute | solution.py:31
  128.2 10.3 %collective-permute-start.25 = (bf16[256,768]{1,0:T(8,128)(2,1)}, bf16[256,768]{1,0:T(8,128)(2,1)}, u32[]{:S(2)}, u32[]{:S(2)}) collective-permute-start(bf16[256,768]{1,0:T(8,128)(2,1)} %get-tuple-element.368), channel_id=1, source_target_pairs={{0,1},{1,0},{2,3},{3,2},{4,5},{5,4},{6,7},{7,6},{8,9},{9,8},{10,11... | collective-permute-start | bytes 1179656 | tf_op jit(solution)/shard_map/ppermute | solution.py:31
  137.4 19.8 %collective-permute-start.32 = (bf16[384,768]{1,0:T(8,128)(2,1)}, bf16[384,768]{1,0:T(8,128)(2,1)}, u32[]{:S(2)}, u32[]{:S(2)}) collective-permute-start(bf16[384,768]{1,0:T(8,128)(2,1)} %collective-permute-done.24.refs_0_), channel_id=1, source_target_pairs={{0,4},{4,0},{8,12},{12,8},{16,20},{20,16},{24,28},{28,24},{1,5},{5... | collective-permute-start | bytes 1769480 | tf_op jit(solution)/shard_map/ppermute | solution.py:36
  145.5 11.7 %collective-permute-start.27 = (bf16[256,768]{1,0:T(8,128)(2,1)}, bf16[256,768]{1,0:T(8,128)(2,1)}, u32[]{:S(2)}, u32[]{:S(2)}) collective-permute-start(bf16[256,768]{1,0:T(8,128)(2,1)} %get-tuple-element.393.x0.refs_0_), channel_id=1, source_target_pairs={{0,2},{1,3},{2,0},{3,1},{4,6},{5,7},{6,4},{7,5},{8,10},{9,11},{10,... | collective-permute-start | bytes 1179656 | tf_op jit(solution)/shard_map/ppermute | solution.py:31
  146.1 11.1 %collective-permute-start.29 = (bf16[256,768]{1,0:T(8,128)(2,1)}, bf16[256,768]{1,0:T(8,128)(2,1)}, u32[]{:S(2)}, u32[]{:S(2)}) collective-permute-start(bf16[256,768]{1,0:T(8,128)(2,1)} %get-tuple-element.393.x0.refs_0_), channel_id=1, source_target_pairs={{0,1},{1,0},{2,3},{3,2},{4,5},{5,4},{6,7},{7,6},{8,9},{9,8},{10,11... | collective-permute-start | bytes 1179656 | tf_op jit(solution)/shard_map/ppermute | solution.py:31
  164.8 9.0 %collective-permute-start.34 = (bf16[128,768]{1,0:T(8,128)(2,1)}, bf16[128,768]{1,0:T(8,128)(2,1)}, u32[]{:S(2)}, u32[]{:S(2)}) collective-permute-start(bf16[128,768]{1,0:T(8,128)(2,1)} %get-tuple-element.383), channel_id=1, source_target_pairs={{0,1},{1,0},{2,3},{3,2},{4,5},{5,4},{6,7},{7,6},{8,9},{9,8},{10,11... | collective-permute-start | bytes 589832 | tf_op jit(solution)/shard_map/ppermute | solution.py:31
  164.8 9.0 %collective-permute-start.35 = (bf16[128,768]{1,0:T(8,128)(2,1)}, bf16[128,768]{1,0:T(8,128)(2,1)}, u32[]{:S(2)}, u32[]{:S(2)}) collective-permute-start(bf16[128,768]{1,0:T(8,128)(2,1)} %add_convert_fusion.11), channel_id=1, source_target_pairs={{0,2},{1,3},{2,0},{3,1},{4,6},{5,7},{6,4},{7,5},{8,10},{9,11},{10,... | collective-permute-start | bytes 589832 | tf_op jit(solution)/shard_map/ppermute | solution.py:31
  168.5 12.4 %collective-permute-start.37 = (bf16[256,768]{1,0:T(8,128)(2,1)}, bf16[256,768]{1,0:T(8,128)(2,1)}, u32[]{:S(2)}, u32[]{:S(2)}) collective-permute-start(bf16[256,768]{1,0:T(8,128)(2,1)} %add_convert_fusion.3), channel_id=1, source_target_pairs={{0,2},{1,3},{2,0},{3,1},{4,6},{5,7},{6,4},{7,5},{8,10},{9,11},{10,... | collective-permute-start | bytes 1179656 | tf_op jit(solution)/shard_map/ppermute | solution.py:31
  183.7 12.1 %collective-permute-start.42 = (bf16[256,768]{1,0:T(8,128)(2,1)}, bf16[256,768]{1,0:T(8,128)(2,1)S(1)}, u32[]{:S(2)}, u32[]{:S(2)}) collective-permute-start(bf16[256,768]{1,0:T(8,128)(2,1)} %get-tuple-element.401.refs_5_.refs_4_), channel_id=1, source_target_pairs={{0,2},{1,3},{2,0},{3,1},{4,6},{5,7},{6,4},{7,5},{8,10},{9,11},{10,... | collective-permute-start | bytes 1179656 | tf_op jit(solution)/shard_map/ppermute | solution.py:31
  185.0 10.8 %collective-permute-start.38 = (bf16[128,768]{1,0:T(8,128)(2,1)S(1)}, bf16[128,768]{1,0:T(8,128)(2,1)S(1)}, u32[]{:S(2)}, u32[]{:S(2)}) collective-permute-start(bf16[128,768]{1,0:T(8,128)(2,1)S(1)} %copy-done.30), channel_id=1, source_target_pairs={{0,1},{1,0},{2,3},{3,2},{4,5},{5,4},{6,7},{7,6},{8,9},{9,8},{10,11... | collective-permute-start | bytes 589832 | tf_op jit(solution)/shard_map/ppermute | solution.py:31
  185.2 14.4 %collective-permute-start.39 = (bf16[128,768]{1,0:T(8,128)(2,1)S(1)}, bf16[128,768]{1,0:T(8,128)(2,1)S(1)}, u32[]{:S(2)}, u32[]{:S(2)}) collective-permute-start(bf16[128,768]{1,0:T(8,128)(2,1)S(1)} %copy-done.30), channel_id=1, source_target_pairs={{0,2},{1,3},{2,0},{3,1},{4,6},{5,7},{6,4},{7,5},{8,10},{9,11},{10,... | collective-permute-start | bytes 589832 | tf_op jit(solution)/shard_map/ppermute | solution.py:31
  246.3 11.1 %collective-permute-start.51 = (bf16[128,768]{1,0:T(8,128)(2,1)}, bf16[128,768]{1,0:T(8,128)(2,1)}, u32[]{:S(2)}, u32[]{:S(2)}) collective-permute-start(bf16[128,768]{1,0:T(8,128)(2,1)} %get-tuple-element.430), channel_id=1, source_target_pairs={{0,1},{1,0},{2,3},{3,2},{4,5},{5,4},{6,7},{7,6},{8,9},{9,8},{10,11... | collective-permute-start | bytes 589832 | tf_op jit(solution)/shard_map/ppermute | solution.py:31
  272.4 13.3 %collective-permute-start.58 = (bf16[128,768]{1,0:T(8,128)(2,1)}, bf16[128,768]{1,0:T(8,128)(2,1)}, u32[]{:S(2)}, u32[]{:S(2)}) collective-permute-start(bf16[128,768]{1,0:T(8,128)(2,1)} %add_convert_fusion.8), channel_id=1, source_target_pairs={{0,2},{1,3},{2,0},{3,1},{4,6},{5,7},{6,4},{7,5},{8,10},{9,11},{10,... | collective-permute-start | bytes 589832 | tf_op jit(solution)/shard_map/ppermute | solution.py:31
  273.2 12.6 %collective-permute-start.57 = (bf16[128,768]{1,0:T(8,128)(2,1)}, bf16[128,768]{1,0:T(8,128)(2,1)}, u32[]{:S(2)}, u32[]{:S(2)}) collective-permute-start(bf16[128,768]{1,0:T(8,128)(2,1)} %get-tuple-element.453), channel_id=1, source_target_pairs={{0,1},{1,0},{2,3},{3,2},{4,5},{5,4},{6,7},{7,6},{8,9},{9,8},{10,11... | collective-permute-start | bytes 589832 | tf_op jit(solution)/shard_map/ppermute | solution.py:31
  273.4 12.4 %collective-permute-start.59 = (bf16[2,1,192,192]{3,2,1,0:T(8,128)(2,1)}, bf16[2,1,192,192]{3,2,1,0:T(8,128)(2,1)}, u32[]{:S(2)}, u32[]{:S(2)}) collective-permute-start(bf16[2,1,192,192]{3,2,1,0:T(8,128)(2,1)} %get-tuple-element.463), channel_id=1, source_target_pairs={{0,2},{1,3},{2,0},{3,1},{4,6},{5,7},{6,4},{7,5},{8,10},{9,11},{10,... | collective-permute-start | bytes 442376 | tf_op jit(solution)/shard_map/ppermute | solution.py:31
  286.3 29.1 %collective-permute-start.69 = (bf16[2,384,768]{2,1,0:T(8,128)(2,1)}, bf16[2,384,768]{2,1,0:T(8,128)(2,1)}, u32[]{:S(2)}, u32[]{:S(2)}) collective-permute-start(bf16[2,384,768]{2,1,0:T(8,128)(2,1)} %get-tuple-element.442), channel_id=1, source_target_pairs={{0,4},{4,0},{8,12},{12,8},{16,20},{20,16},{24,28},{28,24},{1,5},{5... | collective-permute-start | bytes 3538952 | tf_op jit(solution)/shard_map/ppermute | solution.py:36
  290.2 11.5 %collective-permute-start.64 = (bf16[256,768]{1,0:T(8,128)(2,1)}, bf16[256,768]{1,0:T(8,128)(2,1)}, u32[]{:S(2)}, u32[]{:S(2)}) collective-permute-start(bf16[256,768]{1,0:T(8,128)(2,1)} %add_convert_fusion.2), channel_id=1, source_target_pairs={{0,2},{1,3},{2,0},{3,1},{4,6},{5,7},{6,4},{7,5},{8,10},{9,11},{10,... | collective-permute-start | bytes 1179656 | tf_op jit(solution)/shard_map/ppermute | solution.py:31
  297.3 9.2 %collective-permute-start.68 = (bf16[128,768]{1,0:T(8,128)(2,1)}, bf16[128,768]{1,0:T(8,128)(2,1)}, u32[]{:S(2)}, u32[]{:S(2)}) collective-permute-start(bf16[128,768]{1,0:T(8,128)(2,1)} %get-tuple-element.483), channel_id=1, source_target_pairs={{0,1},{1,0},{2,3},{3,2},{4,5},{5,4},{6,7},{7,6},{8,9},{9,8},{10,11... | collective-permute-start | bytes 589832 | tf_op jit(solution)/shard_map/ppermute | solution.py:31
  304.7 10.8 %collective-permute-start.65 = (bf16[256,768]{1,0:T(8,128)(2,1)}, bf16[256,768]{1,0:T(8,128)(2,1)S(1)}, u32[]{:S(2)}, u32[]{:S(2)}) collective-permute-start(bf16[256,768]{1,0:T(8,128)(2,1)} %get-tuple-element.478.d0.refs_4_), channel_id=1, source_target_pairs={{0,1},{1,0},{2,3},{3,2},{4,5},{5,4},{6,7},{7,6},{8,9},{9,8},{10,11... | collective-permute-start | bytes 1179656 | tf_op jit(solution)/shard_map/ppermute | solution.py:31
  304.7 11.8 %collective-permute-start.66 = (bf16[256,768]{1,0:T(8,128)(2,1)}, bf16[256,768]{1,0:T(8,128)(2,1)}, u32[]{:S(2)}, u32[]{:S(2)}) collective-permute-start(bf16[256,768]{1,0:T(8,128)(2,1)} %get-tuple-element.478.d0.refs_4_), channel_id=1, source_target_pairs={{0,2},{1,3},{2,0},{3,1},{4,6},{5,7},{6,4},{7,5},{8,10},{9,11},{10,... | collective-permute-start | bytes 1179656 | tf_op jit(solution)/shard_map/ppermute | solution.py:31
  305.5 18.6 %collective-permute-start.70 = (bf16[1,192,1152]{2,1,0:T(8,128)(2,1)}, bf16[1,192,1152]{2,1,0:T(8,128)(2,1)}, u32[]{:S(2)}, u32[]{:S(2)}) collective-permute-start(bf16[1,192,1152]{2,1,0:T(8,128)(2,1)} %get-tuple-element.473), channel_id=1, source_target_pairs={{0,4},{4,0},{8,12},{12,8},{16,20},{20,16},{24,28},{28,24},{1,5},{5... | collective-permute-start | bytes 1327112 | tf_op jit(solution)/shard_map/ppermute | solution.py:36
  316.6 8.3 %collective-permute-start.67 = (bf16[256,768]{1,0:T(8,128)(2,1)}, bf16[256,768]{1,0:T(8,128)(2,1)}, u32[]{:S(2)}, u32[]{:S(2)}) collective-permute-start(bf16[256,768]{1,0:T(8,128)(2,1)} %collective-permute-done.66.d0.refs_6_), channel_id=1, source_target_pairs={{0,1},{1,0},{2,3},{3,2},{4,5},{5,4},{6,7},{7,6},{8,9},{9,8},{10,11... | collective-permute-start | bytes 1179656 | tf_op jit(solution)/shard_map/ppermute | solution.py:31
  330.5 11.8 %collective-permute-start.73 = (bf16[128,768]{1,0:T(8,128)(2,1)}, bf16[128,768]{1,0:T(8,128)(2,1)}, u32[]{:S(2)}, u32[]{:S(2)}) collective-permute-start(bf16[128,768]{1,0:T(8,128)(2,1)} %get-tuple-element.508), channel_id=1, source_target_pairs={{0,1},{1,0},{2,3},{3,2},{4,5},{5,4},{6,7},{7,6},{8,9},{9,8},{10,11... | collective-permute-start | bytes 589832 | tf_op jit(solution)/shard_map/ppermute | solution.py:31
  331.0 21.5 %collective-permute-start.74 = (bf16[256,768]{1,0:T(8,128)(2,1)}, bf16[256,768]{1,0:T(8,128)(2,1)}, u32[]{:S(2)}, u32[]{:S(2)}) collective-permute-start(bf16[256,768]{1,0:T(8,128)(2,1)} %get-tuple-element.489), channel_id=1, source_target_pairs={{0,1},{1,0},{2,3},{3,2},{4,5},{5,4},{6,7},{7,6},{8,9},{9,8},{10,11... | collective-permute-start | bytes 1179656 | tf_op jit(solution)/shard_map/ppermute | solution.py:31
  334.8 17.7 %collective-permute-start.75 = (bf16[256,768]{1,0:T(8,128)(2,1)}, bf16[256,768]{1,0:T(8,128)(2,1)}, u32[]{:S(2)}, u32[]{:S(2)}) collective-permute-start(bf16[256,768]{1,0:T(8,128)(2,1)} %add_convert_fusion.1), channel_id=1, source_target_pairs={{0,2},{1,3},{2,0},{3,1},{4,6},{5,7},{6,4},{7,5},{8,10},{9,11},{10,... | collective-permute-start | bytes 1179656 | tf_op jit(solution)/shard_map/ppermute | solution.py:31
  347.5 29.4 %collective-permute-start.83 = (bf16[2,384,768]{2,1,0:T(8,128)(2,1)}, bf16[2,384,768]{2,1,0:T(8,128)(2,1)}, u32[]{:S(2)}, u32[]{:S(2)}) collective-permute-start(bf16[2,384,768]{2,1,0:T(8,128)(2,1)} %get-tuple-element.505), channel_id=1, source_target_pairs={{0,4},{4,0},{8,12},{12,8},{16,20},{20,16},{24,28},{28,24},{1,5},{5... | collective-permute-start | bytes 3538952 | tf_op jit(solution)/shard_map/ppermute | solution.py:36
  355.8 11.8 %collective-permute-start.79 = (bf16[256,768]{1,0:T(8,128)(2,1)}, bf16[256,768]{1,0:T(8,128)(2,1)}, u32[]{:S(2)}, u32[]{:S(2)}) collective-permute-start(bf16[256,768]{1,0:T(8,128)(2,1)} %get-tuple-element.513.refs_0_.refs_1_), channel_id=1, source_target_pairs={{0,2},{1,3},{2,0},{3,1},{4,6},{5,7},{6,4},{7,5},{8,10},{9,11},{10,... | collective-permute-start | bytes 1179656 | tf_op jit(solution)/shard_map/ppermute | solution.py:31
  357.6 10.1 %collective-permute-start.81 = (bf16[256,768]{1,0:T(8,128)(2,1)}, bf16[256,768]{1,0:T(8,128)(2,1)}, u32[]{:S(2)}, u32[]{:S(2)}) collective-permute-start(bf16[256,768]{1,0:T(8,128)(2,1)} %get-tuple-element.513.refs_0_.refs_1_), channel_id=1, source_target_pairs={{0,1},{1,0},{2,3},{3,2},{4,5},{5,4},{6,7},{7,6},{8,9},{9,8},{10,11... | collective-permute-start | bytes 1179656 | tf_op jit(solution)/shard_map/ppermute | solution.py:31
  379.1 21.5 %collective-permute-start.84 = (bf16[384,768]{1,0:T(8,128)(2,1)}, bf16[384,768]{1,0:T(8,128)(2,1)}, u32[]{:S(2)}, u32[]{:S(2)}) collective-permute-start(bf16[384,768]{1,0:T(8,128)(2,1)} %feed_hop_1.1), channel_id=1, source_target_pairs={{0,8},{4,12},{8,16},{12,20},{16,24},{20,28},{24,0},{28,4},{1,9},{5... | collective-permute-start | bytes 1769480 | tf_op jit(solution)/shard_map/ppermute | solution.py:65
  381.6 19.0 %collective-permute-start.85 = (bf16[128,768]{1,0:T(8,128)(2,1)}, bf16[128,768]{1,0:T(8,128)(2,1)}, u32[]{:S(2)}, u32[]{:S(2)}) collective-permute-start(bf16[128,768]{1,0:T(8,128)(2,1)} %add_convert_fusion.5), channel_id=1, source_target_pairs={{0,2},{1,3},{2,0},{3,1},{4,6},{5,7},{6,4},{7,5},{8,10},{9,11},{10,... | collective-permute-start | bytes 589832 | tf_op jit(solution)/shard_map/ppermute | solution.py:31
  383.4 17.2 %collective-permute-start.86 = (bf16[2,2,192,192]{3,2,1,0:T(8,128)(2,1)}, bf16[2,2,192,192]{3,2,1,0:T(8,128)(2,1)}, u32[]{:S(2)}, u32[]{:S(2)}) collective-permute-start(bf16[2,2,192,192]{3,2,1,0:T(8,128)(2,1)} %get-tuple-element.548), channel_id=1, source_target_pairs={{0,2},{1,3},{2,0},{3,1},{4,6},{5,7},{6,4},{7,5},{8,10},{9,11},{10,... | collective-permute-start | bytes 884744 | tf_op jit(solution)/shard_map/ppermute | solution.py:31
  401.2 18.9 %collective-permute-start.90 = (bf16[128,768]{1,0:T(8,128)(2,1)}, bf16[128,768]{1,0:T(8,128)(2,1)}, u32[]{:S(2)}, u32[]{:S(2)}) collective-permute-start(bf16[128,768]{1,0:T(8,128)(2,1)} %get-tuple-element.562), channel_id=1, source_target_pairs={{0,1},{1,0},{2,3},{3,2},{4,5},{5,4},{6,7},{7,6},{8,9},{9,8},{10,11... | collective-permute-start | bytes 589832 | tf_op jit(solution)/shard_map/ppermute | solution.py:31
  403.0 9.2 %collective-permute-start.89 = (bf16[2,2,192,192]{3,2,1,0:T(8,128)(2,1)}, bf16[2,2,192,192]{3,2,1,0:T(8,128)(2,1)}, u32[]{:S(2)}, u32[]{:S(2)}) collective-permute-start(bf16[2,2,192,192]{3,2,1,0:T(8,128)(2,1)} %collective-permute-done.86.refs_2_), channel_id=1, source_target_pairs={{0,1},{1,0},{2,3},{3,2},{4,5},{5,4},{6,7},{7,6},{8,9},{9,8},{10,11... | collective-permute-start | bytes 884744 | tf_op jit(solution)/shard_map/ppermute | solution.py:31
  405.5 17.1 %collective-permute-start.92 = (bf16[256,768]{1,0:T(8,128)(2,1)}, bf16[256,768]{1,0:T(8,128)(2,1)}, u32[]{:S(2)}, u32[]{:S(2)}) collective-permute-start(bf16[256,768]{1,0:T(8,128)(2,1)} %add_convert_fusion), channel_id=1, source_target_pairs={{0,2},{1,3},{2,0},{3,1},{4,6},{5,7},{6,4},{7,5},{8,10},{9,11},{10,... | collective-permute-start | bytes 1179656 | tf_op jit(solution)/shard_map/ppermute | solution.py:31
  411.1 16.2 %collective-permute-start.93 = (bf16[1,192,1152]{2,1,0:T(8,128)(2,1)}, bf16[1,192,1152]{2,1,0:T(8,128)(2,1)}, u32[]{:S(2)}, u32[]{:S(2)}) collective-permute-start(bf16[1,192,1152]{2,1,0:T(8,128)(2,1)} %get-tuple-element.553), channel_id=1, source_target_pairs={{0,4},{4,0},{8,12},{12,8},{16,20},{20,16},{24,28},{28,24},{1,5},{5... | collective-permute-start | bytes 1327112 | tf_op jit(solution)/shard_map/ppermute | solution.py:36
  415.6 26.8 %collective-permute-start.94 = (bf16[2,192,1152]{2,1,0:T(8,128)(2,1)}, bf16[2,192,1152]{2,1,0:T(8,128)(2,1)}, u32[]{:S(2)}, u32[]{:S(2)}) collective-permute-start(bf16[2,192,1152]{2,1,0:T(8,128)(2,1)} %get-tuple-element.558), channel_id=1, source_target_pairs={{0,4},{4,0},{8,12},{12,8},{16,20},{20,16},{24,28},{28,24},{1,5},{5... | collective-permute-start | bytes 2654216 | tf_op jit(solution)/shard_map/ppermute | solution.py:36
  419.9 25.5 %collective-permute-start.96 = (bf16[384,768]{1,0:T(8,128)(2,1)}, bf16[384,768]{1,0:T(8,128)(2,1)}, u32[]{:S(2)}, u32[]{:S(2)}) collective-permute-start(bf16[384,768]{1,0:T(8,128)(2,1)} %feed_hop_2.1), channel_id=1, source_target_pairs={{0,8},{4,12},{8,16},{12,20},{16,24},{20,28},{24,0},{28,4},{1,9},{5... | collective-permute-start | bytes 1769480 | tf_op jit(solution)/shard_map/ppermute | solution.py:65
  445.1 16.1 %collective-permute-start.95 = (bf16[208,1152]{1,0:T(8,128)(2,1)}, bf16[208,1152]{1,0:T(8,128)(2,1)}, u32[]{:S(2)}, u32[]{:S(2)}) collective-permute-start(bf16[208,1152]{1,0:T(8,128)(2,1)} %attn_hop_1.1), channel_id=1, source_target_pairs={{0,8},{4,12},{8,16},{12,20},{16,24},{20,28},{24,0},{28,4},{1,9},{5... | collective-permute-start | bytes 1437704 | tf_op jit(solution)/shard_map/ppermute | solution.py:65
  448.8 25.1 %collective-permute-start.99 = (bf16[384,768]{1,0:T(8,128)(2,1)}, bf16[384,768]{1,0:T(8,128)(2,1)}, u32[]{:S(2)}, u32[]{:S(2)}) collective-permute-start(bf16[384,768]{1,0:T(8,128)(2,1)} %feed_hop_3.1), channel_id=1, source_target_pairs={{0,8},{4,12},{8,16},{12,20},{16,24},{20,28},{24,0},{28,4},{1,9},{5... | collective-permute-start | bytes 1769480 | tf_op jit(solution)/shard_map/ppermute | solution.py:65
  464.3 17.7 %collective-permute-start.97 = (bf16[208,1152]{1,0:T(8,128)(2,1)}, bf16[208,1152]{1,0:T(8,128)(2,1)}, u32[]{:S(2)}, u32[]{:S(2)}) collective-permute-start(bf16[208,1152]{1,0:T(8,128)(2,1)} %attn_hop_2.1), channel_id=1, source_target_pairs={{0,8},{4,12},{8,16},{12,20},{16,24},{20,28},{24,0},{28,4},{1,9},{5... | collective-permute-start | bytes 1437704 | tf_op jit(solution)/shard_map/ppermute | solution.py:65
  479.6 8.6 %collective-permute-start.101 = (bf16[96,512]{1,0:T(8,128)(2,1)}, bf16[96,512]{1,0:T(8,128)(2,1)}, u32[]{:S(2)}, u32[]{:S(2)}) collective-permute-start(bf16[96,512]{1,0:T(8,128)(2,1)} %get-tuple-element.587), channel_id=1, source_target_pairs={{0,1},{1,0},{2,3},{3,2},{4,5},{5,4},{6,7},{7,6},{8,9},{9,8},{10,11... | collective-permute-start | bytes 294920 | tf_op jit(solution)/shard_map/ppermute | solution.py:31
  479.6 8.6 %collective-permute-start.102 = (bf16[2,96,512]{2,1,0:T(8,128)(2,1)}, bf16[2,96,512]{2,1,0:T(8,128)(2,1)}, u32[]{:S(2)}, u32[]{:S(2)}) collective-permute-start(bf16[2,96,512]{2,1,0:T(8,128)(2,1)} %get-tuple-element.595), channel_id=1, source_target_pairs={{0,2},{1,3},{2,0},{3,1},{4,6},{5,7},{6,4},{7,5},{8,10},{9,11},{10,... | collective-permute-start | bytes 589832 | tf_op jit(solution)/shard_map/ppermute | solution.py:31
  485.2 13.3 %collective-permute-start.98 = (bf16[208,1152]{1,0:T(8,128)(2,1)}, bf16[208,1152]{1,0:T(8,128)(2,1)}, u32[]{:S(2)}, u32[]{:S(2)}) collective-permute-start(bf16[208,1152]{1,0:T(8,128)(2,1)} %attn_hop_3.1), channel_id=1, source_target_pairs={{0,8},{4,12},{8,16},{12,20},{16,24},{20,28},{24,0},{28,4},{1,9},{5... | collective-permute-start | bytes 1437704 | tf_op jit(solution)/shard_map/ppermute | solution.py:65
  488.2 17.7 %collective-permute-start.103 = (bf16[2,96,512]{2,1,0:T(8,128)(2,1)}, bf16[2,96,512]{2,1,0:T(8,128)(2,1)}, u32[]{:S(2)}, u32[]{:S(2)}) collective-permute-start(bf16[2,96,512]{2,1,0:T(8,128)(2,1)} %collective-permute-done.102.refs_2_), channel_id=1, source_target_pairs={{0,1},{1,0},{2,3},{3,2},{4,5},{5,4},{6,7},{7,6},{8,9},{9,8},{10,11... | collective-permute-start | bytes 589832 | tf_op jit(solution)/shard_map/ppermute | solution.py:31
  504.2 10.3 %collective-permute-start.104 = (bf16[2,208,288]{2,1,0:T(8,128)(2,1)}, bf16[2,208,288]{2,1,0:T(8,128)(2,1)}, u32[]{:S(2)}, u32[]{:S(2)}) collective-permute-start(bf16[2,208,288]{2,1,0:T(8,128)(2,1)} %get-tuple-element.599), channel_id=1, source_target_pairs={{0,2},{1,3},{2,0},{3,1},{4,6},{5,7},{6,4},{7,5},{8,10},{9,11},{10,... | collective-permute-start | bytes 718856 | tf_op jit(solution)/shard_map/ppermute | solution.py:31
  (98 other events, 515.9 us)

commit v2 on v1

--- a/solution.py
+++ b/solution.py
@@ -354,39 +354,30 @@
     return mixed, logs
 
 
-def attend_rows(meta, q_ref, k_ref, v_ref, wo_ref, first, q_rows, k_rows, causal, outs, total_ref):
+def attend_rows(meta, q_ref, k_ref, v_ref, wo_ref, first, q_rows, k_rows, causal, outs):
     logs_ref, mixed_ref = outs[:2]
-    heads = q_ref.shape[1] // HEAD
-
-    def step(t, carry):
-        at = pl.multiple_of(t * q_rows, q_rows)
-        q = q_ref[pl.ds(first + at, q_rows), :]
-        bias = score_bias(meta, first + at, q_rows, q_rows, k_rows, causal)
-        mixed, logs = attend_tile(q, k_ref[...], v_ref[...], bias, heads)
-        low = mixed.astype(BF16)
-        logs_ref[pl.ds(at, q_rows), :] = logs
-        mixed_ref[pl.ds(at, q_rows), :] = low
-        if wo_ref is not None:
-            total_ref[pl.ds(at, q_rows), :] = nn(low, wo_ref[...])
-        return carry
-
-    lax.fori_loop(0, 2, step, 0)
+    heads, rows = q_ref.shape[1] // HEAD, 2 * q_rows
+    bias = score_bias(meta, first, rows, q_rows, k_rows, causal)
+    mixed, logs = attend_tile(q_ref[first : first + rows, :], k_ref[...], v_ref[...], bias, heads)
+    logs_ref[...] = logs
+    mixed_ref[...] = mixed.astype(BF16)
     if wo_ref is not None:
-        outs[2][...] = total_ref[:q_rows, :].astype(outs[2].dtype)
-        outs[3][...] = total_ref[q_rows:, :].astype(BF16)
+        for n in range(2):
+            out = outs[2 + n]
+            out[...] = nn(mixed_ref[n * q_rows : (n + 1) * q_rows, :], wo_ref[...]).astype(out.dtype)
 
 
 def project_body(rows, mixed_ref, wo_ref, keep_ref, send_ref):
-    keep_ref[...] = nn(mixed_ref[:rows, :], wo_ref[...]).astype(BF16)
-    send_ref[...] = nn(mixed_ref[rows:, :], wo_ref[...]).astype(BF16)
-
-
-def project(mixed, out_w, name):
+    for n, out in enumerate((keep_ref, send_ref)):
+        out[...] = nn(mixed_ref[n * rows : (n + 1) * rows, :], wo_ref[...]).astype(out.dtype)
+
+
+def project(mixed, out_w, keep, name):
     rows, dc = mixed.shape[0] // 2, mixed.shape[1]
     return call(
         functools.partial(project_body, rows),
         [(mixed, None), out_weights(out_w)],
-        [((rows, D), BF16), ((rows, D), BF16)],
+        [((rows, D), keep), ((rows, D), BF16)],
         4 * rows * dc * D,
         name=name,
     )
@@ -412,17 +403,18 @@
             rows_ref[j * q_rows : (j + 1) * q_rows, :] = (h * inverse * gain[...]).astype(BF16)
         queries = sources = [rows_ref.at[j * q_rows : (j + 1) * q_rows, :] for j in range(4)]
     q_ref, k_ref, v_ref = refs[:3]
-    outs, total_ref = refs[3 : 7 if fused else 5], (refs[7] if fused else None)
+    outs = refs[3:]
     for j in range(4):
         q_ref[j * q_rows : (j + 1) * q_rows, :] = nt(queries[j][...], wq[...]).astype(BF16)
         rows = sources[j][...]
         k_ref[j * k_rows : (j + 1) * k_rows, :] = nt(rows, wk[...]).astype(BF16)
         v_ref[j * k_rows : (j + 1) * k_rows, :] = nt(rows, wv[...]).astype(BF16)
-    attend_rows(meta, q_ref, k_ref, v_ref, wo, 2 * q_rows, q_rows, k_rows, causal, outs, total_ref)
-
-
-def attend_near_body(causal, q_rows, k_rows, meta, q_ref, k_ref, v_ref, wo, *rest):
-    attend_rows(meta, q_ref, k_ref, v_ref, wo, 0, q_rows, k_rows, causal, rest[:4], rest[4])
+    attend_rows(meta, q_ref, k_ref, v_ref, wo, 2 * q_rows, q_rows, k_rows, causal, outs)
+
+
+def attend_near_body(fused, causal, q_rows, k_rows, meta, q_ref, k_ref, v_ref, *rest):
+    wo, outs = (rest[0], rest[1:]) if fused else (None, rest)
+    attend_rows(meta, q_ref, k_ref, v_ref, wo, 0, q_rows, k_rows, causal, outs)
 
 
 def attn_weights(attn_t, group):
@@ -455,20 +447,19 @@
         + [((4 * q_rows, dc), BF16), ((4 * k_rows, dc), BF16), ((4 * k_rows, dc), BF16)]
         + half_outs(q_rows, dc, BF16)[: 4 if fused else 2],
         flops,
-        [pltpu.VMEM((2 * q_rows, D), F32)] if fused else [],
-        f"attend_far_{group}",
+        name=f"attend_far_{group}",
     )
 
 
 def attend_near(meta, q, k, v, out_w, group, causal):
-    q_rows, k_rows, dc = q.shape[0] // 4, k.shape[0] // 4, q.shape[1]
-    return call(
-        functools.partial(attend_near_body, causal, q_rows, k_rows),
-        [(meta, SCALARS), (q, part((2 * q_rows, dc), 0, 0)), (k, None), (v, None), out_weights(out_w)],
-        half_outs(q_rows, dc, F32),
+    q_rows, k_rows, dc, fused = q.shape[0] // 4, k.shape[0] // 4, q.shape[1], out_w is not None
+    return call(
+        functools.partial(attend_near_body, fused, causal, q_rows, k_rows),
+        [(meta, SCALARS), (q, part((2 * q_rows, dc), 0, 0)), (k, None), (v, None)]
+        + ([out_weights(out_w)] if fused else []),
+        half_outs(q_rows, dc, F32)[: 4 if fused else 2],
         16 * q_rows * k_rows * D,
-        [pltpu.VMEM((2 * q_rows, D), F32)],
-        f"attend_near_{group}",
+        name=f"attend_near_{group}",
     )
 
 
@@ -606,7 +597,7 @@
 def attend_back(meta, dz, qt, attn_t, out_w, group, saved, q_rows, k_rows, causal, cross):
     q, k, v, logs_near, logs_far = saved
     dc = q.shape[1]
-    tile = min(256, 4 * q_rows)
+    tile = min(512, 4 * q_rows)
 
     def four(rows):
         return [((rows, D), F32), ((rows, D), BF16), ((rows, D), BF16), ((rows, D), BF16)]
@@ -833,76 +824,81 @@
 
 
 def head_pack_body(ar, gr, lines, attn_ref, gain_ref, inner_ref, *refs):
-    outs, scratch = refs[0:3], refs[3]
+    outs, feed_outs, scratch, feed_scratch = refs[:3], refs[3:6], refs[6], refs[7]
     s = lax.axis_index("seq")
-    ir, width = inner_ref.shape[0], scratch.shape[2]
-    dc, room, short = D // 4, width - ar, ir // 3
+    width, ir = scratch.shape[2], inner_ref.shape[0]
+    dc, room = D // 4, width - ar
     turned = attn_ref[...].T
     gains = jnp.concatenate([gain_ref[...], jnp.zeros((1, lines * room - gr), F32)], axis=1)
     for t in range(4):
         at = s ^ t
-        scratch[at, :dc, ar:] = jnp.zeros((dc, room), BF16)
-        scratch[at, :dc, :ar] = turned[t * dc : (t + 1) * dc, :].astype(BF16)
+        scratch[at, :, ar:] = jnp.zeros((dc, room), BF16)
+        scratch[at, :, :ar] = turned[t * dc : (t + 1) * dc, :].astype(BF16)
         for n in range(lines):
             scratch[at, n : n + 1, ar:] = gains[:, n * room : (n + 1) * room].astype(BF16)
         for q in range(4):
             low = (4 * q + t) * 128
-            piece = inner_ref[:, low : low + 128].astype(BF16)
-            if q < 3:
-                scratch[at, dc : dc + ir, q * 128 : (q + 1) * 128] = piece
-            else:
-                for n in range(3):
-                    scratch[at, dc + ir :, n * 128 : (n + 1) * 128] = piece[n * short : (n + 1) * short, :]
+            feed_scratch[at, :, q * 128 : (q + 1) * 128] = inner_ref[:, low : low + 128].astype(BF16)
     hand_out(scratch, outs)
-
-
-def head_unpack_body(ar, gr, lines, ir, *refs):
-    ins, outer_ref = refs[0:4], refs[4]
-    attn_ref, feed_ref, scratch = refs[5:8]
+    hand_out(feed_scratch, feed_outs)
+
+
+def attn_unpack_body(ar, gr, lines, *refs):
+    ins, (attn_ref, scratch) = refs[0:4], refs[4:]
     place(scratch, ins, lax.axis_index("seq"))
-    dc, room, short, orow = D // 4, scratch.shape[2] - ar, ir // 3, outer_ref.shape[0]
+    dc, room = D // 4, scratch.shape[2] - ar
     pieces = []
     for k in range(4):
-        attn_ref[:dc, k * ar : (k + 1) * ar] = scratch[k, :dc, :ar]
-        rows = slice(k * ir, (k + 1) * ir)
-        feed_ref[rows, :384] = scratch[k, dc : dc + ir, :]
-        for n in range(3):
-            feed_ref[k * ir + n * short : k * ir + (n + 1) * short, 384:512] = scratch[
-                k, dc + ir :, n * 128 : (n + 1) * 128
-            ]
+        attn_ref[:dc, k * ar : (k + 1) * ar] = scratch[k, :, :ar]
         pieces += [scratch[k, n : n + 1, ar : ar + min(room, gr - n * room)].astype(F32) for n in range(lines)]
-    for g in range(D // 128):
-        r, c = g % 3 * orow, 512 + g // 3 * 128
-        feed_ref[r : r + orow, c : c + 128] = outer_ref[:, g * 128 : (g + 1) * 128].astype(BF16)
     pieces.append(jnp.zeros((1, attn_ref.shape[1] - 4 * gr), F32))
     line = jnp.concatenate(pieces, axis=1)
     fill = jnp.zeros((attn_ref.shape[0] - dc - 1, line.shape[1]), F32)
     attn_ref[dc:, :] = jnp.concatenate([line, fill], axis=0).astype(BF16)
 
 
+def feeds_unpack_body(*refs):
+    ins, outer_ref, feed_ref, scratch = refs[0:4], refs[4], refs[5], refs[6]
+    place(scratch, ins, lax.axis_index("seq"))
+    ir, orow = scratch.shape[1], outer_ref.shape[0]
+    for k in range(4):
+        feed_ref[k * ir : (k + 1) * ir, :512] = scratch[k]
+    for g in range(D // 128):
+        r, c = g % 3 * orow, 512 + g // 3 * 128
+        feed_ref[r : r + orow, c : c + 128] = outer_ref[:, g * 128 : (g + 1) * 128].astype(BF16)
+
+
 def head_exchange(attn_master, inner_master, outer_master, gain_master):
     ar, dc, gr = attn_master.shape[0], D // 4, gain_master.shape[0]
-    ir = inner_master.shape[0]
+    ir, fc = inner_master.shape[0], inner_master.shape[1] // 4
     width = (ar // 128 + 1) * 128
     lines = -(-gr // (width - ar))
-    tall = dc + ir + ir // 3
-    scratch = [pltpu.VMEM((4, tall, width), BF16)]
+    scratch, feed_scratch = pltpu.VMEM((4, dc, width), BF16), pltpu.VMEM((4, ir, fc), BF16)
     outs = call(
         functools.partial(head_pack_body, ar, gr, lines),
         plain([attn_master, gain_master[None], inner_master]),
-        sent_shapes((tall, width), BF16),
+        sent_shapes((dc, width), BF16) + sent_shapes((ir, fc), BF16),
         0,
-        scratch,
+        [scratch, feed_scratch],
         "head_pack",
     )
-    return call(
-        functools.partial(head_unpack_body, ar, gr, lines, ir),
-        plain(send_blocks(outs) + [outer_master]),
-        [((dc + 16, 4 * ar), BF16), ((4 * ir, D), BF16)],
+    attn = call(
+        functools.partial(attn_unpack_body, ar, gr, lines),
+        plain(send_blocks(outs[:3])),
+        [((dc + 16, 4 * ar), BF16)],
         0,
-        scratch,
-        "head_unpack",
-    )
+        [scratch],
+        "attn_unpack",
+    )[0]
+    feeds = call(
+        feeds_unpack_body,
+        plain(send_blocks([outs[3], tie(outs[4], attn), tie(outs[5], attn)]) + [outer_master]),
+        [((4 * ir, D), BF16)],
+        0,
+        [feed_scratch],
+        "feeds_unpack",
+    )[0]
+    return attn, feeds
 
 
 def turn_pack_body(count, *refs):
@@ -1204,6 +1200,25 @@
         [(w.shape, F32)] * 3 + [((1, 128), F32)],
         0,
         name=f"adam_{kind}",
+    )
+
+
+def gain_body(kept_ref, got_ref, w_ref, m_ref, v_ref, weights_ref, s0, s1, s2, grad_ref, *outs):
+    grad_ref[...] = kept_ref[...] + got_ref[...]
+    first_ref, second_ref, update_ref, sums_ref = *outs[:3], outs[4]
+    adam_body(3, w_ref, m_ref, v_ref, grad_ref, first_ref, second_ref, update_ref, sums_ref)
+    outs[3][:, :128] = weights_ref[...]
+    outs[3][:, 128:] = sums_ref[...] + s0[...] + s1[...] + s2[...]
+
+
+def gain_adam(kept, got, w, m, v, weight_sums, sums):
+    return call(
+        gain_body,
+        plain([kept, got, w, m, v, weight_sums, *sums]),
+        [(w.shape, F32)] * 4 + [((1, 256), F32)],
+        0,
+        [pltpu.VMEM((1, 128), F32)],
+        "adam_3",
     )
 
 
@@ -1298,12 +1313,8 @@
 
     gains = attn_t[dc].reshape(nb, ns * ar)[:, : ns * gr].reshape(6, D).astype(F32)
     gain = [gains[i : i + 1] for i in range(6)]
-    out_mine = turn_pack([(attn_t, part((dc, D), 0, 3))], "out_pack_0")
-    out_got = send_blocks(out_mine)
-    out_mine = turn_pack(
-        [(tie(attn_t, out_mine[1]), part((dc, D), 0, 7)), (attn_t, part((dc, D), 0, 11))], "out_pack_1"
-    )
-    rest_got = send_some(out_mine)
+    out_mine = turn_pack([(attn_t, part((dc, D), 0, 4 * g + 3)) for g in range(3)], "out_pack")
+    out_got = send_some(out_mine)
 
     enc_in, dec_in = encoder_layer_input[0], decoder_layer_input[0]
     er, dr = enc_in.shape[0], dec_in.shape[0]
@@ -1322,23 +1333,21 @@
     mark(out_mine[1])
     feed_step()
     rows_a, q0, k0, v0, logs_far0, mixed_far0 = attend_far(
-        tie(now(enc_meta), *out_got[1:]), enc_blocks, None, attn_t, None, 0, False, gain[0]
-    )
-    mark([mixed_far0, rest_got[2]])
-    rest_got = send_rest(rest_got, mixed_far0)
-    out_w = lanes_unpack([now(out_got[0]), *out_got[1:]], "out_unpack_0")
-    kf, sf = project(mixed_far0, (out_w, 0), "project_far_0")
+        now(enc_meta), enc_blocks, None, attn_t, None, 0, False, gain[0]
+    )
+    mark(mixed_far0)
+    logs_near0, mixed_near0 = attend_near(enc_meta, now(q0), k0, v0, None, 0, False)
+    mark([mixed_near0, out_got[2]])
+    feed_step()
+    out_w = lanes_unpack(send_rest([now(out_got[0]), *out_got[1:]], mixed_near0), "out_unpack")
+    kf, sf = project(mixed_far0, (out_w, 0), BF16, "project_far_0")
     mark(sf)
-    feed_step()
-    far = mark(far_payload(kf, now(sf)))
-    x_enc = seq_swap(far, 2)
-    logs_near0, mixed_near0, kn_enc, sn = attend_near(enc_meta, now(q0), k0, v0, (out_w, 0), 0, False)
+    kn_enc, sn = project(now(mixed_near0), (out_w, 0), F32, "project_near_0")
     mark(sn)
-    c_enc = seq_swap(sn, 1)
-    out_rest = lanes_unpack([now(rest_got[0]), *rest_got[1:]], "out_unpack_1")
-    mark(out_rest)
+    far = mark(add_low(now(kf), seq_swap(sf, 1)))
+    x_enc, c_enc = seq_swap(far, 2), seq_swap(sn, 1)
     rows_c, q1, k1, v1, logs_far1, mixed_far1, kf, sf = attend_far(
-        now(dec_meta), dec_blocks, None, attn_t, (out_rest, 0), 1, True, gain[3]
+        now(dec_meta), dec_blocks, None, attn_t, (out_w, 1), 1, True, gain[3]
     )
     mark(sf)
     feed_step()
@@ -1346,10 +1355,11 @@
     mark(norm_b)
     rows_b = gather_blocks(norm_b)
     x_self = seq_swap(mark(far_payload(kf, now(sf))), 2)
-    logs_near1, mixed_near1, kn, sn = attend_near(dec_meta, now(q1), k1, v1, (out_rest, 0), 1, True)
+    logs_near1, mixed_near1, kn, sn = attend_near(dec_meta, now(q1), k1, v1, (out_w, 1), 1, True)
     mark(sn)
     c_self = seq_swap(sn, 1)
     feed_got = [clock.finish(x) for x in feed_rings]
+    feed_got = [[now(got[0]), *got[1:]] for got in feed_got]
     if packed:
         inner_cols, outer_rows = gathered_feeds(feed_got[0], orow, "gather_feeds")
     else:
@@ -1371,11 +1381,11 @@
     mark(q1t)
     rows_d = gather_blocks(now(norm_d))
     q2, k2, v2, logs_far2, mixed_far2, kf, sf = attend_far(
-        now(enc_meta), plain(rows_d), plain(rows_e), attn_t, (out_rest, 1), 2, False
+        now(enc_meta), plain(rows_d), plain(rows_e), attn_t, (out_w, 2), 2, False
     )
     far = mark(far_payload(kf, sf))
     x_dec = seq_swap(far, 2)
-    logs_near2, mixed_near2, kn, sn = attend_near(enc_meta, now(q2), k2, v2, (out_rest, 1), 2, False)
+    logs_near2, mixed_near2, kn, sn = attend_near(enc_meta, now(q2), k2, v2, (out_w, 2), 2, False)
     mark(sn)
     dec_late, norm_f = close(now(kn), seq_swap(tie(sn, x_dec), 1), x_dec, dec_mid, gain[5], "close_cross")
     mark(norm_f)
@@ -1427,7 +1437,7 @@
     c_out = seq_swap(tie(sn_out, out_sent[1]), 1)
     decoder_layer_output = (dec_late + kn_out + c_out.astype(F32) + x_out.astype(F32)).astype(BF16)
     cross_d, outs = attend_back(
-        now(enc_meta), dz_cross, q2t, attn_t, (out_rest, 1), 2, (q2, k2, v2, logs_near2, logs_far2), dr, er, False, True
+        now(enc_meta), dz_cross, q2t, attn_t, (out_w, 2), 2, (q2, k2, v2, logs_near2, logs_far2), dr, er, False, True
     )
     far = mark(far_payload(outs[6], tie(outs[7], x_out, c_out, out_got[2])))
     x_enc, c_enc = seq_swap(far, 2), seq_swap(now(outs[5]), 1)
@@ -1464,7 +1474,7 @@
     mark(low)
     dz_enc = gather_blocks(low)
     self_d, outs = attend_back(
-        now(dec_meta), dz_self, q1t, attn_t, (out_rest, 0), 1, (q1, k1, v1, logs_near1, logs_far1), dr, dr, True, False
+        now(dec_meta), dz_self, q1t, attn_t, (out_w, 1), 1, (q1, k1, v1, logs_near1, logs_far1), dr, dr, True, False
     )
     mark(outs[3])
     self_w = attend_weights(quarters(rows_c), None, (now(self_d[0]), *self_d[1:]), "self_weights")
@@ -1487,11 +1497,13 @@
     enc_d, outs = attend_back(
         now(enc_meta), dz_enc, q0t, attn_t, (out_w, 0), 0, (q0, k0, v0, logs_near0, logs_far0), er, er, False, False
     )
-    far = mark(far_payload(outs[2], tie(outs[3], x_self, got_late[2], *flight)))
-    x_enc, c_enc = seq_swap(far, 2), seq_swap(now(outs[1]), 1)
+    mark([outs[3], x_self, got_late[2], *flight])
+    c_far, c_enc = seq_swap(outs[3], 1), seq_swap(now(outs[1]), 1)
     part_zero = pair_send(
         *self_part(quarters(rows_a), (now(enc_d[0]), *enc_d[1:]), ns * ar, "part_zero")
     )
+    for x in feeds:
+        clock.step(x)
     part_middle = pair_send(
         *attn_parts(
             [now(got_late[0]), *got_late[1:]],
@@ -1500,12 +1512,14 @@
             "part_middle",
         )
     )
+    far = mark(add_low(now(outs[2]), c_far))
+    x_enc = seq_swap(far, 2)
+    decoder_input_gradient, _, gain_three = close_back(
+        now(kn_self), c_self, x_self, dec_in, gain[3], up_four, "back_self"
+    )
+    mark(gain_three)
     for x in feeds:
         clock.step(x)
-    decoder_input_gradient, _, gain_three = close_back(
-        now(kn_self), c_self, x_self, dec_in, gain[3], up_four, "back_self"
-    )
-    mark(gain_three)
     encoder_input_gradient, _, gain_zero = close_back(
         now(outs[0]), c_enc, x_enc, enc_in, gain[0], up_one, "back_enc_attn"
     )
@@ -1518,36 +1532,38 @@
     last_ring = ring_reduce([part_zero, part_middle, part_three], "attn_hop", gain_lines)
     next(last_ring)
     clock.step(last_ring)
-    for x in feeds:
-        clock.step(x)
-    clock.step(last_ring)
     feeds_done = [clock.finish(x)[0] for x in feeds]
-    clock.step(last_ring)
     if packed:
         feed_sent, outer_grad = feed_pack(mark(feeds_done[0]), ir, fc, orow)
         mark(feed_sent[1])
-        feed_got = send_blocks(feed_sent)
+        feed_got = send_some(feed_sent)
     else:
         inner_part, outer_grad = feeds_done
         inner_part = mark(now(inner_part).astype(BF16).reshape(ns, ir, fc))
         inner_part = seq_exchange(inner_part, s)
+    clock.step(last_ring)
     outer_new = adam(2, outer_master, outer_first, outer_second, now(outer_grad))
     mark(outer_new[3])
+    clock.step(last_ring)
+    if packed:
+        inner_grad = feed_unpack(send_rest([now(feed_got[0]), *feed_got[1:]], clock.last))
+    else:
+        inner_grad = inner_part.reshape(ns, ir, cuts, orow).transpose(1, 2, 0, 3).reshape(ir, FF).astype(F32)
+    mark(inner_grad)
     (attn_sum,) = clock.finish(last_ring)
     mine = tail_pack(mark(attn_sum), ar, gr)
-    if packed:
-        mark(mine[1])
-        inner_grad = feed_unpack([now(feed_got[0]), *feed_got[1:]])
-    else:
-        inner_grad = inner_part.reshape(ns, ir, cuts, orow).transpose(1, 2, 0, 3).reshape(ir, FF).astype(F32)
-    inner_new = adam(1, inner_master, inner_first, inner_second, mark(inner_grad))
+    mark(mine[-1])
+    inner_new = adam(1, inner_master, inner_first, inner_second, now(inner_grad))
     mark(inner_new[3])
     attn_grad, gain_kept, gain_sent = tail_unpack(mine, s, ar, gr, now, clock.last)
-    gain_grad = gain_kept + batch_swap(gain_sent, 1)
+    gain_got = batch_swap(gain_sent, 1)
     attn_new = adam(0, attn_master, attn_first, attn_second, attn_grad)
-    gain_new = adam(3, masters[3], gain_first[None], gain_second[None], tie(gain_grad, attn_new[3]))
-    results = (attn_new, inner_new, outer_new, gain_new)
-    all_squares = sum_all(jnp.concatenate([squares, sum(x[3] for x in results)], axis=1))
+    others = (attn_new, inner_new, outer_new)
+    gain_grad, *gain_new, own_squares = gain_adam(
+        gain_kept, tie(gain_got, attn_new[3]), masters[3], gain_first[None], gain_second[None], squares, [x[3] for x in others]
+    )
+    results = (*others, gain_new)
+    all_squares = sum_all(own_squares)
     last = lamb(all_squares, masters, [x[2] for x in results])
     grads = (attn_grad, inner_grad, outer_grad, gain_grad)
 

time: 558 us -> 532 us (0.953)
  Pallas kernels: 257 us -> 245 us
  waiting for transfers between devices: 191 us -> 180 us
    ppermute x17, waiting for transfers between devices: 60.9 us -> 31.5 us  [batch_swap(): return lax.ppermute(x, 'batch', [(i, i ^ k) for i in range(n)])]
    ppermute x12, waiting for transfers between devices: 45.3 us -> 62.5 us  [ring_shift(): lax.ppermute(x, 'batch', [(i, (i + 2) % nb) for i in (range(nb) if active...]
    pallas_call x44, Pallas kernels: 195 us -> 182 us  [call(): pl.pallas_call(body, grid=(1,), in_specs=specs, out_specs=[whole(o) for o...]
  transfers between devices with their start and end apart: 112 -> 112, of which waited for: 49 -> 49; matrix products, arithmetic and copies ran while one was open for 5% -> 5% of each run, Pallas kernels for 38% -> 37%
where the time goes in v2:
time: 532 us; the launch traced here: 526 us
  Pallas kernels  245 us (46%)
  waiting for transfers between devices  180 us (34%)
  starting transfers between devices  62.7 us (12%)
  other arithmetic  22.5 us (4%)
  local copies, waits for them, and re-layouts  12.6 us (2%)
    pallas_call x44, Pallas kernels, call(): pl.pallas_call(body, grid=(1,), in_specs=specs, out_specs=[whole(o) for o...  182 us
    ppermute x83, waiting for transfers between devices, seq_swap(): return lax.ppermute(x, 'seq', [(i, i ^ k) for i in range(n)])  86.5 us
    ppermute x12, waiting for transfers between devices, ring_shift(): lax.ppermute(x, 'batch', [(i, (i + 2) % nb) for i in (range(nb) if active...  62.5 us
    ppermute x83, starting transfers between devices, seq_swap(): return lax.ppermute(x, 'seq', [(i, i ^ k) for i in range(n)])  36.8 us
    ppermute x17, waiting for transfers between devices, batch_swap(): return lax.ppermute(x, 'batch', [(i, i ^ k) for i in range(n)])  31.5 us
    pallas_call x10, Pallas kernels, row_call(): pl.pallas_call(body, grid=(STEPS,), in_specs=[spec(x.shape) for x in ins]...  27 us
    pallas_call x8, Pallas kernels, hop(): pl.pallas_call(functools.partial(hop_body, step, [k.shape[0] for k, _ in...  24.8 us
    ppermute x17, starting transfers between devices, batch_swap(): return lax.ppermute(x, 'batch', [(i, i ^ k) for i in range(n)])  17.9 us
  transfers between devices with their start and end apart: 112, of which 49 were waited for; matrix products, arithmetic and copies ran while one was open for 5% of the time, Pallas kernels for 37%

profile of v2, /device:TPU:0, one launch (start us, length us, event | category | flops | bytes accessed | tf_op | source)
XLA Modules:
  0.0 526.0 jit_solution(506086103804070897)
XLA Ops:
  3.4 2.9 collective-permute-start.1
  7.9 5.6 %collective-permute-done.1.refs_2_ = bf16[2,192,384]{2,1,0:T(8,128)(2,1)S(1)} collective-permute-done((bf16[2,192,384]{2,1,0:T(8,128)(2,1)}, bf16[2,192,384]{2,1,0:T(8,128)(2,1)S(1)}, u32[]{:S(2)}, u32[]{:S(2)}) %collective-permute-start.1) | collective-permute-done | bytes 294944 | tf_op jit(solution)/shard_map/ppermute | solution.py:31
  22.2 11.3 %collective-permute-done.6.refs_2_ = bf16[208,1152]{1,0:T(8,128)(2,1)S(1)} collective-permute-done((bf16[208,1152]{1,0:T(8,128)(2,1)}, bf16[208,1152]{1,0:T(8,128)(2,1)S(1)}, u32[]{:S(2)}, u32[]{:S(2)}) %collective-permute-start.6) | collective-permute-done | bytes 479264 | tf_op jit(solution)/shard_map/ppermute | solution.py:65
  41.9 6.1 %collective-permute-done.8.refs_4_ = bf16[208,1152]{1,0:T(8,128)(2,1)} collective-permute-done((bf16[208,1152]{1,0:T(8,128)(2,1)S(1)}, bf16[208,1152]{1,0:T(8,128)(2,1)}, u32[]{:S(2)}, u32[]{:S(2)}) %collective-permute-start.8) | collective-permute-done | bytes 479264 | tf_op jit(solution)/shard_map/ppermute | solution.py:65
  53.5 6.1 %collective-permute-done.16.refs_3_.d0.refs_6_ = bf16[512,768]{1,0:T(8,128)(2,1)} collective-permute-done((bf16[512,768]{1,0:T(8,128)(2,1)}, bf16[512,768]{1,0:T(8,128)(2,1)}, u32[]{:S(2)}, u32[]{:S(2)}) %collective-permute-start.16) | collective-permute-done | bytes 786464 | tf_op jit(solution)/shard_map/ppermute | solution.py:31
  59.6 2.8 collective-permute-done.10.refs_6_
  66.7 10.0 %collective-permute-done.13.refs_7_ = bf16[208,1152]{1,0:T(8,128)(2,1)} collective-permute-done((bf16[208,1152]{1,0:T(8,128)(2,1)}, bf16[208,1152]{1,0:T(8,128)(2,1)}, u32[]{:S(2)}, u32[]{:S(2)}) %collective-permute-start.13) | collective-permute-done | bytes 479264 | tf_op jit(solution)/shard_map/ppermute | solution.py:36
  76.7 4.1 gather_attn_0.1.refs_0_.refs_1_.refs_2_.refs_6_.refs_7_.refs_8_.refs_9_.refs_10_.refs_11_.refs_12_.refs_13_
  80.8 3.0 out_pack.1
  88.2 6.9 %attend_far_0.1 = (bf16[1024,768]{1,0:T(8,128)(2,1)}, bf16[1024,192]{1,0:T(8,128)(2,1)}, bf16[1024,192]{1,0:T(8,128)(2,1)}, bf16[1024,192]{1,0:T(8,128)(2,1)}, f...) custom-call(s32[2]{0:T(128)} %pad_add_fusion.refs_0_.meta, bf16[512,768]{1,0:T(8,128)(2,1)} %pad_maximum_fusion.refs_1_.d0.refs_4_, ...), custom_call_target="tpu_custom_call" | custom-call | flops 9999999827968 | bytes 10000000000 | tf_op jit(solution)/shard_map/attend_far_0/pallas_call | solution.py:307
  95.1 5.2 attend_near_0.1
  101.2 4.5 collective-permute-done.18.refs_4_
  118.0 5.0 attend_far_1.1
  123.0 5.3 %collective-permute-done.26.far_ref = bf16[256,768]{1,0:T(8,128)(2,1)} collective-permute-done((bf16[256,768]{1,0:T(8,128)(2,1)}, bf16[256,768]{1,0:T(8,128)(2,1)}, u32[]{:S(2)}, u32[]{:S(2)}) %collective-permute-start.26) | collective-permute-done | bytes 393248 | tf_op jit(solution)/shard_map/ppermute | solution.py:31
  133.8 3.3 attend_near_1.1
  137.2 4.1 gather_feeds_0.1
  144.1 3.0 collective-permute-done.32.refs_1_
  149.5 4.6 enc_feed_far.1
  159.2 4.7 enc_feed_near.1
  166.1 4.1 collective-permute-done.37.far_ref
  176.1 9.1 %collective-permute-done.42.refs_7_.refs_6_ = bf16[256,768]{1,0:T(8,128)(2,1)S(1)} collective-permute-done((bf16[256,768]{1,0:T(8,128)(2,1)}, bf16[256,768]{1,0:T(8,128)(2,1)S(1)}, u32[]{:S(2)}, u32[]{:S(2)}) %collective-permute-start.42) | collective-permute-done | bytes 393248 | tf_op jit(solution)/shard_map/ppermute | solution.py:31
  185.2 3.8 collective-permute-done.39.refs_3_.refs_2_
  191.9 6.2 %attend_far_2.1 = (bf16[512,192]{1,0:T(8,128)(2,1)}, bf16[1024,192]{1,0:T(8,128)(2,1)}, bf16[1024,192]{1,0:T(8,128)(2,1)}, f32[256,128]{1,0:T(8,128)}, bf16[256,...) custom-call(s32[2]{0:T(128)} %pad_add_fusion.refs_0_.meta, ...), custom_call_target="tpu_custom_call" | custom-call | flops 9999999827968 | bytes 10000000000 | tf_op jit(solution)/shard_map/attend_far_2/pallas_call | solution.py:307
  202.4 3.9 attend_near_2.1
  215.5 3.7 dec_feed_near.1
  220.8 4.5 dec_feed_back_near.1
  225.3 3.7 dec_feed_far.1
  229.0 4.5 dec_feed_back_far.1
  238.3 6.6 %dec_feed_weight.1 = (bf16[2,384,768]{2,1,0:T(8,128)(2,1)}, bf16[2,384,768]{2,1,0:T(8,128)(2,1)}) custom-call(bf16[128,768]{1,0:T(8,128)(2,1)} %get-tuple-element.421.x0.refs_0_, bf16[128,768]{1,0:T(8,128)(2,1)} %copy-done.33, bf16[128,768]{1,0:T(8,128)(2,1)} %collective-permute-done.48.x0.refs_2_, bf16[128,768]{1,0:T(8,128)(2,1)} %collective-permute-done.49.x1.refs_3_, ...), custom_call_target="tpu_custom_call" | custom-call | flops 9999999827968 | bytes 10000000000 | tf_op jit(solution)/shard_map/dec_feed_weight/pallas_call | solution.py:307
  249.1 5.9 %collective-permute-done.54.refs_2_.refs_3_ = bf16[128,768]{1,0:T(8,128)(2,1)S(1)} collective-permute-done((bf16[128,768]{1,0:T(8,128)(2,1)}, bf16[128,768]{1,0:T(8,128)(2,1)S(1)}, u32[]{:S(2)}, u32[]{:S(2)}) %collective-permute-start.54) | collective-permute-done | bytes 196640 | tf_op jit(solution)/shard_map/ppermute | solution.py:31
  262.2 9.7 %attend_back_2.1 = (bf16[512,192]{1,0:T(8,128)(2,1)}, bf16[192,1024]{1,0:T(8,128)(2,1)}, bf16[192,1024]{1,0:T(8,128)(2,1)}, f32[128,768]{1,0:T(8,128)}, bf16[128...) custom-call(s32[2]{0:T(128)} %pad_add_fusion.refs_0_.meta, ...), custom_call_target="tpu_custom_call" | custom-call | flops 9999999827968 | bytes 10000000000 | tf_op jit(solution)/shard_map/attend_back_2/pallas_call | solution.py:307
  277.5 3.9 cross_weights.1
  284.4 3.4 collective-permute-done.64.far_ref
  287.8 3.1 back_encoded.1
  295.0 6.7 %collective-permute-done.69.refs_3_ = bf16[2,384,768]{2,1,0:T(8,128)(2,1)} collective-permute-done((bf16[2,384,768]{2,1,0:T(8,128)(2,1)}, bf16[2,384,768]{2,1,0:T(8,128)(2,1)}, u32[]{:S(2)}, u32[]{:S(2)}) %collective-permute-start.69) | collective-permute-done | bytes 1179680 | tf_op jit(solution)/shard_map/ppermute | solution.py:36
  302.7 5.2 enc_feed_back_near.1
  311.3 5.1 enc_feed_back_far.1
  321.6 7.3 %enc_feed_weight.1 = (bf16[2,384,768]{2,1,0:T(8,128)(2,1)}, bf16[2,384,768]{2,1,0:T(8,128)(2,1)}) custom-call(bf16[256,768]{1,0:T(8,128)(2,1)} %get-tuple-element.394.x0.refs_0_, bf16[256,768]{1,0:T(8,128)(2,1)} %collective-permute-done.29.x1.refs_1_, bf16[256,768]{1,0:T(8,128)(2,1)} %collective-permute-done.27.x0.refs_2_, ...), custom_call_target="tpu_custom_call" | custom-call | flops 9999999827968 | bytes 10000000000 | tf_op jit(solution)/shard_map/enc_feed_weight/pallas_call | solution.py:307
  334.6 4.4 collective-permute-done.77.refs_3_.refs_8_
  339.1 3.3 back_enc_feed.1
  343.7 6.6 %attend_back_1.1 = (bf16[512,192]{1,0:T(8,128)(2,1)}, bf16[192,512]{1,0:T(8,128)(2,1)}, bf16[192,512]{1,0:T(8,128)(2,1)}, f32[128,768]{1,0:T(8,128)}, bf16[128,7...) custom-call(s32[2]{0:T(128)} %pad_add_fusion.1.refs_0_.meta, ...), custom_call_target="tpu_custom_call" | custom-call | flops 9999999827968 | bytes 10000000000 | tf_op jit(solution)/shard_map/attend_back_1/pallas_call | solution.py:307
  350.3 4.0 collective-permute-done.79.refs_2_.refs_3_
  354.2 3.3 self_weights.1
  358.0 3.8 late_out_weight.1
  368.5 15.6 %attend_back_0.1 = (bf16[1024,192]{1,0:T(8,128)(2,1)}, bf16[192,1024]{1,0:T(8,128)(2,1)}, bf16[192,1024]{1,0:T(8,128)(2,1)}, f32[256,768]{1,0:T(8,128)}, bf16[25...) custom-call(s32[2]{0:T(128)} %pad_add_fusion.refs_0_.meta, ...), custom_call_target="tpu_custom_call" | custom-call | flops 9999999827968 | bytes 10000000000 | tf_op jit(solution)/shard_map/attend_back_0/pallas_call | solution.py:307
  384.7 3.9 part_zero.1
  390.1 3.3 feed_hop_2.1
  394.2 3.4 part_middle.1
  403.5 7.4 %collective-permute-done.87.refs_4_ = bf16[384,768]{1,0:T(8,128)(2,1)} collective-permute-done((bf16[384,768]{1,0:T(8,128)(2,1)}, bf16[384,768]{1,0:T(8,128)(2,1)}, u32[]{:S(2)}, u32[]{:S(2)}) %collective-permute-start.87) | collective-permute-done | bytes 589856 | tf_op jit(solution)/shard_map/ppermute | solution.py:65
  410.9 3.3 feed_hop_3.1
  414.5 3.2 back_enc_attn.1
  422.8 3.1 collective-permute-start.96
  425.9 6.8 %collective-permute-done.97.refs_4_ = bf16[384,768]{1,0:T(8,128)(2,1)} collective-permute-done((bf16[384,768]{1,0:T(8,128)(2,1)}, bf16[384,768]{1,0:T(8,128)(2,1)}, u32[]{:S(2)}, u32[]{:S(2)}) %collective-permute-start.97) | collective-permute-done | bytes 589856 | tf_op jit(solution)/shard_map/ppermute | solution.py:65
  432.7 3.6 feed_hop_4.1.total_ref
  441.1 3.1 attn_hop_2.1
  447.1 10.7 %collective-permute-done.98.refs_6_ = bf16[208,1152]{1,0:T(8,128)(2,1)} collective-permute-done((bf16[208,1152]{1,0:T(8,128)(2,1)}, bf16[208,1152]{1,0:T(8,128)(2,1)}, u32[]{:S(2)}, u32[]{:S(2)}) %collective-permute-start.98) | collective-permute-done | bytes 479264 | tf_op jit(solution)/shard_map/ppermute | solution.py:65
  457.8 3.1 attn_hop_3.1
  465.5 11.0 %collective-permute-done.99.refs_6_ = bf16[208,1152]{1,0:T(8,128)(2,1)} collective-permute-done((bf16[208,1152]{1,0:T(8,128)(2,1)}, bf16[208,1152]{1,0:T(8,128)(2,1)}, u32[]{:S(2)}, u32[]{:S(2)}) %collective-permute-start.99) | collective-permute-done | bytes 479264 | tf_op jit(solution)/shard_map/ppermute | solution.py:65
  476.5 3.3 attn_hop_4.1.total_ref
  483.3 3.9 adam_1.1
  487.2 5.1 collective-permute-done.104.refs_2_
  498.2 4.1 adam_0.1
  513.1 3.6 collective-permute-done.110
  521.7 4.1 lamb.1
  (345 shorter events, 193.3 us)
Async XLA Ops:
  3.4 10.2 %collective-permute-start.1 = (bf16[2,192,384]{2,1,0:T(8,128)(2,1)}, bf16[2,192,384]{2,1,0:T(8,128)(2,1)S(1)}, u32[]{:S(2)}, u32[]{:S(2)}) collective-permute-start(bf16[2,192,384]{2,1,0:T(8,128)(2,1)} %get-tuple-element.332), channel_id=1, source_target_pairs={{0,2},{1,3},{2,0},{3,1},{4,6},{5,7},{6,4},{7,5},{8,10},{9,11},{10,... | collective-permute-start | bytes 884744 | tf_op jit(solution)/shard_map/ppermute | solution.py:31
  18.2 15.3 %collective-permute-start.6 = (bf16[208,1152]{1,0:T(8,128)(2,1)}, bf16[208,1152]{1,0:T(8,128)(2,1)S(1)}, u32[]{:S(2)}, u32[]{:S(2)}) collective-permute-start(bf16[208,1152]{1,0:T(8,128)(2,1)} %attn_unpack.1.refs_0_), channel_id=1, source_target_pairs={{0,8},{4,12},{8,16},{12,20},{16,24},{20,28},{24,0},{28,4},{1,9},{5... | collective-permute-start | bytes 1437704 | tf_op jit(solution)/shard_map/ppermute | solution.py:65
  20.0 13.5 %collective-permute-start.7 = (bf16[208,1152]{1,0:T(8,128)(2,1)}, bf16[208,1152]{1,0:T(8,128)(2,1)S(1)}, u32[]{:S(2)}, u32[]{:S(2)}) collective-permute-start(bf16[208,1152]{1,0:T(8,128)(2,1)} %attn_unpack.1.refs_0_), channel_id=1, source_target_pairs={{0,4},{4,0},{8,12},{12,8},{16,20},{20,16},{24,28},{28,24},{1,5},{5... | collective-permute-start | bytes 1437704 | tf_op jit(solution)/shard_map/ppermute | solution.py:36
  33.5 14.4 %collective-permute-start.8 = (bf16[208,1152]{1,0:T(8,128)(2,1)S(1)}, bf16[208,1152]{1,0:T(8,128)(2,1)}, u32[]{:S(2)}, u32[]{:S(2)}) collective-permute-start(bf16[208,1152]{1,0:T(8,128)(2,1)S(1)} %collective-permute-done.6.refs_2_), channel_id=1, source_target_pairs={{0,8},{4,12},{8,16},{12,20},{16,24},{20,28},{24,0},{28,4},{1,9},{5... | collective-permute-start | bytes 1437704 | tf_op jit(solution)/shard_map/ppermute | solution.py:65
  34.5 13.4 %collective-permute-start.9 = (bf16[208,1152]{1,0:T(8,128)(2,1)S(1)}, bf16[208,1152]{1,0:T(8,128)(2,1)S(1)}, u32[]{:S(2)}, u32[]{:S(2)}) collective-permute-start(bf16[208,1152]{1,0:T(8,128)(2,1)S(1)} %collective-permute-done.6.refs_2_), channel_id=1, source_target_pairs={{0,4},{4,0},{8,12},{12,8},{16,20},{20,16},{24,28},{28,24},{1,5},{5... | collective-permute-start | bytes 1437704 | tf_op jit(solution)/shard_map/ppermute | solution.py:36
  39.3 14.2 %collective-permute-start.15 = (bf16[512,768]{1,0:T(8,128)(2,1)}, bf16[512,768]{1,0:T(8,128)(2,1)}, u32[]{:S(2)}, u32[]{:S(2)}) collective-permute-start(bf16[512,768]{1,0:T(8,128)(2,1)} %pad_maximum_fusion.refs_1_.d0.refs_4_), channel_id=1, source_target_pairs={{0,1},{1,0},{2,3},{3,2},{4,5},{5,4},{6,7},{7,6},{8,9},{9,8},{10,11... | collective-permute-start | bytes 2359304 | tf_op jit(solution)/shard_map/ppermute | solution.py:31
  39.3 20.3 %collective-permute-start.16 = (bf16[512,768]{1,0:T(8,128)(2,1)}, bf16[512,768]{1,0:T(8,128)(2,1)}, u32[]{:S(2)}, u32[]{:S(2)}) collective-permute-start(bf16[512,768]{1,0:T(8,128)(2,1)} %pad_maximum_fusion.refs_1_.d0.refs_4_), channel_id=1, source_target_pairs={{0,2},{1,3},{2,0},{3,1},{4,6},{5,7},{6,4},{7,5},{8,10},{9,11},{10,... | collective-permute-start | bytes 2359304 | tf_op jit(solution)/shard_map/ppermute | solution.py:31
  41.9 21.6 %collective-permute-start.5 = (bf16[2,96,512]{2,1,0:T(8,128)(2,1)}, bf16[2,96,512]{2,1,0:T(8,128)(2,1)}, u32[]{:S(2)}, u32[]{:S(2)}) collective-permute-start(bf16[2,96,512]{2,1,0:T(8,128)(2,1)} %collective-permute-done.4.refs_2_), channel_id=1, source_target_pairs={{0,1},{1,0},{2,3},{3,2},{4,5},{5,4},{6,7},{7,6},{8,9},{9,8},{10,11... | collective-permute-start | bytes 589832 | tf_op jit(solution)/shard_map/ppermute | solution.py:31
  48.7 13.7 %collective-permute-start.10 = (bf16[208,1152]{1,0:T(8,128)(2,1)}, bf16[208,1152]{1,0:T(8,128)(2,1)}, u32[]{:S(2)}, u32[]{:S(2)}) collective-permute-start(bf16[208,1152]{1,0:T(8,128)(2,1)} %collective-permute-done.8.refs_4_), channel_id=1, source_target_pairs={{0,8},{4,12},{8,16},{12,20},{16,24},{20,28},{24,0},{28,4},{1,9},{5... | collective-permute-start | bytes 1437704 | tf_op jit(solution)/shard_map/ppermute | solution.py:65
  48.7 13.7 %collective-permute-start.12 = (bf16[208,1152]{1,0:T(8,128)(2,1)}, bf16[208,1152]{1,0:T(8,128)(2,1)}, u32[]{:S(2)}, u32[]{:S(2)}) collective-permute-start(bf16[208,1152]{1,0:T(8,128)(2,1)} %collective-permute-done.8.refs_4_), channel_id=1, source_target_pairs={{0,4},{4,0},{8,12},{12,8},{16,20},{20,16},{24,28},{28,24},{1,5},{5... | collective-permute-start | bytes 1437704 | tf_op jit(solution)/shard_map/ppermute | solution.py:36
  59.6 28.6 %collective-permute-start.17 = (bf16[512,768]{1,0:T(8,128)(2,1)}, bf16[512,768]{1,0:T(8,128)(2,1)}, u32[]{:S(2)}, u32[]{:S(2)}) collective-permute-start(bf16[512,768]{1,0:T(8,128)(2,1)} %collective-permute-done.16.refs_3_.d0.refs_6_), channel_id=1, source_target_pairs={{0,1},{1,0},{2,3},{3,2},{4,5},{5,4},{6,7},{7,6},{8,9},{9,8},{10,11... | collective-permute-start | bytes 2359304 | tf_op jit(solution)/shard_map/ppermute | solution.py:31
  62.4 14.2 %collective-permute-start.13 = (bf16[208,1152]{1,0:T(8,128)(2,1)}, bf16[208,1152]{1,0:T(8,128)(2,1)}, u32[]{:S(2)}, u32[]{:S(2)}) collective-permute-start(bf16[208,1152]{1,0:T(8,128)(2,1)} %collective-permute-done.10.refs_6_), channel_id=1, source_target_pairs={{0,4},{4,0},{8,12},{12,8},{16,20},{20,16},{24,28},{28,24},{1,5},{5... | collective-permute-start | bytes 1437704 | tf_op jit(solution)/shard_map/ppermute | solution.py:36
  65.6 20.9 %collective-permute-start.11 = (bf16[384,768]{1,0:T(8,128)(2,1)}, bf16[384,768]{1,0:T(8,128)(2,1)}, u32[]{:S(2)}, u32[]{:S(2)}) collective-permute-start(bf16[384,768]{1,0:T(8,128)(2,1)} %feeds_unpack.1.refs_0_), channel_id=1, source_target_pairs={{0,8},{4,12},{8,16},{12,20},{16,24},{20,28},{24,0},{28,4},{1,9},{5... | collective-permute-start | bytes 1769480 | tf_op jit(solution)/shard_map/ppermute | solution.py:65
  65.6 22.4 %collective-permute-start.14 = (bf16[384,768]{1,0:T(8,128)(2,1)}, bf16[384,768]{1,0:T(8,128)(2,1)}, u32[]{:S(2)}, u32[]{:S(2)}) collective-permute-start(bf16[384,768]{1,0:T(8,128)(2,1)} %feeds_unpack.1.refs_0_), channel_id=1, source_target_pairs={{0,4},{4,0},{8,12},{12,8},{16,20},{20,16},{24,28},{28,24},{1,5},{5... | collective-permute-start | bytes 1769480 | tf_op jit(solution)/shard_map/ppermute | solution.py:36
  84.9 15.4 %collective-permute-start.19 = (bf16[2,3,192,192]{3,2,1,0:T(8,128)(2,1)}, bf16[2,3,192,192]{3,2,1,0:T(8,128)(2,1)}, u32[]{:S(2)}, u32[]{:S(2)}) collective-permute-start(bf16[2,3,192,192]{3,2,1,0:T(8,128)(2,1)} %get-tuple-element.361), channel_id=1, source_target_pairs={{0,2},{1,3},{2,0},{3,1},{4,6},{5,7},{6,4},{7,5},{8,10},{9,11},{10,... | collective-permute-start | bytes 1327112 | tf_op jit(solution)/shard_map/ppermute | solution.py:31
  85.9 14.4 %collective-permute-start.21 = (bf16[3,192,192]{2,1,0:T(8,128)(2,1)}, bf16[3,192,192]{2,1,0:T(8,128)(2,1)}, u32[]{:S(2)}, u32[]{:S(2)}) collective-permute-start(bf16[3,192,192]{2,1,0:T(8,128)(2,1)} %get-tuple-element.349), channel_id=1, source_target_pairs={{0,1},{1,0},{2,3},{3,2},{4,5},{5,4},{6,7},{7,6},{8,9},{9,8},{10,11... | collective-permute-start | bytes 663560 | tf_op jit(solution)/shard_map/ppermute | solution.py:31
  86.5 19.8 %collective-permute-start.20 = (bf16[384,768]{1,0:T(8,128)(2,1)}, bf16[384,768]{1,0:T(8,128)(2,1)}, u32[]{:S(2)}, u32[]{:S(2)}) collective-permute-start(bf16[384,768]{1,0:T(8,128)(2,1)} %collective-permute-done.11.refs_2_), channel_id=1, source_target_pairs={{0,4},{4,0},{8,12},{12,8},{16,20},{20,16},{24,28},{28,24},{1,5},{5... | collective-permute-start | bytes 1769480 | tf_op jit(solution)/shard_map/ppermute | solution.py:36
  88.0 17.7 %collective-permute-start.18 = (bf16[384,768]{1,0:T(8,128)(2,1)}, bf16[384,768]{1,0:T(8,128)(2,1)}, u32[]{:S(2)}, u32[]{:S(2)}) collective-permute-start(bf16[384,768]{1,0:T(8,128)(2,1)} %collective-permute-done.11.refs_2_), channel_id=1, source_target_pairs={{0,8},{4,12},{8,16},{12,20},{16,24},{20,28},{24,0},{28,4},{1,9},{5... | collective-permute-start | bytes 1769480 | tf_op jit(solution)/shard_map/ppermute | solution.py:65
  105.8 25.3 %collective-permute-start.31 = (bf16[384,768]{1,0:T(8,128)(2,1)}, bf16[384,768]{1,0:T(8,128)(2,1)}, u32[]{:S(2)}, u32[]{:S(2)}) collective-permute-start(bf16[384,768]{1,0:T(8,128)(2,1)} %collective-permute-done.18.refs_4_), channel_id=1, source_target_pairs={{0,4},{4,0},{8,12},{12,8},{16,20},{20,16},{24,28},{28,24},{1,5},{5... | collective-permute-start | bytes 1769480 | tf_op jit(solution)/shard_map/ppermute | solution.py:36
  106.3 16.7 %collective-permute-start.24 = (bf16[384,768]{1,0:T(8,128)(2,1)}, bf16[384,768]{1,0:T(8,128)(2,1)}, u32[]{:S(2)}, u32[]{:S(2)}) collective-permute-start(bf16[384,768]{1,0:T(8,128)(2,1)} %collective-permute-done.18.refs_4_), channel_id=1, source_target_pairs={{0,8},{4,12},{8,16},{12,20},{16,24},{20,28},{24,0},{28,4},{1,9},{5... | collective-permute-start | bytes 1769480 | tf_op jit(solution)/shard_map/ppermute | solution.py:65
  117.0 11.3 %collective-permute-start.26 = (bf16[256,768]{1,0:T(8,128)(2,1)}, bf16[256,768]{1,0:T(8,128)(2,1)}, u32[]{:S(2)}, u32[]{:S(2)}) collective-permute-start(bf16[256,768]{1,0:T(8,128)(2,1)} %add_convert_fusion.4), channel_id=1, source_target_pairs={{0,2},{1,3},{2,0},{3,1},{4,6},{5,7},{6,4},{7,5},{8,10},{9,11},{10,... | collective-permute-start | bytes 1179656 | tf_op jit(solution)/shard_map/ppermute | solution.py:31
  131.0 16.1 %collective-permute-start.32 = (bf16[384,768]{1,0:T(8,128)(2,1)}, bf16[384,768]{1,0:T(8,128)(2,1)}, u32[]{:S(2)}, u32[]{:S(2)}) collective-permute-start(bf16[384,768]{1,0:T(8,128)(2,1)} %collective-permute-done.24.refs_0_), channel_id=1, source_target_pairs={{0,4},{4,0},{8,12},{12,8},{16,20},{20,16},{24,28},{28,24},{1,5},{5... | collective-permute-start | bytes 1769480 | tf_op jit(solution)/shard_map/ppermute | solution.py:36
  132.6 11.5 %collective-permute-start.27 = (bf16[256,768]{1,0:T(8,128)(2,1)}, bf16[256,768]{1,0:T(8,128)(2,1)}, u32[]{:S(2)}, u32[]{:S(2)}) collective-permute-start(bf16[256,768]{1,0:T(8,128)(2,1)} %get-tuple-element.394.x0.refs_0_), channel_id=1, source_target_pairs={{0,2},{1,3},{2,0},{3,1},{4,6},{5,7},{6,4},{7,5},{8,10},{9,11},{10,... | collective-permute-start | bytes 1179656 | tf_op jit(solution)/shard_map/ppermute | solution.py:31
  133.1 11.0 %collective-permute-start.29 = (bf16[256,768]{1,0:T(8,128)(2,1)}, bf16[256,768]{1,0:T(8,128)(2,1)}, u32[]{:S(2)}, u32[]{:S(2)}) collective-permute-start(bf16[256,768]{1,0:T(8,128)(2,1)} %get-tuple-element.394.x0.refs_0_), channel_id=1, source_target_pairs={{0,1},{1,0},{2,3},{3,2},{4,5},{5,4},{6,7},{7,6},{8,9},{9,8},{10,11... | collective-permute-start | bytes 1179656 | tf_op jit(solution)/shard_map/ppermute | solution.py:31
  154.1 9.8 %collective-permute-start.34 = (bf16[128,768]{1,0:T(8,128)(2,1)}, bf16[128,768]{1,0:T(8,128)(2,1)}, u32[]{:S(2)}, u32[]{:S(2)}) collective-permute-start(bf16[128,768]{1,0:T(8,128)(2,1)} %get-tuple-element.383), channel_id=1, source_target_pairs={{0,1},{1,0},{2,3},{3,2},{4,5},{5,4},{6,7},{7,6},{8,9},{9,8},{10,11... | collective-permute-start | bytes 589832 | tf_op jit(solution)/shard_map/ppermute | solution.py:31
  158.2 12.0 %collective-permute-start.37 = (bf16[256,768]{1,0:T(8,128)(2,1)}, bf16[256,768]{1,0:T(8,128)(2,1)}, u32[]{:S(2)}, u32[]{:S(2)}) collective-permute-start(bf16[256,768]{1,0:T(8,128)(2,1)} %add_convert_fusion.3), channel_id=1, source_target_pairs={{0,2},{1,3},{2,0},{3,1},{4,6},{5,7},{6,4},{7,5},{8,10},{9,11},{10,... | collective-permute-start | bytes 1179656 | tf_op jit(solution)/shard_map/ppermute | solution.py:31
  173.0 12.1 %collective-permute-start.42 = (bf16[256,768]{1,0:T(8,128)(2,1)}, bf16[256,768]{1,0:T(8,128)(2,1)S(1)}, u32[]{:S(2)}, u32[]{:S(2)}) collective-permute-start(bf16[256,768]{1,0:T(8,128)(2,1)} %get-tuple-element.402.refs_5_.refs_4_), channel_id=1, source_target_pairs={{0,2},{1,3},{2,0},{3,1},{4,6},{5,7},{6,4},{7,5},{8,10},{9,11},{10,... | collective-permute-start | bytes 1179656 | tf_op jit(solution)/shard_map/ppermute | solution.py:31
  174.9 10.3 %collective-permute-start.38 = (bf16[128,768]{1,0:T(8,128)(2,1)S(1)}, bf16[128,768]{1,0:T(8,128)(2,1)S(1)}, u32[]{:S(2)}, u32[]{:S(2)}) collective-permute-start(bf16[128,768]{1,0:T(8,128)(2,1)S(1)} %copy-done.26), channel_id=1, source_target_pairs={{0,1},{1,0},{2,3},{3,2},{4,5},{5,4},{6,7},{7,6},{8,9},{9,8},{10,11... | collective-permute-start | bytes 589832 | tf_op jit(solution)/shard_map/ppermute | solution.py:31
  175.1 13.9 %collective-permute-start.39 = (bf16[128,768]{1,0:T(8,128)(2,1)S(1)}, bf16[128,768]{1,0:T(8,128)(2,1)S(1)}, u32[]{:S(2)}, u32[]{:S(2)}) collective-permute-start(bf16[128,768]{1,0:T(8,128)(2,1)S(1)} %copy-done.26), channel_id=1, source_target_pairs={{0,2},{1,3},{2,0},{3,1},{4,6},{5,7},{6,4},{7,5},{8,10},{9,11},{10,... | collective-permute-start | bytes 589832 | tf_op jit(solution)/shard_map/ppermute | solution.py:31
  234.1 10.9 %collective-permute-start.51 = (bf16[128,768]{1,0:T(8,128)(2,1)}, bf16[128,768]{1,0:T(8,128)(2,1)}, u32[]{:S(2)}, u32[]{:S(2)}) collective-permute-start(bf16[128,768]{1,0:T(8,128)(2,1)} %get-tuple-element.431), channel_id=1, source_target_pairs={{0,1},{1,0},{2,3},{3,2},{4,5},{5,4},{6,7},{7,6},{8,9},{9,8},{10,11... | collective-permute-start | bytes 589832 | tf_op jit(solution)/shard_map/ppermute | solution.py:31
  260.0 11.9 %collective-permute-start.58 = (bf16[128,768]{1,0:T(8,128)(2,1)}, bf16[128,768]{1,0:T(8,128)(2,1)}, u32[]{:S(2)}, u32[]{:S(2)}) collective-permute-start(bf16[128,768]{1,0:T(8,128)(2,1)} %add_convert_fusion.8), channel_id=1, source_target_pairs={{0,2},{1,3},{2,0},{3,1},{4,6},{5,7},{6,4},{7,5},{8,10},{9,11},{10,... | collective-permute-start | bytes 589832 | tf_op jit(solution)/shard_map/ppermute | solution.py:31
  261.0 11.0 %collective-permute-start.57 = (bf16[128,768]{1,0:T(8,128)(2,1)}, bf16[128,768]{1,0:T(8,128)(2,1)}, u32[]{:S(2)}, u32[]{:S(2)}) collective-permute-start(bf16[128,768]{1,0:T(8,128)(2,1)} %get-tuple-element.454), channel_id=1, source_target_pairs={{0,1},{1,0},{2,3},{3,2},{4,5},{5,4},{6,7},{7,6},{8,9},{9,8},{10,11... | collective-permute-start | bytes 589832 | tf_op jit(solution)/shard_map/ppermute | solution.py:31
  261.2 10.8 %collective-permute-start.59 = (bf16[2,1,192,192]{3,2,1,0:T(8,128)(2,1)}, bf16[2,1,192,192]{3,2,1,0:T(8,128)(2,1)}, u32[]{:S(2)}, u32[]{:S(2)}) collective-permute-start(bf16[2,1,192,192]{3,2,1,0:T(8,128)(2,1)} %get-tuple-element.464), channel_id=1, source_target_pairs={{0,2},{1,3},{2,0},{3,1},{4,6},{5,7},{6,4},{7,5},{8,10},{9,11},{10,... | collective-permute-start | bytes 442376 | tf_op jit(solution)/shard_map/ppermute | solution.py:31
  272.5 29.1 %collective-permute-start.69 = (bf16[2,384,768]{2,1,0:T(8,128)(2,1)}, bf16[2,384,768]{2,1,0:T(8,128)(2,1)}, u32[]{:S(2)}, u32[]{:S(2)}) collective-permute-start(bf16[2,384,768]{2,1,0:T(8,128)(2,1)} %get-tuple-element.443), channel_id=1, source_target_pairs={{0,4},{4,0},{8,12},{12,8},{16,20},{20,16},{24,28},{28,24},{1,5},{5... | collective-permute-start | bytes 3538952 | tf_op jit(solution)/shard_map/ppermute | solution.py:36
  276.4 11.5 %collective-permute-start.64 = (bf16[256,768]{1,0:T(8,128)(2,1)}, bf16[256,768]{1,0:T(8,128)(2,1)}, u32[]{:S(2)}, u32[]{:S(2)}) collective-permute-start(bf16[256,768]{1,0:T(8,128)(2,1)} %add_convert_fusion.2), channel_id=1, source_target_pairs={{0,2},{1,3},{2,0},{3,1},{4,6},{5,7},{6,4},{7,5},{8,10},{9,11},{10,... | collective-permute-start | bytes 1179656 | tf_op jit(solution)/shard_map/ppermute | solution.py:31
  283.9 9.5 %collective-permute-start.68 = (bf16[128,768]{1,0:T(8,128)(2,1)}, bf16[128,768]{1,0:T(8,128)(2,1)}, u32[]{:S(2)}, u32[]{:S(2)}) collective-permute-start(bf16[128,768]{1,0:T(8,128)(2,1)} %get-tuple-element.484), channel_id=1, source_target_pairs={{0,1},{1,0},{2,3},{3,2},{4,5},{5,4},{6,7},{7,6},{8,9},{9,8},{10,11... | collective-permute-start | bytes 589832 | tf_op jit(solution)/shard_map/ppermute | solution.py:31
  290.9 10.8 %collective-permute-start.65 = (bf16[256,768]{1,0:T(8,128)(2,1)}, bf16[256,768]{1,0:T(8,128)(2,1)S(1)}, u32[]{:S(2)}, u32[]{:S(2)}) collective-permute-start(bf16[256,768]{1,0:T(8,128)(2,1)} %get-tuple-element.479.d0.refs_4_), channel_id=1, source_target_pairs={{0,1},{1,0},{2,3},{3,2},{4,5},{5,4},{6,7},{7,6},{8,9},{9,8},{10,11... | collective-permute-start | bytes 1179656 | tf_op jit(solution)/shard_map/ppermute | solution.py:31
  290.9 11.8 %collective-permute-start.66 = (bf16[256,768]{1,0:T(8,128)(2,1)}, bf16[256,768]{1,0:T(8,128)(2,1)}, u32[]{:S(2)}, u32[]{:S(2)}) collective-permute-start(bf16[256,768]{1,0:T(8,128)(2,1)} %get-tuple-element.479.d0.refs_4_), channel_id=1, source_target_pairs={{0,2},{1,3},{2,0},{3,1},{4,6},{5,7},{6,4},{7,5},{8,10},{9,11},{10,... | collective-permute-start | bytes 1179656 | tf_op jit(solution)/shard_map/ppermute | solution.py:31
  291.9 18.4 %collective-permute-start.70 = (bf16[1,192,1152]{2,1,0:T(8,128)(2,1)}, bf16[1,192,1152]{2,1,0:T(8,128)(2,1)}, u32[]{:S(2)}, u32[]{:S(2)}) collective-permute-start(bf16[1,192,1152]{2,1,0:T(8,128)(2,1)} %get-tuple-element.474), channel_id=1, source_target_pairs={{0,4},{4,0},{8,12},{12,8},{16,20},{20,16},{24,28},{28,24},{1,5},{5... | collective-permute-start | bytes 1327112 | tf_op jit(solution)/shard_map/ppermute | solution.py:36
  316.9 12.0 %collective-permute-start.73 = (bf16[128,768]{1,0:T(8,128)(2,1)}, bf16[128,768]{1,0:T(8,128)(2,1)}, u32[]{:S(2)}, u32[]{:S(2)}) collective-permute-start(bf16[128,768]{1,0:T(8,128)(2,1)} %get-tuple-element.509), channel_id=1, source_target_pairs={{0,1},{1,0},{2,3},{3,2},{4,5},{5,4},{6,7},{7,6},{8,9},{9,8},{10,11... | collective-permute-start | bytes 589832 | tf_op jit(solution)/shard_map/ppermute | solution.py:31
  317.4 21.7 %collective-permute-start.74 = (bf16[256,768]{1,0:T(8,128)(2,1)}, bf16[256,768]{1,0:T(8,128)(2,1)}, u32[]{:S(2)}, u32[]{:S(2)}) collective-permute-start(bf16[256,768]{1,0:T(8,128)(2,1)} %get-tuple-element.490), channel_id=1, source_target_pairs={{0,1},{1,0},{2,3},{3,2},{4,5},{5,4},{6,7},{7,6},{8,9},{9,8},{10,11... | collective-permute-start | bytes 1179656 | tf_op jit(solution)/shard_map/ppermute | solution.py:31
  320.6 18.4 %collective-permute-start.75 = (bf16[256,768]{1,0:T(8,128)(2,1)}, bf16[256,768]{1,0:T(8,128)(2,1)}, u32[]{:S(2)}, u32[]{:S(2)}) collective-permute-start(bf16[256,768]{1,0:T(8,128)(2,1)} %add_convert_fusion.1), channel_id=1, source_target_pairs={{0,2},{1,3},{2,0},{3,1},{4,6},{5,7},{6,4},{7,5},{8,10},{9,11},{10,... | collective-permute-start | bytes 1179656 | tf_op jit(solution)/shard_map/ppermute | solution.py:31
  333.4 30.0 %collective-permute-start.83 = (bf16[2,384,768]{2,1,0:T(8,128)(2,1)}, bf16[2,384,768]{2,1,0:T(8,128)(2,1)}, u32[]{:S(2)}, u32[]{:S(2)}) collective-permute-start(bf16[2,384,768]{2,1,0:T(8,128)(2,1)} %get-tuple-element.506), channel_id=1, source_target_pairs={{0,4},{4,0},{8,12},{12,8},{16,20},{20,16},{24,28},{28,24},{1,5},{5... | collective-permute-start | bytes 3538952 | tf_op jit(solution)/shard_map/ppermute | solution.py:36
  342.4 11.8 %collective-permute-start.79 = (bf16[256,768]{1,0:T(8,128)(2,1)}, bf16[256,768]{1,0:T(8,128)(2,1)}, u32[]{:S(2)}, u32[]{:S(2)}) collective-permute-start(bf16[256,768]{1,0:T(8,128)(2,1)} %get-tuple-element.514.refs_0_.refs_1_), channel_id=1, source_target_pairs={{0,2},{1,3},{2,0},{3,1},{4,6},{5,7},{6,4},{7,5},{8,10},{9,11},{10,... | collective-permute-start | bytes 1179656 | tf_op jit(solution)/shard_map/ppermute | solution.py:31
  343.4 10.8 %collective-permute-start.81 = (bf16[256,768]{1,0:T(8,128)(2,1)}, bf16[256,768]{1,0:T(8,128)(2,1)}, u32[]{:S(2)}, u32[]{:S(2)}) collective-permute-start(bf16[256,768]{1,0:T(8,128)(2,1)} %get-tuple-element.514.refs_0_.refs_1_), channel_id=1, source_target_pairs={{0,1},{1,0},{2,3},{3,2},{4,5},{5,4},{6,7},{7,6},{8,9},{9,8},{10,11... | collective-permute-start | bytes 1179656 | tf_op jit(solution)/shard_map/ppermute | solution.py:31
  358.0 43.0 %collective-permute-start.91 = (bf16[128,768]{1,0:T(8,128)(2,1)}, bf16[128,768]{1,0:T(8,128)(2,1)}, u32[]{:S(2)}, u32[]{:S(2)}) collective-permute-start(bf16[128,768]{1,0:T(8,128)(2,1)} %get-tuple-element.562), channel_id=1, source_target_pairs={{0,1},{1,0},{2,3},{3,2},{4,5},{5,4},{6,7},{7,6},{8,9},{9,8},{10,11... | collective-permute-start | bytes 589832 | tf_op jit(solution)/shard_map/ppermute | solution.py:31
  365.7 19.0 %collective-permute-start.84 = (bf16[384,768]{1,0:T(8,128)(2,1)}, bf16[384,768]{1,0:T(8,128)(2,1)}, u32[]{:S(2)}, u32[]{:S(2)}) collective-permute-start(bf16[384,768]{1,0:T(8,128)(2,1)} %feed_hop_1.1), channel_id=1, source_target_pairs={{0,8},{4,12},{8,16},{12,20},{16,24},{20,28},{24,0},{28,4},{1,9},{5... | collective-permute-start | bytes 1769480 | tf_op jit(solution)/shard_map/ppermute | solution.py:65
  366.1 18.5 %collective-permute-start.85 = (bf16[128,768]{1,0:T(8,128)(2,1)}, bf16[128,768]{1,0:T(8,128)(2,1)}, u32[]{:S(2)}, u32[]{:S(2)}) collective-permute-start(bf16[128,768]{1,0:T(8,128)(2,1)} %add_convert_fusion.5), channel_id=1, source_target_pairs={{0,2},{1,3},{2,0},{3,1},{4,6},{5,7},{6,4},{7,5},{8,10},{9,11},{10,... | collective-permute-start | bytes 589832 | tf_op jit(solution)/shard_map/ppermute | solution.py:31
  367.3 16.8 %collective-permute-start.88 = (bf16[2,192,192]{2,1,0:T(8,128)(2,1)}, bf16[2,192,192]{2,1,0:T(8,128)(2,1)}, u32[]{:S(2)}, u32[]{:S(2)}) collective-permute-start(bf16[2,192,192]{2,1,0:T(8,128)(2,1)} %get-tuple-element.532), channel_id=1, source_target_pairs={{0,1},{1,0},{2,3},{3,2},{4,5},{5,4},{6,7},{7,6},{8,9},{9,8},{10,11... | collective-permute-start | bytes 442376 | tf_op jit(solution)/shard_map/ppermute | solution.py:31
  367.5 16.7 %collective-permute-start.86 = (bf16[2,2,192,192]{3,2,1,0:T(8,128)(2,1)}, bf16[2,2,192,192]{3,2,1,0:T(8,128)(2,1)}, u32[]{:S(2)}, u32[]{:S(2)}) collective-permute-start(bf16[2,2,192,192]{3,2,1,0:T(8,128)(2,1)} %get-tuple-element.545), channel_id=1, source_target_pairs={{0,2},{1,3},{2,0},{3,1},{4,6},{5,7},{6,4},{7,5},{8,10},{9,11},{10,... | collective-permute-start | bytes 884744 | tf_op jit(solution)/shard_map/ppermute | solution.py:31
  384.1 14.0 %collective-permute-start.90 = (bf16[256,768]{1,0:T(8,128)(2,1)}, bf16[256,768]{1,0:T(8,128)(2,1)}, u32[]{:S(2)}, u32[]{:S(2)}) collective-permute-start(bf16[256,768]{1,0:T(8,128)(2,1)} %get-tuple-element.544), channel_id=1, source_target_pairs={{0,1},{1,0},{2,3},{3,2},{4,5},{5,4},{6,7},{7,6},{8,9},{9,8},{10,11... | collective-permute-start | bytes 1179656 | tf_op jit(solution)/shard_map/ppermute | solution.py:31
  384.2 10.0 %collective-permute-start.89 = (bf16[2,2,192,192]{3,2,1,0:T(8,128)(2,1)}, bf16[2,2,192,192]{3,2,1,0:T(8,128)(2,1)}, u32[]{:S(2)}, u32[]{:S(2)}) collective-permute-start(bf16[2,2,192,192]{3,2,1,0:T(8,128)(2,1)} %collective-permute-done.86.refs_2_), channel_id=1, source_target_pairs={{0,1},{1,0},{2,3},{3,2},{4,5},{5,4},{6,7},{7,6},{8,9},{9,8},{10,11... | collective-permute-start | bytes 884744 | tf_op jit(solution)/shard_map/ppermute | solution.py:31
  388.6 30.6 %collective-permute-start.94 = (bf16[1,192,1152]{2,1,0:T(8,128)(2,1)}, bf16[1,192,1152]{2,1,0:T(8,128)(2,1)}, u32[]{:S(2)}, u32[]{:S(2)}) collective-permute-start(bf16[1,192,1152]{2,1,0:T(8,128)(2,1)} %get-tuple-element.549), channel_id=1, source_target_pairs={{0,4},{4,0},{8,12},{12,8},{16,20},{20,16},{24,28},{28,24},{1,5},{5... | collective-permute-start | bytes 1327112 | tf_op jit(solution)/shard_map/ppermute | solution.py:36
  393.4 17.4 %collective-permute-start.87 = (bf16[384,768]{1,0:T(8,128)(2,1)}, bf16[384,768]{1,0:T(8,128)(2,1)}, u32[]{:S(2)}, u32[]{:S(2)}) collective-permute-start(bf16[384,768]{1,0:T(8,128)(2,1)} %feed_hop_2.1), channel_id=1, source_target_pairs={{0,8},{4,12},{8,16},{12,20},{16,24},{20,28},{24,0},{28,4},{1,9},{5... | collective-permute-start | bytes 1769480 | tf_op jit(solution)/shard_map/ppermute | solution.py:65
  397.7 22.3 %collective-permute-start.95 = (bf16[2,192,1152]{2,1,0:T(8,128)(2,1)}, bf16[2,192,1152]{2,1,0:T(8,128)(2,1)}, u32[]{:S(2)}, u32[]{:S(2)}) collective-permute-start(bf16[2,192,1152]{2,1,0:T(8,128)(2,1)} %get-tuple-element.558), channel_id=1, source_target_pairs={{0,4},{4,0},{8,12},{12,8},{16,20},{20,16},{24,28},{28,24},{1,5},{5... | collective-permute-start | bytes 2654216 | tf_op jit(solution)/shard_map/ppermute | solution.py:36
  400.0 14.5 %collective-permute-start.93 = (bf16[256,768]{1,0:T(8,128)(2,1)}, bf16[256,768]{1,0:T(8,128)(2,1)}, u32[]{:S(2)}, u32[]{:S(2)}) collective-permute-start(bf16[256,768]{1,0:T(8,128)(2,1)} %add_convert_fusion), channel_id=1, source_target_pairs={{0,2},{1,3},{2,0},{3,1},{4,6},{5,7},{6,4},{7,5},{8,10},{9,11},{10,... | collective-permute-start | bytes 1179656 | tf_op jit(solution)/shard_map/ppermute | solution.py:31
  401.0 13.4 %collective-permute-start.92 = (bf16[256,768]{1,0:T(8,128)(2,1)}, bf16[256,768]{1,0:T(8,128)(2,1)}, u32[]{:S(2)}, u32[]{:S(2)}) collective-permute-start(bf16[256,768]{1,0:T(8,128)(2,1)} %get-tuple-element.568), channel_id=1, source_target_pairs={{0,1},{1,0},{2,3},{3,2},{4,5},{5,4},{6,7},{7,6},{8,9},{9,8},{10,11... | collective-permute-start | bytes 1179656 | tf_op jit(solution)/shard_map/ppermute | solution.py:31
  414.2 18.4 %collective-permute-start.97 = (bf16[384,768]{1,0:T(8,128)(2,1)}, bf16[384,768]{1,0:T(8,128)(2,1)}, u32[]{:S(2)}, u32[]{:S(2)}) collective-permute-start(bf16[384,768]{1,0:T(8,128)(2,1)} %feed_hop_3.1), channel_id=1, source_target_pairs={{0,8},{4,12},{8,16},{12,20},{16,24},{20,28},{24,0},{28,4},{1,9},{5... | collective-permute-start | bytes 1769480 | tf_op jit(solution)/shard_map/ppermute | solution.py:65
  422.8 18.3 %collective-permute-start.96 = (bf16[208,1152]{1,0:T(8,128)(2,1)}, bf16[208,1152]{1,0:T(8,128)(2,1)}, u32[]{:S(2)}, u32[]{:S(2)}) collective-permute-start(bf16[208,1152]{1,0:T(8,128)(2,1)} %attn_hop_1.1), channel_id=1, source_target_pairs={{0,8},{4,12},{8,16},{12,20},{16,24},{20,28},{24,0},{28,4},{1,9},{5... | collective-permute-start | bytes 1437704 | tf_op jit(solution)/shard_map/ppermute | solution.py:65
  438.4 22.5 %collective-permute-start.100 = (bf16[96,512]{1,0:T(8,128)(2,1)}, bf16[96,512]{1,0:T(8,128)(2,1)}, u32[]{:S(2)}, u32[]{:S(2)}) collective-permute-start(bf16[96,512]{1,0:T(8,128)(2,1)} %get-tuple-element.584), channel_id=1, source_target_pairs={{0,1},{1,0},{2,3},{3,2},{4,5},{5,4},{6,7},{7,6},{8,9},{9,8},{10,11... | collective-permute-start | bytes 294920 | tf_op jit(solution)/shard_map/ppermute | solution.py:31
  438.4 22.5 %collective-permute-start.101 = (bf16[2,96,512]{2,1,0:T(8,128)(2,1)}, bf16[2,96,512]{2,1,0:T(8,128)(2,1)}, u32[]{:S(2)}, u32[]{:S(2)}) collective-permute-start(bf16[2,96,512]{2,1,0:T(8,128)(2,1)} %get-tuple-element.592), channel_id=1, source_target_pairs={{0,2},{1,3},{2,0},{3,1},{4,6},{5,7},{6,4},{7,5},{8,10},{9,11},{10,... | collective-permute-start | bytes 589832 | tf_op jit(solution)/shard_map/ppermute | solution.py:31
  444.2 13.6 %collective-permute-start.98 = (bf16[208,1152]{1,0:T(8,128)(2,1)}, bf16[208,1152]{1,0:T(8,128)(2,1)}, u32[]{:S(2)}, u32[]{:S(2)}) collective-permute-start(bf16[208,1152]{1,0:T(8,128)(2,1)} %attn_hop_2.1), channel_id=1, source_target_pairs={{0,8},{4,12},{8,16},{12,20},{16,24},{20,28},{24,0},{28,4},{1,9},{5... | collective-permute-start | bytes 1437704 | tf_op jit(solution)/shard_map/ppermute | solution.py:65
  461.0 15.5 %collective-permute-start.99 = (bf16[208,1152]{1,0:T(8,128)(2,1)}, bf16[208,1152]{1,0:T(8,128)(2,1)}, u32[]{:S(2)}, u32[]{:S(2)}) collective-permute-start(bf16[208,1152]{1,0:T(8,128)(2,1)} %attn_hop_3.1), channel_id=1, source_target_pairs={{0,8},{4,12},{8,16},{12,20},{16,24},{20,28},{24,0},{28,4},{1,9},{5... | collective-permute-start | bytes 1437704 | tf_op jit(solution)/shard_map/ppermute | solution.py:65
  482.1 10.3 %collective-permute-start.104 = (bf16[2,208,288]{2,1,0:T(8,128)(2,1)}, bf16[2,208,288]{2,1,0:T(8,128)(2,1)}, u32[]{:S(2)}, u32[]{:S(2)}) collective-permute-start(bf16[2,208,288]{2,1,0:T(8,128)(2,1)} %get-tuple-element.600), channel_id=1, source_target_pairs={{0,2},{1,3},{2,0},{3,1},{4,6},{5,7},{6,4},{7,5},{8,10},{9,11},{10,... | collective-permute-start | bytes 718856 | tf_op jit(solution)/shard_map/ppermute | solution.py:31
  (93 other events, 515.3 us)

commit v3 on v2

--- a/solution.py
+++ b/solution.py
@@ -597,7 +597,7 @@
 def attend_back(meta, dz, qt, attn_t, out_w, group, saved, q_rows, k_rows, causal, cross):
     q, k, v, logs_near, logs_far = saved
     dc = q.shape[1]
-    tile = min(512, 4 * q_rows)
+    tile = min(1024, 4 * q_rows)
 
     def four(rows):
         return [((rows, D), F32), ((rows, D), BF16), ((rows, D), BF16), ((rows, D), BF16)]
@@ -1374,12 +1374,13 @@
     c_enc = seq_swap(sn, 1)
     dec_mid, norm_d = close(now(kn), c_self, x_self, dec_in, gain[4], "close_self")
     mark(norm_d)
+    rows_d = gather_blocks(norm_d)
     enc_out, norm_e = close(now(kn_enc), c_enc, x_enc, enc_mid, gain[2], "close_enc_feed")
     mark(norm_e)
     rows_e = gather_blocks(norm_e)
+    mark([norm_e, rows_d[2]])
     q0t, q1t = now(q0).T, now(q1).T
     mark(q1t)
-    rows_d = gather_blocks(now(norm_d))
     q2, k2, v2, logs_far2, mixed_far2, kf, sf = attend_far(
         now(enc_meta), plain(rows_d), plain(rows_e), attn_t, (out_w, 2), 2, False
     )
@@ -1545,14 +1546,13 @@
     outer_new = adam(2, outer_master, outer_first, outer_second, now(outer_grad))
     mark(outer_new[3])
     clock.step(last_ring)
-    if packed:
-        inner_grad = feed_unpack(send_rest([now(feed_got[0]), *feed_got[1:]], clock.last))
-    else:
+    if not packed:
         inner_grad = inner_part.reshape(ns, ir, cuts, orow).transpose(1, 2, 0, 3).reshape(ir, FF).astype(F32)
-    mark(inner_grad)
     (attn_sum,) = clock.finish(last_ring)
     mine = tail_pack(mark(attn_sum), ar, gr)
     mark(mine[-1])
+    if packed:
+        inner_grad = feed_unpack(send_rest([now(feed_got[0]), *feed_got[1:]]))
     inner_new = adam(1, inner_master, inner_first, inner_second, now(inner_grad))
     mark(inner_new[3])
     attn_grad, gain_kept, gain_sent = tail_unpack(mine, s, ar, gr, now, clock.last)

time: 532 us -> 529 us (level)
  transfers between devices with their start and end apart: 112 -> 112, of which waited for: 49 -> 50; matrix products, arithmetic and copies ran while one was open for 5% -> 5% of each run, Pallas kernels for 37% -> 37%
where the time goes in v3:
time: 529 us; the launch traced here: 523 us
  Pallas kernels  244 us (46%)
  waiting for transfers between devices  178 us (34%)
  starting transfers between devices  62.6 us (12%)
  other arithmetic  22.5 us (4%)
  local copies, waits for them, and re-layouts  12.7 us (2%)
    pallas_call x44, Pallas kernels, call(): pl.pallas_call(body, grid=(1,), in_specs=specs, out_specs=[whole(o) for o...  182 us
    ppermute x83, waiting for transfers between devices, seq_swap(): return lax.ppermute(x, 'seq', [(i, i ^ k) for i in range(n)])  89.8 us
    ppermute x12, waiting for transfers between devices, ring_shift(): lax.ppermute(x, 'batch', [(i, (i + 2) % nb) for i in (range(nb) if active...  57.6 us
    ppermute x83, starting transfers between devices, seq_swap(): return lax.ppermute(x, 'seq', [(i, i ^ k) for i in range(n)])  36.5 us
    ppermute x17, waiting for transfers between devices, batch_swap(): return lax.ppermute(x, 'batch', [(i, i ^ k) for i in range(n)])  30.9 us
    pallas_call x10, Pallas kernels, row_call(): pl.pallas_call(body, grid=(STEPS,), in_specs=[spec(x.shape) for x in ins]...  27 us
    pallas_call x8, Pallas kernels, hop(): pl.pallas_call(functools.partial(hop_body, step, [k.shape[0] for k, _ in...  25 us
    ppermute x17, starting transfers between devices, batch_swap(): return lax.ppermute(x, 'batch', [(i, i ^ k) for i in range(n)])  18.4 us
  transfers between devices with their start and end apart: 112, of which 50 were waited for; matrix products, arithmetic and copies ran while one was open for 5% of the time, Pallas kernels for 37%

profile of v3, /device:TPU:0, one launch (start us, length us, event | category | flops | bytes accessed | tf_op | source)
XLA Modules:
  0.0 523.1 jit_solution(12673645289914977543)
XLA Ops:
  3.4 2.9 collective-permute-start.1
  7.9 5.6 %collective-permute-done.1.refs_2_ = bf16[2,192,384]{2,1,0:T(8,128)(2,1)S(1)} collective-permute-done((bf16[2,192,384]{2,1,0:T(8,128)(2,1)}, bf16[2,192,384]{2,1,0:T(8,128)(2,1)S(1)}, u32[]{:S(2)}, u32[]{:S(2)}) %collective-permute-start.1) | collective-permute-done | bytes 294944 | tf_op jit(solution)/shard_map/ppermute | solution.py:31
  22.2 11.3 %collective-permute-done.6.refs_2_ = bf16[208,1152]{1,0:T(8,128)(2,1)S(1)} collective-permute-done((bf16[208,1152]{1,0:T(8,128)(2,1)}, bf16[208,1152]{1,0:T(8,128)(2,1)S(1)}, u32[]{:S(2)}, u32[]{:S(2)}) %collective-permute-start.6) | collective-permute-done | bytes 479264 | tf_op jit(solution)/shard_map/ppermute | solution.py:65
  41.9 6.1 %collective-permute-done.8.refs_4_ = bf16[208,1152]{1,0:T(8,128)(2,1)} collective-permute-done((bf16[208,1152]{1,0:T(8,128)(2,1)S(1)}, bf16[208,1152]{1,0:T(8,128)(2,1)}, u32[]{:S(2)}, u32[]{:S(2)}) %collective-permute-start.8) | collective-permute-done | bytes 479264 | tf_op jit(solution)/shard_map/ppermute | solution.py:65
  53.6 6.0 %collective-permute-done.16.refs_3_.d0.refs_6_ = bf16[512,768]{1,0:T(8,128)(2,1)} collective-permute-done((bf16[512,768]{1,0:T(8,128)(2,1)}, bf16[512,768]{1,0:T(8,128)(2,1)}, u32[]{:S(2)}, u32[]{:S(2)}) %collective-permute-start.16) | collective-permute-done | bytes 786464 | tf_op jit(solution)/shard_map/ppermute | solution.py:31
  66.7 10.0 %collective-permute-done.13.refs_7_ = bf16[208,1152]{1,0:T(8,128)(2,1)} collective-permute-done((bf16[208,1152]{1,0:T(8,128)(2,1)}, bf16[208,1152]{1,0:T(8,128)(2,1)}, u32[]{:S(2)}, u32[]{:S(2)}) %collective-permute-start.13) | collective-permute-done | bytes 479264 | tf_op jit(solution)/shard_map/ppermute | solution.py:36
  76.7 4.1 gather_attn_0.1.refs_0_.refs_1_.refs_2_.refs_6_.refs_7_.refs_8_.refs_9_.refs_10_.refs_11_.refs_12_.refs_13_
  80.7 3.0 out_pack.1
  88.2 6.9 %attend_far_0.1 = (bf16[1024,768]{1,0:T(8,128)(2,1)}, bf16[1024,192]{1,0:T(8,128)(2,1)}, bf16[1024,192]{1,0:T(8,128)(2,1)}, bf16[1024,192]{1,0:T(8,128)(2,1)}, f...) custom-call(s32[2]{0:T(128)} %pad_add_fusion.refs_0_.meta, bf16[512,768]{1,0:T(8,128)(2,1)} %pad_maximum_fusion.refs_1_.d0.refs_4_, ...), custom_call_target="tpu_custom_call" | custom-call | flops 9999999827968 | bytes 10000000000 | tf_op jit(solution)/shard_map/attend_far_0/pallas_call | solution.py:307
  95.1 5.2 attend_near_0.1
  101.2 4.5 collective-permute-done.18.refs_4_
  118.0 5.0 attend_far_1.1
  123.0 5.3 %collective-permute-done.26.far_ref = bf16[256,768]{1,0:T(8,128)(2,1)} collective-permute-done((bf16[256,768]{1,0:T(8,128)(2,1)}, bf16[256,768]{1,0:T(8,128)(2,1)}, u32[]{:S(2)}, u32[]{:S(2)}) %collective-permute-start.26) | collective-permute-done | bytes 393248 | tf_op jit(solution)/shard_map/ppermute | solution.py:31
  133.9 3.3 attend_near_1.1
  137.2 4.1 gather_feeds_0.1
  144.1 3.0 collective-permute-done.32.refs_1_
  149.5 4.6 enc_feed_far.1
  159.2 4.7 enc_feed_near.1
  166.0 4.1 collective-permute-done.37.far_ref
  175.0 10.1 %collective-permute-done.42.refs_7_.refs_6_ = bf16[256,768]{1,0:T(8,128)(2,1)S(1)} collective-permute-done((bf16[256,768]{1,0:T(8,128)(2,1)}, bf16[256,768]{1,0:T(8,128)(2,1)S(1)}, u32[]{:S(2)}, u32[]{:S(2)}) %collective-permute-start.42) | collective-permute-done | bytes 393248 | tf_op jit(solution)/shard_map/ppermute | solution.py:31
  185.1 3.8 collective-permute-done.38.refs_3_.refs_2_
  191.9 6.2 %attend_far_2.1 = (bf16[512,192]{1,0:T(8,128)(2,1)}, bf16[1024,192]{1,0:T(8,128)(2,1)}, bf16[1024,192]{1,0:T(8,128)(2,1)}, f32[256,128]{1,0:T(8,128)}, bf16[256,...) custom-call(s32[2]{0:T(128)} %pad_add_fusion.refs_0_.meta, ...), custom_call_target="tpu_custom_call" | custom-call | flops 9999999827968 | bytes 10000000000 | tf_op jit(solution)/shard_map/attend_far_2/pallas_call | solution.py:307
  202.4 3.9 attend_near_2.1
  215.5 3.8 dec_feed_near.1
  220.8 4.5 dec_feed_back_near.1
  225.3 3.7 dec_feed_far.1
  229.0 4.5 dec_feed_back_far.1
  238.2 6.6 %dec_feed_weight.1 = (bf16[2,384,768]{2,1,0:T(8,128)(2,1)}, bf16[2,384,768]{2,1,0:T(8,128)(2,1)}) custom-call(bf16[128,768]{1,0:T(8,128)(2,1)} %get-tuple-element.419.x0.refs_0_, bf16[128,768]{1,0:T(8,128)(2,1)} %copy-done.34, bf16[128,768]{1,0:T(8,128)(2,1)} %collective-permute-done.48.x0.refs_2_, bf16[128,768]{1,0:T(8,128)(2,1)} %collective-permute-done.49.x1.refs_3_, ...), custom_call_target="tpu_custom_call" | custom-call | flops 9999999827968 | bytes 10000000000 | tf_op jit(solution)/shard_map/dec_feed_weight/pallas_call | solution.py:307
  249.0 5.9 %collective-permute-done.54.refs_2_.refs_3_ = bf16[128,768]{1,0:T(8,128)(2,1)S(1)} collective-permute-done((bf16[128,768]{1,0:T(8,128)(2,1)}, bf16[128,768]{1,0:T(8,128)(2,1)S(1)}, u32[]{:S(2)}, u32[]{:S(2)}) %collective-permute-start.54) | collective-permute-done | bytes 196640 | tf_op jit(solution)/shard_map/ppermute | solution.py:31
  262.0 9.7 %attend_back_2.1 = (bf16[512,192]{1,0:T(8,128)(2,1)}, bf16[192,1024]{1,0:T(8,128)(2,1)}, bf16[192,1024]{1,0:T(8,128)(2,1)}, f32[128,768]{1,0:T(8,128)}, bf16[128...) custom-call(s32[2]{0:T(128)} %pad_add_fusion.refs_0_.meta, ...), custom_call_target="tpu_custom_call" | custom-call | flops 9999999827968 | bytes 10000000000 | tf_op jit(solution)/shard_map/attend_back_2/pallas_call | solution.py:307
  277.4 3.9 cross_weights.1
  284.4 3.3 collective-permute-done.64.far_ref
  287.6 3.1 back_encoded.1
  294.9 6.5 %collective-permute-done.69.refs_3_ = bf16[2,384,768]{2,1,0:T(8,128)(2,1)} collective-permute-done((bf16[2,384,768]{2,1,0:T(8,128)(2,1)}, bf16[2,384,768]{2,1,0:T(8,128)(2,1)}, u32[]{:S(2)}, u32[]{:S(2)}) %collective-permute-start.69) | collective-permute-done | bytes 1179680 | tf_op jit(solution)/shard_map/ppermute | solution.py:36
  302.6 5.2 enc_feed_back_near.1
  311.1 5.1 enc_feed_back_far.1
  321.5 7.3 %enc_feed_weight.1 = (bf16[2,384,768]{2,1,0:T(8,128)(2,1)}, bf16[2,384,768]{2,1,0:T(8,128)(2,1)}) custom-call(bf16[256,768]{1,0:T(8,128)(2,1)} %get-tuple-element.393.x0.refs_0_, bf16[256,768]{1,0:T(8,128)(2,1)} %collective-permute-done.29.x1.refs_1_, bf16[256,768]{1,0:T(8,128)(2,1)} %collective-permute-done.27.x0.refs_2_, ...), custom_call_target="tpu_custom_call" | custom-call | flops 9999999827968 | bytes 10000000000 | tf_op jit(solution)/shard_map/enc_feed_weight/pallas_call | solution.py:307
  334.6 4.3 collective-permute-done.77.refs_3_.refs_8_
  338.9 3.3 back_enc_feed.1
  343.5 6.6 %attend_back_1.1 = (bf16[512,192]{1,0:T(8,128)(2,1)}, bf16[192,512]{1,0:T(8,128)(2,1)}, bf16[192,512]{1,0:T(8,128)(2,1)}, f32[128,768]{1,0:T(8,128)}, bf16[128,7...) custom-call(s32[2]{0:T(128)} %pad_add_fusion.1.refs_0_.meta, ...), custom_call_target="tpu_custom_call" | custom-call | flops 9999999827968 | bytes 10000000000 | tf_op jit(solution)/shard_map/attend_back_1/pallas_call | solution.py:307
  350.1 4.0 collective-permute-done.79.refs_2_.refs_3_
  354.1 3.3 self_weights.1
  357.9 3.8 late_out_weight.1
  368.3 14.8 %attend_back_0.1 = (bf16[1024,192]{1,0:T(8,128)(2,1)}, bf16[192,1024]{1,0:T(8,128)(2,1)}, bf16[192,1024]{1,0:T(8,128)(2,1)}, f32[256,768]{1,0:T(8,128)}, bf16[25...) custom-call(s32[2]{0:T(128)} %pad_add_fusion.refs_0_.meta, ...), custom_call_target="tpu_custom_call" | custom-call | flops 9999999827968 | bytes 10000000000 | tf_op jit(solution)/shard_map/attend_back_0/pallas_call | solution.py:307
  384.0 3.9 part_zero.1
  389.4 3.5 feed_hop_2.1
  393.4 3.4 part_middle.1
  402.7 7.4 %collective-permute-done.87.refs_4_ = bf16[384,768]{1,0:T(8,128)(2,1)} collective-permute-done((bf16[384,768]{1,0:T(8,128)(2,1)}, bf16[384,768]{1,0:T(8,128)(2,1)}, u32[]{:S(2)}, u32[]{:S(2)}) %collective-permute-start.87) | collective-permute-done | bytes 589856 | tf_op jit(solution)/shard_map/ppermute | solution.py:65
  410.1 3.3 feed_hop_3.1
  413.7 3.2 back_enc_attn.1
  421.9 3.2 collective-permute-start.96
  425.1 6.7 %collective-permute-done.97.refs_4_ = bf16[384,768]{1,0:T(8,128)(2,1)} collective-permute-done((bf16[384,768]{1,0:T(8,128)(2,1)}, bf16[384,768]{1,0:T(8,128)(2,1)}, u32[]{:S(2)}, u32[]{:S(2)}) %collective-permute-start.97) | collective-permute-done | bytes 589856 | tf_op jit(solution)/shard_map/ppermute | solution.py:65
  431.9 3.5 feed_hop_4.1.total_ref
  439.9 3.1 attn_hop_2.1
  445.7 10.2 %collective-permute-done.98.refs_6_ = bf16[208,1152]{1,0:T(8,128)(2,1)} collective-permute-done((bf16[208,1152]{1,0:T(8,128)(2,1)}, bf16[208,1152]{1,0:T(8,128)(2,1)}, u32[]{:S(2)}, u32[]{:S(2)}) %collective-permute-start.98) | collective-permute-done | bytes 479264 | tf_op jit(solution)/shard_map/ppermute | solution.py:65
  455.9 3.2 attn_hop_3.1
  461.4 3.7 collective-permute-done.101.refs_2_
  465.0 6.0 %collective-permute-done.99.refs_6_ = bf16[208,1152]{1,0:T(8,128)(2,1)S(1)} collective-permute-done((bf16[208,1152]{1,0:T(8,128)(2,1)}, bf16[208,1152]{1,0:T(8,128)(2,1)S(1)}, u32[]{:S(2)}, u32[]{:S(2)}) %collective-permute-start.99) | collective-permute-done | bytes 479264 | tf_op jit(solution)/shard_map/ppermute | solution.py:65
  471.8 3.3 attn_hop_4.1.total_ref
  480.3 3.9 adam_1.1
  484.1 5.6 %collective-permute-done.104.refs_2_ = bf16[2,208,288]{2,1,0:T(8,128)(2,1)} collective-permute-done((bf16[2,208,288]{2,1,0:T(8,128)(2,1)}, bf16[2,208,288]{2,1,0:T(8,128)(2,1)}, u32[]{:S(2)}, u32[]{:S(2)}) %collective-permute-start.104) | collective-permute-done | bytes 239648 | tf_op jit(solution)/shard_map/ppermute | solution.py:31
  495.4 4.1 adam_0.1
  510.2 3.6 collective-permute-done.110
  518.8 4.1 lamb.1
  (351 shorter events, 194.6 us)
Async XLA Ops:
  3.4 10.2 %collective-permute-start.1 = (bf16[2,192,384]{2,1,0:T(8,128)(2,1)}, bf16[2,192,384]{2,1,0:T(8,128)(2,1)S(1)}, u32[]{:S(2)}, u32[]{:S(2)}) collective-permute-start(bf16[2,192,384]{2,1,0:T(8,128)(2,1)} %get-tuple-element.331), channel_id=1, source_target_pairs={{0,2},{1,3},{2,0},{3,1},{4,6},{5,7},{6,4},{7,5},{8,10},{9,11},{10,... | collective-permute-start | bytes 884744 | tf_op jit(solution)/shard_map/ppermute | solution.py:31
  18.2 15.3 %collective-permute-start.6 = (bf16[208,1152]{1,0:T(8,128)(2,1)}, bf16[208,1152]{1,0:T(8,128)(2,1)S(1)}, u32[]{:S(2)}, u32[]{:S(2)}) collective-permute-start(bf16[208,1152]{1,0:T(8,128)(2,1)} %attn_unpack.1.refs_0_), channel_id=1, source_target_pairs={{0,8},{4,12},{8,16},{12,20},{16,24},{20,28},{24,0},{28,4},{1,9},{5... | collective-permute-start | bytes 1437704 | tf_op jit(solution)/shard_map/ppermute | solution.py:65
  20.0 13.5 %collective-permute-start.7 = (bf16[208,1152]{1,0:T(8,128)(2,1)}, bf16[208,1152]{1,0:T(8,128)(2,1)S(1)}, u32[]{:S(2)}, u32[]{:S(2)}) collective-permute-start(bf16[208,1152]{1,0:T(8,128)(2,1)} %attn_unpack.1.refs_0_), channel_id=1, source_target_pairs={{0,4},{4,0},{8,12},{12,8},{16,20},{20,16},{24,28},{28,24},{1,5},{5... | collective-permute-start | bytes 1437704 | tf_op jit(solution)/shard_map/ppermute | solution.py:36
  33.5 14.4 %collective-permute-start.8 = (bf16[208,1152]{1,0:T(8,128)(2,1)S(1)}, bf16[208,1152]{1,0:T(8,128)(2,1)}, u32[]{:S(2)}, u32[]{:S(2)}) collective-permute-start(bf16[208,1152]{1,0:T(8,128)(2,1)S(1)} %collective-permute-done.6.refs_2_), channel_id=1, source_target_pairs={{0,8},{4,12},{8,16},{12,20},{16,24},{20,28},{24,0},{28,4},{1,9},{5... | collective-permute-start | bytes 1437704 | tf_op jit(solution)/shard_map/ppermute | solution.py:65
  34.5 13.4 %collective-permute-start.9 = (bf16[208,1152]{1,0:T(8,128)(2,1)S(1)}, bf16[208,1152]{1,0:T(8,128)(2,1)S(1)}, u32[]{:S(2)}, u32[]{:S(2)}) collective-permute-start(bf16[208,1152]{1,0:T(8,128)(2,1)S(1)} %collective-permute-done.6.refs_2_), channel_id=1, source_target_pairs={{0,4},{4,0},{8,12},{12,8},{16,20},{20,16},{24,28},{28,24},{1,5},{5... | collective-permute-start | bytes 1437704 | tf_op jit(solution)/shard_map/ppermute | solution.py:36
  39.3 14.3 %collective-permute-start.15 = (bf16[512,768]{1,0:T(8,128)(2,1)}, bf16[512,768]{1,0:T(8,128)(2,1)}, u32[]{:S(2)}, u32[]{:S(2)}) collective-permute-start(bf16[512,768]{1,0:T(8,128)(2,1)} %pad_maximum_fusion.refs_1_.d0.refs_4_), channel_id=1, source_target_pairs={{0,1},{1,0},{2,3},{3,2},{4,5},{5,4},{6,7},{7,6},{8,9},{9,8},{10,11... | collective-permute-start | bytes 2359304 | tf_op jit(solution)/shard_map/ppermute | solution.py:31
  39.3 20.3 %collective-permute-start.16 = (bf16[512,768]{1,0:T(8,128)(2,1)}, bf16[512,768]{1,0:T(8,128)(2,1)}, u32[]{:S(2)}, u32[]{:S(2)}) collective-permute-start(bf16[512,768]{1,0:T(8,128)(2,1)} %pad_maximum_fusion.refs_1_.d0.refs_4_), channel_id=1, source_target_pairs={{0,2},{1,3},{2,0},{3,1},{4,6},{5,7},{6,4},{7,5},{8,10},{9,11},{10,... | collective-permute-start | bytes 2359304 | tf_op jit(solution)/shard_map/ppermute | solution.py:31
  41.9 21.6 %collective-permute-start.5 = (bf16[2,96,512]{2,1,0:T(8,128)(2,1)}, bf16[2,96,512]{2,1,0:T(8,128)(2,1)}, u32[]{:S(2)}, u32[]{:S(2)}) collective-permute-start(bf16[2,96,512]{2,1,0:T(8,128)(2,1)} %collective-permute-done.4.refs_2_), channel_id=1, source_target_pairs={{0,1},{1,0},{2,3},{3,2},{4,5},{5,4},{6,7},{7,6},{8,9},{9,8},{10,11... | collective-permute-start | bytes 589832 | tf_op jit(solution)/shard_map/ppermute | solution.py:31
  48.7 13.7 %collective-permute-start.10 = (bf16[208,1152]{1,0:T(8,128)(2,1)}, bf16[208,1152]{1,0:T(8,128)(2,1)}, u32[]{:S(2)}, u32[]{:S(2)}) collective-permute-start(bf16[208,1152]{1,0:T(8,128)(2,1)} %collective-permute-done.8.refs_4_), channel_id=1, source_target_pairs={{0,8},{4,12},{8,16},{12,20},{16,24},{20,28},{24,0},{28,4},{1,9},{5... | collective-permute-start | bytes 1437704 | tf_op jit(solution)/shard_map/ppermute | solution.py:65
  48.7 13.7 %collective-permute-start.12 = (bf16[208,1152]{1,0:T(8,128)(2,1)}, bf16[208,1152]{1,0:T(8,128)(2,1)}, u32[]{:S(2)}, u32[]{:S(2)}) collective-permute-start(bf16[208,1152]{1,0:T(8,128)(2,1)} %collective-permute-done.8.refs_4_), channel_id=1, source_target_pairs={{0,4},{4,0},{8,12},{12,8},{16,20},{20,16},{24,28},{28,24},{1,5},{5... | collective-permute-start | bytes 1437704 | tf_op jit(solution)/shard_map/ppermute | solution.py:36
  59.6 28.6 %collective-permute-start.17 = (bf16[512,768]{1,0:T(8,128)(2,1)}, bf16[512,768]{1,0:T(8,128)(2,1)}, u32[]{:S(2)}, u32[]{:S(2)}) collective-permute-start(bf16[512,768]{1,0:T(8,128)(2,1)} %collective-permute-done.16.refs_3_.d0.refs_6_), channel_id=1, source_target_pairs={{0,1},{1,0},{2,3},{3,2},{4,5},{5,4},{6,7},{7,6},{8,9},{9,8},{10,11... | collective-permute-start | bytes 2359304 | tf_op jit(solution)/shard_map/ppermute | solution.py:31
  62.4 14.2 %collective-permute-start.13 = (bf16[208,1152]{1,0:T(8,128)(2,1)}, bf16[208,1152]{1,0:T(8,128)(2,1)}, u32[]{:S(2)}, u32[]{:S(2)}) collective-permute-start(bf16[208,1152]{1,0:T(8,128)(2,1)} %collective-permute-done.10.refs_6_), channel_id=1, source_target_pairs={{0,4},{4,0},{8,12},{12,8},{16,20},{20,16},{24,28},{28,24},{1,5},{5... | collective-permute-start | bytes 1437704 | tf_op jit(solution)/shard_map/ppermute | solution.py:36
  65.6 20.9 %collective-permute-start.11 = (bf16[384,768]{1,0:T(8,128)(2,1)}, bf16[384,768]{1,0:T(8,128)(2,1)}, u32[]{:S(2)}, u32[]{:S(2)}) collective-permute-start(bf16[384,768]{1,0:T(8,128)(2,1)} %feeds_unpack.1.refs_0_), channel_id=1, source_target_pairs={{0,8},{4,12},{8,16},{12,20},{16,24},{20,28},{24,0},{28,4},{1,9},{5... | collective-permute-start | bytes 1769480 | tf_op jit(solution)/shard_map/ppermute | solution.py:65
  65.6 22.4 %collective-permute-start.14 = (bf16[384,768]{1,0:T(8,128)(2,1)}, bf16[384,768]{1,0:T(8,128)(2,1)}, u32[]{:S(2)}, u32[]{:S(2)}) collective-permute-start(bf16[384,768]{1,0:T(8,128)(2,1)} %feeds_unpack.1.refs_0_), channel_id=1, source_target_pairs={{0,4},{4,0},{8,12},{12,8},{16,20},{20,16},{24,28},{28,24},{1,5},{5... | collective-permute-start | bytes 1769480 | tf_op jit(solution)/shard_map/ppermute | solution.py:36
  84.9 15.5 %collective-permute-start.19 = (bf16[2,3,192,192]{3,2,1,0:T(8,128)(2,1)}, bf16[2,3,192,192]{3,2,1,0:T(8,128)(2,1)}, u32[]{:S(2)}, u32[]{:S(2)}) collective-permute-start(bf16[2,3,192,192]{3,2,1,0:T(8,128)(2,1)} %get-tuple-element.360), channel_id=1, source_target_pairs={{0,2},{1,3},{2,0},{3,1},{4,6},{5,7},{6,4},{7,5},{8,10},{9,11},{10,... | collective-permute-start | bytes 1327112 | tf_op jit(solution)/shard_map/ppermute | solution.py:31
  85.9 14.5 %collective-permute-start.21 = (bf16[3,192,192]{2,1,0:T(8,128)(2,1)}, bf16[3,192,192]{2,1,0:T(8,128)(2,1)}, u32[]{:S(2)}, u32[]{:S(2)}) collective-permute-start(bf16[3,192,192]{2,1,0:T(8,128)(2,1)} %get-tuple-element.348), channel_id=1, source_target_pairs={{0,1},{1,0},{2,3},{3,2},{4,5},{5,4},{6,7},{7,6},{8,9},{9,8},{10,11... | collective-permute-start | bytes 663560 | tf_op jit(solution)/shard_map/ppermute | solution.py:31
  86.5 19.8 %collective-permute-start.20 = (bf16[384,768]{1,0:T(8,128)(2,1)}, bf16[384,768]{1,0:T(8,128)(2,1)}, u32[]{:S(2)}, u32[]{:S(2)}) collective-permute-start(bf16[384,768]{1,0:T(8,128)(2,1)} %collective-permute-done.11.refs_2_), channel_id=1, source_target_pairs={{0,4},{4,0},{8,12},{12,8},{16,20},{20,16},{24,28},{28,24},{1,5},{5... | collective-permute-start | bytes 1769480 | tf_op jit(solution)/shard_map/ppermute | solution.py:36
  88.1 17.7 %collective-permute-start.18 = (bf16[384,768]{1,0:T(8,128)(2,1)}, bf16[384,768]{1,0:T(8,128)(2,1)}, u32[]{:S(2)}, u32[]{:S(2)}) collective-permute-start(bf16[384,768]{1,0:T(8,128)(2,1)} %collective-permute-done.11.refs_2_), channel_id=1, source_target_pairs={{0,8},{4,12},{8,16},{12,20},{16,24},{20,28},{24,0},{28,4},{1,9},{5... | collective-permute-start | bytes 1769480 | tf_op jit(solution)/shard_map/ppermute | solution.py:65
  105.8 25.2 %collective-permute-start.31 = (bf16[384,768]{1,0:T(8,128)(2,1)}, bf16[384,768]{1,0:T(8,128)(2,1)}, u32[]{:S(2)}, u32[]{:S(2)}) collective-permute-start(bf16[384,768]{1,0:T(8,128)(2,1)} %collective-permute-done.18.refs_4_), channel_id=1, source_target_pairs={{0,4},{4,0},{8,12},{12,8},{16,20},{20,16},{24,28},{28,24},{1,5},{5... | collective-permute-start | bytes 1769480 | tf_op jit(solution)/shard_map/ppermute | solution.py:36
  106.3 16.7 %collective-permute-start.24 = (bf16[384,768]{1,0:T(8,128)(2,1)}, bf16[384,768]{1,0:T(8,128)(2,1)}, u32[]{:S(2)}, u32[]{:S(2)}) collective-permute-start(bf16[384,768]{1,0:T(8,128)(2,1)} %collective-permute-done.18.refs_4_), channel_id=1, source_target_pairs={{0,8},{4,12},{8,16},{12,20},{16,24},{20,28},{24,0},{28,4},{1,9},{5... | collective-permute-start | bytes 1769480 | tf_op jit(solution)/shard_map/ppermute | solution.py:65
  116.9 11.3 %collective-permute-start.26 = (bf16[256,768]{1,0:T(8,128)(2,1)}, bf16[256,768]{1,0:T(8,128)(2,1)}, u32[]{:S(2)}, u32[]{:S(2)}) collective-permute-start(bf16[256,768]{1,0:T(8,128)(2,1)} %add_convert_fusion.4), channel_id=1, source_target_pairs={{0,2},{1,3},{2,0},{3,1},{4,6},{5,7},{6,4},{7,5},{8,10},{9,11},{10,... | collective-permute-start | bytes 1179656 | tf_op jit(solution)/shard_map/ppermute | solution.py:31
  131.0 16.1 %collective-permute-start.32 = (bf16[384,768]{1,0:T(8,128)(2,1)}, bf16[384,768]{1,0:T(8,128)(2,1)}, u32[]{:S(2)}, u32[]{:S(2)}) collective-permute-start(bf16[384,768]{1,0:T(8,128)(2,1)} %collective-permute-done.24.refs_0_), channel_id=1, source_target_pairs={{0,4},{4,0},{8,12},{12,8},{16,20},{20,16},{24,28},{28,24},{1,5},{5... | collective-permute-start | bytes 1769480 | tf_op jit(solution)/shard_map/ppermute | solution.py:36
  132.6 11.5 %collective-permute-start.27 = (bf16[256,768]{1,0:T(8,128)(2,1)}, bf16[256,768]{1,0:T(8,128)(2,1)}, u32[]{:S(2)}, u32[]{:S(2)}) collective-permute-start(bf16[256,768]{1,0:T(8,128)(2,1)} %get-tuple-element.393.x0.refs_0_), channel_id=1, source_target_pairs={{0,2},{1,3},{2,0},{3,1},{4,6},{5,7},{6,4},{7,5},{8,10},{9,11},{10,... | collective-permute-start | bytes 1179656 | tf_op jit(solution)/shard_map/ppermute | solution.py:31
  133.1 11.0 %collective-permute-start.29 = (bf16[256,768]{1,0:T(8,128)(2,1)}, bf16[256,768]{1,0:T(8,128)(2,1)}, u32[]{:S(2)}, u32[]{:S(2)}) collective-permute-start(bf16[256,768]{1,0:T(8,128)(2,1)} %get-tuple-element.393.x0.refs_0_), channel_id=1, source_target_pairs={{0,1},{1,0},{2,3},{3,2},{4,5},{5,4},{6,7},{7,6},{8,9},{9,8},{10,11... | collective-permute-start | bytes 1179656 | tf_op jit(solution)/shard_map/ppermute | solution.py:31
  154.1 9.8 %collective-permute-start.34 = (bf16[128,768]{1,0:T(8,128)(2,1)}, bf16[128,768]{1,0:T(8,128)(2,1)}, u32[]{:S(2)}, u32[]{:S(2)}) collective-permute-start(bf16[128,768]{1,0:T(8,128)(2,1)} %get-tuple-element.382), channel_id=1, source_target_pairs={{0,1},{1,0},{2,3},{3,2},{4,5},{5,4},{6,7},{7,6},{8,9},{9,8},{10,11... | collective-permute-start | bytes 589832 | tf_op jit(solution)/shard_map/ppermute | solution.py:31
  154.6 9.3 %collective-permute-start.35 = (bf16[128,768]{1,0:T(8,128)(2,1)}, bf16[128,768]{1,0:T(8,128)(2,1)}, u32[]{:S(2)}, u32[]{:S(2)}) collective-permute-start(bf16[128,768]{1,0:T(8,128)(2,1)} %add_convert_fusion.11), channel_id=1, source_target_pairs={{0,2},{1,3},{2,0},{3,1},{4,6},{5,7},{6,4},{7,5},{8,10},{9,11},{10,... | collective-permute-start | bytes 589832 | tf_op jit(solution)/shard_map/ppermute | solution.py:31
  158.1 12.0 %collective-permute-start.37 = (bf16[256,768]{1,0:T(8,128)(2,1)}, bf16[256,768]{1,0:T(8,128)(2,1)}, u32[]{:S(2)}, u32[]{:S(2)}) collective-permute-start(bf16[256,768]{1,0:T(8,128)(2,1)} %add_convert_fusion.3), channel_id=1, source_target_pairs={{0,2},{1,3},{2,0},{3,1},{4,6},{5,7},{6,4},{7,5},{8,10},{9,11},{10,... | collective-permute-start | bytes 1179656 | tf_op jit(solution)/shard_map/ppermute | solution.py:31
  173.0 12.1 %collective-permute-start.42 = (bf16[256,768]{1,0:T(8,128)(2,1)}, bf16[256,768]{1,0:T(8,128)(2,1)S(1)}, u32[]{:S(2)}, u32[]{:S(2)}) collective-permute-start(bf16[256,768]{1,0:T(8,128)(2,1)} %get-tuple-element.401.refs_5_.refs_4_), channel_id=1, source_target_pairs={{0,2},{1,3},{2,0},{3,1},{4,6},{5,7},{6,4},{7,5},{8,10},{9,11},{10,... | collective-permute-start | bytes 1179656 | tf_op jit(solution)/shard_map/ppermute | solution.py:31
  174.0 14.9 %collective-permute-start.38 = (bf16[128,768]{1,0:T(8,128)(2,1)S(1)}, bf16[128,768]{1,0:T(8,128)(2,1)S(1)}, u32[]{:S(2)}, u32[]{:S(2)}) collective-permute-start(bf16[128,768]{1,0:T(8,128)(2,1)S(1)} %copy-done.27), channel_id=1, source_target_pairs={{0,2},{1,3},{2,0},{3,1},{4,6},{5,7},{6,4},{7,5},{8,10},{9,11},{10,... | collective-permute-start | bytes 589832 | tf_op jit(solution)/shard_map/ppermute | solution.py:31
  175.0 13.9 %collective-permute-start.39 = (bf16[128,768]{1,0:T(8,128)(2,1)S(1)}, bf16[128,768]{1,0:T(8,128)(2,1)S(1)}, u32[]{:S(2)}, u32[]{:S(2)}) collective-permute-start(bf16[128,768]{1,0:T(8,128)(2,1)S(1)} %copy-done.27), channel_id=1, source_target_pairs={{0,1},{1,0},{2,3},{3,2},{4,5},{5,4},{6,7},{7,6},{8,9},{9,8},{10,11... | collective-permute-start | bytes 589832 | tf_op jit(solution)/shard_map/ppermute | solution.py:31
  234.0 10.8 %collective-permute-start.51 = (bf16[128,768]{1,0:T(8,128)(2,1)}, bf16[128,768]{1,0:T(8,128)(2,1)}, u32[]{:S(2)}, u32[]{:S(2)}) collective-permute-start(bf16[128,768]{1,0:T(8,128)(2,1)} %get-tuple-element.429), channel_id=1, source_target_pairs={{0,1},{1,0},{2,3},{3,2},{4,5},{5,4},{6,7},{7,6},{8,9},{9,8},{10,11... | collective-permute-start | bytes 589832 | tf_op jit(solution)/shard_map/ppermute | solution.py:31
  259.8 11.9 %collective-permute-start.58 = (bf16[128,768]{1,0:T(8,128)(2,1)}, bf16[128,768]{1,0:T(8,128)(2,1)}, u32[]{:S(2)}, u32[]{:S(2)}) collective-permute-start(bf16[128,768]{1,0:T(8,128)(2,1)} %add_convert_fusion.8), channel_id=1, source_target_pairs={{0,2},{1,3},{2,0},{3,1},{4,6},{5,7},{6,4},{7,5},{8,10},{9,11},{10,... | collective-permute-start | bytes 589832 | tf_op jit(solution)/shard_map/ppermute | solution.py:31
  260.8 10.9 %collective-permute-start.57 = (bf16[128,768]{1,0:T(8,128)(2,1)}, bf16[128,768]{1,0:T(8,128)(2,1)}, u32[]{:S(2)}, u32[]{:S(2)}) collective-permute-start(bf16[128,768]{1,0:T(8,128)(2,1)} %get-tuple-element.452), channel_id=1, source_target_pairs={{0,1},{1,0},{2,3},{3,2},{4,5},{5,4},{6,7},{7,6},{8,9},{9,8},{10,11... | collective-permute-start | bytes 589832 | tf_op jit(solution)/shard_map/ppermute | solution.py:31
  261.0 10.7 %collective-permute-start.59 = (bf16[2,1,192,192]{3,2,1,0:T(8,128)(2,1)}, bf16[2,1,192,192]{3,2,1,0:T(8,128)(2,1)}, u32[]{:S(2)}, u32[]{:S(2)}) collective-permute-start(bf16[2,1,192,192]{3,2,1,0:T(8,128)(2,1)} %get-tuple-element.462), channel_id=1, source_target_pairs={{0,2},{1,3},{2,0},{3,1},{4,6},{5,7},{6,4},{7,5},{8,10},{9,11},{10,... | collective-permute-start | bytes 442376 | tf_op jit(solution)/shard_map/ppermute | solution.py:31
  272.3 29.1 %collective-permute-start.69 = (bf16[2,384,768]{2,1,0:T(8,128)(2,1)}, bf16[2,384,768]{2,1,0:T(8,128)(2,1)}, u32[]{:S(2)}, u32[]{:S(2)}) collective-permute-start(bf16[2,384,768]{2,1,0:T(8,128)(2,1)} %get-tuple-element.441), channel_id=1, source_target_pairs={{0,4},{4,0},{8,12},{12,8},{16,20},{20,16},{24,28},{28,24},{1,5},{5... | collective-permute-start | bytes 3538952 | tf_op jit(solution)/shard_map/ppermute | solution.py:36
  276.2 11.5 %collective-permute-start.64 = (bf16[256,768]{1,0:T(8,128)(2,1)}, bf16[256,768]{1,0:T(8,128)(2,1)}, u32[]{:S(2)}, u32[]{:S(2)}) collective-permute-start(bf16[256,768]{1,0:T(8,128)(2,1)} %add_convert_fusion.2), channel_id=1, source_target_pairs={{0,2},{1,3},{2,0},{3,1},{4,6},{5,7},{6,4},{7,5},{8,10},{9,11},{10,... | collective-permute-start | bytes 1179656 | tf_op jit(solution)/shard_map/ppermute | solution.py:31
  283.9 9.4 %collective-permute-start.68 = (bf16[128,768]{1,0:T(8,128)(2,1)}, bf16[128,768]{1,0:T(8,128)(2,1)}, u32[]{:S(2)}, u32[]{:S(2)}) collective-permute-start(bf16[128,768]{1,0:T(8,128)(2,1)} %get-tuple-element.482), channel_id=1, source_target_pairs={{0,1},{1,0},{2,3},{3,2},{4,5},{5,4},{6,7},{7,6},{8,9},{9,8},{10,11... | collective-permute-start | bytes 589832 | tf_op jit(solution)/shard_map/ppermute | solution.py:31
  290.7 10.8 %collective-permute-start.65 = (bf16[256,768]{1,0:T(8,128)(2,1)}, bf16[256,768]{1,0:T(8,128)(2,1)S(1)}, u32[]{:S(2)}, u32[]{:S(2)}) collective-permute-start(bf16[256,768]{1,0:T(8,128)(2,1)} %get-tuple-element.477.d0.refs_4_), channel_id=1, source_target_pairs={{0,1},{1,0},{2,3},{3,2},{4,5},{5,4},{6,7},{7,6},{8,9},{9,8},{10,11... | collective-permute-start | bytes 1179656 | tf_op jit(solution)/shard_map/ppermute | solution.py:31
  290.7 11.8 %collective-permute-start.66 = (bf16[256,768]{1,0:T(8,128)(2,1)}, bf16[256,768]{1,0:T(8,128)(2,1)}, u32[]{:S(2)}, u32[]{:S(2)}) collective-permute-start(bf16[256,768]{1,0:T(8,128)(2,1)} %get-tuple-element.477.d0.refs_4_), channel_id=1, source_target_pairs={{0,2},{1,3},{2,0},{3,1},{4,6},{5,7},{6,4},{7,5},{8,10},{9,11},{10,... | collective-permute-start | bytes 1179656 | tf_op jit(solution)/shard_map/ppermute | solution.py:31
  291.7 18.4 %collective-permute-start.70 = (bf16[1,192,1152]{2,1,0:T(8,128)(2,1)}, bf16[1,192,1152]{2,1,0:T(8,128)(2,1)}, u32[]{:S(2)}, u32[]{:S(2)}) collective-permute-start(bf16[1,192,1152]{2,1,0:T(8,128)(2,1)} %get-tuple-element.472), channel_id=1, source_target_pairs={{0,4},{4,0},{8,12},{12,8},{16,20},{20,16},{24,28},{28,24},{1,5},{5... | collective-permute-start | bytes 1327112 | tf_op jit(solution)/shard_map/ppermute | solution.py:36
  316.7 12.1 %collective-permute-start.73 = (bf16[128,768]{1,0:T(8,128)(2,1)}, bf16[128,768]{1,0:T(8,128)(2,1)}, u32[]{:S(2)}, u32[]{:S(2)}) collective-permute-start(bf16[128,768]{1,0:T(8,128)(2,1)} %get-tuple-element.507), channel_id=1, source_target_pairs={{0,1},{1,0},{2,3},{3,2},{4,5},{5,4},{6,7},{7,6},{8,9},{9,8},{10,11... | collective-permute-start | bytes 589832 | tf_op jit(solution)/shard_map/ppermute | solution.py:31
  317.2 21.7 %collective-permute-start.74 = (bf16[256,768]{1,0:T(8,128)(2,1)}, bf16[256,768]{1,0:T(8,128)(2,1)}, u32[]{:S(2)}, u32[]{:S(2)}) collective-permute-start(bf16[256,768]{1,0:T(8,128)(2,1)} %get-tuple-element.488), channel_id=1, source_target_pairs={{0,1},{1,0},{2,3},{3,2},{4,5},{5,4},{6,7},{7,6},{8,9},{9,8},{10,11... | collective-permute-start | bytes 1179656 | tf_op jit(solution)/shard_map/ppermute | solution.py:31
  320.4 18.5 %collective-permute-start.75 = (bf16[256,768]{1,0:T(8,128)(2,1)}, bf16[256,768]{1,0:T(8,128)(2,1)}, u32[]{:S(2)}, u32[]{:S(2)}) collective-permute-start(bf16[256,768]{1,0:T(8,128)(2,1)} %add_convert_fusion.1), channel_id=1, source_target_pairs={{0,2},{1,3},{2,0},{3,1},{4,6},{5,7},{6,4},{7,5},{8,10},{9,11},{10,... | collective-permute-start | bytes 1179656 | tf_op jit(solution)/shard_map/ppermute | solution.py:31
  333.2 30.1 %collective-permute-start.83 = (bf16[2,384,768]{2,1,0:T(8,128)(2,1)}, bf16[2,384,768]{2,1,0:T(8,128)(2,1)}, u32[]{:S(2)}, u32[]{:S(2)}) collective-permute-start(bf16[2,384,768]{2,1,0:T(8,128)(2,1)} %get-tuple-element.504), channel_id=1, source_target_pairs={{0,4},{4,0},{8,12},{12,8},{16,20},{20,16},{24,28},{28,24},{1,5},{5... | collective-permute-start | bytes 3538952 | tf_op jit(solution)/shard_map/ppermute | solution.py:36
  342.3 11.8 %collective-permute-start.79 = (bf16[256,768]{1,0:T(8,128)(2,1)}, bf16[256,768]{1,0:T(8,128)(2,1)}, u32[]{:S(2)}, u32[]{:S(2)}) collective-permute-start(bf16[256,768]{1,0:T(8,128)(2,1)} %get-tuple-element.512.refs_0_.refs_1_), channel_id=1, source_target_pairs={{0,2},{1,3},{2,0},{3,1},{4,6},{5,7},{6,4},{7,5},{8,10},{9,11},{10,... | collective-permute-start | bytes 1179656 | tf_op jit(solution)/shard_map/ppermute | solution.py:31
  343.3 10.8 %collective-permute-start.81 = (bf16[256,768]{1,0:T(8,128)(2,1)}, bf16[256,768]{1,0:T(8,128)(2,1)}, u32[]{:S(2)}, u32[]{:S(2)}) collective-permute-start(bf16[256,768]{1,0:T(8,128)(2,1)} %get-tuple-element.512.refs_0_.refs_1_), channel_id=1, source_target_pairs={{0,1},{1,0},{2,3},{3,2},{4,5},{5,4},{6,7},{7,6},{8,9},{9,8},{10,11... | collective-permute-start | bytes 1179656 | tf_op jit(solution)/shard_map/ppermute | solution.py:31
  357.9 42.4 %collective-permute-start.91 = (bf16[128,768]{1,0:T(8,128)(2,1)}, bf16[128,768]{1,0:T(8,128)(2,1)}, u32[]{:S(2)}, u32[]{:S(2)}) collective-permute-start(bf16[128,768]{1,0:T(8,128)(2,1)} %get-tuple-element.560), channel_id=1, source_target_pairs={{0,1},{1,0},{2,3},{3,2},{4,5},{5,4},{6,7},{7,6},{8,9},{9,8},{10,11... | collective-permute-start | bytes 589832 | tf_op jit(solution)/shard_map/ppermute | solution.py:31
  365.5 18.5 %collective-permute-start.84 = (bf16[384,768]{1,0:T(8,128)(2,1)}, bf16[384,768]{1,0:T(8,128)(2,1)}, u32[]{:S(2)}, u32[]{:S(2)}) collective-permute-start(bf16[384,768]{1,0:T(8,128)(2,1)} %feed_hop_1.1), channel_id=1, source_target_pairs={{0,8},{4,12},{8,16},{12,20},{16,24},{20,28},{24,0},{28,4},{1,9},{5... | collective-permute-start | bytes 1769480 | tf_op jit(solution)/shard_map/ppermute | solution.py:65
  366.0 17.7 %collective-permute-start.85 = (bf16[128,768]{1,0:T(8,128)(2,1)}, bf16[128,768]{1,0:T(8,128)(2,1)}, u32[]{:S(2)}, u32[]{:S(2)}) collective-permute-start(bf16[128,768]{1,0:T(8,128)(2,1)} %add_convert_fusion.5), channel_id=1, source_target_pairs={{0,2},{1,3},{2,0},{3,1},{4,6},{5,7},{6,4},{7,5},{8,10},{9,11},{10,... | collective-permute-start | bytes 589832 | tf_op jit(solution)/shard_map/ppermute | solution.py:31
  367.1 16.1 %collective-permute-start.88 = (bf16[2,192,192]{2,1,0:T(8,128)(2,1)}, bf16[2,192,192]{2,1,0:T(8,128)(2,1)}, u32[]{:S(2)}, u32[]{:S(2)}) collective-permute-start(bf16[2,192,192]{2,1,0:T(8,128)(2,1)} %get-tuple-element.530), channel_id=1, source_target_pairs={{0,1},{1,0},{2,3},{3,2},{4,5},{5,4},{6,7},{7,6},{8,9},{9,8},{10,11... | collective-permute-start | bytes 442376 | tf_op jit(solution)/shard_map/ppermute | solution.py:31
  367.3 15.9 %collective-permute-start.86 = (bf16[2,2,192,192]{3,2,1,0:T(8,128)(2,1)}, bf16[2,2,192,192]{3,2,1,0:T(8,128)(2,1)}, u32[]{:S(2)}, u32[]{:S(2)}) collective-permute-start(bf16[2,2,192,192]{3,2,1,0:T(8,128)(2,1)} %get-tuple-element.543), channel_id=1, source_target_pairs={{0,2},{1,3},{2,0},{3,1},{4,6},{5,7},{6,4},{7,5},{8,10},{9,11},{10,... | collective-permute-start | bytes 884744 | tf_op jit(solution)/shard_map/ppermute | solution.py:31
  383.1 14.2 %collective-permute-start.90 = (bf16[256,768]{1,0:T(8,128)(2,1)}, bf16[256,768]{1,0:T(8,128)(2,1)}, u32[]{:S(2)}, u32[]{:S(2)}) collective-permute-start(bf16[256,768]{1,0:T(8,128)(2,1)} %get-tuple-element.542), channel_id=1, source_target_pairs={{0,1},{1,0},{2,3},{3,2},{4,5},{5,4},{6,7},{7,6},{8,9},{9,8},{10,11... | collective-permute-start | bytes 1179656 | tf_op jit(solution)/shard_map/ppermute | solution.py:31
  383.2 10.2 %collective-permute-start.89 = (bf16[2,2,192,192]{3,2,1,0:T(8,128)(2,1)}, bf16[2,2,192,192]{3,2,1,0:T(8,128)(2,1)}, u32[]{:S(2)}, u32[]{:S(2)}) collective-permute-start(bf16[2,2,192,192]{3,2,1,0:T(8,128)(2,1)} %collective-permute-done.86.refs_2_), channel_id=1, source_target_pairs={{0,1},{1,0},{2,3},{3,2},{4,5},{5,4},{6,7},{7,6},{8,9},{9,8},{10,11... | collective-permute-start | bytes 884744 | tf_op jit(solution)/shard_map/ppermute | solution.py:31
  387.9 30.5 %collective-permute-start.94 = (bf16[1,192,1152]{2,1,0:T(8,128)(2,1)}, bf16[1,192,1152]{2,1,0:T(8,128)(2,1)}, u32[]{:S(2)}, u32[]{:S(2)}) collective-permute-start(bf16[1,192,1152]{2,1,0:T(8,128)(2,1)} %get-tuple-element.547), channel_id=1, source_target_pairs={{0,4},{4,0},{8,12},{12,8},{16,20},{20,16},{24,28},{28,24},{1,5},{5... | collective-permute-start | bytes 1327112 | tf_op jit(solution)/shard_map/ppermute | solution.py:36
  393.0 17.1 %collective-permute-start.87 = (bf16[384,768]{1,0:T(8,128)(2,1)}, bf16[384,768]{1,0:T(8,128)(2,1)}, u32[]{:S(2)}, u32[]{:S(2)}) collective-permute-start(bf16[384,768]{1,0:T(8,128)(2,1)} %feed_hop_2.1), channel_id=1, source_target_pairs={{0,8},{4,12},{8,16},{12,20},{16,24},{20,28},{24,0},{28,4},{1,9},{5... | collective-permute-start | bytes 1769480 | tf_op jit(solution)/shard_map/ppermute | solution.py:65
  396.8 22.3 %collective-permute-start.95 = (bf16[2,192,1152]{2,1,0:T(8,128)(2,1)}, bf16[2,192,1152]{2,1,0:T(8,128)(2,1)}, u32[]{:S(2)}, u32[]{:S(2)}) collective-permute-start(bf16[2,192,1152]{2,1,0:T(8,128)(2,1)} %get-tuple-element.556), channel_id=1, source_target_pairs={{0,4},{4,0},{8,12},{12,8},{16,20},{20,16},{24,28},{28,24},{1,5},{5... | collective-permute-start | bytes 2654216 | tf_op jit(solution)/shard_map/ppermute | solution.py:36
  399.2 14.5 %collective-permute-start.93 = (bf16[256,768]{1,0:T(8,128)(2,1)}, bf16[256,768]{1,0:T(8,128)(2,1)}, u32[]{:S(2)}, u32[]{:S(2)}) collective-permute-start(bf16[256,768]{1,0:T(8,128)(2,1)} %add_convert_fusion), channel_id=1, source_target_pairs={{0,2},{1,3},{2,0},{3,1},{4,6},{5,7},{6,4},{7,5},{8,10},{9,11},{10,... | collective-permute-start | bytes 1179656 | tf_op jit(solution)/shard_map/ppermute | solution.py:31
  400.2 13.5 %collective-permute-start.92 = (bf16[256,768]{1,0:T(8,128)(2,1)}, bf16[256,768]{1,0:T(8,128)(2,1)}, u32[]{:S(2)}, u32[]{:S(2)}) collective-permute-start(bf16[256,768]{1,0:T(8,128)(2,1)} %get-tuple-element.566), channel_id=1, source_target_pairs={{0,1},{1,0},{2,3},{3,2},{4,5},{5,4},{6,7},{7,6},{8,9},{9,8},{10,11... | collective-permute-start | bytes 1179656 | tf_op jit(solution)/shard_map/ppermute | solution.py:31
  413.4 18.4 %collective-permute-start.97 = (bf16[384,768]{1,0:T(8,128)(2,1)}, bf16[384,768]{1,0:T(8,128)(2,1)}, u32[]{:S(2)}, u32[]{:S(2)}) collective-permute-start(bf16[384,768]{1,0:T(8,128)(2,1)} %feed_hop_3.1), channel_id=1, source_target_pairs={{0,8},{4,12},{8,16},{12,20},{16,24},{20,28},{24,0},{28,4},{1,9},{5... | collective-permute-start | bytes 1769480 | tf_op jit(solution)/shard_map/ppermute | solution.py:65
  421.9 18.0 %collective-permute-start.96 = (bf16[208,1152]{1,0:T(8,128)(2,1)}, bf16[208,1152]{1,0:T(8,128)(2,1)}, u32[]{:S(2)}, u32[]{:S(2)}) collective-permute-start(bf16[208,1152]{1,0:T(8,128)(2,1)} %attn_hop_1.1), channel_id=1, source_target_pairs={{0,8},{4,12},{8,16},{12,20},{16,24},{20,28},{24,0},{28,4},{1,9},{5... | collective-permute-start | bytes 1437704 | tf_op jit(solution)/shard_map/ppermute | solution.py:65
  443.0 12.9 %collective-permute-start.98 = (bf16[208,1152]{1,0:T(8,128)(2,1)}, bf16[208,1152]{1,0:T(8,128)(2,1)}, u32[]{:S(2)}, u32[]{:S(2)}) collective-permute-start(bf16[208,1152]{1,0:T(8,128)(2,1)} %attn_hop_2.1), channel_id=1, source_target_pairs={{0,8},{4,12},{8,16},{12,20},{16,24},{20,28},{24,0},{28,4},{1,9},{5... | collective-permute-start | bytes 1437704 | tf_op jit(solution)/shard_map/ppermute | solution.py:65
  459.1 11.9 %collective-permute-start.99 = (bf16[208,1152]{1,0:T(8,128)(2,1)}, bf16[208,1152]{1,0:T(8,128)(2,1)S(1)}, u32[]{:S(2)}, u32[]{:S(2)}) collective-permute-start(bf16[208,1152]{1,0:T(8,128)(2,1)} %attn_hop_3.1), channel_id=1, source_target_pairs={{0,8},{4,12},{8,16},{12,20},{16,24},{20,28},{24,0},{28,4},{1,9},{5... | collective-permute-start | bytes 1437704 | tf_op jit(solution)/shard_map/ppermute | solution.py:65
  465.0 12.3 %collective-permute-start.102 = (bf16[2,96,512]{2,1,0:T(8,128)(2,1)}, bf16[2,96,512]{2,1,0:T(8,128)(2,1)}, u32[]{:S(2)}, u32[]{:S(2)}) collective-permute-start(bf16[2,96,512]{2,1,0:T(8,128)(2,1)} %collective-permute-done.101.refs_2_), channel_id=1, source_target_pairs={{0,1},{1,0},{2,3},{3,2},{4,5},{5,4},{6,7},{7,6},{8,9},{9,8},{10,11... | collective-permute-start | bytes 589832 | tf_op jit(solution)/shard_map/ppermute | solution.py:31
  479.5 10.3 %collective-permute-start.104 = (bf16[2,208,288]{2,1,0:T(8,128)(2,1)}, bf16[2,208,288]{2,1,0:T(8,128)(2,1)}, u32[]{:S(2)}, u32[]{:S(2)}) collective-permute-start(bf16[2,208,288]{2,1,0:T(8,128)(2,1)} %get-tuple-element.598), channel_id=1, source_target_pairs={{0,2},{1,3},{2,0},{3,1},{4,6},{5,7},{6,4},{7,5},{8,10},{9,11},{10,... | collective-permute-start | bytes 718856 | tf_op jit(solution)/shard_map/ppermute | solution.py:31
  (96 other events, 535.0 us)

commit v4 on v3

--- a/solution.py
+++ b/solution.py
@@ -745,6 +745,38 @@
         list(dz_half) + [(gate, None), (up, None)] + feed_weights(inner_cols, outer_rows, which),
         [((2 * rows, fc), BF16), ((2 * rows, fc), BF16), ((rows, D), keep), ((rows, D), BF16)],
         12 * rows * fc * D,
+        name=name,
+    )
+
+
+def feed_both_body(rows, x0, x1, d0, d1, wg, wu, wd, hidden_ref, keep_ref, send_ref, dgate_ref, dup_ref, *backs):
+    for j, (x_ref, d_ref) in enumerate(((x0, d0), (x1, d1))):
+        at = slice(j * rows, (j + 1) * rows)
+        x = x_ref[...]
+        t, up = nn(x, wg[...]), nn(x, wu[...])
+        dh = nt(d_ref[...], wd[...])
+        square = t * t
+        inner = jnp.tanh(GELU_A * t * (1.0 + GELU_B * square))
+        act = 0.5 * t * (1.0 + inner)
+        slope = 0.5 * (1.0 + inner) + 0.5 * t * (1.0 - inner * inner) * (
+            GELU_A * (1.0 + 3.0 * GELU_B * square)
+        )
+        hidden_ref[at, :] = (act * up).astype(BF16)
+        dgate_ref[at, :] = (dh * up * slope).astype(BF16)
+        dup_ref[at, :] = (dh * act).astype(BF16)
+        out, back = (keep_ref, send_ref)[j], backs[j]
+        back[...] = (nt(dgate_ref[at, :], wg[...]) + nt(dup_ref[at, :], wu[...])).astype(back.dtype)
+        out[...] = nn(hidden_ref[at, :], wd[...]).astype(out.dtype)
+
+
+def feed_both(half, dz_half, inner_cols, outer_rows, which, keep, name):
+    rows, fc = half[0].shape[0], inner_cols.shape[1]
+    wide, tall = ((2 * rows, fc), BF16), [((rows, D), keep), ((rows, D), BF16)]
+    return call(
+        functools.partial(feed_both_body, rows),
+        plain(half) + list(dz_half) + feed_weights(inner_cols, outer_rows, which),
+        [wide] + tall + [wide, wide] + tall,
+        24 * rows * fc * D,
         name=name,
     )
 
@@ -1391,20 +1423,14 @@
     dec_late, norm_f = close(now(kn), seq_swap(tie(sn, x_dec), 1), x_dec, dec_mid, gain[5], "close_cross")
     mark(norm_f)
     rows_f = gather_blocks(norm_f)
-    dg0, du0, dh0, kn_out, sn_out = feed_forward(
-        (now(rows_f[0]), rows_f[1]), inner_cols, outer_rows, 1, F32, "dec_feed_near"
-    )
-    mark(dh0)
-    a0, b0, kn_dec, sn_dec = feed_back(
-        seed_blocks[:2], now(dg0), du0, inner_cols, outer_rows, 1, F32, "dec_feed_back_near"
+    dh0, kn_out, sn_out, a0, b0, kn_dec, sn_dec = feed_both(
+        (now(rows_f[0]), rows_f[1]), seed_blocks[:2], inner_cols, outer_rows, 1, F32, "dec_feed_near"
     )
     mark(sn_dec)
     c_dec = seq_swap(sn_dec, 1)
-    dg1, du1, dh1, kf_out, sf_out = feed_forward(
-        (now(rows_f[2]), rows_f[3]), inner_cols, outer_rows, 1, BF16, "dec_feed_far"
-    )
-    mark(dh1)
-    a1, b1, kf, sf = feed_back(seed_blocks[2:], now(dg1), du1, inner_cols, outer_rows, 1, BF16, "dec_feed_back_far")
+    dh1, kf_out, sf_out, a1, b1, kf, sf = feed_both(
+        (now(rows_f[2]), rows_f[3]), seed_blocks[2:], inner_cols, outer_rows, 1, BF16, "dec_feed_far"
+    )
 
     far = mark(far_payload(kf, sf))
     x_dec = seq_swap(far, 2)

time: 529 us -> 527 us (level)
  Pallas kernels: 244 us -> 238 us
  waiting for transfers between devices: 178 us -> 184 us
    pallas_call x44 -> x42, Pallas kernels: 182 us -> 175 us  [call(): pl.pallas_call(body, grid=(1,), in_specs=specs, out_specs=[whole(o) for o...]
    ppermute x83, waiting for transfers between devices: 89.8 us -> 95.8 us  [seq_swap(): return lax.ppermute(x, 'seq', [(i, i ^ k) for i in range(n)])]
where the time goes in v4:
time: 527 us; the launch traced here: 521 us
  Pallas kernels  238 us (45%)
  waiting for transfers between devices  184 us (35%)
  starting transfers between devices  60.8 us (12%)
  other arithmetic  22.5 us (4%)
  local copies, waits for them, and re-layouts  12.7 us (2%)
    pallas_call x42, Pallas kernels, call(): pl.pallas_call(body, grid=(1,), in_specs=specs, out_specs=[whole(o) for o...  175 us
    ppermute x83, waiting for transfers between devices, seq_swap(): return lax.ppermute(x, 'seq', [(i, i ^ k) for i in range(n)])  95.8 us
    ppermute x12, waiting for transfers between devices, ring_shift(): lax.ppermute(x, 'batch', [(i, (i + 2) % nb) for i in (range(nb) if active...  57.6 us
    ppermute x83, starting transfers between devices, seq_swap(): return lax.ppermute(x, 'seq', [(i, i ^ k) for i in range(n)])  35.5 us
    ppermute x17, waiting for transfers between devices, batch_swap(): return lax.ppermute(x, 'batch', [(i, i ^ k) for i in range(n)])  30.8 us
    pallas_call x10, Pallas kernels, row_call(): pl.pallas_call(body, grid=(STEPS,), in_specs=[spec(x.shape) for x in ins]...  27 us
    pallas_call x8, Pallas kernels, hop(): pl.pallas_call(functools.partial(hop_body, step, [k.shape[0] for k, _ in...  25.1 us
    ppermute x17, starting transfers between devices, batch_swap(): return lax.ppermute(x, 'batch', [(i, i ^ k) for i in range(n)])  17.6 us
  transfers between devices with their start and end apart: 112, of which 50 were waited for; matrix products, arithmetic and copies ran while one was open for 5% of the time, Pallas kernels for 37%

profile of v4, /device:TPU:0, one launch (start us, length us, event | category | flops | bytes accessed | tf_op | source)
XLA Modules:
  0.0 521.2 jit_solution(350910164524594014)
XLA Ops:
  3.4 2.9 collective-permute-start.1
  7.9 5.6 %collective-permute-done.1.refs_2_ = bf16[2,192,384]{2,1,0:T(8,128)(2,1)S(1)} collective-permute-done((bf16[2,192,384]{2,1,0:T(8,128)(2,1)}, bf16[2,192,384]{2,1,0:T(8,128)(2,1)S(1)}, u32[]{:S(2)}, u32[]{:S(2)}) %collective-permute-start.1) | collective-permute-done | bytes 294944 | tf_op jit(solution)/shard_map/ppermute | solution.py:31
  22.2 11.3 %collective-permute-done.6.refs_2_ = bf16[208,1152]{1,0:T(8,128)(2,1)S(1)} collective-permute-done((bf16[208,1152]{1,0:T(8,128)(2,1)}, bf16[208,1152]{1,0:T(8,128)(2,1)S(1)}, u32[]{:S(2)}, u32[]{:S(2)}) %collective-permute-start.6) | collective-permute-done | bytes 479264 | tf_op jit(solution)/shard_map/ppermute | solution.py:65
  41.9 6.1 %collective-permute-done.8.refs_4_ = bf16[208,1152]{1,0:T(8,128)(2,1)} collective-permute-done((bf16[208,1152]{1,0:T(8,128)(2,1)S(1)}, bf16[208,1152]{1,0:T(8,128)(2,1)}, u32[]{:S(2)}, u32[]{:S(2)}) %collective-permute-start.8) | collective-permute-done | bytes 479264 | tf_op jit(solution)/shard_map/ppermute | solution.py:65
  53.5 6.1 %collective-permute-done.16.refs_3_.d0.refs_6_ = bf16[512,768]{1,0:T(8,128)(2,1)} collective-permute-done((bf16[512,768]{1,0:T(8,128)(2,1)}, bf16[512,768]{1,0:T(8,128)(2,1)}, u32[]{:S(2)}, u32[]{:S(2)}) %collective-permute-start.16) | collective-permute-done | bytes 786464 | tf_op jit(solution)/shard_map/ppermute | solution.py:31
  66.7 10.0 %collective-permute-done.13.refs_7_ = bf16[208,1152]{1,0:T(8,128)(2,1)} collective-permute-done((bf16[208,1152]{1,0:T(8,128)(2,1)}, bf16[208,1152]{1,0:T(8,128)(2,1)}, u32[]{:S(2)}, u32[]{:S(2)}) %collective-permute-start.13) | collective-permute-done | bytes 479264 | tf_op jit(solution)/shard_map/ppermute | solution.py:36
  76.7 4.0 gather_attn_0.1.refs_0_.refs_1_.refs_2_.refs_6_.refs_7_.refs_8_.refs_9_.refs_10_.refs_11_.refs_12_.refs_13_
  80.7 3.0 out_pack.1
  88.2 6.9 %attend_far_0.1 = (bf16[1024,768]{1,0:T(8,128)(2,1)}, bf16[1024,192]{1,0:T(8,128)(2,1)}, bf16[1024,192]{1,0:T(8,128)(2,1)}, bf16[1024,192]{1,0:T(8,128)(2,1)}, f...) custom-call(s32[2]{0:T(128)} %pad_add_fusion.refs_0_.meta, bf16[512,768]{1,0:T(8,128)(2,1)} %pad_maximum_fusion.refs_1_.d0.refs_4_, ...), custom_call_target="tpu_custom_call" | custom-call | flops 9999999827968 | bytes 10000000000 | tf_op jit(solution)/shard_map/attend_far_0/pallas_call | solution.py:307
  95.1 5.2 %attend_near_0.1 = (f32[512,128]{1,0:T(8,128)}, bf16[512,192]{1,0:T(8,128)(2,1)}) custom-call(s32[2]{0:T(128)} %pad_add_fusion.refs_0_.meta, bf16[1024,192]{1,0:T(8,128)(2,1)} %get-tuple-element.524.q_ref.refs_5_, bf16[1024,192]{1,0:T(8,128)(2,1)} %get-tuple-element.351.k_ref.refs_7_, bf16[1024,192]{1,0:T(8,128)(2,1)} %get-tuple-element.352.v_ref.refs_8_), custom_call_target="tpu_custom_call" | custom-call | flops 9999999827968 | bytes 10000000000 | tf_op jit(solution)/shard_map/attend_near_0/pallas_call | solution.py:307
  101.2 4.5 collective-permute-done.18.refs_4_
  118.0 5.0 attend_far_1.1
  123.0 5.3 %collective-permute-done.26.far_ref = bf16[256,768]{1,0:T(8,128)(2,1)} collective-permute-done((bf16[256,768]{1,0:T(8,128)(2,1)}, bf16[256,768]{1,0:T(8,128)(2,1)}, u32[]{:S(2)}, u32[]{:S(2)}) %collective-permute-start.26) | collective-permute-done | bytes 393248 | tf_op jit(solution)/shard_map/ppermute | solution.py:31
  133.9 3.3 attend_near_1.1
  137.2 4.1 gather_feeds_0.1
  144.1 2.9 collective-permute-done.32.refs_1_
  149.5 4.6 enc_feed_far.1
  159.2 4.7 enc_feed_near.1
  166.1 4.1 collective-permute-done.37.far_ref
  170.2 2.8 close_enc_feed.1
  175.1 10.1 %collective-permute-done.42.refs_7_.refs_6_ = bf16[256,768]{1,0:T(8,128)(2,1)S(1)} collective-permute-done((bf16[256,768]{1,0:T(8,128)(2,1)}, bf16[256,768]{1,0:T(8,128)(2,1)S(1)}, u32[]{:S(2)}, u32[]{:S(2)}) %collective-permute-start.42) | collective-permute-done | bytes 393248 | tf_op jit(solution)/shard_map/ppermute | solution.py:31
  185.2 3.8 collective-permute-done.38.refs_3_.refs_2_
  191.9 6.2 %attend_far_2.1 = (bf16[512,192]{1,0:T(8,128)(2,1)}, bf16[1024,192]{1,0:T(8,128)(2,1)}, bf16[1024,192]{1,0:T(8,128)(2,1)}, f32[256,128]{1,0:T(8,128)}, bf16[256,...) custom-call(s32[2]{0:T(128)} %pad_add_fusion.refs_0_.meta, ...), custom_call_target="tpu_custom_call" | custom-call | flops 9999999827968 | bytes 10000000000 | tf_op jit(solution)/shard_map/attend_far_2/pallas_call | solution.py:307
  202.4 3.9 attend_near_2.1
  214.2 6.2 %collective-permute-done.48.x0.refs_2_ = bf16[128,768]{1,0:T(8,128)(2,1)} collective-permute-done((bf16[128,768]{1,0:T(8,128)(2,1)}, bf16[128,768]{1,0:T(8,128)(2,1)}, u32[]{:S(2)}, u32[]{:S(2)}) %collective-permute-start.48) | collective-permute-done | bytes 196640 | tf_op jit(solution)/shard_map/ppermute | solution.py:31
  221.1 5.0 dec_feed_near.1
  226.1 5.0 dec_feed_far.1
  235.5 6.5 %dec_feed_weight.1 = (bf16[2,384,768]{2,1,0:T(8,128)(2,1)}, bf16[2,384,768]{2,1,0:T(8,128)(2,1)}) custom-call(bf16[128,768]{1,0:T(8,128)(2,1)} %get-tuple-element.413.x0.refs_0_, bf16[128,768]{1,0:T(8,128)(2,1)} %copy-done.36, bf16[128,768]{1,0:T(8,128)(2,1)} %collective-permute-done.48.x0.refs_2_, bf16[128,768]{1,0:T(8,128)(2,1)} %collective-permute-done.49.x1.refs_3_, ...), custom_call_target="tpu_custom_call" | custom-call | flops 9999999827968 | bytes 10000000000 | tf_op jit(solution)/shard_map/dec_feed_weight/pallas_call | solution.py:307
  246.2 5.9 %collective-permute-done.54.refs_2_.refs_3_ = bf16[128,768]{1,0:T(8,128)(2,1)S(1)} collective-permute-done((bf16[128,768]{1,0:T(8,128)(2,1)}, bf16[128,768]{1,0:T(8,128)(2,1)S(1)}, u32[]{:S(2)}, u32[]{:S(2)}) %collective-permute-start.54) | collective-permute-done | bytes 196640 | tf_op jit(solution)/shard_map/ppermute | solution.py:31
  259.3 9.9 %attend_back_2.1 = (bf16[512,192]{1,0:T(8,128)(2,1)}, bf16[192,1024]{1,0:T(8,128)(2,1)}, bf16[192,1024]{1,0:T(8,128)(2,1)}, f32[128,768]{1,0:T(8,128)}, bf16[128...) custom-call(s32[2]{0:T(128)} %pad_add_fusion.refs_0_.meta, ...), custom_call_target="tpu_custom_call" | custom-call | flops 9999999827968 | bytes 10000000000 | tf_op jit(solution)/shard_map/attend_back_2/pallas_call | solution.py:307
  274.7 3.9 cross_weights.1
  281.7 3.4 collective-permute-done.64.far_ref
  285.0 3.1 back_encoded.1
  292.3 6.6 %collective-permute-done.69.refs_3_ = bf16[2,384,768]{2,1,0:T(8,128)(2,1)} collective-permute-done((bf16[2,384,768]{2,1,0:T(8,128)(2,1)}, bf16[2,384,768]{2,1,0:T(8,128)(2,1)}, u32[]{:S(2)}, u32[]{:S(2)}) %collective-permute-start.69) | collective-permute-done | bytes 1179680 | tf_op jit(solution)/shard_map/ppermute | solution.py:36
  300.0 5.2 enc_feed_back_near.1
  308.5 5.1 enc_feed_back_far.1
  319.1 7.6 %enc_feed_weight.1 = (bf16[2,384,768]{2,1,0:T(8,128)(2,1)}, bf16[2,384,768]{2,1,0:T(8,128)(2,1)}) custom-call(bf16[256,768]{1,0:T(8,128)(2,1)} %get-tuple-element.387.x0.refs_0_, bf16[256,768]{1,0:T(8,128)(2,1)} %collective-permute-done.29.x1.refs_1_, bf16[256,768]{1,0:T(8,128)(2,1)} %collective-permute-done.27.x0.refs_2_, ...), custom_call_target="tpu_custom_call" | custom-call | flops 9999999827968 | bytes 10000000000 | tf_op jit(solution)/shard_map/enc_feed_weight/pallas_call | solution.py:307
  332.0 4.9 collective-permute-done.77.refs_3_.refs_8_
  336.9 3.3 back_enc_feed.1
  341.5 6.6 %attend_back_1.1 = (bf16[512,192]{1,0:T(8,128)(2,1)}, bf16[192,512]{1,0:T(8,128)(2,1)}, bf16[192,512]{1,0:T(8,128)(2,1)}, f32[128,768]{1,0:T(8,128)}, bf16[128,7...) custom-call(s32[2]{0:T(128)} %pad_add_fusion.1.refs_0_.meta, ...), custom_call_target="tpu_custom_call" | custom-call | flops 9999999827968 | bytes 10000000000 | tf_op jit(solution)/shard_map/attend_back_1/pallas_call | solution.py:307
  348.1 3.9 collective-permute-done.79.refs_2_.refs_3_
  352.1 3.3 self_weights.1
  355.9 3.8 late_out_weight.1
  366.3 14.8 %attend_back_0.1 = (bf16[1024,192]{1,0:T(8,128)(2,1)}, bf16[192,1024]{1,0:T(8,128)(2,1)}, bf16[192,1024]{1,0:T(8,128)(2,1)}, f32[256,768]{1,0:T(8,128)}, bf16[25...) custom-call(s32[2]{0:T(128)} %pad_add_fusion.refs_0_.meta, ...), custom_call_target="tpu_custom_call" | custom-call | flops 9999999827968 | bytes 10000000000 | tf_op jit(solution)/shard_map/attend_back_0/pallas_call | solution.py:307
  382.1 3.9 part_zero.1
  387.5 3.5 feed_hop_2.1
  391.4 3.4 part_middle.1
  400.7 7.4 %collective-permute-done.87.refs_4_ = bf16[384,768]{1,0:T(8,128)(2,1)} collective-permute-done((bf16[384,768]{1,0:T(8,128)(2,1)}, bf16[384,768]{1,0:T(8,128)(2,1)}, u32[]{:S(2)}, u32[]{:S(2)}) %collective-permute-start.87) | collective-permute-done | bytes 589856 | tf_op jit(solution)/shard_map/ppermute | solution.py:65
  408.1 3.3 feed_hop_3.1
  411.8 3.2 back_enc_attn.1
  420.0 3.2 collective-permute-start.96
  423.2 6.7 %collective-permute-done.97.refs_4_ = bf16[384,768]{1,0:T(8,128)(2,1)} collective-permute-done((bf16[384,768]{1,0:T(8,128)(2,1)}, bf16[384,768]{1,0:T(8,128)(2,1)}, u32[]{:S(2)}, u32[]{:S(2)}) %collective-permute-start.97) | collective-permute-done | bytes 589856 | tf_op jit(solution)/shard_map/ppermute | solution.py:65
  429.9 3.6 feed_hop_4.1.total_ref
  438.0 3.1 attn_hop_2.1
  443.8 10.2 %collective-permute-done.98.refs_6_ = bf16[208,1152]{1,0:T(8,128)(2,1)} collective-permute-done((bf16[208,1152]{1,0:T(8,128)(2,1)}, bf16[208,1152]{1,0:T(8,128)(2,1)}, u32[]{:S(2)}, u32[]{:S(2)}) %collective-permute-start.98) | collective-permute-done | bytes 479264 | tf_op jit(solution)/shard_map/ppermute | solution.py:65
  454.0 3.2 attn_hop_3.1
  459.2 3.9 collective-permute-done.101.refs_2_
  463.1 5.9 %collective-permute-done.99.refs_6_ = bf16[208,1152]{1,0:T(8,128)(2,1)S(1)} collective-permute-done((bf16[208,1152]{1,0:T(8,128)(2,1)}, bf16[208,1152]{1,0:T(8,128)(2,1)S(1)}, u32[]{:S(2)}, u32[]{:S(2)}) %collective-permute-start.99) | collective-permute-done | bytes 479264 | tf_op jit(solution)/shard_map/ppermute | solution.py:65
  469.8 3.3 attn_hop_4.1.total_ref
  478.2 3.9 adam_1.1
  482.1 5.7 %collective-permute-done.104.refs_2_ = bf16[2,208,288]{2,1,0:T(8,128)(2,1)} collective-permute-done((bf16[2,208,288]{2,1,0:T(8,128)(2,1)}, bf16[2,208,288]{2,1,0:T(8,128)(2,1)}, u32[]{:S(2)}, u32[]{:S(2)}) %collective-permute-start.104) | collective-permute-done | bytes 239648 | tf_op jit(solution)/shard_map/ppermute | solution.py:31
  493.4 4.1 adam_0.1
  508.2 3.6 collective-permute-done.110
  516.9 4.1 lamb.1
  (349 shorter events, 188.5 us)
Async XLA Ops:
  3.4 10.2 %collective-permute-start.1 = (bf16[2,192,384]{2,1,0:T(8,128)(2,1)}, bf16[2,192,384]{2,1,0:T(8,128)(2,1)S(1)}, u32[]{:S(2)}, u32[]{:S(2)}) collective-permute-start(bf16[2,192,384]{2,1,0:T(8,128)(2,1)} %get-tuple-element.325), channel_id=1, source_target_pairs={{0,2},{1,3},{2,0},{3,1},{4,6},{5,7},{6,4},{7,5},{8,10},{9,11},{10,... | collective-permute-start | bytes 884744 | tf_op jit(solution)/shard_map/ppermute | solution.py:31
  18.2 15.3 %collective-permute-start.6 = (bf16[208,1152]{1,0:T(8,128)(2,1)}, bf16[208,1152]{1,0:T(8,128)(2,1)S(1)}, u32[]{:S(2)}, u32[]{:S(2)}) collective-permute-start(bf16[208,1152]{1,0:T(8,128)(2,1)} %attn_unpack.1.refs_0_), channel_id=1, source_target_pairs={{0,8},{4,12},{8,16},{12,20},{16,24},{20,28},{24,0},{28,4},{1,9},{5... | collective-permute-start | bytes 1437704 | tf_op jit(solution)/shard_map/ppermute | solution.py:65
  20.0 13.5 %collective-permute-start.7 = (bf16[208,1152]{1,0:T(8,128)(2,1)}, bf16[208,1152]{1,0:T(8,128)(2,1)S(1)}, u32[]{:S(2)}, u32[]{:S(2)}) collective-permute-start(bf16[208,1152]{1,0:T(8,128)(2,1)} %attn_unpack.1.refs_0_), channel_id=1, source_target_pairs={{0,4},{4,0},{8,12},{12,8},{16,20},{20,16},{24,28},{28,24},{1,5},{5... | collective-permute-start | bytes 1437704 | tf_op jit(solution)/shard_map/ppermute | solution.py:36
  33.5 14.4 %collective-permute-start.8 = (bf16[208,1152]{1,0:T(8,128)(2,1)S(1)}, bf16[208,1152]{1,0:T(8,128)(2,1)}, u32[]{:S(2)}, u32[]{:S(2)}) collective-permute-start(bf16[208,1152]{1,0:T(8,128)(2,1)S(1)} %collective-permute-done.6.refs_2_), channel_id=1, source_target_pairs={{0,8},{4,12},{8,16},{12,20},{16,24},{20,28},{24,0},{28,4},{1,9},{5... | collective-permute-start | bytes 1437704 | tf_op jit(solution)/shard_map/ppermute | solution.py:65
  34.5 13.4 %collective-permute-start.9 = (bf16[208,1152]{1,0:T(8,128)(2,1)S(1)}, bf16[208,1152]{1,0:T(8,128)(2,1)S(1)}, u32[]{:S(2)}, u32[]{:S(2)}) collective-permute-start(bf16[208,1152]{1,0:T(8,128)(2,1)S(1)} %collective-permute-done.6.refs_2_), channel_id=1, source_target_pairs={{0,4},{4,0},{8,12},{12,8},{16,20},{20,16},{24,28},{28,24},{1,5},{5... | collective-permute-start | bytes 1437704 | tf_op jit(solution)/shard_map/ppermute | solution.py:36
  39.3 14.2 %collective-permute-start.15 = (bf16[512,768]{1,0:T(8,128)(2,1)}, bf16[512,768]{1,0:T(8,128)(2,1)}, u32[]{:S(2)}, u32[]{:S(2)}) collective-permute-start(bf16[512,768]{1,0:T(8,128)(2,1)} %pad_maximum_fusion.refs_1_.d0.refs_4_), channel_id=1, source_target_pairs={{0,1},{1,0},{2,3},{3,2},{4,5},{5,4},{6,7},{7,6},{8,9},{9,8},{10,11... | collective-permute-start | bytes 2359304 | tf_op jit(solution)/shard_map/ppermute | solution.py:31
  39.3 20.3 %collective-permute-start.16 = (bf16[512,768]{1,0:T(8,128)(2,1)}, bf16[512,768]{1,0:T(8,128)(2,1)}, u32[]{:S(2)}, u32[]{:S(2)}) collective-permute-start(bf16[512,768]{1,0:T(8,128)(2,1)} %pad_maximum_fusion.refs_1_.d0.refs_4_), channel_id=1, source_target_pairs={{0,2},{1,3},{2,0},{3,1},{4,6},{5,7},{6,4},{7,5},{8,10},{9,11},{10,... | collective-permute-start | bytes 2359304 | tf_op jit(solution)/shard_map/ppermute | solution.py:31
  41.9 21.6 %collective-permute-start.5 = (bf16[2,96,512]{2,1,0:T(8,128)(2,1)}, bf16[2,96,512]{2,1,0:T(8,128)(2,1)}, u32[]{:S(2)}, u32[]{:S(2)}) collective-permute-start(bf16[2,96,512]{2,1,0:T(8,128)(2,1)} %collective-permute-done.4.refs_2_), channel_id=1, source_target_pairs={{0,1},{1,0},{2,3},{3,2},{4,5},{5,4},{6,7},{7,6},{8,9},{9,8},{10,11... | collective-permute-start | bytes 589832 | tf_op jit(solution)/shard_map/ppermute | solution.py:31
  48.7 13.7 %collective-permute-start.10 = (bf16[208,1152]{1,0:T(8,128)(2,1)}, bf16[208,1152]{1,0:T(8,128)(2,1)}, u32[]{:S(2)}, u32[]{:S(2)}) collective-permute-start(bf16[208,1152]{1,0:T(8,128)(2,1)} %collective-permute-done.8.refs_4_), channel_id=1, source_target_pairs={{0,8},{4,12},{8,16},{12,20},{16,24},{20,28},{24,0},{28,4},{1,9},{5... | collective-permute-start | bytes 1437704 | tf_op jit(solution)/shard_map/ppermute | solution.py:65
  48.7 13.7 %collective-permute-start.12 = (bf16[208,1152]{1,0:T(8,128)(2,1)}, bf16[208,1152]{1,0:T(8,128)(2,1)}, u32[]{:S(2)}, u32[]{:S(2)}) collective-permute-start(bf16[208,1152]{1,0:T(8,128)(2,1)} %collective-permute-done.8.refs_4_), channel_id=1, source_target_pairs={{0,4},{4,0},{8,12},{12,8},{16,20},{20,16},{24,28},{28,24},{1,5},{5... | collective-permute-start | bytes 1437704 | tf_op jit(solution)/shard_map/ppermute | solution.py:36
  59.6 28.6 %collective-permute-start.17 = (bf16[512,768]{1,0:T(8,128)(2,1)}, bf16[512,768]{1,0:T(8,128)(2,1)}, u32[]{:S(2)}, u32[]{:S(2)}) collective-permute-start(bf16[512,768]{1,0:T(8,128)(2,1)} %collective-permute-done.16.refs_3_.d0.refs_6_), channel_id=1, source_target_pairs={{0,1},{1,0},{2,3},{3,2},{4,5},{5,4},{6,7},{7,6},{8,9},{9,8},{10,11... | collective-permute-start | bytes 2359304 | tf_op jit(solution)/shard_map/ppermute | solution.py:31
  62.4 14.2 %collective-permute-start.13 = (bf16[208,1152]{1,0:T(8,128)(2,1)}, bf16[208,1152]{1,0:T(8,128)(2,1)}, u32[]{:S(2)}, u32[]{:S(2)}) collective-permute-start(bf16[208,1152]{1,0:T(8,128)(2,1)} %collective-permute-done.10.refs_6_), channel_id=1, source_target_pairs={{0,4},{4,0},{8,12},{12,8},{16,20},{20,16},{24,28},{28,24},{1,5},{5... | collective-permute-start | bytes 1437704 | tf_op jit(solution)/shard_map/ppermute | solution.py:36
  65.6 20.8 %collective-permute-start.11 = (bf16[384,768]{1,0:T(8,128)(2,1)}, bf16[384,768]{1,0:T(8,128)(2,1)}, u32[]{:S(2)}, u32[]{:S(2)}) collective-permute-start(bf16[384,768]{1,0:T(8,128)(2,1)} %feeds_unpack.1.refs_0_), channel_id=1, source_target_pairs={{0,8},{4,12},{8,16},{12,20},{16,24},{20,28},{24,0},{28,4},{1,9},{5... | collective-permute-start | bytes 1769480 | tf_op jit(solution)/shard_map/ppermute | solution.py:65
  65.6 22.4 %collective-permute-start.14 = (bf16[384,768]{1,0:T(8,128)(2,1)}, bf16[384,768]{1,0:T(8,128)(2,1)}, u32[]{:S(2)}, u32[]{:S(2)}) collective-permute-start(bf16[384,768]{1,0:T(8,128)(2,1)} %feeds_unpack.1.refs_0_), channel_id=1, source_target_pairs={{0,4},{4,0},{8,12},{12,8},{16,20},{20,16},{24,28},{28,24},{1,5},{5... | collective-permute-start | bytes 1769480 | tf_op jit(solution)/shard_map/ppermute | solution.py:36
  84.9 15.5 %collective-permute-start.19 = (bf16[2,3,192,192]{3,2,1,0:T(8,128)(2,1)}, bf16[2,3,192,192]{3,2,1,0:T(8,128)(2,1)}, u32[]{:S(2)}, u32[]{:S(2)}) collective-permute-start(bf16[2,3,192,192]{3,2,1,0:T(8,128)(2,1)} %get-tuple-element.354), channel_id=1, source_target_pairs={{0,2},{1,3},{2,0},{3,1},{4,6},{5,7},{6,4},{7,5},{8,10},{9,11},{10,... | collective-permute-start | bytes 1327112 | tf_op jit(solution)/shard_map/ppermute | solution.py:31
  85.8 14.5 %collective-permute-start.21 = (bf16[3,192,192]{2,1,0:T(8,128)(2,1)}, bf16[3,192,192]{2,1,0:T(8,128)(2,1)}, u32[]{:S(2)}, u32[]{:S(2)}) collective-permute-start(bf16[3,192,192]{2,1,0:T(8,128)(2,1)} %get-tuple-element.342), channel_id=1, source_target_pairs={{0,1},{1,0},{2,3},{3,2},{4,5},{5,4},{6,7},{7,6},{8,9},{9,8},{10,11... | collective-permute-start | bytes 663560 | tf_op jit(solution)/shard_map/ppermute | solution.py:31
  86.5 19.8 %collective-permute-start.20 = (bf16[384,768]{1,0:T(8,128)(2,1)}, bf16[384,768]{1,0:T(8,128)(2,1)}, u32[]{:S(2)}, u32[]{:S(2)}) collective-permute-start(bf16[384,768]{1,0:T(8,128)(2,1)} %collective-permute-done.11.refs_2_), channel_id=1, source_target_pairs={{0,4},{4,0},{8,12},{12,8},{16,20},{20,16},{24,28},{28,24},{1,5},{5... | collective-permute-start | bytes 1769480 | tf_op jit(solution)/shard_map/ppermute | solution.py:36
  88.1 17.7 %collective-permute-start.18 = (bf16[384,768]{1,0:T(8,128)(2,1)}, bf16[384,768]{1,0:T(8,128)(2,1)}, u32[]{:S(2)}, u32[]{:S(2)}) collective-permute-start(bf16[384,768]{1,0:T(8,128)(2,1)} %collective-permute-done.11.refs_2_), channel_id=1, source_target_pairs={{0,8},{4,12},{8,16},{12,20},{16,24},{20,28},{24,0},{28,4},{1,9},{5... | collective-permute-start | bytes 1769480 | tf_op jit(solution)/shard_map/ppermute | solution.py:65
  105.8 25.2 %collective-permute-start.31 = (bf16[384,768]{1,0:T(8,128)(2,1)}, bf16[384,768]{1,0:T(8,128)(2,1)}, u32[]{:S(2)}, u32[]{:S(2)}) collective-permute-start(bf16[384,768]{1,0:T(8,128)(2,1)} %collective-permute-done.18.refs_4_), channel_id=1, source_target_pairs={{0,4},{4,0},{8,12},{12,8},{16,20},{20,16},{24,28},{28,24},{1,5},{5... | collective-permute-start | bytes 1769480 | tf_op jit(solution)/shard_map/ppermute | solution.py:36
  106.3 16.7 %collective-permute-start.24 = (bf16[384,768]{1,0:T(8,128)(2,1)}, bf16[384,768]{1,0:T(8,128)(2,1)}, u32[]{:S(2)}, u32[]{:S(2)}) collective-permute-start(bf16[384,768]{1,0:T(8,128)(2,1)} %collective-permute-done.18.refs_4_), channel_id=1, source_target_pairs={{0,8},{4,12},{8,16},{12,20},{16,24},{20,28},{24,0},{28,4},{1,9},{5... | collective-permute-start | bytes 1769480 | tf_op jit(solution)/shard_map/ppermute | solution.py:65
  116.9 11.3 %collective-permute-start.26 = (bf16[256,768]{1,0:T(8,128)(2,1)}, bf16[256,768]{1,0:T(8,128)(2,1)}, u32[]{:S(2)}, u32[]{:S(2)}) collective-permute-start(bf16[256,768]{1,0:T(8,128)(2,1)} %add_convert_fusion.4), channel_id=1, source_target_pairs={{0,2},{1,3},{2,0},{3,1},{4,6},{5,7},{6,4},{7,5},{8,10},{9,11},{10,... | collective-permute-start | bytes 1179656 | tf_op jit(solution)/shard_map/ppermute | solution.py:31
  131.0 16.1 %collective-permute-start.32 = (bf16[384,768]{1,0:T(8,128)(2,1)}, bf16[384,768]{1,0:T(8,128)(2,1)}, u32[]{:S(2)}, u32[]{:S(2)}) collective-permute-start(bf16[384,768]{1,0:T(8,128)(2,1)} %collective-permute-done.24.refs_0_), channel_id=1, source_target_pairs={{0,4},{4,0},{8,12},{12,8},{16,20},{20,16},{24,28},{28,24},{1,5},{5... | collective-permute-start | bytes 1769480 | tf_op jit(solution)/shard_map/ppermute | solution.py:36
  132.6 11.5 %collective-permute-start.27 = (bf16[256,768]{1,0:T(8,128)(2,1)}, bf16[256,768]{1,0:T(8,128)(2,1)}, u32[]{:S(2)}, u32[]{:S(2)}) collective-permute-start(bf16[256,768]{1,0:T(8,128)(2,1)} %get-tuple-element.387.x0.refs_0_), channel_id=1, source_target_pairs={{0,2},{1,3},{2,0},{3,1},{4,6},{5,7},{6,4},{7,5},{8,10},{9,11},{10,... | collective-permute-start | bytes 1179656 | tf_op jit(solution)/shard_map/ppermute | solution.py:31
  133.1 11.0 %collective-permute-start.29 = (bf16[256,768]{1,0:T(8,128)(2,1)}, bf16[256,768]{1,0:T(8,128)(2,1)}, u32[]{:S(2)}, u32[]{:S(2)}) collective-permute-start(bf16[256,768]{1,0:T(8,128)(2,1)} %get-tuple-element.387.x0.refs_0_), channel_id=1, source_target_pairs={{0,1},{1,0},{2,3},{3,2},{4,5},{5,4},{6,7},{7,6},{8,9},{9,8},{10,11... | collective-permute-start | bytes 1179656 | tf_op jit(solution)/shard_map/ppermute | solution.py:31
  154.1 9.8 %collective-permute-start.34 = (bf16[128,768]{1,0:T(8,128)(2,1)}, bf16[128,768]{1,0:T(8,128)(2,1)}, u32[]{:S(2)}, u32[]{:S(2)}) collective-permute-start(bf16[128,768]{1,0:T(8,128)(2,1)} %get-tuple-element.376), channel_id=1, source_target_pairs={{0,1},{1,0},{2,3},{3,2},{4,5},{5,4},{6,7},{7,6},{8,9},{9,8},{10,11... | collective-permute-start | bytes 589832 | tf_op jit(solution)/shard_map/ppermute | solution.py:31
  154.6 9.3 %collective-permute-start.35 = (bf16[128,768]{1,0:T(8,128)(2,1)}, bf16[128,768]{1,0:T(8,128)(2,1)}, u32[]{:S(2)}, u32[]{:S(2)}) collective-permute-start(bf16[128,768]{1,0:T(8,128)(2,1)} %add_convert_fusion.11), channel_id=1, source_target_pairs={{0,2},{1,3},{2,0},{3,1},{4,6},{5,7},{6,4},{7,5},{8,10},{9,11},{10,... | collective-permute-start | bytes 589832 | tf_op jit(solution)/shard_map/ppermute | solution.py:31
  158.2 12.0 %collective-permute-start.37 = (bf16[256,768]{1,0:T(8,128)(2,1)}, bf16[256,768]{1,0:T(8,128)(2,1)}, u32[]{:S(2)}, u32[]{:S(2)}) collective-permute-start(bf16[256,768]{1,0:T(8,128)(2,1)} %add_convert_fusion.3), channel_id=1, source_target_pairs={{0,2},{1,3},{2,0},{3,1},{4,6},{5,7},{6,4},{7,5},{8,10},{9,11},{10,... | collective-permute-start | bytes 1179656 | tf_op jit(solution)/shard_map/ppermute | solution.py:31
  173.0 12.1 %collective-permute-start.42 = (bf16[256,768]{1,0:T(8,128)(2,1)}, bf16[256,768]{1,0:T(8,128)(2,1)S(1)}, u32[]{:S(2)}, u32[]{:S(2)}) collective-permute-start(bf16[256,768]{1,0:T(8,128)(2,1)} %get-tuple-element.395.refs_5_.refs_4_), channel_id=1, source_target_pairs={{0,2},{1,3},{2,0},{3,1},{4,6},{5,7},{6,4},{7,5},{8,10},{9,11},{10,... | collective-permute-start | bytes 1179656 | tf_op jit(solution)/shard_map/ppermute | solution.py:31
  174.1 14.9 %collective-permute-start.38 = (bf16[128,768]{1,0:T(8,128)(2,1)S(1)}, bf16[128,768]{1,0:T(8,128)(2,1)S(1)}, u32[]{:S(2)}, u32[]{:S(2)}) collective-permute-start(bf16[128,768]{1,0:T(8,128)(2,1)S(1)} %copy-done.27), channel_id=1, source_target_pairs={{0,2},{1,3},{2,0},{3,1},{4,6},{5,7},{6,4},{7,5},{8,10},{9,11},{10,... | collective-permute-start | bytes 589832 | tf_op jit(solution)/shard_map/ppermute | solution.py:31
  175.1 13.9 %collective-permute-start.39 = (bf16[128,768]{1,0:T(8,128)(2,1)S(1)}, bf16[128,768]{1,0:T(8,128)(2,1)S(1)}, u32[]{:S(2)}, u32[]{:S(2)}) collective-permute-start(bf16[128,768]{1,0:T(8,128)(2,1)S(1)} %copy-done.27), channel_id=1, source_target_pairs={{0,1},{1,0},{2,3},{3,2},{4,5},{5,4},{6,7},{7,6},{8,9},{9,8},{10,11... | collective-permute-start | bytes 589832 | tf_op jit(solution)/shard_map/ppermute | solution.py:31
  231.1 11.0 %collective-permute-start.51 = (bf16[128,768]{1,0:T(8,128)(2,1)}, bf16[128,768]{1,0:T(8,128)(2,1)}, u32[]{:S(2)}, u32[]{:S(2)}) collective-permute-start(bf16[128,768]{1,0:T(8,128)(2,1)} %get-tuple-element.419), channel_id=1, source_target_pairs={{0,1},{1,0},{2,3},{3,2},{4,5},{5,4},{6,7},{7,6},{8,9},{9,8},{10,11... | collective-permute-start | bytes 589832 | tf_op jit(solution)/shard_map/ppermute | solution.py:31
  257.0 12.1 %collective-permute-start.58 = (bf16[128,768]{1,0:T(8,128)(2,1)}, bf16[128,768]{1,0:T(8,128)(2,1)}, u32[]{:S(2)}, u32[]{:S(2)}) collective-permute-start(bf16[128,768]{1,0:T(8,128)(2,1)} %add_convert_fusion.8), channel_id=1, source_target_pairs={{0,2},{1,3},{2,0},{3,1},{4,6},{5,7},{6,4},{7,5},{8,10},{9,11},{10,... | collective-permute-start | bytes 589832 | tf_op jit(solution)/shard_map/ppermute | solution.py:31
  258.0 11.2 %collective-permute-start.57 = (bf16[128,768]{1,0:T(8,128)(2,1)}, bf16[128,768]{1,0:T(8,128)(2,1)}, u32[]{:S(2)}, u32[]{:S(2)}) collective-permute-start(bf16[128,768]{1,0:T(8,128)(2,1)} %get-tuple-element.440), channel_id=1, source_target_pairs={{0,1},{1,0},{2,3},{3,2},{4,5},{5,4},{6,7},{7,6},{8,9},{9,8},{10,11... | collective-permute-start | bytes 589832 | tf_op jit(solution)/shard_map/ppermute | solution.py:31
  258.2 10.9 %collective-permute-start.59 = (bf16[2,1,192,192]{3,2,1,0:T(8,128)(2,1)}, bf16[2,1,192,192]{3,2,1,0:T(8,128)(2,1)}, u32[]{:S(2)}, u32[]{:S(2)}) collective-permute-start(bf16[2,1,192,192]{3,2,1,0:T(8,128)(2,1)} %get-tuple-element.450), channel_id=1, source_target_pairs={{0,2},{1,3},{2,0},{3,1},{4,6},{5,7},{6,4},{7,5},{8,10},{9,11},{10,... | collective-permute-start | bytes 442376 | tf_op jit(solution)/shard_map/ppermute | solution.py:31
  269.8 29.1 %collective-permute-start.69 = (bf16[2,384,768]{2,1,0:T(8,128)(2,1)}, bf16[2,384,768]{2,1,0:T(8,128)(2,1)}, u32[]{:S(2)}, u32[]{:S(2)}) collective-permute-start(bf16[2,384,768]{2,1,0:T(8,128)(2,1)} %get-tuple-element.429), channel_id=1, source_target_pairs={{0,4},{4,0},{8,12},{12,8},{16,20},{20,16},{24,28},{28,24},{1,5},{5... | collective-permute-start | bytes 3538952 | tf_op jit(solution)/shard_map/ppermute | solution.py:36
  273.6 11.5 %collective-permute-start.64 = (bf16[256,768]{1,0:T(8,128)(2,1)}, bf16[256,768]{1,0:T(8,128)(2,1)}, u32[]{:S(2)}, u32[]{:S(2)}) collective-permute-start(bf16[256,768]{1,0:T(8,128)(2,1)} %add_convert_fusion.2), channel_id=1, source_target_pairs={{0,2},{1,3},{2,0},{3,1},{4,6},{5,7},{6,4},{7,5},{8,10},{9,11},{10,... | collective-permute-start | bytes 1179656 | tf_op jit(solution)/shard_map/ppermute | solution.py:31
  281.2 9.4 %collective-permute-start.68 = (bf16[128,768]{1,0:T(8,128)(2,1)}, bf16[128,768]{1,0:T(8,128)(2,1)}, u32[]{:S(2)}, u32[]{:S(2)}) collective-permute-start(bf16[128,768]{1,0:T(8,128)(2,1)} %get-tuple-element.470), channel_id=1, source_target_pairs={{0,1},{1,0},{2,3},{3,2},{4,5},{5,4},{6,7},{7,6},{8,9},{9,8},{10,11... | collective-permute-start | bytes 589832 | tf_op jit(solution)/shard_map/ppermute | solution.py:31
  288.1 10.8 %collective-permute-start.65 = (bf16[256,768]{1,0:T(8,128)(2,1)}, bf16[256,768]{1,0:T(8,128)(2,1)S(1)}, u32[]{:S(2)}, u32[]{:S(2)}) collective-permute-start(bf16[256,768]{1,0:T(8,128)(2,1)} %get-tuple-element.465.d0.refs_4_), channel_id=1, source_target_pairs={{0,1},{1,0},{2,3},{3,2},{4,5},{5,4},{6,7},{7,6},{8,9},{9,8},{10,11... | collective-permute-start | bytes 1179656 | tf_op jit(solution)/shard_map/ppermute | solution.py:31
  288.1 11.8 %collective-permute-start.66 = (bf16[256,768]{1,0:T(8,128)(2,1)}, bf16[256,768]{1,0:T(8,128)(2,1)}, u32[]{:S(2)}, u32[]{:S(2)}) collective-permute-start(bf16[256,768]{1,0:T(8,128)(2,1)} %get-tuple-element.465.d0.refs_4_), channel_id=1, source_target_pairs={{0,2},{1,3},{2,0},{3,1},{4,6},{5,7},{6,4},{7,5},{8,10},{9,11},{10,... | collective-permute-start | bytes 1179656 | tf_op jit(solution)/shard_map/ppermute | solution.py:31
  289.1 18.4 %collective-permute-start.70 = (bf16[1,192,1152]{2,1,0:T(8,128)(2,1)}, bf16[1,192,1152]{2,1,0:T(8,128)(2,1)}, u32[]{:S(2)}, u32[]{:S(2)}) collective-permute-start(bf16[1,192,1152]{2,1,0:T(8,128)(2,1)} %get-tuple-element.460), channel_id=1, source_target_pairs={{0,4},{4,0},{8,12},{12,8},{16,20},{20,16},{24,28},{28,24},{1,5},{5... | collective-permute-start | bytes 1327112 | tf_op jit(solution)/shard_map/ppermute | solution.py:36
  313.9 12.9 %collective-permute-start.73 = (bf16[128,768]{1,0:T(8,128)(2,1)}, bf16[128,768]{1,0:T(8,128)(2,1)}, u32[]{:S(2)}, u32[]{:S(2)}) collective-permute-start(bf16[128,768]{1,0:T(8,128)(2,1)} %get-tuple-element.495), channel_id=1, source_target_pairs={{0,1},{1,0},{2,3},{3,2},{4,5},{5,4},{6,7},{7,6},{8,9},{9,8},{10,11... | collective-permute-start | bytes 589832 | tf_op jit(solution)/shard_map/ppermute | solution.py:31
  314.4 22.5 %collective-permute-start.74 = (bf16[256,768]{1,0:T(8,128)(2,1)}, bf16[256,768]{1,0:T(8,128)(2,1)}, u32[]{:S(2)}, u32[]{:S(2)}) collective-permute-start(bf16[256,768]{1,0:T(8,128)(2,1)} %get-tuple-element.476), channel_id=1, source_target_pairs={{0,1},{1,0},{2,3},{3,2},{4,5},{5,4},{6,7},{7,6},{8,9},{9,8},{10,11... | collective-permute-start | bytes 1179656 | tf_op jit(solution)/shard_map/ppermute | solution.py:31
  318.2 18.7 %collective-permute-start.75 = (bf16[256,768]{1,0:T(8,128)(2,1)}, bf16[256,768]{1,0:T(8,128)(2,1)}, u32[]{:S(2)}, u32[]{:S(2)}) collective-permute-start(bf16[256,768]{1,0:T(8,128)(2,1)} %add_convert_fusion.1), channel_id=1, source_target_pairs={{0,2},{1,3},{2,0},{3,1},{4,6},{5,7},{6,4},{7,5},{8,10},{9,11},{10,... | collective-permute-start | bytes 1179656 | tf_op jit(solution)/shard_map/ppermute | solution.py:31
  331.3 30.0 %collective-permute-start.83 = (bf16[2,384,768]{2,1,0:T(8,128)(2,1)}, bf16[2,384,768]{2,1,0:T(8,128)(2,1)}, u32[]{:S(2)}, u32[]{:S(2)}) collective-permute-start(bf16[2,384,768]{2,1,0:T(8,128)(2,1)} %get-tuple-element.492), channel_id=1, source_target_pairs={{0,4},{4,0},{8,12},{12,8},{16,20},{20,16},{24,28},{28,24},{1,5},{5... | collective-permute-start | bytes 3538952 | tf_op jit(solution)/shard_map/ppermute | solution.py:36
  340.2 11.8 %collective-permute-start.79 = (bf16[256,768]{1,0:T(8,128)(2,1)}, bf16[256,768]{1,0:T(8,128)(2,1)}, u32[]{:S(2)}, u32[]{:S(2)}) collective-permute-start(bf16[256,768]{1,0:T(8,128)(2,1)} %get-tuple-element.500.refs_0_.refs_1_), channel_id=1, source_target_pairs={{0,2},{1,3},{2,0},{3,1},{4,6},{5,7},{6,4},{7,5},{8,10},{9,11},{10,... | collective-permute-start | bytes 1179656 | tf_op jit(solution)/shard_map/ppermute | solution.py:31
  341.3 10.8 %collective-permute-start.81 = (bf16[256,768]{1,0:T(8,128)(2,1)}, bf16[256,768]{1,0:T(8,128)(2,1)}, u32[]{:S(2)}, u32[]{:S(2)}) collective-permute-start(bf16[256,768]{1,0:T(8,128)(2,1)} %get-tuple-element.500.refs_0_.refs_1_), channel_id=1, source_target_pairs={{0,1},{1,0},{2,3},{3,2},{4,5},{5,4},{6,7},{7,6},{8,9},{9,8},{10,11... | collective-permute-start | bytes 1179656 | tf_op jit(solution)/shard_map/ppermute | solution.py:31
  355.9 42.4 %collective-permute-start.91 = (bf16[128,768]{1,0:T(8,128)(2,1)}, bf16[128,768]{1,0:T(8,128)(2,1)}, u32[]{:S(2)}, u32[]{:S(2)}) collective-permute-start(bf16[128,768]{1,0:T(8,128)(2,1)} %get-tuple-element.548), channel_id=1, source_target_pairs={{0,1},{1,0},{2,3},{3,2},{4,5},{5,4},{6,7},{7,6},{8,9},{9,8},{10,11... | collective-permute-start | bytes 589832 | tf_op jit(solution)/shard_map/ppermute | solution.py:31
  363.5 18.5 %collective-permute-start.84 = (bf16[384,768]{1,0:T(8,128)(2,1)}, bf16[384,768]{1,0:T(8,128)(2,1)}, u32[]{:S(2)}, u32[]{:S(2)}) collective-permute-start(bf16[384,768]{1,0:T(8,128)(2,1)} %feed_hop_1.1), channel_id=1, source_target_pairs={{0,8},{4,12},{8,16},{12,20},{16,24},{20,28},{24,0},{28,4},{1,9},{5... | collective-permute-start | bytes 1769480 | tf_op jit(solution)/shard_map/ppermute | solution.py:65
  364.0 17.7 %collective-permute-start.85 = (bf16[128,768]{1,0:T(8,128)(2,1)}, bf16[128,768]{1,0:T(8,128)(2,1)}, u32[]{:S(2)}, u32[]{:S(2)}) collective-permute-start(bf16[128,768]{1,0:T(8,128)(2,1)} %add_convert_fusion.5), channel_id=1, source_target_pairs={{0,2},{1,3},{2,0},{3,1},{4,6},{5,7},{6,4},{7,5},{8,10},{9,11},{10,... | collective-permute-start | bytes 589832 | tf_op jit(solution)/shard_map/ppermute | solution.py:31
  365.2 16.0 %collective-permute-start.88 = (bf16[2,192,192]{2,1,0:T(8,128)(2,1)}, bf16[2,192,192]{2,1,0:T(8,128)(2,1)}, u32[]{:S(2)}, u32[]{:S(2)}) collective-permute-start(bf16[2,192,192]{2,1,0:T(8,128)(2,1)} %get-tuple-element.518), channel_id=1, source_target_pairs={{0,1},{1,0},{2,3},{3,2},{4,5},{5,4},{6,7},{7,6},{8,9},{9,8},{10,11... | collective-permute-start | bytes 442376 | tf_op jit(solution)/shard_map/ppermute | solution.py:31
  365.4 15.9 %collective-permute-start.86 = (bf16[2,2,192,192]{3,2,1,0:T(8,128)(2,1)}, bf16[2,2,192,192]{3,2,1,0:T(8,128)(2,1)}, u32[]{:S(2)}, u32[]{:S(2)}) collective-permute-start(bf16[2,2,192,192]{3,2,1,0:T(8,128)(2,1)} %get-tuple-element.531), channel_id=1, source_target_pairs={{0,2},{1,3},{2,0},{3,1},{4,6},{5,7},{6,4},{7,5},{8,10},{9,11},{10,... | collective-permute-start | bytes 884744 | tf_op jit(solution)/shard_map/ppermute | solution.py:31
  381.1 14.2 %collective-permute-start.90 = (bf16[256,768]{1,0:T(8,128)(2,1)}, bf16[256,768]{1,0:T(8,128)(2,1)}, u32[]{:S(2)}, u32[]{:S(2)}) collective-permute-start(bf16[256,768]{1,0:T(8,128)(2,1)} %get-tuple-element.530), channel_id=1, source_target_pairs={{0,1},{1,0},{2,3},{3,2},{4,5},{5,4},{6,7},{7,6},{8,9},{9,8},{10,11... | collective-permute-start | bytes 1179656 | tf_op jit(solution)/shard_map/ppermute | solution.py:31
  381.2 10.2 %collective-permute-start.89 = (bf16[2,2,192,192]{3,2,1,0:T(8,128)(2,1)}, bf16[2,2,192,192]{3,2,1,0:T(8,128)(2,1)}, u32[]{:S(2)}, u32[]{:S(2)}) collective-permute-start(bf16[2,2,192,192]{3,2,1,0:T(8,128)(2,1)} %collective-permute-done.86.refs_2_), channel_id=1, source_target_pairs={{0,1},{1,0},{2,3},{3,2},{4,5},{5,4},{6,7},{7,6},{8,9},{9,8},{10,11... | collective-permute-start | bytes 884744 | tf_op jit(solution)/shard_map/ppermute | solution.py:31
  385.9 30.5 %collective-permute-start.94 = (bf16[1,192,1152]{2,1,0:T(8,128)(2,1)}, bf16[1,192,1152]{2,1,0:T(8,128)(2,1)}, u32[]{:S(2)}, u32[]{:S(2)}) collective-permute-start(bf16[1,192,1152]{2,1,0:T(8,128)(2,1)} %get-tuple-element.535), channel_id=1, source_target_pairs={{0,4},{4,0},{8,12},{12,8},{16,20},{20,16},{24,28},{28,24},{1,5},{5... | collective-permute-start | bytes 1327112 | tf_op jit(solution)/shard_map/ppermute | solution.py:36
  391.1 17.1 %collective-permute-start.87 = (bf16[384,768]{1,0:T(8,128)(2,1)}, bf16[384,768]{1,0:T(8,128)(2,1)}, u32[]{:S(2)}, u32[]{:S(2)}) collective-permute-start(bf16[384,768]{1,0:T(8,128)(2,1)} %feed_hop_2.1), channel_id=1, source_target_pairs={{0,8},{4,12},{8,16},{12,20},{16,24},{20,28},{24,0},{28,4},{1,9},{5... | collective-permute-start | bytes 1769480 | tf_op jit(solution)/shard_map/ppermute | solution.py:65
  394.9 22.3 %collective-permute-start.95 = (bf16[2,192,1152]{2,1,0:T(8,128)(2,1)}, bf16[2,192,1152]{2,1,0:T(8,128)(2,1)}, u32[]{:S(2)}, u32[]{:S(2)}) collective-permute-start(bf16[2,192,1152]{2,1,0:T(8,128)(2,1)} %get-tuple-element.544), channel_id=1, source_target_pairs={{0,4},{4,0},{8,12},{12,8},{16,20},{20,16},{24,28},{28,24},{1,5},{5... | collective-permute-start | bytes 2654216 | tf_op jit(solution)/shard_map/ppermute | solution.py:36
  397.2 14.6 %collective-permute-start.93 = (bf16[256,768]{1,0:T(8,128)(2,1)}, bf16[256,768]{1,0:T(8,128)(2,1)}, u32[]{:S(2)}, u32[]{:S(2)}) collective-permute-start(bf16[256,768]{1,0:T(8,128)(2,1)} %add_convert_fusion), channel_id=1, source_target_pairs={{0,2},{1,3},{2,0},{3,1},{4,6},{5,7},{6,4},{7,5},{8,10},{9,11},{10,... | collective-permute-start | bytes 1179656 | tf_op jit(solution)/shard_map/ppermute | solution.py:31
  398.3 13.5 %collective-permute-start.92 = (bf16[256,768]{1,0:T(8,128)(2,1)}, bf16[256,768]{1,0:T(8,128)(2,1)}, u32[]{:S(2)}, u32[]{:S(2)}) collective-permute-start(bf16[256,768]{1,0:T(8,128)(2,1)} %get-tuple-element.554), channel_id=1, source_target_pairs={{0,1},{1,0},{2,3},{3,2},{4,5},{5,4},{6,7},{7,6},{8,9},{9,8},{10,11... | collective-permute-start | bytes 1179656 | tf_op jit(solution)/shard_map/ppermute | solution.py:31
  411.5 18.4 %collective-permute-start.97 = (bf16[384,768]{1,0:T(8,128)(2,1)}, bf16[384,768]{1,0:T(8,128)(2,1)}, u32[]{:S(2)}, u32[]{:S(2)}) collective-permute-start(bf16[384,768]{1,0:T(8,128)(2,1)} %feed_hop_3.1), channel_id=1, source_target_pairs={{0,8},{4,12},{8,16},{12,20},{16,24},{20,28},{24,0},{28,4},{1,9},{5... | collective-permute-start | bytes 1769480 | tf_op jit(solution)/shard_map/ppermute | solution.py:65
  420.0 18.0 %collective-permute-start.96 = (bf16[208,1152]{1,0:T(8,128)(2,1)}, bf16[208,1152]{1,0:T(8,128)(2,1)}, u32[]{:S(2)}, u32[]{:S(2)}) collective-permute-start(bf16[208,1152]{1,0:T(8,128)(2,1)} %attn_hop_1.1), channel_id=1, source_target_pairs={{0,8},{4,12},{8,16},{12,20},{16,24},{20,28},{24,0},{28,4},{1,9},{5... | collective-permute-start | bytes 1437704 | tf_op jit(solution)/shard_map/ppermute | solution.py:65
  441.1 12.9 %collective-permute-start.98 = (bf16[208,1152]{1,0:T(8,128)(2,1)}, bf16[208,1152]{1,0:T(8,128)(2,1)}, u32[]{:S(2)}, u32[]{:S(2)}) collective-permute-start(bf16[208,1152]{1,0:T(8,128)(2,1)} %attn_hop_2.1), channel_id=1, source_target_pairs={{0,8},{4,12},{8,16},{12,20},{16,24},{20,28},{24,0},{28,4},{1,9},{5... | collective-permute-start | bytes 1437704 | tf_op jit(solution)/shard_map/ppermute | solution.py:65
  457.2 11.9 %collective-permute-start.99 = (bf16[208,1152]{1,0:T(8,128)(2,1)}, bf16[208,1152]{1,0:T(8,128)(2,1)S(1)}, u32[]{:S(2)}, u32[]{:S(2)}) collective-permute-start(bf16[208,1152]{1,0:T(8,128)(2,1)} %attn_hop_3.1), channel_id=1, source_target_pairs={{0,8},{4,12},{8,16},{12,20},{16,24},{20,28},{24,0},{28,4},{1,9},{5... | collective-permute-start | bytes 1437704 | tf_op jit(solution)/shard_map/ppermute | solution.py:65
  463.1 12.3 %collective-permute-start.102 = (bf16[2,96,512]{2,1,0:T(8,128)(2,1)}, bf16[2,96,512]{2,1,0:T(8,128)(2,1)}, u32[]{:S(2)}, u32[]{:S(2)}) collective-permute-start(bf16[2,96,512]{2,1,0:T(8,128)(2,1)} %collective-permute-done.101.refs_2_), channel_id=1, source_target_pairs={{0,1},{1,0},{2,3},{3,2},{4,5},{5,4},{6,7},{7,6},{8,9},{9,8},{10,11... | collective-permute-start | bytes 589832 | tf_op jit(solution)/shard_map/ppermute | solution.py:31
  477.5 10.3 %collective-permute-start.104 = (bf16[2,208,288]{2,1,0:T(8,128)(2,1)}, bf16[2,208,288]{2,1,0:T(8,128)(2,1)}, u32[]{:S(2)}, u32[]{:S(2)}) collective-permute-start(bf16[2,208,288]{2,1,0:T(8,128)(2,1)} %get-tuple-element.586), channel_id=1, source_target_pairs={{0,2},{1,3},{2,0},{3,1},{4,6},{5,7},{6,4},{7,5},{8,10},{9,11},{10,... | collective-permute-start | bytes 718856 | tf_op jit(solution)/shard_map/ppermute | solution.py:31
  (96 other events, 540.3 us)
